TPU v7x, 128 devices: a whole 4x4x4 slice. The times are simulated.
128 devices in a mesh: section: 2 (over core), dp: 16 (over z, x), mp: 4 (over y).
Axes of the slice: x: 4, y: 4, z: 4, core: 2. Of those that a mesh axis runs over, the one named last changes fastest.
Arguments:
- states: bfloat16 [2, 2048, 4096], P('section', 'dp'), may hold values from -6 to 6
- gains: float32 [2, 4096], P('section'), may hold values from 0.25 to 1.75
- proj_a: bfloat16 [2, 4096, 4096], P('section', None, 'mp'), may hold values from -0.03125 to 0.03125
- proj_b: bfloat16 [2, 4096, 4096], P('section', None, 'mp'), may hold values from -0.09375 to 0.09375
- cotangent: bfloat16 [2048, 4096], P('dp'), may hold values from -12 to 12
- src_len: int32 [16, 16], replicated, may hold values from 1 to 16, 128 in all within a row
- tgt_len: int32 [16, 16], replicated, may hold values from 1 to 16, 128 in all within a row
- dest: int32 [16, 16], replicated, may hold values from 0 to 255, as said below
Outputs:
- grad_states: bfloat16 [2, 2048, 4096], P('section', 'dp')
- grad_a: float32 [2, 4096, 4096], P('section', 'dp', 'mp')
- grad_b: float32 [2, 4096, 4096], P('section', 'dp', 'mp')
Inputs may be any that keep to these rules, and one draw needn't show every extreme that they name: `src_len`: each row sums to 128. `tgt_len`: each row sums to 128. `dest`: every value from 0 to 255 appears once; each row holds exactly 1 values in each range d * 16 to (d + 1) * 16 - 1.
All inputs are finite; a program needn't handle non-finite values.
Results may differ from a plain program's by a relative error of at most 0.014.
Values may be sent and summed in bfloat16 or wider, within the bound.
No kernel may reach another device: no remote copies, remote signals or barrier semaphores. Data moves between devices by JAX's collectives and lax.ppermute only.
A program may use at most 128 MiB of HBM per device.

v0:
```python
import jax
import jax.numpy as jnp
from jax import lax
from jax.sharding import PartitionSpec as P

HEAD_DIM = 64
SEQ_DEV = 16
MAXLEN = 16


EPS = 1e-06


def swapped(shard, axis, apart):
    return lax.ppermute(shard, axis, [(i, i ^ 1 << apart) for i in range(lax.axis_size(axis))])


def rms_forward(states_row, gain):
    xf = states_row.astype(jnp.float32)
    scale = lax.rsqrt(jnp.mean(xf * xf, axis=-1, keepdims=True) + EPS)
    return (xf, scale, (xf * scale * gain).astype(jnp.bfloat16))


def rms_backward(xf, scale, gain, dnorm):
    upper = gain * dnorm
    inner = jnp.mean(xf * upper, axis=-1, keepdims=True)
    return (scale * upper - xf * scale * scale * scale * inner).astype(jnp.bfloat16)


def route(slots):
    return lax.all_to_all(slots, "dp", split_axis=0, concat_axis=0, tiled=True)


def cross_groups(slots):
    return swapped(slots, "section", 0)


def pack(rows, starts, lengths, picked):
    steps = jnp.arange(MAXLEN, dtype=jnp.int32)
    index = starts[picked][:, None] + steps[None, :]
    valid = steps[None, :] < lengths[picked][:, None]
    taken = rows[jnp.minimum(index, rows.shape[0] - 1)]
    return jnp.where(valid[:, :, None], taken, jnp.zeros((), rows.dtype))


def unpack(padded, starts, lengths, picked, tokens):
    ends = starts + lengths
    place = jnp.arange(tokens, dtype=jnp.int32)
    which = jnp.sum((place[:, None] >= ends[None, :]).astype(jnp.int32), axis=-1)
    position = jnp.argsort(picked)
    flat = position[which] * MAXLEN + place - starts[which]
    return padded.reshape(-1, padded.shape[-1])[flat]


def spare(own, remote, key_len):
    return (jnp.zeros_like(own), jnp.zeros_like(own))


def attend(own, remote, key_len):
    seqs, length, width = own.shape
    cols = width // 2
    heads = cols // HEAD_DIM
    query = own[..., :cols].reshape(seqs, length, heads, HEAD_DIM)
    dout = own[..., cols:].reshape(seqs, length, heads, HEAD_DIM)
    keys = remote[..., :cols].reshape(seqs, length, heads, HEAD_DIM)
    values = remote[..., cols:].reshape(seqs, length, heads, HEAD_DIM)
    scores = jnp.einsum("sqhd,skhd->shqk", query, keys, preferred_element_type=jnp.float32)
    live = jnp.arange(length, dtype=jnp.int32)[None, None, None, :] < key_len[:, None, None, None]
    expo = jnp.where(live, jnp.exp(scores), jnp.float32(0.0))
    weight = expo / jnp.sum(expo, axis=-1, keepdims=True)
    weight_b = weight.astype(jnp.bfloat16)
    attended = jnp.einsum(
        "shqk,skhd->sqhd", weight_b, values, preferred_element_type=jnp.float32
    ).astype(jnp.bfloat16)
    dweight = jnp.einsum("sqhd,skhd->shqk", dout, values, preferred_element_type=jnp.float32)
    total = jnp.sum(weight * dweight, axis=-1, keepdims=True)
    dscore = (weight * (dweight - total)).astype(jnp.bfloat16)
    dquery = jnp.einsum("shqk,skhd->sqhd", dscore, keys, preferred_element_type=jnp.float32).astype(
        jnp.bfloat16
    )
    dkeys = jnp.einsum("shqk,sqhd->skhd", dscore, query, preferred_element_type=jnp.float32).astype(
        jnp.bfloat16
    )
    dvalues = jnp.einsum(
        "shqk,sqhd->skhd", weight_b, dout, preferred_element_type=jnp.float32
    ).astype(jnp.bfloat16)
    front = jnp.concatenate(
        [dquery.reshape(seqs, length, cols), attended.reshape(seqs, length, cols)], axis=-1
    )
    back = jnp.concatenate(
        [dkeys.reshape(seqs, length, cols), dvalues.reshape(seqs, length, cols)], axis=-1
    )
    return (front, back)


def left_product(left, right):
    return lax.dot_general(
        left, right, (((0,), (0,)), ((), ())), preferred_element_type=jnp.float32
    )


def right_product(rows, weight):
    return lax.dot_general(
        rows, weight, (((1,), (1,)), ((), ())), preferred_element_type=jnp.float32
    )


def per_device(states, gains, proj_a, proj_b, cotangent, src_len, tgt_len, dest):
    encoder = lax.axis_index("section") == 0
    member = lax.axis_index("dp")
    members = lax.axis_size("dp")
    group = SEQ_DEV // members
    gain = gains[0]
    weight_a = proj_a[0]
    weight_b = proj_b[0]
    cols = weight_a.shape[1]
    tokens = states.shape[1]
    xf, scale, normed = rms_forward(states[0], gain)
    second_left = jnp.where(encoder, normed, cotangent)
    first = jnp.dot(normed, weight_a, preferred_element_type=jnp.float32).astype(jnp.bfloat16)
    second = jnp.dot(second_left, weight_b, preferred_element_type=jnp.float32).astype(jnp.bfloat16)
    paired = jnp.concatenate([first, second], axis=1)
    order = jnp.argsort(dest, axis=1)
    sorted_dest = jnp.take_along_axis(dest, order, axis=1)
    sorted_len = jnp.take_along_axis(src_len, order, axis=1)
    begin = member * group
    anchor = jnp.int32(0)
    incoming = (
        lax.dynamic_slice(sorted_dest, (anchor, begin), (members, group)).reshape(-1)
        - member * SEQ_DEV
    )
    key_len = lax.dynamic_slice(sorted_len, (anchor, begin), (members, group)).reshape(-1)
    picked = jnp.where(encoder, order[member], incoming)
    lengths = jnp.where(encoder, src_len[member], tgt_len[member])
    starts = jnp.cumsum(lengths) - lengths
    slots = pack(paired, starts, lengths, picked)
    remote = cross_groups(route(slots))
    front, back = lax.cond(encoder, spare, attend, slots, remote, key_len)
    returned = route(cross_groups(back))
    padded = jnp.where(encoder, returned, front)
    rows = unpack(padded, starts, lengths, picked, tokens)
    grad_first = rows[:, :cols]
    grad_second = rows[:, cols:]
    used_second = jnp.where(encoder, grad_second, jnp.zeros((), jnp.bfloat16))
    partial_norm = right_product(grad_first, weight_a) + right_product(used_second, weight_b)
    dnorm = lax.psum(partial_norm, "mp")
    grad_states = rms_backward(xf, scale, gain, dnorm)
    summed = lax.psum_scatter(
        jnp.concatenate(
            [left_product(normed, grad_first), left_product(second_left, grad_second)], axis=1
        ).astype(jnp.bfloat16),
        "dp",
        scatter_dimension=0,
        tiled=True,
    ).astype(jnp.float32)
    grad_a = summed[:, :cols]
    grad_b = summed[:, cols:]
    return (grad_states[None], grad_a[None], grad_b[None])


def solution(mesh):
    return jax.shard_map(
        per_device,
        mesh=mesh,
        in_specs=(
            P("section", "dp", None),
            P("section", None),
            P("section", None, "mp"),
            P("section", None, "mp"),
            P("dp", None),
            P(),
            P(),
            P(),
        ),
        out_specs=(P("section", "dp", None), P("section", "dp", "mp"), P("section", "dp", "mp")),
        check_vma=False,
    )
```

profile of v0, /device:TPU:0, one launch (start us, length us, event | category | flops | bytes accessed | tf_op | source)
XLA Modules:
  0.0 271.3 jit_solution(91106585542771045)
XLA Ops:
  8.0 0.8 copy.52
  8.8 0.7 sort.34
  9.6 0.1 reshape.419
  9.7 1.9 gather_fusion.5
  11.8 0.2 dynamic-slice_reduce_fusion
  12.1 0.1 copy.64
  12.2 0.7 broadcast_select_fusion.7
  12.9 0.1 copy.57
  13.0 0.1 reduce.1
  13.1 0.7 gather_fusion.1
  13.9 0.1 reshape.289
  14.0 0.3 fusion.42
  14.3 0.7 gather_fusion
  15.0 4.8 %fusion.46 = bf16[128,1024]{1,0:T(8,128)(2,1)S(1)} fusion(bf16[1,4096,1024]{2,1,0:T(8,128)(2,1)} %param.14, bf16[1,128,4096]{2,1,0:T(8,128)(2,1)S(1)} %copy-done.2, f32[4096]{0:T(1024)S(1)} %bitcast.366, f32[128]{0:T(128)S(1)} %add_rsqrt_fusion), kind=kOutput, calls=%fused_computation.66 | convolution fusion | flops 1075970048 | bytes 9716224 | tf_op jit(solution)/shard_map/dot_general | solution.py:120
  19.8 4.7 %fusion.49 = bf16[128,1024]{1,0:T(8,128)(2,1)S(1)} fusion(bf16[1,4096,1024]{2,1,0:T(8,128)(2,1)} %param.15, bf16[128,4096]{1,0:T(8,128)(2,1)S(1)} %copy-done.6, pred[]{:T(512)S(6)} %eq.3, bf16[1,128,4096]{2,1,0:T(8,128)(2,1)S(1)} %copy-done.2, f32[4096]{0:T(1024)S(1)} %bitcast.367, f32[128]{0:T(128)S(1)} %add_rsqrt_fusion), kind=kOutput, calls=%fused_computation.67 | convolution fusion | flops 1076494336 | bytes 10764801 | tf_op jit(solution)/shard_map/dot_general | solution.py:121
  24.6 1.4 gather_fusion.2
  26.0 0.1 broadcast_select_fusion.1
  26.1 24.9 %all_to_all.10 = bf16[16,16,2048]{2,1,0:T(8,128)(2,1)S(1)} all-to-all(bf16[16,16,2048]{2,1,0:T(8,128)(2,1)S(1)} %broadcast_select_fusion.1), channel_id=1, replica_groups=mesh['section'=2,'dp'=16,'mp'=4] {'dp'}, dimensions={0} | all-to-all | bytes 2097152 | tf_op jit(solution)/shard_map/all_to_all | solution.py:31
  51.1 1.9 gather_fusion.4
  53.0 0.8 collective-permute-done
  53.8 2.2 conditional.1
  53.8 1.1 broadcast.169
  54.9 1.1 broadcast.169.clone
  56.0 33.4 %collective-permute-start.1 = (bf16[16,16,2048]{2,1,0:T(8,128)(2,1)}, bf16[16,16,2048]{2,1,0:T(8,128)(2,1)}, u32[]{:S(2)}, u32[]{:S(2)}) collective-permute-start(bf16[16,16,2048]{2,1,0:T(8,128)(2,1)} %get-tuple-element.31), channel_id=1, source_target_pairs={{0,64},{64,0},{1,65},{65,1},{2,66},{66,2},{3,67},{67,3},{4,68},{68... | collective-permute-start | bytes 3145736 | tf_op jit(solution)/shard_map/ppermute | solution.py:15
  89.4 2.6 collective-permute-done.1
  92.0 3.7 %all-to-all-start.1 = ((bf16[16,16,2048]{2,1,0:T(8,128)(2,1)}), bf16[16,16,2048]{2,1,0:T(8,128)(2,1)S(1)}, u32[]{:S(2)}, u32[]{:S(2)}) async-start(bf16[16,16,2048]{2,1,0:T(8,128)(2,1)} %collective-permute-done.1), calls=%async_computation.1 | async-start | bytes 2097152 | tf_op jit(solution)/shard_map/all_to_all | solution.py:31
  95.8 1.2 sort.35
  97.0 0.7 fusion.82
  97.7 0.7 fusion.81
  98.4 0.1 convert_reduce_fusion
  98.5 20.0 %fusion.72 = s32[128]{0:T(128)S(1)} fusion(s32[128]{0:T(128)S(1)} %convert_reduce_fusion, s32[]{:T(128)} %bitcast.55, s32[]{:T(128)} %bitcast.37, s32[]{:T(128)} %bitcast.56, s32[]{:T(128)} %bitcast.38, s32[]{:T(128)} %bitcast.57, s32[]{:T(128)} %bitcast.39, s32[]{:T(128)} %bitcast.58, s32[]{:T(128)} %bitcast.40, s32[]{:T(128)} %bitcast.59, s32[]{:T(128)} %bitcast.41, ...), kind=kLoop, calls=%fused_computation.144 | loop fusion | flops 6912 | bytes 1152 | tf_op jit(solution)/shard_map/select_n | solution.py:52
  118.6 0.1 broadcast_select_fusion.2
  118.7 0.9 gather_fusion.3
  119.7 6.3 %fusion.21 = f32[128,4096]{1,0:T(8,128)S(1)} fusion(bf16[1,4096,1024]{2,1,0:T(8,128)(2,1)} %param.15, pred[]{:T(512)S(6)} %eq.3, bf16[128,2048]{1,0:T(8,128)(2,1)S(1)} %gather_fusion.3), kind=kOutput, calls=%fused_computation.39 | convolution fusion | flops 1073872896 | bytes 10747905 | tf_op jit(solution)/shard_map/dot_general | solution.py:103
  125.9 7.6 %fusion.29 = f32[128,4096]{1,0:T(8,128)} fusion(f32[128,4096]{1,0:T(8,128)S(1)} %fusion.21, bf16[1,4096,1024]{2,1,0:T(8,128)(2,1)} %param.14, bf16[128,2048]{1,0:T(8,128)(2,1)S(1)} %gather_fusion.3), kind=kOutput, calls=%fused_computation.49 | convolution fusion | flops 1074266112 | bytes 12845056 | tf_op jit(solution)/shard_map/dot_general | solution.py:103
  133.5 0.3 reduce-scatter.2.cloned.1.call-start
  133.9 2.4 convolution_convert_fusion.5
  136.3 2.5 convolution_convert_fusion.4
  138.7 7.6 %pad_maximum_fusion.2 = bf16[4096,2048]{0,1:T(8,128)(2,1)} fusion(bf16[4096,1024]{0,1:T(8,128)(2,1)S(1)} %convolution_convert_fusion.4, bf16[4096,1024]{0,1:T(8,128)(2,1)S(1)} %convolution_convert_fusion.5), kind=kLoop, calls=%fused_computation.38 | loop fusion | flops 33554432 | bytes 33554432 | tf_op jit(solution)/shard_map/concatenate | solution.py:149
  146.3 48.7 %all-reduce.2.cloned.1.call-done = f32[128,4096]{1,0:T(8,128)} async-done(((f32[128,4096]{1,0:T(8,128)}), f32[128,4096]{1,0:T(8,128)}) %all-reduce.2.cloned.1.call-update) | async-done | bytes 2097168 | tf_op jit(solution)/shard_map/psum | solution.py:146
  195.0 2.2 fusion.43
  197.2 0.3 copy-done.3
  197.5 1.6 fusion.54
  199.2 60.5 %reduce-scatter.2.cloned.1.call-done = bf16[256,2048]{0,1:T(8,128)(2,1)} async-done(((bf16[4096,2048]{0,1:T(8,128)(2,1)}), bf16[256,2048]{0,1:T(8,128)(2,1)}) %reduce-scatter.2.cloned.1.call-update) | async-done | bytes 1048592 | tf_op jit(solution)/shard_map/reduce_scatter | solution.py:148
  259.7 1.4 convert_element_type.83
  261.1 0.1 slice_bitcast_fusion
  261.2 1.3 copy.58
  262.5 1.3 copy.59
  (38 shorter events, 0.7 us)
Async XLA Ops:
  8.0 1.7 copy-start
  9.7 2.5 copy-start.1
  9.7 4.2 %copy-start.2 = (bf16[1,128,4096]{2,1,0:T(8,128)(2,1)S(1)}, bf16[1,128,4096]{2,1,0:T(8,128)(2,1)}, u32[]{:S(2)}) copy-start(bf16[1,128,4096]{2,1,0:T(8,128)(2,1)} %param.12) | copy-start | bytes 3145732
  11.7 3.3 %copy-start.11 = (f32[1,4096]{1,0:T(1,128)S(1)}, f32[1,4096]{1,0:T(1,128)}, u32[]{:S(2)}) copy-start(f32[1,4096]{1,0:T(1,128)} %param.13) | copy-start | bytes 49156
  15.0 4.8 %copy-start.6 = (bf16[128,4096]{1,0:T(8,128)(2,1)S(1)}, bf16[128,4096]{1,0:T(8,128)(2,1)}, u32[]{:S(2)}) copy-start(bf16[128,4096]{1,0:T(8,128)(2,1)} %param.16) | copy-start | bytes 3145732
  51.1 2.8 %collective-permute-start = (bf16[16,16,2048]{2,1,0:T(8,128)(2,1)S(1)}, bf16[16,16,2048]{2,1,0:T(8,128)(2,1)}, u32[]{:S(2)}, u32[]{:S(2)}) collective-permute-start(bf16[16,16,2048]{2,1,0:T(8,128)(2,1)S(1)} %all_to_all.10), channel_id=1, source_target_pairs={{0,64},{64,0},{1,65},{65,1},{2,66},{66,2},{3,67},{67,3},{4,68},{68... | collective-permute-start | bytes 3145736 | tf_op jit(solution)/shard_map/ppermute | solution.py:15
  56.0 36.0 %collective-permute-start.1 = (bf16[16,16,2048]{2,1,0:T(8,128)(2,1)}, bf16[16,16,2048]{2,1,0:T(8,128)(2,1)}, u32[]{:S(2)}, u32[]{:S(2)}) collective-permute-start(bf16[16,16,2048]{2,1,0:T(8,128)(2,1)} %get-tuple-element.31), channel_id=1, source_target_pairs={{0,64},{64,0},{1,65},{65,1},{2,66},{66,2},{3,67},{67,3},{4,68},{68... | collective-permute-start | bytes 3145736 | tf_op jit(solution)/shard_map/ppermute | solution.py:15
  92.0 26.5 %all-to-all-start.1 = ((bf16[16,16,2048]{2,1,0:T(8,128)(2,1)}), bf16[16,16,2048]{2,1,0:T(8,128)(2,1)S(1)}, u32[]{:S(2)}, u32[]{:S(2)}) async-start(bf16[16,16,2048]{2,1,0:T(8,128)(2,1)} %collective-permute-done.1), calls=%async_computation.1 | async-start | bytes 2097152 | tf_op jit(solution)/shard_map/all_to_all | solution.py:31
  95.7 99.3 %all-reduce.2.cloned.1.call-start = ((), (), s32[]{:S(2)}) async-start(), calls=%async_computation.3 | async-start | bytes 4194304 | tf_op jit(solution)/shard_map/psum | solution.py:146
  133.5 2.8 %copy-start.7 = (bf16[128,4096]{1,0:T(8,128)(2,1)S(1)}, bf16[128,4096]{1,0:T(8,128)(2,1)}, u32[]{:S(2)}) copy-start(bf16[128,4096]{1,0:T(8,128)(2,1)} %param.16) | copy-start | bytes 3145732
  133.5 126.1 %reduce-scatter.2.cloned.1.call-start = ((), (), s32[]{:S(2)}) async-start(), calls=%async_computation.4 | async-start | bytes 17825792 | tf_op jit(solution)/shard_map/reduce_scatter | solution.py:148
  195.0 2.5 copy-start.3
Sparse Core Ops, SparseCore 0:
  133.7 61.3 all-reduce.1
Sparse Core Ops, SparseCore 1:
  146.4 113.2 reduce-scatter.1
where the time goes:
time: 273 us; the launch traced here: 271 us
  waiting for transfers between devices  113 us (41%)
  starting transfers between devices  37.4 us (14%)
  other arithmetic  36.5 us (13%)
  matrix products  28.2 us (10%)
  blocking collectives  24.9 us (9%)
  local copies, waits for them, and re-layouts  15.8 us (6%)
  between operations  15.8 us (6%)
    reduce_scatter x1, waiting for transfers between devices, per_device(): lax.psum_scatter(jnp.concatenate([left_product(normed, grad_first), left_...  60.5 us
    psum x1, waiting for transfers between devices, per_device(): dnorm = lax.psum(partial_norm, 'mp')  48.7 us
    ppermute x2, starting transfers between devices, swapped(): lax.ppermute(shard, axis, [(i, i ^ 1 << apart) for i in range(lax.axis_si...  33.4 us
    all_to_all x1, blocking collectives, route(): return lax.all_to_all(slots, 'dp', split_axis=0, concat_axis=0, tiled=True)  24.9 us
    select_n x1, other arithmetic, unpack(): return padded.reshape(-1, padded.shape[-1])[flat]  20 us
    dot_general x2, matrix products, right_product(): lax.dot_general(rows, weight, (((1,), (1,)), ((), ())), preferred_element...  13.8 us
    concatenate x1, other arithmetic, per_device(): jnp.concatenate([left_product(normed, grad_first), left_product(second_le...  7.58 us
  transfers between devices with their start and end apart: 5, of which 4 were waited for; matrix products, arithmetic and copies ran while one was open for 15% of the time, Pallas kernels for 0%

commit v1 on v0

v1 whole, which is shorter than its diff:
```python
import functools

import jax
import jax.numpy as jnp
from jax import lax
from jax.experimental import pallas as pl
from jax.experimental.pallas import tpu as pltpu
from jax.sharding import PartitionSpec as P

HEAD_DIM = 64
SEQ_DEV = 16
MAXLEN = 16
TOK = 128
SLOTS = 256
RING = 4
EPS = 1e-06
F32 = jnp.float32
BF16 = jnp.bfloat16
VMEM = pl.BlockSpec(memory_space=pltpu.VMEM)
SMEM = pl.BlockSpec(memory_space=pltpu.SMEM)


def iota(shape, dim):
    return lax.broadcasted_iota(jnp.int32, shape, dim)


def total(value, axis):
    return jnp.sum(value.astype(F32), axis=axis, keepdims=True)


def cost(flops, nbytes):
    return pl.CostEstimate(flops=flops, bytes_accessed=nbytes, transcendentals=0)


def params(mib=32, **more):
    return pltpu.CompilerParams(vmem_limit_bytes=mib << 20, **more)


def column_of(row):
    square = jnp.broadcast_to(row, (SEQ_DEV, SEQ_DEV))
    same = iota((SEQ_DEV, SEQ_DEV), 0) == iota((SEQ_DEV, SEQ_DEV), 1)
    return total(jnp.where(same, square, 0), 1)


def slot_onehot(member, src_len, dest):
    i, j = iota((SEQ_DEV, SEQ_DEV), 0), iota((SEQ_DEV, SEQ_DEV), 1)
    lengths = src_len[pl.ds(member, 1), :]
    ends = total(jnp.where(j <= i, jnp.broadcast_to(lengths, (SEQ_DEV, SEQ_DEV)), 0), 1)
    begins = ends - column_of(lengths)
    place = column_of(dest[pl.ds(member, 1), :] >> 4) * MAXLEN
    row = iota((SEQ_DEV, TOK), 1).astype(F32)
    inside = (row >= begins) & (row < ends)
    target = total(jnp.where(inside, place + row - begins, 0.0), 0)
    hit = iota((SLOTS, TOK), 0).astype(F32) == target
    return jnp.where(hit, 1.0, 0.0).astype(BF16)


def pair_mask(member, src_len, tgt_len, dest):
    i, j = iota((SEQ_DEV, SEQ_DEV), 0), iota((SEQ_DEV, SEQ_DEV), 1)
    column = column_of(tgt_len[pl.ds(member, 1), :])
    ends = total(jnp.where(i <= j, jnp.broadcast_to(column, (SEQ_DEV, SEQ_DEV)), 0.0), 0)
    row = iota((TOK, SEQ_DEV), 0).astype(F32)
    mine = total(jnp.where(row >= ends, 1.0, 0.0), 1)
    codes = dest[...]
    to_me = (codes >> 4) == member
    target = total(jnp.where(to_me, codes & 15, 0), 1)
    length = total(jnp.where(to_me, src_len[...], 0), 1)
    lane = iota((SEQ_DEV, SLOTS), 1)
    own = (lane >> 4) == iota((SEQ_DEV, SLOTS), 0)
    target = total(jnp.where(own, target, 0.0), 0)
    length = total(jnp.where(own, length, 0.0), 0)
    step = (iota((1, SLOTS), 1) & 15).astype(F32)
    target = jnp.where(step < length, target, -1.0)
    return mine == target


def norm_kernel(where_ref, x_ref, gain_ref, cot_ref, normed_ref, left_ref, by_x_ref, by_z_ref):
    xf = x_ref[...].astype(F32)
    scale = lax.rsqrt(jnp.mean(xf * xf, axis=-1, keepdims=True) + EPS)
    normed = (xf * scale * gain_ref[...]).astype(BF16)
    normed_ref[...] = normed
    block = normed.shape[1] // (RING * RING)
    for xd in range(RING):
        for zd in range(RING):
            at = (zd * RING + xd) * block
            by_x_ref[xd, :, zd * block : (zd + 1) * block] = normed[:, at : at + block]

    @pl.when(where_ref[0] == 0)
    def _():
        left_ref[...] = normed_ref[...]

    @pl.when(where_ref[0] != 0)
    def _():
        left_ref[...] = cot_ref[...]

    span = RING * block
    for zd in range(RING):
        by_z_ref[zd] = left_ref[:, zd * span : (zd + 1) * span]


def normalise(where, x, gain, cot):
    rows, width = x.shape
    return pl.pallas_call(
        norm_kernel,
        in_specs=[SMEM, VMEM, VMEM, VMEM],
        out_specs=[VMEM] * 4,
        out_shape=[
            jax.ShapeDtypeStruct((rows, width), BF16),
            jax.ShapeDtypeStruct((rows, width), BF16),
            jax.ShapeDtypeStruct((RING, rows, width // RING), BF16),
            jax.ShapeDtypeStruct((RING, rows, width // RING), BF16),
        ],
        compiler_params=params(),
        cost_estimate=cost(5 * rows * width, 12 * rows * width),
        name="norm",
    )(where, x, gain, cot)


def project_kernel(where_ref, n_ref, l_ref, a_ref, b_ref, keep_ref, send_ref, acc_a, acc_b):
    k = pl.program_id(0)

    @pl.when(k == 0)
    def _():
        acc_a[...] = jnp.zeros_like(acc_a)
        acc_b[...] = jnp.zeros_like(acc_b)

    acc_a[...] += jnp.dot(n_ref[...], a_ref[...], preferred_element_type=F32)
    acc_b[...] += jnp.dot(l_ref[...], b_ref[...], preferred_element_type=F32)

    @pl.when(k == pl.num_programs(0) - 1)
    def _():
        half = acc_a.shape[1] // 2
        mine = pl.multiple_of(where_ref[0] * half, half)
        other = pl.multiple_of((1 - where_ref[0]) * half, half)
        keep_ref[:, :half] = acc_a[:, pl.ds(mine, half)].astype(BF16)
        keep_ref[:, half:] = acc_b[:, pl.ds(mine, half)].astype(BF16)
        send_ref[:, :half] = acc_a[:, pl.ds(other, half)].astype(BF16)
        send_ref[:, half:] = acc_b[:, pl.ds(other, half)].astype(BF16)


def project(where, normed, left, weight_a, weight_b):
    rows, width = normed.shape
    cols = weight_a.shape[1]
    step = 512
    half = jax.ShapeDtypeStruct((rows, cols), BF16)
    return pl.pallas_call(
        project_kernel,
        grid=(width // step,),
        in_specs=[
            SMEM,
            pl.BlockSpec((rows, step), lambda k: (0, k)),
            pl.BlockSpec((rows, step), lambda k: (0, k)),
            pl.BlockSpec((step, cols), lambda k: (k, 0)),
            pl.BlockSpec((step, cols), lambda k: (k, 0)),
        ],
        out_specs=[pl.BlockSpec((rows, cols), lambda k: (0, 0))] * 2,
        out_shape=[half, half],
        scratch_shapes=[pltpu.VMEM((rows, cols), F32)] * 2,
        compiler_params=params(dimension_semantics=("arbitrary",)),
        cost_estimate=cost(4 * rows * width * cols, 4 * width * cols),
        name="project",
    )(where, normed, left, weight_a, weight_b)


def pack_kernel(where_ref, keep_ref, got_ref, src_ref, dest_ref, out_ref):
    spread = slot_onehot(where_ref[1], src_ref, dest_ref)

    @pl.when(where_ref[0] == 0)
    def _():
        out_ref[...] = jnp.dot(spread, keep_ref[...], preferred_element_type=F32).astype(BF16)

    @pl.when(where_ref[0] != 0)
    def _():
        out_ref[...] = jnp.dot(spread, got_ref[...], preferred_element_type=F32).astype(BF16)


def pack(where, keep, got, src_len, dest):
    width = keep.shape[1]
    return pl.pallas_call(
        pack_kernel,
        in_specs=[SMEM] + [VMEM] * 4,
        out_specs=VMEM,
        out_shape=jax.ShapeDtypeStruct((SLOTS, width), BF16),
        compiler_params=params(),
        cost_estimate=cost(2 * SLOTS * TOK * width, 2 * SLOTS * width),
        name="pack",
    )(where, keep, got, src_len, dest)


def attend_kernel(
    where_ref, keep_ref, got_ref, slots_ref, src_ref, tgt_ref, dest_ref, front_ref, back_ref, own_ref
):
    mask = pair_mask(where_ref[1], src_ref, tgt_ref, dest_ref)

    @pl.when(where_ref[0] == 0)
    def _():
        own_ref[...] = got_ref[...]

    @pl.when(where_ref[0] != 0)
    def _():
        own_ref[...] = keep_ref[...]

    half = own_ref.shape[1] // 2
    pair = 2 * HEAD_DIM
    low = iota((1, pair), 1) < HEAD_DIM
    nothing = jnp.zeros((), BF16)

    def both(value):
        return jnp.concatenate(
            [jnp.where(low, value, nothing), jnp.where(low, nothing, value)], axis=0
        )

    def nt(left, right):
        return lax.dot_general(left, right, (((1,), (1,)), ((), ())), preferred_element_type=F32)

    def tn(left, right):
        return lax.dot_general(left, right, (((0,), (0,)), ((), ())), preferred_element_type=F32)

    def one(score, dweight):
        expo = jnp.where(mask, jnp.exp(score), 0.0)
        weight = expo * (1.0 / jnp.sum(expo, axis=-1, keepdims=True))
        mean = jnp.sum(weight * dweight, axis=-1, keepdims=True)
        return weight.astype(BF16), (weight * (dweight - mean)).astype(BF16)

    def fold(value):
        return jnp.where(low, value[:SLOTS], value[SLOTS:]).astype(BF16)

    for p in range(half // pair):
        first = slice(p * pair, (p + 1) * pair)
        second = slice(half + p * pair, half + (p + 1) * pair)
        query, dout = own_ref[:, first], own_ref[:, second]
        keys, values = both(slots_ref[:, first]), both(slots_ref[:, second])
        score, dweight = nt(query, keys), nt(dout, values)
        weight_0, dscore_0 = one(score[:, :SLOTS], dweight[:, :SLOTS])
        weight_1, dscore_1 = one(score[:, SLOTS:], dweight[:, SLOTS:])
        weight = jnp.concatenate([weight_0, weight_1], axis=1)
        dscore = jnp.concatenate([dscore_0, dscore_1], axis=1)
        front_ref[:, first] = jnp.dot(dscore, keys, preferred_element_type=F32).astype(BF16)
        front_ref[:, second] = jnp.dot(weight, values, preferred_element_type=F32).astype(BF16)
        back_ref[:, first] = fold(tn(dscore, query))
        back_ref[:, second] = fold(tn(weight, dout))


def attend(where, keep, got, slots, src_len, tgt_len, dest):
    rows, width = keep.shape
    return pl.pallas_call(
        attend_kernel,
        in_specs=[SMEM] + [VMEM] * 6,
        out_specs=[VMEM] * 2,
        out_shape=[
            jax.ShapeDtypeStruct((rows, width), BF16),
            jax.ShapeDtypeStruct((SLOTS, width), BF16),
        ],
        scratch_shapes=[pltpu.VMEM((rows, width), BF16)],
        compiler_params=params(),
        cost_estimate=cost(24 * rows * SLOTS * width, 8 * SLOTS * width),
        name="attend",
    )(where, keep, got, slots, src_len, tgt_len, dest)


def unpack_kernel(where_ref, back_ref, front_ref, src_ref, dest_ref, keep_ref, send_ref):
    spread = slot_onehot(where_ref[1], src_ref, dest_ref)
    rows = lax.dot_general(
        spread, back_ref[...], (((0,), (0,)), ((), ())), preferred_element_type=F32
    ).astype(BF16)

    @pl.when(where_ref[0] == 0)
    def _():
        keep_ref[...] = rows
        send_ref[...] = front_ref[...]

    @pl.when(where_ref[0] != 0)
    def _():
        keep_ref[...] = front_ref[...]
        send_ref[...] = rows


def unpack(where, back, front, src_len, dest):
    width = front.shape[1]
    half = jax.ShapeDtypeStruct((TOK, width), BF16)
    return pl.pallas_call(
        unpack_kernel,
        in_specs=[SMEM] + [VMEM] * 4,
        out_specs=[VMEM] * 2,
        out_shape=[half, half],
        compiler_params=params(),
        cost_estimate=cost(2 * SLOTS * TOK * width, 4 * SLOTS * width),
        name="unpack",
    )(where, back, front, src_len, dest)


def join_kernel(where_ref, keep_ref, got_ref, first_ref, second_ref):
    half = keep_ref.shape[1] // 2
    mine = pl.multiple_of(where_ref[0] * half, half)
    other = pl.multiple_of((1 - where_ref[0]) * half, half)
    first_ref[:, pl.ds(mine, half)] = keep_ref[:, :half]
    first_ref[:, pl.ds(other, half)] = got_ref[:, :half]
    second_ref[:, pl.ds(mine, half)] = keep_ref[:, half:]
    second_ref[:, pl.ds(other, half)] = got_ref[:, half:]


def join(where, keep, got):
    shape = jax.ShapeDtypeStruct(keep.shape, BF16)
    return pl.pallas_call(
        join_kernel,
        in_specs=[SMEM, VMEM, VMEM],
        out_specs=[VMEM] * 2,
        out_shape=[shape, shape],
        compiler_params=params(),
        cost_estimate=cost(0, 8 * keep.size),
        name="join",
    )(where, keep, got)


def dnorm_kernel(where_ref, first_ref, second_ref, a_ref, b_ref, out_ref):
    def nt(left, right):
        return lax.dot_general(left, right, (((1,), (1,)), ((), ())), preferred_element_type=F32)

    @pl.when(where_ref[0] == 0)
    def _():
        out_ref[...] = (
            nt(first_ref[...], a_ref[...]) + nt(second_ref[...], b_ref[...])
        ).astype(BF16)

    @pl.when(where_ref[0] != 0)
    def _():
        out_ref[...] = nt(first_ref[...], a_ref[...]).astype(BF16)


def dnorm_partial(where, first, second, weight_a, weight_b):
    rows, cols = first.shape
    width = weight_a.shape[0]
    step = 512
    return pl.pallas_call(
        dnorm_kernel,
        grid=(width // step,),
        in_specs=[
            SMEM,
            pl.BlockSpec((rows, cols), lambda k: (0, 0)),
            pl.BlockSpec((rows, cols), lambda k: (0, 0)),
            pl.BlockSpec((step, cols), lambda k: (k, 0)),
            pl.BlockSpec((step, cols), lambda k: (k, 0)),
        ],
        out_specs=pl.BlockSpec((rows, step), lambda k: (0, k)),
        out_shape=jax.ShapeDtypeStruct((rows, width), BF16),
        compiler_params=params(dimension_semantics=("arbitrary",)),
        cost_estimate=cost(4 * rows * width * cols, 4 * width * cols),
        name="dnorm",
    )(where, first, second, weight_a, weight_b)


def rms_back_kernel(where_ref, x_ref, gain_ref, parts_ref, out_ref):
    rows = out_ref.shape[0]
    mine = pl.multiple_of(where_ref[2] * rows, rows)
    xf = x_ref[pl.ds(mine, rows), :].astype(F32)
    scale = lax.rsqrt(jnp.mean(xf * xf, axis=-1, keepdims=True) + EPS)
    dnorm = parts_ref[0].astype(F32)
    for i in range(1, RING):
        dnorm += parts_ref[i].astype(F32)
    upper = gain_ref[...] * dnorm
    inner = jnp.mean(xf * upper, axis=-1, keepdims=True)
    out_ref[...] = (scale * upper - xf * (scale * scale * scale * inner)).astype(BF16)


def rms_back(where, x, gain, parts):
    rows, width = parts.shape[1:]
    return pl.pallas_call(
        rms_back_kernel,
        in_specs=[SMEM] + [VMEM] * 3,
        out_specs=VMEM,
        out_shape=jax.ShapeDtypeStruct((rows, width), BF16),
        compiler_params=params(),
        cost_estimate=cost(10 * rows * width, 12 * rows * width),
        name="rms_back",
    )(where, x, gain, parts)


def place_kernel(where_ref, own_ref, left_ref, right_ref, far_a_ref, far_b_ref, out_ref):
    rows = own_ref.shape[0]
    half = rows // 2

    def at(k):
        return pl.multiple_of(((where_ref[2] + k) % RING) * rows, rows)

    out_ref[pl.ds(at(0), rows), :] = own_ref[...]
    out_ref[pl.ds(at(3), rows), :] = left_ref[...]
    out_ref[pl.ds(at(1), rows), :] = right_ref[...]
    out_ref[pl.ds(at(2), half), :] = far_a_ref[...]
    out_ref[pl.ds(pl.multiple_of(at(2) + half, half), half), :] = far_b_ref[...]


def place(where, pieces):
    rows, width = pieces[0].shape
    return pl.pallas_call(
        place_kernel,
        in_specs=[SMEM] + [VMEM] * 5,
        out_specs=VMEM,
        out_shape=jax.ShapeDtypeStruct((RING * rows, width), BF16),
        compiler_params=params(),
        cost_estimate=cost(0, 4 * RING * rows * width),
        name="place",
    )(where, *pieces)


def shift(value, axis, k):
    return lax.ppermute(value, axis, [(i, (i + k) % RING) for i in range(RING)])


def gathered(block, axis):
    half = block.shape[0] // 2
    left, right = shift(block, axis, 1), shift(block, axis, 3)
    far_a, far_b = shift(left[:half], axis, 1), shift(right[half:], axis, 3)
    return [block, left, right, far_a, far_b]


def exchanged(slices, axis):
    me = lax.axis_index(axis)

    def take(k):
        return lax.dynamic_index_in_dim(slices, (me + k) % RING, 0, keepdims=False)

    return [take(0), shift(take(1), axis, 1), shift(take(3), axis, 3), shift(take(2), axis, 2)]


def outer_kernel(ks, slot, where_ref, *refs):
    lefts, rights = refs[:4], refs[4:9]
    outs, left, right = refs[9:-2], refs[-2], refs[-1]
    at = 0
    for ref in lefts:
        left[at : at + ref.shape[0], :] = ref[...]
        at += ref.shape[0]
    at = 0
    for ref in rights:
        right[at : at + ref.shape[0], :] = ref[...]
        at += ref.shape[0]
    block = left.shape[1] // RING
    for k, out in zip(ks, outs, strict=True):
        column = pl.multiple_of(((where_ref[slot] + k) % RING) * block, block)
        out[...] = lax.dot_general(
            left[:, pl.ds(column, block)],
            right[...],
            (((0,), (0,)), ((), ())),
            preferred_element_type=F32,
        ).astype(out.dtype)


def outer(where, slot, lefts, rights, ks, kinds):
    rows = sum(piece.shape[0] for piece in lefts)
    width, cols = lefts[0].shape[1], rights[0].shape[1]
    block = width // RING
    return pl.pallas_call(
        functools.partial(outer_kernel, ks, slot),
        in_specs=[SMEM] + [VMEM] * 9,
        out_specs=[VMEM] * len(ks),
        out_shape=[jax.ShapeDtypeStruct((block, cols), kind) for kind in kinds],
        scratch_shapes=[pltpu.VMEM((rows, width), BF16), pltpu.VMEM((rows, cols), BF16)],
        compiler_params=params(),
        cost_estimate=cost(2 * rows * block * cols * len(ks), 4 * rows * cols),
        name="outer",
    )(where, *lefts, *rights)


def reduced(where, slot, lefts, rights, axis):
    (far,) = outer(where, slot, lefts, rights, (2,), (BF16,))
    half = far.shape[0] // 2
    from_left, from_right = shift(far[:half], axis, 1), shift(far[half:], axis, 3)
    right, left, own = outer(where, slot, lefts, rights, (1, 3, 0), (BF16, BF16, F32))
    right = jnp.concatenate([right[:half] + from_left, right[half:]], axis=0)
    left = jnp.concatenate([left[:half], left[half:] + from_right], axis=0)
    a, b = shift(right, axis, 1), shift(left, axis, 3)
    return own + a.astype(F32) + b.astype(F32)


def per_device(states, gains, proj_a, proj_b, cotangent, src_len, tgt_len, dest):
    z, x = lax.axis_index("z"), lax.axis_index("x")
    member = z * RING + x
    where = jnp.stack([lax.axis_index("section"), member, lax.axis_index("mp"), z, x]).astype(jnp.int32)
    weight_a, weight_b = proj_a[0], proj_b[0]
    rows = states[0]
    normed, left, by_x, by_z = normalise(where, rows, gains, cotangent)
    keep, send = project(where, normed, left, weight_a, weight_b)
    swap = [(0, 1), (1, 0)]
    got = lax.ppermute(send, "section", swap)
    slots = pack(where, keep, got, src_len, dest)
    width = slots.shape[1]
    slots = slots.reshape(SEQ_DEV, MAXLEN, width)
    slots = lax.all_to_all(slots, ("z", "x"), split_axis=0, concat_axis=0, tiled=True)
    slots = slots.reshape(SLOTS, width)
    lefts_a, lefts_b = exchanged(by_x, "x"), exchanged(by_z, "z")
    front, back = attend(where, keep, got, slots, src_len, tgt_len, dest)
    back = back.reshape(SEQ_DEV, MAXLEN, width)
    back = lax.all_to_all(back, ("z", "x"), split_axis=0, concat_axis=0, tiled=True)
    keep, send = unpack(where, back.reshape(SLOTS, width), front, src_len, dest)
    got = lax.ppermute(send, "section", swap)
    first, second = join(where, keep, got)

    rights_a, rights_b = gathered(first, "x"), gathered(second, "z")
    partial = dnorm_partial(where, first, second, weight_a, weight_b)
    parts = lax.all_to_all(
        partial.reshape(RING, TOK // RING, -1), "mp", split_axis=0, concat_axis=0, tiled=True
    )
    quarter = rms_back(where, rows, gains, parts)
    grad_states = place(where, gathered(quarter, "mp"))

    grad_a = reduced(where, 3, lefts_a, rights_a, "z")
    grad_b = reduced(where, 4, lefts_b, rights_b, "x")
    return (grad_states[None], grad_a[None], grad_b[None])


def solution(mesh):
    split = jax.sharding.Mesh(mesh.devices.reshape(2, RING, RING, RING), ("section", "z", "x", "mp"))
    dp = ("z", "x")
    return jax.shard_map(
        per_device,
        mesh=split,
        in_specs=(
            P("section", dp, None),
            P("section", None),
            P("section", None, "mp"),
            P("section", None, "mp"),
            P(dp, None),
            P(),
            P(),
            P(),
        ),
        out_specs=(P("section", dp, None), P("section", dp, "mp"), P("section", dp, "mp")),
        check_vma=False,
    )
```

time: 273 us -> 157 us (0.58)
  waiting for transfers between devices: 113 us -> 18.9 us
  Pallas kernels: 0 us -> 29.7 us
  other arithmetic: 36.5 us -> 6.82 us
  matrix products: 28.2 us -> 0 us
  between operations: 15.8 us -> 0.94 us
  local copies, waits for them, and re-layouts: 15.8 us -> 28.5 us
  blocking collectives: 24.9 us -> 33.6 us
    reduce_scatter x1 -> x0, waiting for transfers between devices: 60.5 us -> none  [per_device(): lax.psum_scatter(jnp.concatenate([left_product(normed, grad_first), left_...]
    psum x1 -> x0, waiting for transfers between devices: 48.7 us -> none  [per_device(): dnorm = lax.psum(partial_norm, 'mp')]
    pallas_call x0 -> x13, Pallas kernels: none -> 29.7 us  [the longest x1 8.09 us: dnorm_partial(): pl.pallas_call(dnorm_kernel, grid=(width // step,), in_specs=[SMEM, pl.Bl...]
    dot_general x6 -> x0, matrix products: 28.2 us -> none  [the longest x2 13.8 us: right_product(): lax.dot_general(rows, weight, (((1,), (1,)), ((), ())), preferred_element...]
    select_n x7 -> x0, other arithmetic: 21.1 us -> none  [the longest x1 20 us: unpack(): return padded.reshape(-1, padded.shape[-1])[flat]]
    unnamed x18 -> x50, local copies, waits for them, and re-layouts: 3.89 us -> 23 us
    ppermute x2 -> x28, waiting for transfers between devices: 3.46 us -> 18.9 us  [the longest x26 15.9 us: shift(): return lax.ppermute(value, axis, [(i, (i + k) % RING) for i in range(RING)])]
    gather x11 -> x0, local copies, waits for them, and re-layouts: 9.16 us -> none  [the longest x3 2.1 us: per_device(): sorted_len = jnp.take_along_axis(src_len, order, axis=1)]
  transfers between devices with their start and end apart: 5 -> 29, of which waited for: 4 -> 10; matrix products, arithmetic and copies ran while one was open for 15% -> 7% of each run, Pallas kernels for 0% -> 12%
where the time goes in v1:
time: 157 us; the launch traced here: 156 us
  starting transfers between devices  37.9 us (24%)
  blocking collectives  33.6 us (21%)
  Pallas kernels  29.7 us (19%)
  local copies, waits for them, and re-layouts  28.5 us (18%)
  waiting for transfers between devices  18.9 us (12%)
  other arithmetic  6.82 us (4%)
    ppermute x26, starting transfers between devices, shift(): return lax.ppermute(value, axis, [(i, (i + k) % RING) for i in range(RING)])  33.3 us
    unnamed x50, local copies, waits for them, and re-layouts  23 us
    all_to_all x1, blocking collectives, per_device(): lax.all_to_all(slots, ('z', 'x'), split_axis=0, concat_axis=0, tiled=True)  19.6 us
    ppermute x26, waiting for transfers between devices, shift(): return lax.ppermute(value, axis, [(i, (i + k) % RING) for i in range(RING)])  15.9 us
    all_to_all x1, blocking collectives, per_device(): lax.all_to_all(back, ('z', 'x'), split_axis=0, concat_axis=0, tiled=True)  14 us
    pallas_call x1, Pallas kernels, dnorm_partial(): pl.pallas_call(dnorm_kernel, grid=(width // step,), in_specs=[SMEM, pl.Bl...  8.09 us
    pallas_call x4, Pallas kernels, outer(): pl.pallas_call(functools.partial(outer_kernel, ks, slot), in_specs=[SMEM]...  7.82 us
    pallas_call x1, Pallas kernels, project(): pl.pallas_call(project_kernel, grid=(width // step,), in_specs=[SMEM, pl....  4.82 us
  transfers between devices with their start and end apart: 29, of which 10 were waited for; matrix products, arithmetic and copies ran while one was open for 7% of the time, Pallas kernels for 12%

profile of v1, /device:TPU:0, one launch (start us, length us, event | category | flops | bytes accessed | tf_op | source)
XLA Modules:
  0.0 156.3 jit_solution(17133206735396363459)
XLA Ops:
  0.7 1.2 copy-done.4
  2.0 1.2 copy-done.10
  3.9 1.3 norm.1
  5.2 3.4 %copy-done = bf16[1,4096,1024]{2,1,0:T(8,128)(2,1)S(1)} copy-done((bf16[1,4096,1024]{2,1,0:T(8,128)(2,1)S(1)}, bf16[1,4096,1024]{2,1,0:T(8,128)(2,1)}, u32[]{:S(2)}) %copy-start) | copy-done | bytes 8388632
  8.6 3.4 %copy-done.2 = bf16[1,4096,1024]{2,1,0:T(8,128)(2,1)S(1)} copy-done((bf16[1,4096,1024]{2,1,0:T(8,128)(2,1)S(1)}, bf16[1,4096,1024]{2,1,0:T(8,128)(2,1)}, u32[]{:S(2)}) %copy-start.2) | copy-done | bytes 8388632
  12.0 4.8 %project.1 = (bf16[128,1024]{1,0:T(8,128)(2,1)S(1)}, bf16[128,1024]{1,0:T(8,128)(2,1)S(1)}) custom-call(s32[5]{0:T(128)S(1)} %stack.23.where_ref, bf16[128,4096]{1,0:T(8,128)(2,1)S(1)} %get-tuple-element.21.n_ref, bf16[128,4096]{1,0:T(8,128)(2,1)S(1)} %get-tuple-element.22.l_ref, bf16[4096,1024]{1,0:T(8,128)(2,1)S(1)} %bitcast.34, ...), custom_call_target="tpu_custom_call" | custom-call | flops 2147483648 | bytes 16777216 | tf_op jit(solution)/shard_map/project/pallas_call | solution.py:146
  16.9 1.5 collective-permute-done.got_ref
  18.4 0.9 pack.1
  19.4 19.6 %all_to_all.15 = bf16[16,16,1024]{2,1,0:T(8,128)(2,1)S(1)} all-to-all(bf16[16,16,1024]{2,1,0:T(8,128)(2,1)S(1)} %bitcast.41), channel_id=1, replica_groups=mesh['section'=2,'z'=4,'x'=4,'mp'=4] {'z','x'}, dimensions={0} | all-to-all | bytes 1048576 | tf_op jit(solution)/shard_map/all_to_all | solution.py:487
  38.9 2.7 %attend.1 = (bf16[128,1024]{1,0:T(8,128)(2,1)S(1)}, bf16[256,1024]{1,0:T(8,128)(2,1)S(1)}) custom-call(s32[5]{0:T(128)S(1)} %stack.23.where_ref, bf16[128,1024]{1,0:T(8,128)(2,1)S(1)} %get-tuple-element.23.keep_ref, bf16[128,1024]{1,0:T(8,128)(2,1)S(1)} %collective-permute-done.got_ref, bf16[256,1024]{1,0:T(8,128)(2,1)S(1)} %bitcast.42, ...), custom_call_target="tpu_custom_call" | custom-call | flops 805306368 | bytes 2097152 | tf_op jit(solution)/shard_map/attend/pallas_call | solution.py:246
  41.6 14.0 %all_to_all.16 = bf16[16,16,1024]{2,1,0:T(8,128)(2,1)S(1)} all-to-all(bf16[16,16,1024]{2,1,0:T(8,128)(2,1)S(1)} %bitcast.43), channel_id=1, replica_groups=mesh['section'=2,'z'=4,'x'=4,'mp'=4] {'z','x'}, dimensions={0} | all-to-all | bytes 1048576 | tf_op jit(solution)/shard_map/all_to_all | solution.py:492
  55.6 0.9 unpack.1
  56.7 1.5 collective-permute-done.1.got_ref
  58.9 3.2 %collective-permute-start.21 = (bf16[128,1024]{1,0:T(8,128)(2,1)S(1)}, bf16[128,1024]{1,0:T(8,128)(2,1)}, u32[]{:S(2)}, u32[]{:S(2)}) collective-permute-start(bf16[128,1024]{1,0:T(8,128)(2,1)S(1)} %get-tuple-element.30.second_ref.refs_4_), channel_id=1, source_target_pairs={{0,48},{16,0},{32,16},{48,32},{1,49},{17,1},{33,17},{49,33},{2,50}... | collective-permute-start | bytes 786440 | tf_op jit(solution)/shard_map/ppermute | solution.py:406
  62.6 2.7 %collective-permute-start.10 = (bf16[128,1024]{1,0:T(8,128)(2,1)S(1)}, bf16[128,1024]{1,0:T(8,128)(2,1)}, u32[]{:S(2)}, u32[]{:S(2)}) collective-permute-start(bf16[128,1024]{1,0:T(8,128)(2,1)S(1)} %get-tuple-element.29.first_ref.refs_4_), channel_id=1, source_target_pairs={{0,12},{4,0},{8,4},{12,8},{1,13},{5,1},{9,5},{13,9},{2,14},{6,2},{... | collective-permute-start | bytes 786440 | tf_op jit(solution)/shard_map/ppermute | solution.py:406
  66.2 2.2 %collective-permute-done.20.refs_5_ = bf16[128,1024]{1,0:T(8,128)(2,1)S(1)} collective-permute-done((bf16[128,1024]{1,0:T(8,128)(2,1)S(1)}, bf16[128,1024]{1,0:T(8,128)(2,1)S(1)}, u32[]{:S(2)}, u32[]{:S(2)}) %collective-permute-start.20) | collective-permute-done | bytes 262176 | tf_op jit(solution)/shard_map/ppermute | solution.py:406
  68.4 1.1 collective-permute-start.18
  70.9 0.9 slice.79
  71.8 2.4 %collective-permute-start.22 = (bf16[64,1024]{1,0:T(8,128)(2,1)S(1)}, bf16[64,1024]{1,0:T(8,128)(2,1)S(1)}, u32[]{:S(2)}, u32[]{:S(2)}) collective-permute-start(bf16[64,1024]{1,0:T(8,128)(2,1)S(1)} %slice.78), channel_id=1, source_target_pairs={{0,16},{16,32},{32,48},{48,0},{1,17},{17,33},{33,49},{49,1},{2,18}... | collective-permute-start | bytes 393224 | tf_op jit(solution)/shard_map/ppermute | solution.py:406
  75.1 3.4 %copy-done.1 = bf16[1,4096,1024]{2,1,0:T(8,128)(2,1)S(1)} copy-done((bf16[1,4096,1024]{2,1,0:T(8,128)(2,1)S(1)}, bf16[1,4096,1024]{2,1,0:T(8,128)(2,1)}, u32[]{:S(2)}) %copy-start.1) | copy-done | bytes 8388632
  78.5 3.4 %copy-done.3 = bf16[1,4096,1024]{2,1,0:T(8,128)(2,1)S(1)} copy-done((bf16[1,4096,1024]{2,1,0:T(8,128)(2,1)S(1)}, bf16[1,4096,1024]{2,1,0:T(8,128)(2,1)}, u32[]{:S(2)}) %copy-start.3) | copy-done | bytes 8388632
  81.9 8.1 %dnorm.1 = bf16[128,4096]{1,0:T(8,128)(2,1)} custom-call(s32[5]{0:T(128)S(1)} %stack.23.where_ref, bf16[128,1024]{1,0:T(8,128)(2,1)S(1)} %get-tuple-element.29.first_ref.refs_4_, bf16[128,1024]{1,0:T(8,128)(2,1)S(1)} %get-tuple-element.30.second_ref.refs_4_, bf16[4096,1024]{1,0:T(8,128)(2,1)S(1)} %bitcast.35, bf16[4096,1024]{1,0:T(8,128)(2,1)S(1)} %bitcast.37), custom_call_target="tpu_custom_call" | custom-call | flops 2147483648 | bytes 16777216 | tf_op jit(solution)/shard_map/dnorm/pallas_call | solution.py:334
  90.0 4.5 %all-to-all-start.2 = ((bf16[4,32,4096]{2,1,0:T(8,128)(2,1)}), bf16[4,32,4096]{2,1,0:T(8,128)(2,1)S(1)}, u32[]{:S(2)}, u32[]{:S(2)}) async-start(bf16[4,32,4096]{2,1,0:T(8,128)(2,1)} %bitcast.12), calls=%async_computation.2 | async-start | bytes 2097152 | tf_op jit(solution)/shard_map/all_to_all | solution.py:499
  94.4 0.9 slice.74
  95.4 0.9 slice.75
  96.3 0.9 collective-permute-start.6
  97.2 2.4 %collective-permute-start.7 = (bf16[128,1024]{1,0:T(8,128)(2,1)}, bf16[128,1024]{1,0:T(8,128)(2,1)S(1)}, u32[]{:S(2)}, u32[]{:S(2)}) collective-permute-start(bf16[128,1024]{1,0:T(8,128)(2,1)} %get-tuple-element.44), channel_id=1, source_target_pairs={{0,12},{4,0},{8,4},{12,8},{1,13},{5,1},{9,5},{13,9},{2,14},{6,2},{... | collective-permute-start | bytes 786440 | tf_op jit(solution)/shard_map/ppermute | solution.py:406
  101.2 2.4 %collective-permute-start.12 = (bf16[64,1024]{1,0:T(8,128)(2,1)S(1)}, bf16[64,1024]{1,0:T(8,128)(2,1)S(1)}, u32[]{:S(2)}, u32[]{:S(2)}) collective-permute-start(bf16[64,1024]{1,0:T(8,128)(2,1)S(1)} %slice.75), channel_id=1, source_target_pairs={{0,12},{4,0},{8,4},{12,8},{1,13},{5,1},{9,5},{13,9},{2,14},{6,2},{... | collective-permute-start | bytes 393224 | tf_op jit(solution)/shard_map/ppermute | solution.py:406
  105.2 1.8 %outer.7 = bf16[256,1024]{1,0:T(8,128)(2,1)S(1)} custom-call(s32[5]{0:T(128)S(1)} %copy-done.19, bf16[128,1024]{1,0:T(8,128)(2,1)S(1)} %get-tuple-element.42.refs_0_, bf16[128,1024]{1,0:T(8,128)(2,1)} %collective-permute-done.17.refs_1_, bf16[128,1024]{1,0:T(8,128)(2,1)} %collective-permute-done.18.refs_2_, ...), custom_call_target="tpu_custom_call" | custom-call | flops 268435456 | bytes 2097152 | tf_op jit(solution)/shard_map/outer/pallas_call | solution.py:451
  107.5 3.4 %collective-permute-start.26 = (bf16[128,1024]{1,0:T(8,128)(2,1)S(1)}, bf16[128,1024]{1,0:T(8,128)(2,1)S(1)}, u32[]{:S(2)}, u32[]{:S(2)}) collective-permute-start(bf16[128,1024]{1,0:T(8,128)(2,1)S(1)} %get-tuple-element.50), channel_id=1, source_target_pairs={{0,12},{4,0},{8,4},{12,8},{1,13},{5,1},{9,5},{13,9},{2,14},{6,2},{... | collective-permute-start | bytes 786440 | tf_op jit(solution)/shard_map/ppermute | solution.py:406
  112.8 1.6 %outer.5 = bf16[256,1024]{1,0:T(8,128)(2,1)S(1)} custom-call(s32[5]{0:T(128)S(1)} %copy-done.20, bf16[128,1024]{1,0:T(8,128)(2,1)S(1)} %get-tuple-element.46.refs_0_, bf16[128,1024]{1,0:T(8,128)(2,1)S(1)} %collective-permute-done.6.refs_1_, bf16[128,1024]{1,0:T(8,128)(2,1)S(1)} %collective-permute-done.7.refs_2_, ...), custom_call_target="tpu_custom_call" | custom-call | flops 268435456 | bytes 2097152 | tf_op jit(solution)/shard_map/outer/pallas_call | solution.py:451
  116.0 2.4 %collective-permute-start.15 = (bf16[128,1024]{1,0:T(8,128)(2,1)}, bf16[128,1024]{1,0:T(8,128)(2,1)}, u32[]{:S(2)}, u32[]{:S(2)}) collective-permute-start(bf16[128,1024]{1,0:T(8,128)(2,1)} %get-tuple-element.56), channel_id=1, source_target_pairs={{0,48},{16,0},{32,16},{48,32},{1,49},{17,1},{33,17},{49,33},{2,50}... | collective-permute-start | bytes 786440 | tf_op jit(solution)/shard_map/ppermute | solution.py:406
  119.4 2.3 %outer.6 = (bf16[256,1024]{1,0:T(8,128)(2,1)S(1)}, bf16[256,1024]{1,0:T(8,128)(2,1)S(1)}, f32[256,1024]{1,0:T(8,128)S(1)}) custom-call(s32[5]{0:T(128)S(1)} %copy-done.20, bf16[128,1024]{1,0:T(8,128)(2,1)S(1)} %get-tuple-element.42.refs_0_, bf16[128,1024]{1,0:T(8,128)(2,1)} %collective-permute-done.17.refs_1_, ...), custom_call_target="tpu_custom_call" | custom-call | flops 805306368 | bytes 2097152 | tf_op jit(solution)/shard_map/outer/pallas_call | solution.py:451
  121.7 1.0 copy-done.6
  122.7 2.1 %outer.4 = (bf16[256,1024]{1,0:T(8,128)(2,1)S(1)}, bf16[256,1024]{1,0:T(8,128)(2,1)S(1)}, f32[256,1024]{1,0:T(8,128)S(1)}) custom-call(s32[5]{0:T(128)S(1)} %copy-done.20, bf16[128,1024]{1,0:T(8,128)(2,1)S(1)} %get-tuple-element.46.refs_0_, bf16[128,1024]{1,0:T(8,128)(2,1)S(1)} %collective-permute-done.6.refs_1_, ...), custom_call_target="tpu_custom_call" | custom-call | flops 805306368 | bytes 2097152 | tf_op jit(solution)/shard_map/outer/pallas_call | solution.py:451
  126.6 1.0 collective-permute-start.25
  128.4 2.2 %collective-permute-start.27 = (bf16[256,1024]{1,0:T(8,128)(2,1)}, bf16[256,1024]{1,0:T(8,128)(2,1)}, u32[]{:S(2)}, u32[]{:S(2)}) collective-permute-start(bf16[256,1024]{1,0:T(8,128)(2,1)} %pad_maximum_fusion.3), channel_id=1, source_target_pairs={{0,12},{4,0},{8,4},{12,8},{1,13},{5,1},{9,5},{13,9},{2,14},{6,2},{... | collective-permute-start | bytes 1572872 | tf_op jit(solution)/shard_map/ppermute | solution.py:406
  131.3 0.9 rms_back.1.own_ref
  132.2 1.8 %collective-permute-start.2 = (bf16[32,4096]{1,0:T(8,128)(2,1)S(1)}, bf16[32,4096]{1,0:T(8,128)(2,1)S(1)}, u32[]{:S(2)}, u32[]{:S(2)}) collective-permute-start(bf16[32,4096]{1,0:T(8,128)(2,1)S(1)} %rms_back.1.own_ref), channel_id=1, source_target_pairs={{0,1},{1,2},{2,3},{3,0},{4,5},{5,6},{6,7},{7,4},{8,9},{9,10},{10,1... | collective-permute-start | bytes 786440 | tf_op jit(solution)/shard_map/ppermute | solution.py:406
  134.1 1.5 collective-permute-start.3
  135.6 1.4 slice_add_fusion.3
  137.1 2.8 %collective-permute-done.2.left_ref = bf16[32,4096]{1,0:T(8,128)(2,1)S(1)} collective-permute-done((bf16[32,4096]{1,0:T(8,128)(2,1)S(1)}, bf16[32,4096]{1,0:T(8,128)(2,1)S(1)}, u32[]{:S(2)}, u32[]{:S(2)}) %collective-permute-start.2) | collective-permute-done | bytes 262176 | tf_op jit(solution)/shard_map/ppermute | solution.py:406
  140.5 1.3 collective-permute-done.3.right_ref
  142.3 3.9 %collective-permute-done.4.far_a_ref = bf16[16,4096]{1,0:T(8,128)(2,1)S(1)} collective-permute-done((bf16[16,4096]{1,0:T(8,128)(2,1)S(1)}, bf16[16,4096]{1,0:T(8,128)(2,1)S(1)}, u32[]{:S(2)}, u32[]{:S(2)}) %collective-permute-start.4) | collective-permute-done | bytes 131104 | tf_op jit(solution)/shard_map/ppermute | solution.py:406
  146.7 4.4 %collective-permute-done.5.far_b_ref = bf16[16,4096]{1,0:T(8,128)(2,1)S(1)} collective-permute-done((bf16[16,4096]{1,0:T(8,128)(2,1)S(1)}, bf16[16,4096]{1,0:T(8,128)(2,1)S(1)}, u32[]{:S(2)}, u32[]{:S(2)}) %collective-permute-start.5) | collective-permute-done | bytes 131104 | tf_op jit(solution)/shard_map/ppermute | solution.py:406
  151.1 1.6 %place.1 = bf16[128,4096]{1,0:T(8,128)(2,1)} custom-call(s32[5]{0:T(128)S(1)} %copy-done.21, bf16[32,4096]{1,0:T(8,128)(2,1)S(1)} %rms_back.1.own_ref, bf16[32,4096]{1,0:T(8,128)(2,1)S(1)} %collective-permute-done.2.left_ref, bf16[32,4096]{1,0:T(8,128)(2,1)S(1)} %collective-permute-done.3.right_ref, bf16[16,4096]{1,0:T(8,128)(2,1)S(1)} %collective-permute-done.4.far_a_ref, ...), custom_call_target="tpu_custom_call" | custom-call | bytes 2097152 | tf_op jit(solution)/shard_map/place/pallas_call | solution.py:394
  152.7 2.4 %add_bitcast_fusion = f32[1,256,1024]{2,1,0:T(8,128)} fusion(bf16[256,1024]{1,0:T(8,128)(2,1)} %collective-permute-done.27, f32[256,1024]{1,0:T(8,128)S(1)} %copy-done.7, bf16[256,1024]{1,0:T(8,128)(2,1)} %collective-permute-done.25), kind=kLoop, calls=%fused_computation | loop fusion | flops 1048576 | bytes 3145728 | tf_op jit(solution)/shard_map/broadcast_in_dim | solution.py:507
  155.1 1.2 add_bitcast_fusion.1
  (94 shorter events, 18.5 us)
Async XLA Ops:
  0.7 74.4 %copy-start.18 = (s32[5]{0:T(128)}, s32[5]{0:T(128)S(1)}, u32[]{:S(2)}) copy-start(s32[5]{0:T(128)S(1)} %stack.23.where_ref) | copy-start | bytes 64
  0.7 1.2 copy-start.4
  2.0 1.2 copy-start.10
  5.2 3.4 %copy-start = (bf16[1,4096,1024]{2,1,0:T(8,128)(2,1)S(1)}, bf16[1,4096,1024]{2,1,0:T(8,128)(2,1)}, u32[]{:S(2)}) copy-start(bf16[1,4096,1024]{2,1,0:T(8,128)(2,1)} %param.10) | copy-start | bytes 25165828
  8.6 3.4 %copy-start.2 = (bf16[1,4096,1024]{2,1,0:T(8,128)(2,1)S(1)}, bf16[1,4096,1024]{2,1,0:T(8,128)(2,1)}, u32[]{:S(2)}) copy-start(bf16[1,4096,1024]{2,1,0:T(8,128)(2,1)} %param.11) | copy-start | bytes 25165828
  12.0 6.5 %copy-start.22 = (s32[16,16]{1,0:T(8,128)S(1)}, s32[16,16]{1,0:T(8,128)}, u32[]{:S(2)}) copy-start(s32[16,16]{1,0:T(8,128)} %src_ref.5) | copy-start | bytes 3076
  12.0 6.5 %copy-start.23 = (s32[16,16]{1,0:T(8,128)S(1)}, s32[16,16]{1,0:T(8,128)}, u32[]{:S(2)}) copy-start(s32[16,16]{1,0:T(8,128)} %dest_ref.5) | copy-start | bytes 3076
  12.0 27.0 %copy-start.24 = (s32[16,16]{1,0:T(8,128)S(1)}, s32[16,16]{1,0:T(8,128)}, u32[]{:S(2)}) copy-start(s32[16,16]{1,0:T(8,128)} %tgt_ref.1) | copy-start | bytes 3076
  16.8 1.6 %collective-permute-start = (bf16[128,1024]{1,0:T(8,128)(2,1)S(1)}, bf16[128,1024]{1,0:T(8,128)(2,1)S(1)}, u32[]{:S(2)}, u32[]{:S(2)}) collective-permute-start(bf16[128,1024]{1,0:T(8,128)(2,1)S(1)} %get-tuple-element.24), channel_id=1, source_target_pairs={{0,64},{64,0},{1,65},{65,1},{2,66},{66,2},{3,67},{67,3},{4,68},{68... | collective-permute-start | bytes 786440 | tf_op jit(solution)/shard_map/ppermute | solution.py:483
  56.6 1.6 %collective-permute-start.1 = (bf16[128,1024]{1,0:T(8,128)(2,1)S(1)}, bf16[128,1024]{1,0:T(8,128)(2,1)S(1)}, u32[]{:S(2)}, u32[]{:S(2)}) collective-permute-start(bf16[128,1024]{1,0:T(8,128)(2,1)S(1)} %get-tuple-element.28), channel_id=1, source_target_pairs={{0,64},{64,0},{1,65},{65,1},{2,66},{66,2},{3,67},{67,3},{4,68},{68... | collective-permute-start | bytes 786440 | tf_op jit(solution)/shard_map/ppermute | solution.py:494
  58.8 9.6 %collective-permute-start.20 = (bf16[128,1024]{1,0:T(8,128)(2,1)S(1)}, bf16[128,1024]{1,0:T(8,128)(2,1)S(1)}, u32[]{:S(2)}, u32[]{:S(2)}) collective-permute-start(bf16[128,1024]{1,0:T(8,128)(2,1)S(1)} %get-tuple-element.30.second_ref.refs_4_), channel_id=1, source_target_pairs={{0,16},{16,32},{32,48},{48,0},{1,17},{17,33},{33,49},{49,1},{2,18}... | collective-permute-start | bytes 786440 | tf_op jit(solution)/shard_map/ppermute | solution.py:406
  58.9 10.6 %collective-permute-start.21 = (bf16[128,1024]{1,0:T(8,128)(2,1)S(1)}, bf16[128,1024]{1,0:T(8,128)(2,1)}, u32[]{:S(2)}, u32[]{:S(2)}) collective-permute-start(bf16[128,1024]{1,0:T(8,128)(2,1)S(1)} %get-tuple-element.30.second_ref.refs_4_), channel_id=1, source_target_pairs={{0,48},{16,0},{32,16},{48,32},{1,49},{17,1},{33,17},{49,33},{2,50}... | collective-permute-start | bytes 786440 | tf_op jit(solution)/shard_map/ppermute | solution.py:406
  62.1 9.7 %collective-permute-start.9 = (bf16[128,1024]{1,0:T(8,128)(2,1)S(1)}, bf16[128,1024]{1,0:T(8,128)(2,1)}, u32[]{:S(2)}, u32[]{:S(2)}) collective-permute-start(bf16[128,1024]{1,0:T(8,128)(2,1)S(1)} %get-tuple-element.29.first_ref.refs_4_), channel_id=1, source_target_pairs={{0,4},{4,8},{8,12},{12,0},{1,5},{5,9},{9,13},{13,1},{2,6},{6,10},{... | collective-permute-start | bytes 786440 | tf_op jit(solution)/shard_map/ppermute | solution.py:406
  62.6 11.6 %collective-permute-start.10 = (bf16[128,1024]{1,0:T(8,128)(2,1)S(1)}, bf16[128,1024]{1,0:T(8,128)(2,1)}, u32[]{:S(2)}, u32[]{:S(2)}) collective-permute-start(bf16[128,1024]{1,0:T(8,128)(2,1)S(1)} %get-tuple-element.29.first_ref.refs_4_), channel_id=1, source_target_pairs={{0,12},{4,0},{8,4},{12,8},{1,13},{5,1},{9,5},{13,9},{2,14},{6,2},{... | collective-permute-start | bytes 786440 | tf_op jit(solution)/shard_map/ppermute | solution.py:406
  66.2 30.1 %collective-permute-start.17 = (bf16[128,1024]{1,0:T(8,128)(2,1)}, bf16[128,1024]{1,0:T(8,128)(2,1)}, u32[]{:S(2)}, u32[]{:S(2)}) collective-permute-start(bf16[128,1024]{1,0:T(8,128)(2,1)} %get-tuple-element.41), channel_id=1, source_target_pairs={{0,16},{16,32},{32,48},{48,0},{1,17},{17,33},{33,49},{49,1},{2,18}... | collective-permute-start | bytes 786440 | tf_op jit(solution)/shard_map/ppermute | solution.py:406
  68.4 28.8 %collective-permute-start.18 = (bf16[128,1024]{1,0:T(8,128)(2,1)}, bf16[128,1024]{1,0:T(8,128)(2,1)}, u32[]{:S(2)}, u32[]{:S(2)}) collective-permute-start(bf16[128,1024]{1,0:T(8,128)(2,1)} %get-tuple-element.40), channel_id=1, source_target_pairs={{0,48},{16,0},{32,16},{48,32},{1,49},{17,1},{33,17},{49,33},{2,50}... | collective-permute-start | bytes 786440 | tf_op jit(solution)/shard_map/ppermute | solution.py:406
  69.5 30.1 %collective-permute-start.19 = (bf16[128,1024]{1,0:T(8,128)(2,1)}, bf16[128,1024]{1,0:T(8,128)(2,1)}, u32[]{:S(2)}, u32[]{:S(2)}) collective-permute-start(bf16[128,1024]{1,0:T(8,128)(2,1)} %get-tuple-element.39), channel_id=1, source_target_pairs={{0,32},{16,48},{32,0},{48,16},{1,33},{17,49},{33,1},{49,17},{2,34}... | collective-permute-start | bytes 786440 | tf_op jit(solution)/shard_map/ppermute | solution.py:406
  71.8 27.9 %collective-permute-start.22 = (bf16[64,1024]{1,0:T(8,128)(2,1)S(1)}, bf16[64,1024]{1,0:T(8,128)(2,1)S(1)}, u32[]{:S(2)}, u32[]{:S(2)}) collective-permute-start(bf16[64,1024]{1,0:T(8,128)(2,1)S(1)} %slice.78), channel_id=1, source_target_pairs={{0,16},{16,32},{32,48},{48,0},{1,17},{17,33},{33,49},{49,1},{2,18}... | collective-permute-start | bytes 393224 | tf_op jit(solution)/shard_map/ppermute | solution.py:406
  74.2 26.3 %collective-permute-start.23 = (bf16[64,1024]{1,0:T(8,128)(2,1)S(1)}, bf16[64,1024]{1,0:T(8,128)(2,1)S(1)}, u32[]{:S(2)}, u32[]{:S(2)}) collective-permute-start(bf16[64,1024]{1,0:T(8,128)(2,1)S(1)} %slice.79), channel_id=1, source_target_pairs={{0,48},{16,0},{32,16},{48,32},{1,49},{17,1},{33,17},{49,33},{2,50}... | collective-permute-start | bytes 393224 | tf_op jit(solution)/shard_map/ppermute | solution.py:406
  75.1 3.4 %copy-start.1 = (bf16[1,4096,1024]{2,1,0:T(8,128)(2,1)S(1)}, bf16[1,4096,1024]{2,1,0:T(8,128)(2,1)}, u32[]{:S(2)}) copy-start(bf16[1,4096,1024]{2,1,0:T(8,128)(2,1)} %param.10) | copy-start | bytes 25165828
  78.5 3.4 %copy-start.3 = (bf16[1,4096,1024]{2,1,0:T(8,128)(2,1)S(1)}, bf16[1,4096,1024]{2,1,0:T(8,128)(2,1)}, u32[]{:S(2)}) copy-start(bf16[1,4096,1024]{2,1,0:T(8,128)(2,1)} %param.11) | copy-start | bytes 25165828
  90.0 40.7 %all-to-all-start.2 = ((bf16[4,32,4096]{2,1,0:T(8,128)(2,1)}), bf16[4,32,4096]{2,1,0:T(8,128)(2,1)S(1)}, u32[]{:S(2)}, u32[]{:S(2)}) async-start(bf16[4,32,4096]{2,1,0:T(8,128)(2,1)} %bitcast.12), calls=%async_computation.2 | async-start | bytes 2097152 | tf_op jit(solution)/shard_map/all_to_all | solution.py:499
  96.3 10.8 %collective-permute-start.6 = (bf16[128,1024]{1,0:T(8,128)(2,1)}, bf16[128,1024]{1,0:T(8,128)(2,1)S(1)}, u32[]{:S(2)}, u32[]{:S(2)}) collective-permute-start(bf16[128,1024]{1,0:T(8,128)(2,1)} %get-tuple-element.45), channel_id=1, source_target_pairs={{0,4},{4,8},{8,12},{12,0},{1,5},{5,9},{9,13},{13,1},{2,6},{6,10},{... | collective-permute-start | bytes 786440 | tf_op jit(solution)/shard_map/ppermute | solution.py:406
  97.2 10.2 %collective-permute-start.7 = (bf16[128,1024]{1,0:T(8,128)(2,1)}, bf16[128,1024]{1,0:T(8,128)(2,1)S(1)}, u32[]{:S(2)}, u32[]{:S(2)}) collective-permute-start(bf16[128,1024]{1,0:T(8,128)(2,1)} %get-tuple-element.44), channel_id=1, source_target_pairs={{0,12},{4,0},{8,4},{12,8},{1,13},{5,1},{9,5},{13,9},{2,14},{6,2},{... | collective-permute-start | bytes 786440 | tf_op jit(solution)/shard_map/ppermute | solution.py:406
  99.6 11.7 %collective-permute-start.8 = (bf16[128,1024]{1,0:T(8,128)(2,1)}, bf16[128,1024]{1,0:T(8,128)(2,1)S(1)}, u32[]{:S(2)}, u32[]{:S(2)}) collective-permute-start(bf16[128,1024]{1,0:T(8,128)(2,1)} %get-tuple-element.43), channel_id=1, source_target_pairs={{0,8},{4,12},{8,0},{12,4},{1,9},{5,13},{9,1},{13,5},{2,10},{6,14},... | collective-permute-start | bytes 786440 | tf_op jit(solution)/shard_map/ppermute | solution.py:406
  99.7 12.2 %collective-permute-start.11 = (bf16[64,1024]{1,0:T(8,128)(2,1)S(1)}, bf16[64,1024]{1,0:T(8,128)(2,1)S(1)}, u32[]{:S(2)}, u32[]{:S(2)}) collective-permute-start(bf16[64,1024]{1,0:T(8,128)(2,1)S(1)} %slice.74), channel_id=1, source_target_pairs={{0,4},{4,8},{8,12},{12,0},{1,5},{5,9},{9,13},{13,1},{2,6},{6,10},{... | collective-permute-start | bytes 393224 | tf_op jit(solution)/shard_map/ppermute | solution.py:406
  101.2 10.9 %collective-permute-start.12 = (bf16[64,1024]{1,0:T(8,128)(2,1)S(1)}, bf16[64,1024]{1,0:T(8,128)(2,1)S(1)}, u32[]{:S(2)}, u32[]{:S(2)}) collective-permute-start(bf16[64,1024]{1,0:T(8,128)(2,1)S(1)} %slice.75), channel_id=1, source_target_pairs={{0,12},{4,0},{8,4},{12,8},{1,13},{5,1},{9,5},{13,9},{2,14},{6,2},{... | collective-permute-start | bytes 393224 | tf_op jit(solution)/shard_map/ppermute | solution.py:406
  103.6 0.9 copy-start.14
  105.2 25.4 %copy-start.5 = (bf16[1,128,4096]{2,1,0:T(8,128)(2,1)S(1)}, bf16[1,128,4096]{2,1,0:T(8,128)(2,1)}, u32[]{:S(2)}) copy-start(bf16[1,128,4096]{2,1,0:T(8,128)(2,1)} %param.8) | copy-start | bytes 3145732
  105.2 25.4 %copy-start.17 = (f32[1,4096]{1,0:T(1,128)S(1)}, f32[1,4096]{1,0:T(1,128)}, u32[]{:S(2)}) copy-start(f32[1,4096]{1,0:T(1,128)} %gain_ref.3) | copy-start | bytes 49156
  107.1 18.5 %collective-permute-start.24 = (bf16[128,1024]{1,0:T(8,128)(2,1)S(1)}, bf16[128,1024]{1,0:T(8,128)(2,1)S(1)}, u32[]{:S(2)}, u32[]{:S(2)}) collective-permute-start(bf16[128,1024]{1,0:T(8,128)(2,1)S(1)} %get-tuple-element.49), channel_id=1, source_target_pairs={{0,4},{4,8},{8,12},{12,0},{1,5},{5,9},{9,13},{13,1},{2,6},{6,10},{... | collective-permute-start | bytes 786440 | tf_op jit(solution)/shard_map/ppermute | solution.py:406
  107.5 18.2 %collective-permute-start.26 = (bf16[128,1024]{1,0:T(8,128)(2,1)S(1)}, bf16[128,1024]{1,0:T(8,128)(2,1)S(1)}, u32[]{:S(2)}, u32[]{:S(2)}) collective-permute-start(bf16[128,1024]{1,0:T(8,128)(2,1)S(1)} %get-tuple-element.50), channel_id=1, source_target_pairs={{0,12},{4,0},{8,4},{12,8},{1,13},{5,1},{9,5},{13,9},{2,14},{6,2},{... | collective-permute-start | bytes 786440 | tf_op jit(solution)/shard_map/ppermute | solution.py:406
  115.2 18.8 %collective-permute-start.13 = (bf16[128,1024]{1,0:T(8,128)(2,1)}, bf16[128,1024]{1,0:T(8,128)(2,1)}, u32[]{:S(2)}, u32[]{:S(2)}) collective-permute-start(bf16[128,1024]{1,0:T(8,128)(2,1)} %get-tuple-element.55), channel_id=1, source_target_pairs={{0,16},{16,32},{32,48},{48,0},{1,17},{17,33},{33,49},{49,1},{2,18}... | collective-permute-start | bytes 786440 | tf_op jit(solution)/shard_map/ppermute | solution.py:406
  116.0 19.5 %collective-permute-start.15 = (bf16[128,1024]{1,0:T(8,128)(2,1)}, bf16[128,1024]{1,0:T(8,128)(2,1)}, u32[]{:S(2)}, u32[]{:S(2)}) collective-permute-start(bf16[128,1024]{1,0:T(8,128)(2,1)} %get-tuple-element.56), channel_id=1, source_target_pairs={{0,48},{16,0},{32,16},{48,32},{1,49},{17,1},{33,17},{49,33},{2,50}... | collective-permute-start | bytes 786440 | tf_op jit(solution)/shard_map/ppermute | solution.py:406
  118.5 0.9 copy-start.15
  121.7 1.0 copy-start.6
  125.6 2.8 %copy-start.8 = (f32[256,1024]{1,0:T(8,128)}, f32[256,1024]{1,0:T(8,128)S(1)}, u32[]{:S(2)}) copy-start(f32[256,1024]{1,0:T(8,128)S(1)} %get-tuple-element.32) | copy-start | bytes 3145732
  125.6 2.8 %copy-start.11 = (bf16[256,1024]{1,0:T(8,128)(2,1)}, bf16[256,1024]{1,0:T(8,128)(2,1)S(1)}, u32[]{:S(2)}) copy-start(bf16[256,1024]{1,0:T(8,128)(2,1)S(1)} %get-tuple-element.33) | copy-start | bytes 1572868
  125.6 27.1 %copy-start.7 = (f32[256,1024]{1,0:T(8,128)S(1)}, f32[256,1024]{1,0:T(8,128)}, u32[]{:S(2)}) copy-start(f32[256,1024]{1,0:T(8,128)} %copy-done.6) | copy-start | bytes 3145732
  126.6 26.1 %collective-permute-start.25 = (bf16[256,1024]{1,0:T(8,128)(2,1)}, bf16[256,1024]{1,0:T(8,128)(2,1)}, u32[]{:S(2)}, u32[]{:S(2)}) collective-permute-start(bf16[256,1024]{1,0:T(8,128)(2,1)} %pad_maximum_fusion.2), channel_id=1, source_target_pairs={{0,4},{4,8},{8,12},{12,0},{1,5},{5,9},{9,13},{13,1},{2,6},{6,10},{... | collective-permute-start | bytes 1572872 | tf_op jit(solution)/shard_map/ppermute | solution.py:406
  128.4 24.3 %collective-permute-start.27 = (bf16[256,1024]{1,0:T(8,128)(2,1)}, bf16[256,1024]{1,0:T(8,128)(2,1)}, u32[]{:S(2)}, u32[]{:S(2)}) collective-permute-start(bf16[256,1024]{1,0:T(8,128)(2,1)} %pad_maximum_fusion.3), channel_id=1, source_target_pairs={{0,12},{4,0},{8,4},{12,8},{1,13},{5,1},{9,5},{13,9},{2,14},{6,2},{... | collective-permute-start | bytes 1572872 | tf_op jit(solution)/shard_map/ppermute | solution.py:406
  131.3 23.8 %copy-start.9 = (f32[256,1024]{1,0:T(8,128)S(1)}, f32[256,1024]{1,0:T(8,128)}, u32[]{:S(2)}) copy-start(f32[256,1024]{1,0:T(8,128)} %copy-done.8) | copy-start | bytes 3145732
  132.2 7.7 %collective-permute-start.2 = (bf16[32,4096]{1,0:T(8,128)(2,1)S(1)}, bf16[32,4096]{1,0:T(8,128)(2,1)S(1)}, u32[]{:S(2)}, u32[]{:S(2)}) collective-permute-start(bf16[32,4096]{1,0:T(8,128)(2,1)S(1)} %rms_back.1.own_ref), channel_id=1, source_target_pairs={{0,1},{1,2},{2,3},{3,0},{4,5},{5,6},{6,7},{7,4},{8,9},{9,10},{10,1... | collective-permute-start | bytes 786440 | tf_op jit(solution)/shard_map/ppermute | solution.py:406
  134.1 7.8 %collective-permute-start.3 = (bf16[32,4096]{1,0:T(8,128)(2,1)S(1)}, bf16[32,4096]{1,0:T(8,128)(2,1)S(1)}, u32[]{:S(2)}, u32[]{:S(2)}) collective-permute-start(bf16[32,4096]{1,0:T(8,128)(2,1)S(1)} %rms_back.1.own_ref), channel_id=1, source_target_pairs={{0,3},{1,0},{2,1},{3,2},{4,7},{5,4},{6,5},{7,6},{8,11},{9,8},{10,9... | collective-permute-start | bytes 786440 | tf_op jit(solution)/shard_map/ppermute | solution.py:406
  137.0 18.1 %collective-permute-start.14 = (bf16[256,1024]{1,0:T(8,128)(2,1)S(1)}, bf16[256,1024]{1,0:T(8,128)(2,1)S(1)}, u32[]{:S(2)}, u32[]{:S(2)}) collective-permute-start(bf16[256,1024]{1,0:T(8,128)(2,1)S(1)} %pad_maximum_fusion), channel_id=1, source_target_pairs={{0,16},{16,32},{32,48},{48,0},{1,17},{17,33},{33,49},{49,1},{2,18}... | collective-permute-start | bytes 1572872 | tf_op jit(solution)/shard_map/ppermute | solution.py:406
  139.9 6.2 %collective-permute-start.4 = (bf16[16,4096]{1,0:T(8,128)(2,1)S(1)}, bf16[16,4096]{1,0:T(8,128)(2,1)S(1)}, u32[]{:S(2)}, u32[]{:S(2)}) collective-permute-start(bf16[16,4096]{1,0:T(8,128)(2,1)S(1)} %slice.72), channel_id=1, source_target_pairs={{0,1},{1,2},{2,3},{3,0},{4,5},{5,6},{6,7},{7,4},{8,9},{9,10},{10,1... | collective-permute-start | bytes 393224 | tf_op jit(solution)/shard_map/ppermute | solution.py:406
  141.8 13.3 %collective-permute-start.16 = (bf16[256,1024]{1,0:T(8,128)(2,1)S(1)}, bf16[256,1024]{1,0:T(8,128)(2,1)S(1)}, u32[]{:S(2)}, u32[]{:S(2)}) collective-permute-start(bf16[256,1024]{1,0:T(8,128)(2,1)S(1)} %pad_maximum_fusion.1), channel_id=1, source_target_pairs={{0,48},{16,0},{32,16},{48,32},{1,49},{17,1},{33,17},{49,33},{2,50}... | collective-permute-start | bytes 1572872 | tf_op jit(solution)/shard_map/ppermute | solution.py:406
  146.2 5.0 %collective-permute-start.5 = (bf16[16,4096]{1,0:T(8,128)(2,1)S(1)}, bf16[16,4096]{1,0:T(8,128)(2,1)S(1)}, u32[]{:S(2)}, u32[]{:S(2)}) collective-permute-start(bf16[16,4096]{1,0:T(8,128)(2,1)S(1)} %slice.73), channel_id=1, source_target_pairs={{0,3},{1,0},{2,1},{3,2},{4,7},{5,4},{6,5},{7,6},{8,11},{9,8},{10,9... | collective-permute-start | bytes 393224 | tf_op jit(solution)/shard_map/ppermute | solution.py:406
  (6 other events, 4.2 us)

commit v2 on v1

v2 whole, which is shorter than its diff:
```python
import jax
import jax.numpy as jnp
from jax import lax
from jax.experimental import pallas as pl
from jax.experimental.pallas import tpu as pltpu
from jax.sharding import PartitionSpec as P

HEAD_DIM = 64
SEQ_DEV = 16
MAXLEN = 16
TOK = 128
SLOTS = 256
RING = 4
EPS = 1e-06
F32 = jnp.float32
BF16 = jnp.bfloat16
VMEM = pl.BlockSpec(memory_space=pltpu.VMEM)
HBM = pl.BlockSpec(memory_space=pltpu.HBM)


def iota(shape, dim):
    return lax.broadcasted_iota(jnp.int32, shape, dim)


def total(value, axis):
    return jnp.sum(value.astype(F32), axis=axis, keepdims=True)


def cost(flops, nbytes):
    return pl.CostEstimate(flops=flops, bytes_accessed=nbytes, transcendentals=0)


def params(mib=12, **more):
    return pltpu.CompilerParams(vmem_limit_bytes=mib << 20, **more)


def column_of(row):
    square = jnp.broadcast_to(row, (SEQ_DEV, SEQ_DEV))
    same = iota((SEQ_DEV, SEQ_DEV), 0) == iota((SEQ_DEV, SEQ_DEV), 1)
    return total(jnp.where(same, square, 0), 1)


def member_index():
    return lax.axis_index("z") * RING + lax.axis_index("x")


def slot_onehot(member, src_len, dest):
    i, j = iota((SEQ_DEV, SEQ_DEV), 0), iota((SEQ_DEV, SEQ_DEV), 1)
    lengths = src_len[pl.ds(member, 1), :]
    ends = total(jnp.where(j <= i, jnp.broadcast_to(lengths, (SEQ_DEV, SEQ_DEV)), 0), 1)
    begins = ends - column_of(lengths)
    place = column_of(dest[pl.ds(member, 1), :] >> 4) * MAXLEN
    row = iota((SEQ_DEV, TOK), 1).astype(F32)
    inside = (row >= begins) & (row < ends)
    target = total(jnp.where(inside, place + row - begins, 0.0), 0)
    hit = iota((SLOTS, TOK), 0).astype(F32) == target
    return jnp.where(hit, 1.0, 0.0).astype(BF16)


def pair_mask(member, src_len, tgt_len, dest):
    i, j = iota((SEQ_DEV, SEQ_DEV), 0), iota((SEQ_DEV, SEQ_DEV), 1)
    column = column_of(tgt_len[pl.ds(member, 1), :])
    ends = total(jnp.where(i <= j, jnp.broadcast_to(column, (SEQ_DEV, SEQ_DEV)), 0.0), 0)
    row = iota((TOK, SEQ_DEV), 0).astype(F32)
    mine = total(jnp.where(row >= ends, 1.0, 0.0), 1)
    codes = dest[...]
    to_me = (codes >> 4) == member
    target = total(jnp.where(to_me, codes & 15, 0), 1)
    length = total(jnp.where(to_me, src_len[...], 0), 1)
    lane = iota((SEQ_DEV, SLOTS), 1)
    own = (lane >> 4) == iota((SEQ_DEV, SLOTS), 0)
    target = total(jnp.where(own, target, 0.0), 0)
    length = total(jnp.where(own, length, 0.0), 0)
    step = (iota((1, SLOTS), 1) & 15).astype(F32)
    target = jnp.where(step < length, target, -1.0)
    return mine == target


def forward_kernel(
    x_ref, gain_ref, cot_ref, a_hbm, b_hbm, keep_ref, send_ref, *rest
):
    by_x, by_z = rest[:RING], rest[RING : 2 * RING]
    a_buf, b_buf, normed_ref, left_ref, a_sem, b_sem = rest[2 * RING :]
    count, step, cols = a_buf.shape

    def fetch(k):
        rows = pl.ds(k * step, step)
        return (
            pltpu.make_async_copy(a_hbm.at[rows, :], a_buf.at[k], a_sem.at[k]),
            pltpu.make_async_copy(b_hbm.at[rows, :], b_buf.at[k], b_sem.at[k]),
        )

    for k in range(count):
        for copy in fetch(k):
            copy.start()
    xf = x_ref[...].astype(F32)
    scale = lax.rsqrt(jnp.mean(xf * xf, axis=-1, keepdims=True) + EPS)
    normed_ref[...] = (xf * scale * gain_ref[...]).astype(BF16)
    core = lax.axis_index("section")

    @pl.when(core == 0)
    def _():
        left_ref[...] = normed_ref[...]

    @pl.when(core != 0)
    def _():
        left_ref[...] = cot_ref[...]

    acc_a = acc_b = None
    for k in range(count):
        for copy in fetch(k):
            copy.wait()
        at = slice(k * step, (k + 1) * step)
        part_a = jnp.dot(normed_ref[:, at], a_buf[k], preferred_element_type=F32)
        part_b = jnp.dot(left_ref[:, at], b_buf[k], preferred_element_type=F32)
        acc_a = part_a if acc_a is None else acc_a + part_a
        acc_b = part_b if acc_b is None else acc_b + part_b
    half = cols // 2
    parts = [[acc[:, i * half : (i + 1) * half].astype(BF16) for acc in (acc_a, acc_b)] for i in range(2)]

    def put(ref, pieces):
        ref[:, :half] = pieces[0]
        ref[:, half:] = pieces[1]

    @pl.when(core == 0)
    def _():
        put(keep_ref, parts[0])
        put(send_ref, parts[1])

    @pl.when(core != 0)
    def _():
        put(keep_ref, parts[1])
        put(send_ref, parts[0])

    z, x = lax.axis_index("z"), lax.axis_index("x")
    block = cols // RING
    for k in range(RING):
        for j in range(RING):
            to = slice(j * block, (j + 1) * block)
            at = ((z + j) % RING * RING + (x + k) % RING) * block
            by_x[k][:, to] = normed_ref[:, pl.ds(pl.multiple_of(at, block), block)]
            at = ((z + k) % RING * RING + (x + j) % RING) * block
            by_z[k][:, to] = left_ref[:, pl.ds(pl.multiple_of(at, block), block)]


def forward(x, gain, cot, weight_a, weight_b):
    rows, width = x.shape
    cols = weight_a.shape[1]
    step = 512
    count = width // step
    half = jax.ShapeDtypeStruct((rows, cols), BF16)
    outs = pl.pallas_call(
        forward_kernel,
        in_specs=[VMEM] * 3 + [HBM] * 2,
        out_specs=[VMEM] * (2 + 2 * RING),
        out_shape=[half] * (2 + 2 * RING),
        scratch_shapes=[pltpu.VMEM((count, step, cols), BF16)] * 2
        + [pltpu.VMEM((rows, width), BF16)] * 2
        + [pltpu.SemaphoreType.DMA((count,))] * 2,
        compiler_params=params(32),
        cost_estimate=cost(4 * rows * width * cols, 4 * width * cols),
        name="forward",
    )(x, gain, cot, weight_a, weight_b)
    return outs[0], outs[1], outs[2 : 2 + RING], outs[2 + RING :]


def pack_kernel(keep_ref, got_ref, src_ref, dest_ref, out_ref):
    spread = slot_onehot(member_index(), src_ref, dest_ref)

    @pl.when(lax.axis_index("section") == 0)
    def _():
        out_ref[...] = jnp.dot(spread, keep_ref[...], preferred_element_type=F32).astype(BF16)

    @pl.when(lax.axis_index("section") != 0)
    def _():
        out_ref[...] = jnp.dot(spread, got_ref[...], preferred_element_type=F32).astype(BF16)


def pack(keep, got, src_len, dest):
    width = keep.shape[1]
    return pl.pallas_call(
        pack_kernel,
        in_specs=[VMEM] * 4,
        out_specs=VMEM,
        out_shape=jax.ShapeDtypeStruct((SLOTS, width), BF16),
        compiler_params=params(),
        cost_estimate=cost(2 * SLOTS * TOK * width, 2 * SLOTS * width),
        name="pack",
    )(keep, got, src_len, dest)


def attend_kernel(
    keep_ref, got_ref, slots_ref, src_ref, tgt_ref, dest_ref, front_ref, back_ref, own_ref
):
    mask = pair_mask(member_index(), src_ref, tgt_ref, dest_ref)

    @pl.when(lax.axis_index("section") == 0)
    def _():
        own_ref[...] = got_ref[...]

    @pl.when(lax.axis_index("section") != 0)
    def _():
        own_ref[...] = keep_ref[...]

    half = own_ref.shape[1] // 2
    pair = 2 * HEAD_DIM
    low = iota((1, pair), 1) < HEAD_DIM
    nothing = jnp.zeros((), BF16)

    def both(value):
        return jnp.concatenate(
            [jnp.where(low, value, nothing), jnp.where(low, nothing, value)], axis=0
        )

    def nt(left, right):
        return lax.dot_general(left, right, (((1,), (1,)), ((), ())), preferred_element_type=F32)

    def tn(left, right):
        return lax.dot_general(left, right, (((0,), (0,)), ((), ())), preferred_element_type=F32)

    def one(score, dweight):
        expo = jnp.where(mask, jnp.exp(score), 0.0)
        weight = expo * (1.0 / jnp.sum(expo, axis=-1, keepdims=True))
        mean = jnp.sum(weight * dweight, axis=-1, keepdims=True)
        return weight.astype(BF16), (weight * (dweight - mean)).astype(BF16)

    def fold(value):
        return jnp.where(low, value[:SLOTS], value[SLOTS:]).astype(BF16)

    for p in range(half // pair):
        first = slice(p * pair, (p + 1) * pair)
        second = slice(half + p * pair, half + (p + 1) * pair)
        query, dout = own_ref[:, first], own_ref[:, second]
        keys, values = both(slots_ref[:, first]), both(slots_ref[:, second])
        score, dweight = nt(query, keys), nt(dout, values)
        weight_0, dscore_0 = one(score[:, :SLOTS], dweight[:, :SLOTS])
        weight_1, dscore_1 = one(score[:, SLOTS:], dweight[:, SLOTS:])
        weight = jnp.concatenate([weight_0, weight_1], axis=1)
        dscore = jnp.concatenate([dscore_0, dscore_1], axis=1)
        front_ref[:, first] = jnp.dot(dscore, keys, preferred_element_type=F32).astype(BF16)
        front_ref[:, second] = jnp.dot(weight, values, preferred_element_type=F32).astype(BF16)
        back_ref[:, first] = fold(tn(dscore, query))
        back_ref[:, second] = fold(tn(weight, dout))


def attend(keep, got, slots, src_len, tgt_len, dest):
    rows, width = keep.shape
    return pl.pallas_call(
        attend_kernel,
        in_specs=[VMEM] * 6,
        out_specs=[VMEM] * 2,
        out_shape=[
            jax.ShapeDtypeStruct((rows, width), BF16),
            jax.ShapeDtypeStruct((SLOTS, width), BF16),
        ],
        scratch_shapes=[pltpu.VMEM((rows, width), BF16)],
        compiler_params=params(),
        cost_estimate=cost(24 * rows * SLOTS * width, 8 * SLOTS * width),
        name="attend",
    )(keep, got, slots, src_len, tgt_len, dest)


def unpack_kernel(back_ref, front_ref, src_ref, dest_ref, keep_ref, send_ref):
    spread = slot_onehot(member_index(), src_ref, dest_ref)
    rows = lax.dot_general(
        spread, back_ref[...], (((0,), (0,)), ((), ())), preferred_element_type=F32
    ).astype(BF16)

    @pl.when(lax.axis_index("section") == 0)
    def _():
        keep_ref[...] = rows
        send_ref[...] = front_ref[...]

    @pl.when(lax.axis_index("section") != 0)
    def _():
        keep_ref[...] = front_ref[...]
        send_ref[...] = rows


def unpack(back, front, src_len, dest):
    width = front.shape[1]
    half = jax.ShapeDtypeStruct((TOK, width), BF16)
    return pl.pallas_call(
        unpack_kernel,
        in_specs=[VMEM] * 4,
        out_specs=[VMEM] * 2,
        out_shape=[half, half],
        compiler_params=params(),
        cost_estimate=cost(2 * SLOTS * TOK * width, 4 * SLOTS * width),
        name="unpack",
    )(back, front, src_len, dest)


def join_kernel(keep_ref, got_ref, first_ref, second_ref):
    half = keep_ref.shape[1] // 2
    mine = pl.multiple_of(lax.axis_index("section") * half, half)
    other = pl.multiple_of((1 - lax.axis_index("section")) * half, half)
    first_ref[:, pl.ds(mine, half)] = keep_ref[:, :half]
    first_ref[:, pl.ds(other, half)] = got_ref[:, :half]
    second_ref[:, pl.ds(mine, half)] = keep_ref[:, half:]
    second_ref[:, pl.ds(other, half)] = got_ref[:, half:]


def join(keep, got):
    shape = jax.ShapeDtypeStruct(keep.shape, BF16)
    return pl.pallas_call(
        join_kernel,
        in_specs=[VMEM, VMEM],
        out_specs=[VMEM] * 2,
        out_shape=[shape, shape],
        compiler_params=params(),
        cost_estimate=cost(0, 8 * keep.size),
        name="join",
    )(keep, got)


def dnorm_kernel(first_ref, second_ref, a_hbm, b_hbm, out_ref, a_buf, b_buf, a_sem, b_sem):
    count, step, _ = a_buf.shape
    source = lax.axis_index("section") == 0

    def nt(left, right):
        return lax.dot_general(left, right, (((1,), (1,)), ((), ())), preferred_element_type=F32)

    def fetch(k):
        rows = pl.ds(k * step, step)
        return (
            pltpu.make_async_copy(a_hbm.at[rows, :], a_buf.at[k], a_sem.at[k]),
            pltpu.make_async_copy(b_hbm.at[rows, :], b_buf.at[k], b_sem.at[k]),
        )

    for k in range(count):
        for copy in fetch(k):
            copy.start()
    for k in range(count):
        at = slice(k * step, (k + 1) * step)
        for copy in fetch(k):
            copy.wait()

        @pl.when(source)
        def _(k=k, at=at):
            out_ref[:, at] = (
                nt(first_ref[...], a_buf[k]) + nt(second_ref[...], b_buf[k])
            ).astype(BF16)

        @pl.when(jnp.logical_not(source))
        def _(k=k, at=at):
            out_ref[:, at] = nt(first_ref[...], a_buf[k]).astype(BF16)


def dnorm_partial(first, second, weight_a, weight_b):
    rows, cols = first.shape
    width = weight_a.shape[0]
    step = 512
    count = width // step
    return pl.pallas_call(
        dnorm_kernel,
        in_specs=[VMEM] * 2 + [HBM] * 2,
        out_specs=VMEM,
        out_shape=jax.ShapeDtypeStruct((rows, width), BF16),
        scratch_shapes=[pltpu.VMEM((count, step, cols), BF16)] * 2
        + [pltpu.SemaphoreType.DMA((count,))] * 2,
        compiler_params=params(24),
        cost_estimate=cost(4 * rows * width * cols, 4 * width * cols),
        name="dnorm",
    )(first, second, weight_a, weight_b)


def rms_back_kernel(x_ref, gain_ref, parts_ref, out_ref):
    rows = out_ref.shape[0]
    mine = pl.multiple_of(lax.axis_index("mp") * rows, rows)
    xf = x_ref[pl.ds(mine, rows), :].astype(F32)
    scale = lax.rsqrt(jnp.mean(xf * xf, axis=-1, keepdims=True) + EPS)
    dnorm = parts_ref[0].astype(F32)
    for i in range(1, RING):
        dnorm += parts_ref[i].astype(F32)
    upper = gain_ref[...] * dnorm
    inner = jnp.mean(xf * upper, axis=-1, keepdims=True)
    out_ref[...] = (scale * upper - xf * (scale * scale * scale * inner)).astype(BF16)


def rms_back(x, gain, parts):
    rows, width = parts.shape[1:]
    return pl.pallas_call(
        rms_back_kernel,
        in_specs=[VMEM] * 3,
        out_specs=VMEM,
        out_shape=jax.ShapeDtypeStruct((rows, width), BF16),
        compiler_params=params(),
        cost_estimate=cost(10 * rows * width, 12 * rows * width),
        name="rms_back",
    )(x, gain, parts)


def place_kernel(own_ref, left_ref, right_ref, far_a_ref, far_b_ref, out_ref):
    rows = own_ref.shape[0]
    half = rows // 2

    def at(k):
        return pl.multiple_of(((lax.axis_index("mp") + k) % RING) * rows, rows)

    out_ref[pl.ds(at(0), rows), :] = own_ref[...]
    out_ref[pl.ds(at(3), rows), :] = left_ref[...]
    out_ref[pl.ds(at(1), rows), :] = right_ref[...]
    out_ref[pl.ds(at(2), half), :] = far_a_ref[...]
    out_ref[pl.ds(pl.multiple_of(at(2) + half, half), half), :] = far_b_ref[...]


def place(pieces):
    rows, width = pieces[0].shape
    return pl.pallas_call(
        place_kernel,
        in_specs=[VMEM] * 5,
        out_specs=VMEM,
        out_shape=jax.ShapeDtypeStruct((RING * rows, width), BF16),
        compiler_params=params(),
        cost_estimate=cost(0, 4 * RING * rows * width),
        name="place",
    )(*pieces)


def shift(value, axis, k):
    return lax.ppermute(value, axis, [(i, (i + k) % RING) for i in range(RING)])


def gathered(block, axis):
    half = block.shape[0] // 2
    left, right = shift(block, axis, 1), shift(block, axis, 3)
    far_a, far_b = shift(left[:half], axis, 1), shift(right[half:], axis, 3)
    return [block, left, right, far_a, far_b]


def spread(block, axis):
    far = shift(block, axis, 2)
    return [block, shift(block, axis, 1), shift(block, axis, 3), far]


def exchanged(slices, axis):
    far = shift(slices[2], axis, 2)
    return [slices[0], shift(slices[1], axis, 1), shift(slices[3], axis, 3), far]


def turn_kernel(*refs):
    pieces, out_ref = refs[:-1], refs[-1]
    block, rows = out_ref.shape[1], pieces[0].shape[0]
    for k in range(RING):
        for p, piece in enumerate(pieces):
            out_ref[k, :, p * rows : (p + 1) * rows] = piece[:, k * block : (k + 1) * block].T


def turned(pieces):
    rows, width = pieces[0].shape
    return pl.pallas_call(
        turn_kernel,
        in_specs=[VMEM] * RING,
        out_specs=VMEM,
        out_shape=jax.ShapeDtypeStruct((RING, width // RING, RING * rows), BF16),
        compiler_params=params(),
        cost_estimate=cost(0, 4 * RING * rows * width),
        name="turn",
    )(*pieces)


def far_kernel(left_ref, own_ref, near_ref, next_ref, far_ref, top_ref, low_ref, rows_ref):
    rows = own_ref.shape[0]
    for p, piece in enumerate((own_ref, near_ref, next_ref, far_ref)):
        rows_ref[p * rows : (p + 1) * rows, :] = piece[...]
    half = top_ref.shape[0]
    for i, out in enumerate((top_ref, low_ref)):
        out[...] = jnp.dot(
            left_ref[2, i * half : (i + 1) * half, :], rows_ref[...], preferred_element_type=F32
        ).astype(BF16)


def far_block(left, pieces):
    rows, cols = pieces[0].shape
    block = left.shape[1]
    half = jax.ShapeDtypeStruct((block // 2, cols), BF16)
    return pl.pallas_call(
        far_kernel,
        in_specs=[VMEM] * (1 + RING),
        out_specs=[VMEM] * 3,
        out_shape=[half, half, jax.ShapeDtypeStruct((RING * rows, cols), BF16)],
        compiler_params=params(),
        cost_estimate=cost(2 * RING * rows * block * cols, 8 * RING * rows * cols),
        name="far",
    )(left, *pieces)


def side_kernel(left_ref, rows_ref, from_left_ref, from_right_ref, right_out, left_out):
    half = from_left_ref.shape[0]

    def product(k):
        return jnp.dot(left_ref[k], rows_ref[...], preferred_element_type=F32)

    block = product(1)
    right_out[:half, :] = (block[:half] + from_left_ref[...].astype(F32)).astype(BF16)
    right_out[half:, :] = block[half:].astype(BF16)
    block = product(3)
    left_out[:half, :] = block[:half].astype(BF16)
    left_out[half:, :] = (block[half:] + from_right_ref[...].astype(F32)).astype(BF16)


def side_blocks(left, rows, from_left, from_right):
    block, cols = left.shape[1], rows.shape[1]
    shape = jax.ShapeDtypeStruct((block, cols), BF16)
    return pl.pallas_call(
        side_kernel,
        in_specs=[VMEM] * 4,
        out_specs=[VMEM] * 2,
        out_shape=[shape, shape],
        compiler_params=params(),
        cost_estimate=cost(4 * rows.shape[0] * block * cols, 4 * rows.size),
        name="side",
    )(left, rows, from_left, from_right)


def own_kernel(left_ref, rows_ref, a_ref, b_ref, out_ref):
    block = jnp.dot(left_ref[0], rows_ref[...], preferred_element_type=F32)
    out_ref[...] = block + a_ref[...].astype(F32) + b_ref[...].astype(F32)


def own_block(left, rows, a, b):
    block, cols = left.shape[1], rows.shape[1]
    return pl.pallas_call(
        own_kernel,
        in_specs=[VMEM] * 4,
        out_specs=VMEM,
        out_shape=jax.ShapeDtypeStruct((block, cols), F32),
        compiler_params=params(),
        cost_estimate=cost(2 * rows.shape[0] * block * cols, 8 * rows.size),
        name="own",
    )(left, rows, a, b)


def reduced(left, pieces, axis):
    top, low, rows = far_block(left, pieces)
    from_left, from_right = shift(top, axis, 1), shift(low, axis, 3)
    to_right, to_left = side_blocks(left, rows, from_left, from_right)
    return own_block(left, rows, shift(to_right, axis, 1), shift(to_left, axis, 3))


def per_device(states, gains, proj_a, proj_b, cotangent, src_len, tgt_len, dest):
    weight_a, weight_b = proj_a[0], proj_b[0]
    rows = states[0]
    keep, send, by_x, by_z = forward(rows, gains, cotangent, weight_a, weight_b)
    swap = [(0, 1), (1, 0)]
    got = lax.ppermute(send, "section", swap)
    slots = pack(keep, got, src_len, dest)
    width = slots.shape[1]
    slots = slots.reshape(SEQ_DEV, MAXLEN, width)
    slots = lax.all_to_all(slots, ("z", "x"), split_axis=0, concat_axis=0, tiled=True)
    slots = slots.reshape(SLOTS, width)
    lefts_a, lefts_b = exchanged(by_x, "x"), exchanged(by_z, "z")
    slots, lefts_a = lax.optimization_barrier((slots, lefts_a))
    front, back = attend(keep, got, slots, src_len, tgt_len, dest)
    back = back.reshape(SEQ_DEV, MAXLEN, width)
    back = lax.all_to_all(back, ("z", "x"), split_axis=0, concat_axis=0, tiled=True)
    left_a, left_b = turned(lefts_a), turned(lefts_b)
    back, left_a, left_b = lax.optimization_barrier((back, left_a, left_b))
    keep, send = unpack(back.reshape(SLOTS, width), front, src_len, dest)
    got = lax.ppermute(send, "section", swap)
    first, second = join(keep, got)

    rights_a, rights_b = spread(first, "x"), spread(second, "z")
    partial = dnorm_partial(first, second, weight_a, weight_b)
    parts = lax.all_to_all(
        partial.reshape(RING, TOK // RING, -1), "mp", split_axis=0, concat_axis=0, tiled=True
    )
    quarter = rms_back(rows, gains, parts)
    grad_states = place(gathered(quarter, "mp"))

    grad_a = reduced(left_a, rights_a, "z")
    grad_b = reduced(left_b, rights_b, "x")
    return (grad_states[None], grad_a[None], grad_b[None])


def solution(mesh):
    split = jax.sharding.Mesh(mesh.devices.reshape(2, RING, RING, RING), ("section", "z", "x", "mp"))
    dp = ("z", "x")
    return jax.shard_map(
        per_device,
        mesh=split,
        in_specs=(
            P("section", dp, None),
            P("section", None),
            P("section", None, "mp"),
            P("section", None, "mp"),
            P(dp, None),
            P(),
            P(),
            P(),
        ),
        out_specs=(P("section", dp, None), P("section", dp, "mp"), P("section", dp, "mp")),
        check_vma=False,
    )
```

time: 157 us -> 165 us (1.051)
  blocking collectives: 33.6 us -> 0 us
  starting transfers between devices: 37.9 us -> 60.3 us
  waiting for transfers between devices: 18.9 us -> 40.3 us
  other arithmetic: 6.82 us -> 0 us
  local copies, waits for them, and re-layouts: 28.5 us -> 31.8 us
    all_to_all x2 -> x0, blocking collectives: 33.6 us -> none  [the longest x1 19.6 us: per_device(): lax.all_to_all(slots, ('z', 'x'), split_axis=0, concat_axis=0, tiled=True)]
    ppermute x26 -> x24, waiting for transfers between devices: 15.9 us -> 37.3 us  [shift(): return lax.ppermute(value, axis, [(i, (i + k) % RING) for i in range(RING)])]
    all_to_all x0 -> x2, starting transfers between devices: none -> 12.8 us  [the longest x1 7.88 us: per_device(): lax.all_to_all(slots, ('z', 'x'), split_axis=0, concat_axis=0, tiled=True)]
    ppermute x26 -> x24, starting transfers between devices: 33.3 us -> 43 us  [shift(): return lax.ppermute(value, axis, [(i, (i + k) % RING) for i in range(RING)])]
    unnamed x50 -> x62, local copies, waits for them, and re-layouts: 23 us -> 31.8 us
    broadcast_in_dim x2 -> x0, other arithmetic: 3.57 us -> none  [per_device(): return (grad_states[None], grad_a[None], grad_b[None])]
    slice x6 -> x2, local copies, waits for them, and re-layouts: 2.77 us -> 0.02 us  [gathered(): far_a, far_b = (shift(left[:half], axis, 1), shift(right[half:], axis, 3))]
    squeeze x2 -> x0, local copies, waits for them, and re-layouts: 1.79 us -> none  [take(): return lax.dynamic_index_in_dim(slices, (me + k) % RING, 0, keepdims=False)]
  transfers between devices with their start and end apart: 29 -> 29, of which waited for: 10 -> 10; matrix products, arithmetic and copies ran while one was open for 7% -> 0% of each run, Pallas kernels for 12% -> 6%
where the time goes in v2:
time: 165 us; the launch traced here: 164 us
  starting transfers between devices  60.3 us (37%)
  waiting for transfers between devices  40.3 us (24%)
  local copies, waits for them, and re-layouts  31.8 us (19%)
  Pallas kernels  30.3 us (18%)
    ppermute x24, starting transfers between devices, shift(): return lax.ppermute(value, axis, [(i, (i + k) % RING) for i in range(RING)])  43 us
    ppermute x24, waiting for transfers between devices, shift(): return lax.ppermute(value, axis, [(i, (i + k) % RING) for i in range(RING)])  37.3 us
    unnamed x62, local copies, waits for them, and re-layouts  31.8 us
    pallas_call x1, Pallas kernels, dnorm_partial(): pl.pallas_call(dnorm_kernel, in_specs=[VMEM] * 2 + [HBM] * 2, out_specs=V...  9.08 us
    all_to_all x1, starting transfers between devices, per_device(): lax.all_to_all(slots, ('z', 'x'), split_axis=0, concat_axis=0, tiled=True)  7.88 us
    pallas_call x1, Pallas kernels, forward(): pl.pallas_call(forward_kernel, in_specs=[VMEM] * 3 + [HBM] * 2, out_specs...  5.97 us
    all_to_all x1, starting transfers between devices, per_device(): lax.all_to_all(back, ('z', 'x'), split_axis=0, concat_axis=0, tiled=True)  4.96 us
    all_to_all x1, starting transfers between devices, per_device(): lax.all_to_all(partial.reshape(RING, TOK // RING, -1), 'mp', split_axis=0...  4.46 us
  transfers between devices with their start and end apart: 29, of which 10 were waited for; matrix products, arithmetic and copies ran while one was open for 0% of the time, Pallas kernels for 6%

profile of v2, /device:TPU:0, one launch (start us, length us, event | category | flops | bytes accessed | tf_op | source)
XLA Modules:
  0.0 163.6 jit_solution(5187655854145393733)
XLA Ops:
  0.6 3.4 %copy-done = bf16[1,4096,1024]{2,1,0:T(8,128)(2,1)S(1)} copy-done((bf16[1,4096,1024]{2,1,0:T(8,128)(2,1)S(1)}, bf16[1,4096,1024]{2,1,0:T(8,128)(2,1)}, u32[]{:S(2)}) %copy-start) | copy-done | bytes 8388632
  4.0 3.4 %copy-done.2 = bf16[1,4096,1024]{2,1,0:T(8,128)(2,1)S(1)} copy-done((bf16[1,4096,1024]{2,1,0:T(8,128)(2,1)S(1)}, bf16[1,4096,1024]{2,1,0:T(8,128)(2,1)}, u32[]{:S(2)}) %copy-start.2) | copy-done | bytes 8388632
  7.4 1.2 copy-done.8
  8.6 1.2 copy-done.12
  10.6 6.0 %forward.1 = (bf16[128,1024]{1,0:T(8,128)(2,1)S(1)}, bf16[128,1024]{1,0:T(8,128)(2,1)S(1)}, bf16[128,1024]{1,0:T(8,128)(2,1)S(1)}, bf16[128,1024]{1,0:T(8,128)(2...) custom-call(bf16[128,4096]{1,0:T(8,128)(2,1)S(1)} %bitcast.15, ...), custom_call_target="tpu_custom_call" | custom-call | flops 2147483648 | bytes 16777216 | tf_op jit(solution)/shard_map/forward/pallas_call | solution.py:152
  20.8 1.5 collective-permute-done.got_ref
  23.5 7.9 %all-to-all-start = ((bf16[16,16,1024]{2,1,0:T(8,128)(2,1)}), bf16[16,16,1024]{2,1,0:T(8,128)(2,1)S(1)}, u32[]{:S(2)}, u32[]{:S(2)}) async-start(bf16[16,16,1024]{2,1,0:T(8,128)(2,1)} %bitcast.3), calls=%async_computation | async-start | bytes 1048576 | tf_op jit(solution)/shard_map/all_to_all | solution.py:551
  31.4 1.9 %collective-permute-start.1 = (bf16[128,1024]{1,0:T(8,128)(2,1)}, bf16[128,1024]{1,0:T(8,128)(2,1)S(1)}, u32[]{:S(2)}, u32[]{:S(2)}) collective-permute-start(bf16[128,1024]{1,0:T(8,128)(2,1)} %get-tuple-element.40), channel_id=1, source_target_pairs={{0,4},{4,8},{8,12},{12,0},{1,5},{5,9},{9,13},{13,1},{2,6},{6,10},{... | collective-permute-start | bytes 786440 | tf_op jit(solution)/shard_map/ppermute | solution.py:422
  33.3 1.4 collective-permute-start.2
  34.7 2.2 %collective-permute-start.3 = (bf16[128,1024]{1,0:T(8,128)(2,1)}, bf16[128,1024]{1,0:T(8,128)(2,1)S(1)}, u32[]{:S(2)}, u32[]{:S(2)}) collective-permute-start(bf16[128,1024]{1,0:T(8,128)(2,1)} %copy-done.28), channel_id=1, source_target_pairs={{0,8},{4,12},{8,0},{12,4},{1,9},{5,13},{9,1},{13,5},{2,10},{6,14},... | collective-permute-start | bytes 786440 | tf_op jit(solution)/shard_map/ppermute | solution.py:422
  36.8 10.3 %collective-permute-done.1.refs_1_ = bf16[128,1024]{1,0:T(8,128)(2,1)S(1)} collective-permute-done((bf16[128,1024]{1,0:T(8,128)(2,1)}, bf16[128,1024]{1,0:T(8,128)(2,1)S(1)}, u32[]{:S(2)}, u32[]{:S(2)}) %collective-permute-start.1) | collective-permute-done | bytes 262176 | tf_op jit(solution)/shard_map/ppermute | solution.py:422
  48.5 3.8 %collective-permute-done.3.refs_3_ = bf16[128,1024]{1,0:T(8,128)(2,1)S(1)} collective-permute-done((bf16[128,1024]{1,0:T(8,128)(2,1)}, bf16[128,1024]{1,0:T(8,128)(2,1)S(1)}, u32[]{:S(2)}, u32[]{:S(2)}) %collective-permute-start.3) | collective-permute-done | bytes 262176 | tf_op jit(solution)/shard_map/ppermute | solution.py:422
  52.3 3.0 %attend.1 = (bf16[128,1024]{1,0:T(8,128)(2,1)S(1)}, bf16[256,1024]{1,0:T(8,128)(2,1)}) custom-call(bf16[128,1024]{1,0:T(8,128)(2,1)S(1)} %get-tuple-element.37.keep_ref, bf16[128,1024]{1,0:T(8,128)(2,1)S(1)} %collective-permute-done.got_ref, bf16[256,1024]{1,0:T(8,128)(2,1)S(1)} %bitcast.18, s32[16,16]{1,0:T(8,128)S(1)} %copy-done.23, ...), custom_call_target="tpu_custom_call" | custom-call | flops 805306368 | bytes 2097152 | tf_op jit(solution)/shard_map/attend/pallas_call | solution.py:248
  55.3 5.0 %all-to-all-start.1 = ((bf16[16,16,1024]{2,1,0:T(8,128)(2,1)}), bf16[16,16,1024]{2,1,0:T(8,128)(2,1)S(1)}, u32[]{:S(2)}, u32[]{:S(2)}) async-start(bf16[16,16,1024]{2,1,0:T(8,128)(2,1)} %bitcast.5), calls=%async_computation.1 | async-start | bytes 1048576 | tf_op jit(solution)/shard_map/all_to_all | solution.py:557
  60.3 1.9 %collective-permute-start.4 = (bf16[128,1024]{1,0:T(8,128)(2,1)}, bf16[128,1024]{1,0:T(8,128)(2,1)S(1)}, u32[]{:S(2)}, u32[]{:S(2)}) collective-permute-start(bf16[128,1024]{1,0:T(8,128)(2,1)} %copy-done.27), channel_id=1, source_target_pairs={{0,16},{16,32},{32,48},{48,0},{1,17},{17,33},{33,49},{49,1},{2,18}... | collective-permute-start | bytes 786440 | tf_op jit(solution)/shard_map/ppermute | solution.py:422
  62.2 1.4 collective-permute-start.5
  63.6 2.2 %collective-permute-start.6 = (bf16[128,1024]{1,0:T(8,128)(2,1)}, bf16[128,1024]{1,0:T(8,128)(2,1)S(1)}, u32[]{:S(2)}, u32[]{:S(2)}) collective-permute-start(bf16[128,1024]{1,0:T(8,128)(2,1)} %copy-done.25), channel_id=1, source_target_pairs={{0,32},{16,48},{32,0},{48,16},{1,33},{17,49},{33,1},{49,17},{2,34}... | collective-permute-start | bytes 786440 | tf_op jit(solution)/shard_map/ppermute | solution.py:422
  65.7 9.9 %collective-permute-done.4.refs_1_ = bf16[128,1024]{1,0:T(8,128)(2,1)S(1)} collective-permute-done((bf16[128,1024]{1,0:T(8,128)(2,1)}, bf16[128,1024]{1,0:T(8,128)(2,1)S(1)}, u32[]{:S(2)}, u32[]{:S(2)}) %collective-permute-start.4) | collective-permute-done | bytes 262176 | tf_op jit(solution)/shard_map/ppermute | solution.py:422
  75.6 4.7 %collective-permute-done.6.refs_3_ = bf16[128,1024]{1,0:T(8,128)(2,1)S(1)} collective-permute-done((bf16[128,1024]{1,0:T(8,128)(2,1)}, bf16[128,1024]{1,0:T(8,128)(2,1)S(1)}, u32[]{:S(2)}, u32[]{:S(2)}) %collective-permute-start.6) | collective-permute-done | bytes 262176 | tf_op jit(solution)/shard_map/ppermute | solution.py:422
  85.3 1.5 collective-permute-done.7.got_ref
  86.9 3.5 %copy-done.1 = bf16[1,4096,1024]{2,1,0:T(8,128)(2,1)S(1)} copy-done((bf16[1,4096,1024]{2,1,0:T(8,128)(2,1)S(1)}, bf16[1,4096,1024]{2,1,0:T(8,128)(2,1)}, u32[]{:S(2)}) %copy-start.1) | copy-done | bytes 8388632
  90.3 3.4 %copy-done.3 = bf16[1,4096,1024]{2,1,0:T(8,128)(2,1)S(1)} copy-done((bf16[1,4096,1024]{2,1,0:T(8,128)(2,1)S(1)}, bf16[1,4096,1024]{2,1,0:T(8,128)(2,1)}, u32[]{:S(2)}) %copy-start.3) | copy-done | bytes 8388632
  93.7 9.1 %dnorm.1 = bf16[128,4096]{1,0:T(8,128)(2,1)} custom-call(bf16[128,1024]{1,0:T(8,128)(2,1)S(1)} %get-tuple-element.57.first_ref.own_ref, bf16[128,1024]{1,0:T(8,128)(2,1)S(1)} %get-tuple-element.58.second_ref.own_ref, bf16[4096,1024]{1,0:T(8,128)(2,1)S(1)} %bitcast.12, bf16[4096,1024]{1,0:T(8,128)(2,1)S(1)} %bitcast.14), custom_call_target="tpu_custom_call" | custom-call | flops 2147483648 | bytes 16777216 | tf_op jit(solution)/shard_map/dnorm/pallas_call | solution.py:355
  102.8 4.5 %all-to-all-start.2 = ((bf16[4,32,4096]{2,1,0:T(8,128)(2,1)}), bf16[4,32,4096]{2,1,0:T(8,128)(2,1)S(1)}, u32[]{:S(2)}, u32[]{:S(2)}) async-start(bf16[4,32,4096]{2,1,0:T(8,128)(2,1)} %bitcast.7), calls=%async_computation.2 | async-start | bytes 2097152 | tf_op jit(solution)/shard_map/all_to_all | solution.py:566
  108.4 2.1 %collective-permute-start.20 = (bf16[128,1024]{1,0:T(8,128)(2,1)}, bf16[128,1024]{1,0:T(8,128)(2,1)S(1)}, u32[]{:S(2)}, u32[]{:S(2)}) collective-permute-start(bf16[128,1024]{1,0:T(8,128)(2,1)} %copy-done.10), channel_id=1, source_target_pairs={{0,48},{16,0},{32,16},{48,32},{1,49},{17,1},{33,17},{49,33},{2,50}... | collective-permute-start | bytes 786440 | tf_op jit(solution)/shard_map/ppermute | solution.py:422
  110.5 1.5 collective-permute-start.12
  112.0 1.8 %collective-permute-start.13 = (bf16[128,1024]{1,0:T(8,128)(2,1)S(1)}, bf16[128,1024]{1,0:T(8,128)(2,1)S(1)}, u32[]{:S(2)}, u32[]{:S(2)}) collective-permute-start(bf16[128,1024]{1,0:T(8,128)(2,1)S(1)} %get-tuple-element.57.first_ref.own_ref), channel_id=1, source_target_pairs={{0,12},{4,0},{8,4},{12,8},{1,13},{5,1},{9,5},{13,9},{2,14},{6,2},{... | collective-permute-start | bytes 786440 | tf_op jit(solution)/shard_map/ppermute | solution.py:422
  113.7 3.3 %collective-permute-done.19.near_ref = bf16[128,1024]{1,0:T(8,128)(2,1)S(1)} collective-permute-done((bf16[128,1024]{1,0:T(8,128)(2,1)}, bf16[128,1024]{1,0:T(8,128)(2,1)S(1)}, u32[]{:S(2)}, u32[]{:S(2)}) %collective-permute-start.19) | collective-permute-done | bytes 262176 | tf_op jit(solution)/shard_map/ppermute | solution.py:422
  117.0 5.9 %collective-permute-start.14 = (bf16[128,1024]{1,0:T(8,128)(2,1)S(1)}, bf16[128,1024]{1,0:T(8,128)(2,1)S(1)}, u32[]{:S(2)}, u32[]{:S(2)}) collective-permute-start(bf16[128,1024]{1,0:T(8,128)(2,1)S(1)} %get-tuple-element.57.first_ref.own_ref), channel_id=1, source_target_pairs={{0,8},{4,12},{8,0},{12,4},{1,9},{5,13},{9,1},{13,5},{2,10},{6,14},... | collective-permute-start | bytes 786440 | tf_op jit(solution)/shard_map/ppermute | solution.py:422
  123.8 1.2 far.3
  125.4 2.8 %collective-permute-start.23 = (bf16[128,1024]{1,0:T(8,128)(2,1)}, bf16[128,1024]{1,0:T(8,128)(2,1)}, u32[]{:S(2)}, u32[]{:S(2)}) collective-permute-start(bf16[128,1024]{1,0:T(8,128)(2,1)} %get-tuple-element.68), channel_id=1, source_target_pairs={{0,12},{4,0},{8,4},{12,8},{1,13},{5,1},{9,5},{13,9},{2,14},{6,2},{... | collective-permute-start | bytes 786440 | tf_op jit(solution)/shard_map/ppermute | solution.py:422
  128.7 1.2 far.2
  130.8 3.2 %collective-permute-start.16 = (bf16[128,1024]{1,0:T(8,128)(2,1)}, bf16[128,1024]{1,0:T(8,128)(2,1)}, u32[]{:S(2)}, u32[]{:S(2)}) collective-permute-start(bf16[128,1024]{1,0:T(8,128)(2,1)} %get-tuple-element.62), channel_id=1, source_target_pairs={{0,48},{16,0},{32,16},{48,32},{1,49},{17,1},{33,17},{49,33},{2,50}... | collective-permute-start | bytes 786440 | tf_op jit(solution)/shard_map/ppermute | solution.py:422
  134.1 1.2 copy-done.9
  135.7 1.5 collective-permute-start.8
  137.2 1.2 copy-done.5
  138.4 1.7 %side.3 = (bf16[256,1024]{1,0:T(8,128)(2,1)S(1)}, bf16[256,1024]{1,0:T(8,128)(2,1)S(1)}) custom-call(bf16[4,256,512]{2,1,0:T(8,128)(2,1)S(1)} %turn.3.left_ref, bf16[512,1024]{1,0:T(8,128)(2,1)S(1)} %copy-done.5, bf16[128,1024]{1,0:T(8,128)(2,1)} %collective-permute-done.22.from_left_ref, bf16[128,1024]{1,0:T(8,128)(2,1)} %collective-permute-done.23.from_right_ref), custom_call_target="tpu_custom_call" | custom-call | flops 536870912 | bytes 2097152 | tf_op jit(solution)/shard_map/side/pallas_call | solution.py:506
  140.1 1.2 collective-permute-start.24
  141.4 2.1 %collective-permute-start.25 = (bf16[256,1024]{1,0:T(8,128)(2,1)S(1)}, bf16[256,1024]{1,0:T(8,128)(2,1)S(1)}, u32[]{:S(2)}, u32[]{:S(2)}) collective-permute-start(bf16[256,1024]{1,0:T(8,128)(2,1)S(1)} %get-tuple-element.70), channel_id=1, source_target_pairs={{0,12},{4,0},{8,4},{12,8},{1,13},{5,1},{9,5},{13,9},{2,14},{6,2},{... | collective-permute-start | bytes 1572872 | tf_op jit(solution)/shard_map/ppermute | solution.py:422
  143.5 1.2 copy-done.7
  144.7 1.7 %side.2 = (bf16[256,1024]{1,0:T(8,128)(2,1)S(1)}, bf16[256,1024]{1,0:T(8,128)(2,1)S(1)}) custom-call(bf16[4,256,512]{2,1,0:T(8,128)(2,1)S(1)} %turn.2.left_ref, bf16[512,1024]{1,0:T(8,128)(2,1)S(1)} %copy-done.7, bf16[128,1024]{1,0:T(8,128)(2,1)S(1)} %collective-permute-done.15.from_left_ref, bf16[128,1024]{1,0:T(8,128)(2,1)} %collective-permute-done.16.from_right_ref), custom_call_target="tpu_custom_call" | custom-call | flops 536870912 | bytes 2097152 | tf_op jit(solution)/shard_map/side/pallas_call | solution.py:506
  146.4 3.2 %collective-permute-start.18 = (bf16[256,1024]{1,0:T(8,128)(2,1)S(1)}, bf16[256,1024]{1,0:T(8,128)(2,1)S(1)}, u32[]{:S(2)}, u32[]{:S(2)}) collective-permute-start(bf16[256,1024]{1,0:T(8,128)(2,1)S(1)} %get-tuple-element.64), channel_id=1, source_target_pairs={{0,48},{16,0},{32,16},{48,32},{1,49},{17,1},{33,17},{49,33},{2,50}... | collective-permute-start | bytes 1572872 | tf_op jit(solution)/shard_map/ppermute | solution.py:422
  149.7 1.8 %collective-permute-start.9 = (bf16[32,4096]{1,0:T(8,128)(2,1)S(1)}, bf16[32,4096]{1,0:T(8,128)(2,1)S(1)}, u32[]{:S(2)}, u32[]{:S(2)}) collective-permute-start(bf16[32,4096]{1,0:T(8,128)(2,1)S(1)} %rms_back.1.own_ref), channel_id=1, source_target_pairs={{0,3},{1,0},{2,1},{3,2},{4,7},{5,4},{6,5},{7,6},{8,11},{9,8},{10,9... | collective-permute-start | bytes 786440 | tf_op jit(solution)/shard_map/ppermute | solution.py:422
  151.5 4.6 %collective-permute-done.9.right_ref = bf16[32,4096]{1,0:T(8,128)(2,1)S(1)} collective-permute-done((bf16[32,4096]{1,0:T(8,128)(2,1)S(1)}, bf16[32,4096]{1,0:T(8,128)(2,1)S(1)}, u32[]{:S(2)}, u32[]{:S(2)}) %collective-permute-start.9) | collective-permute-done | bytes 262176 | tf_op jit(solution)/shard_map/ppermute | solution.py:422
  156.0 1.5 collective-permute-start.10
  157.5 1.8 %collective-permute-start.11 = (bf16[16,4096]{1,0:T(8,128)(2,1)S(1)}, bf16[16,4096]{1,0:T(8,128)(2,1)S(1)}, u32[]{:S(2)}, u32[]{:S(2)}) collective-permute-start(bf16[16,4096]{1,0:T(8,128)(2,1)S(1)} %slice.9), channel_id=1, source_target_pairs={{0,3},{1,0},{2,1},{3,2},{4,7},{5,4},{6,5},{7,6},{8,11},{9,8},{10,9... | collective-permute-start | bytes 393224 | tf_op jit(solution)/shard_map/ppermute | solution.py:422
  159.4 1.4 own.3
  160.8 1.4 own.2
  (90 shorter events, 18.3 us)
Async XLA Ops:
  0.6 3.4 %copy-start = (bf16[1,4096,1024]{2,1,0:T(8,128)(2,1)S(1)}, bf16[1,4096,1024]{2,1,0:T(8,128)(2,1)}, u32[]{:S(2)}) copy-start(bf16[1,4096,1024]{2,1,0:T(8,128)(2,1)} %param.10) | copy-start | bytes 25165828
  4.0 3.4 %copy-start.2 = (bf16[1,4096,1024]{2,1,0:T(8,128)(2,1)S(1)}, bf16[1,4096,1024]{2,1,0:T(8,128)(2,1)}, u32[]{:S(2)}) copy-start(bf16[1,4096,1024]{2,1,0:T(8,128)(2,1)} %param.11) | copy-start | bytes 25165828
  7.4 1.2 copy-start.8
  8.6 1.2 copy-start.12
  10.6 11.7 %copy-start.23 = (s32[16,16]{1,0:T(8,128)S(1)}, s32[16,16]{1,0:T(8,128)}, u32[]{:S(2)}) copy-start(s32[16,16]{1,0:T(8,128)} %src_ref.5) | copy-start | bytes 3076
  10.6 11.7 %copy-start.24 = (s32[16,16]{1,0:T(8,128)S(1)}, s32[16,16]{1,0:T(8,128)}, u32[]{:S(2)}) copy-start(s32[16,16]{1,0:T(8,128)} %dest_ref.5) | copy-start | bytes 3076
  10.6 41.8 %copy-start.30 = (s32[16,16]{1,0:T(8,128)S(1)}, s32[16,16]{1,0:T(8,128)}, u32[]{:S(2)}) copy-start(s32[16,16]{1,0:T(8,128)} %tgt_ref.1) | copy-start | bytes 3076
  20.8 1.5 collective-permute-start
  23.5 28.9 %all-to-all-start = ((bf16[16,16,1024]{2,1,0:T(8,128)(2,1)}), bf16[16,16,1024]{2,1,0:T(8,128)(2,1)S(1)}, u32[]{:S(2)}, u32[]{:S(2)}) async-start(bf16[16,16,1024]{2,1,0:T(8,128)(2,1)} %bitcast.3), calls=%async_computation | async-start | bytes 1048576 | tf_op jit(solution)/shard_map/all_to_all | solution.py:551
  31.4 15.7 %collective-permute-start.1 = (bf16[128,1024]{1,0:T(8,128)(2,1)}, bf16[128,1024]{1,0:T(8,128)(2,1)S(1)}, u32[]{:S(2)}, u32[]{:S(2)}) collective-permute-start(bf16[128,1024]{1,0:T(8,128)(2,1)} %get-tuple-element.40), channel_id=1, source_target_pairs={{0,4},{4,8},{8,12},{12,0},{1,5},{5,9},{9,13},{13,1},{2,6},{6,10},{... | collective-permute-start | bytes 786440 | tf_op jit(solution)/shard_map/ppermute | solution.py:422
  33.3 14.5 %collective-permute-start.2 = (bf16[128,1024]{1,0:T(8,128)(2,1)}, bf16[128,1024]{1,0:T(8,128)(2,1)S(1)}, u32[]{:S(2)}, u32[]{:S(2)}) collective-permute-start(bf16[128,1024]{1,0:T(8,128)(2,1)} %copy-done.29), channel_id=1, source_target_pairs={{0,12},{4,0},{8,4},{12,8},{1,13},{5,1},{9,5},{13,9},{2,14},{6,2},{... | collective-permute-start | bytes 786440 | tf_op jit(solution)/shard_map/ppermute | solution.py:422
  34.7 17.7 %collective-permute-start.3 = (bf16[128,1024]{1,0:T(8,128)(2,1)}, bf16[128,1024]{1,0:T(8,128)(2,1)S(1)}, u32[]{:S(2)}, u32[]{:S(2)}) collective-permute-start(bf16[128,1024]{1,0:T(8,128)(2,1)} %copy-done.28), channel_id=1, source_target_pairs={{0,8},{4,12},{8,0},{12,4},{1,9},{5,13},{9,1},{13,5},{2,10},{6,14},... | collective-permute-start | bytes 786440 | tf_op jit(solution)/shard_map/ppermute | solution.py:422
  52.3 28.0 %copy-start.19 = (bf16[128,1024]{1,0:T(8,128)(2,1)}, bf16[128,1024]{1,0:T(8,128)(2,1)S(1)}, u32[]{:S(2)}) copy-start(bf16[128,1024]{1,0:T(8,128)(2,1)S(1)} %collective-permute-done.3.refs_3_) | copy-start | bytes 786436
  55.3 29.5 %all-to-all-start.1 = ((bf16[16,16,1024]{2,1,0:T(8,128)(2,1)}), bf16[16,16,1024]{2,1,0:T(8,128)(2,1)S(1)}, u32[]{:S(2)}, u32[]{:S(2)}) async-start(bf16[16,16,1024]{2,1,0:T(8,128)(2,1)} %bitcast.5), calls=%async_computation.1 | async-start | bytes 1048576 | tf_op jit(solution)/shard_map/all_to_all | solution.py:557
  60.3 15.4 %collective-permute-start.4 = (bf16[128,1024]{1,0:T(8,128)(2,1)}, bf16[128,1024]{1,0:T(8,128)(2,1)S(1)}, u32[]{:S(2)}, u32[]{:S(2)}) collective-permute-start(bf16[128,1024]{1,0:T(8,128)(2,1)} %copy-done.27), channel_id=1, source_target_pairs={{0,16},{16,32},{32,48},{48,0},{1,17},{17,33},{33,49},{49,1},{2,18}... | collective-permute-start | bytes 786440 | tf_op jit(solution)/shard_map/ppermute | solution.py:422
  62.2 13.4 %collective-permute-start.5 = (bf16[128,1024]{1,0:T(8,128)(2,1)}, bf16[128,1024]{1,0:T(8,128)(2,1)S(1)}, u32[]{:S(2)}, u32[]{:S(2)}) collective-permute-start(bf16[128,1024]{1,0:T(8,128)(2,1)} %copy-done.26), channel_id=1, source_target_pairs={{0,48},{16,0},{32,16},{48,32},{1,49},{17,1},{33,17},{49,33},{2,50}... | collective-permute-start | bytes 786440 | tf_op jit(solution)/shard_map/ppermute | solution.py:422
  63.6 16.7 %collective-permute-start.6 = (bf16[128,1024]{1,0:T(8,128)(2,1)}, bf16[128,1024]{1,0:T(8,128)(2,1)S(1)}, u32[]{:S(2)}, u32[]{:S(2)}) collective-permute-start(bf16[128,1024]{1,0:T(8,128)(2,1)} %copy-done.25), channel_id=1, source_target_pairs={{0,32},{16,48},{32,0},{48,16},{1,33},{17,49},{33,1},{49,17},{2,34}... | collective-permute-start | bytes 786440 | tf_op jit(solution)/shard_map/ppermute | solution.py:422
  81.6 1.0 copy-start.16
  85.2 1.6 collective-permute-start.7
  86.8 16.0 %copy-start.10 = (bf16[128,1024]{1,0:T(8,128)(2,1)}, bf16[128,1024]{1,0:T(8,128)(2,1)S(1)}, u32[]{:S(2)}) copy-start(bf16[128,1024]{1,0:T(8,128)(2,1)S(1)} %get-tuple-element.58.second_ref.own_ref) | copy-start | bytes 786436
  86.8 3.5 %copy-start.1 = (bf16[1,4096,1024]{2,1,0:T(8,128)(2,1)S(1)}, bf16[1,4096,1024]{2,1,0:T(8,128)(2,1)}, u32[]{:S(2)}) copy-start(bf16[1,4096,1024]{2,1,0:T(8,128)(2,1)} %param.10) | copy-start | bytes 25165828
  90.3 3.4 %copy-start.3 = (bf16[1,4096,1024]{2,1,0:T(8,128)(2,1)S(1)}, bf16[1,4096,1024]{2,1,0:T(8,128)(2,1)}, u32[]{:S(2)}) copy-start(bf16[1,4096,1024]{2,1,0:T(8,128)(2,1)} %param.11) | copy-start | bytes 25165828
  93.7 40.4 %copy-start.22 = (f32[1,4096]{1,0:T(1,128)S(1)}, f32[1,4096]{1,0:T(1,128)}, u32[]{:S(2)}) copy-start(f32[1,4096]{1,0:T(1,128)} %gain_ref.3) | copy-start | bytes 49156
  102.8 31.3 %all-to-all-start.2 = ((bf16[4,32,4096]{2,1,0:T(8,128)(2,1)}), bf16[4,32,4096]{2,1,0:T(8,128)(2,1)S(1)}, u32[]{:S(2)}, u32[]{:S(2)}) async-start(bf16[4,32,4096]{2,1,0:T(8,128)(2,1)} %bitcast.7), calls=%async_computation.2 | async-start | bytes 2097152 | tf_op jit(solution)/shard_map/all_to_all | solution.py:566
  107.3 9.7 %collective-permute-start.19 = (bf16[128,1024]{1,0:T(8,128)(2,1)}, bf16[128,1024]{1,0:T(8,128)(2,1)S(1)}, u32[]{:S(2)}, u32[]{:S(2)}) collective-permute-start(bf16[128,1024]{1,0:T(8,128)(2,1)} %copy-done.10), channel_id=1, source_target_pairs={{0,16},{16,32},{32,48},{48,0},{1,17},{17,33},{33,49},{49,1},{2,18}... | collective-permute-start | bytes 786440 | tf_op jit(solution)/shard_map/ppermute | solution.py:422
  108.4 14.5 %collective-permute-start.20 = (bf16[128,1024]{1,0:T(8,128)(2,1)}, bf16[128,1024]{1,0:T(8,128)(2,1)S(1)}, u32[]{:S(2)}, u32[]{:S(2)}) collective-permute-start(bf16[128,1024]{1,0:T(8,128)(2,1)} %copy-done.10), channel_id=1, source_target_pairs={{0,48},{16,0},{32,16},{48,32},{1,49},{17,1},{33,17},{49,33},{2,50}... | collective-permute-start | bytes 786440 | tf_op jit(solution)/shard_map/ppermute | solution.py:422
  110.5 12.4 %collective-permute-start.21 = (bf16[128,1024]{1,0:T(8,128)(2,1)}, bf16[128,1024]{1,0:T(8,128)(2,1)S(1)}, u32[]{:S(2)}, u32[]{:S(2)}) collective-permute-start(bf16[128,1024]{1,0:T(8,128)(2,1)} %copy-done.10), channel_id=1, source_target_pairs={{0,32},{16,48},{32,0},{48,16},{1,33},{17,49},{33,1},{49,17},{2,34}... | collective-permute-start | bytes 786440 | tf_op jit(solution)/shard_map/ppermute | solution.py:422
  110.5 17.8 %collective-permute-start.12 = (bf16[128,1024]{1,0:T(8,128)(2,1)S(1)}, bf16[128,1024]{1,0:T(8,128)(2,1)S(1)}, u32[]{:S(2)}, u32[]{:S(2)}) collective-permute-start(bf16[128,1024]{1,0:T(8,128)(2,1)S(1)} %get-tuple-element.57.first_ref.own_ref), channel_id=1, source_target_pairs={{0,4},{4,8},{8,12},{12,0},{1,5},{5,9},{9,13},{13,1},{2,6},{6,10},{... | collective-permute-start | bytes 786440 | tf_op jit(solution)/shard_map/ppermute | solution.py:422
  112.0 16.3 %collective-permute-start.13 = (bf16[128,1024]{1,0:T(8,128)(2,1)S(1)}, bf16[128,1024]{1,0:T(8,128)(2,1)S(1)}, u32[]{:S(2)}, u32[]{:S(2)}) collective-permute-start(bf16[128,1024]{1,0:T(8,128)(2,1)S(1)} %get-tuple-element.57.first_ref.own_ref), channel_id=1, source_target_pairs={{0,12},{4,0},{8,4},{12,8},{1,13},{5,1},{9,5},{13,9},{2,14},{6,2},{... | collective-permute-start | bytes 786440 | tf_op jit(solution)/shard_map/ppermute | solution.py:422
  117.0 11.7 %collective-permute-start.14 = (bf16[128,1024]{1,0:T(8,128)(2,1)S(1)}, bf16[128,1024]{1,0:T(8,128)(2,1)S(1)}, u32[]{:S(2)}, u32[]{:S(2)}) collective-permute-start(bf16[128,1024]{1,0:T(8,128)(2,1)S(1)} %get-tuple-element.57.first_ref.own_ref), channel_id=1, source_target_pairs={{0,8},{4,12},{8,0},{12,4},{1,9},{5,13},{9,1},{13,5},{2,10},{6,14},... | collective-permute-start | bytes 786440 | tf_op jit(solution)/shard_map/ppermute | solution.py:422
  122.9 1.0 copy-start.11
  125.0 5.8 %copy-start.4 = (bf16[512,1024]{1,0:T(8,128)(2,1)}, bf16[512,1024]{1,0:T(8,128)(2,1)S(1)}, u32[]{:S(2)}) copy-start(bf16[512,1024]{1,0:T(8,128)(2,1)S(1)} %get-tuple-element.66.rows_ref) | copy-start | bytes 3145732
  125.0 12.1 %collective-permute-start.22 = (bf16[128,1024]{1,0:T(8,128)(2,1)}, bf16[128,1024]{1,0:T(8,128)(2,1)}, u32[]{:S(2)}, u32[]{:S(2)}) collective-permute-start(bf16[128,1024]{1,0:T(8,128)(2,1)} %get-tuple-element.67), channel_id=1, source_target_pairs={{0,4},{4,8},{8,12},{12,0},{1,5},{5,9},{9,13},{13,1},{2,6},{6,10},{... | collective-permute-start | bytes 786440 | tf_op jit(solution)/shard_map/ppermute | solution.py:422
  125.4 11.8 %collective-permute-start.23 = (bf16[128,1024]{1,0:T(8,128)(2,1)}, bf16[128,1024]{1,0:T(8,128)(2,1)}, u32[]{:S(2)}, u32[]{:S(2)}) collective-permute-start(bf16[128,1024]{1,0:T(8,128)(2,1)} %get-tuple-element.68), channel_id=1, source_target_pairs={{0,12},{4,0},{8,4},{12,8},{1,13},{5,1},{9,5},{13,9},{2,14},{6,2},{... | collective-permute-start | bytes 786440 | tf_op jit(solution)/shard_map/ppermute | solution.py:422
  129.9 1.0 copy-start.6
  130.8 12.6 %collective-permute-start.15 = (bf16[128,1024]{1,0:T(8,128)(2,1)}, bf16[128,1024]{1,0:T(8,128)(2,1)S(1)}, u32[]{:S(2)}, u32[]{:S(2)}) collective-permute-start(bf16[128,1024]{1,0:T(8,128)(2,1)} %get-tuple-element.61), channel_id=1, source_target_pairs={{0,16},{16,32},{32,48},{48,0},{1,17},{17,33},{33,49},{49,1},{2,18}... | collective-permute-start | bytes 786440 | tf_op jit(solution)/shard_map/ppermute | solution.py:422
  130.8 12.6 %collective-permute-start.16 = (bf16[128,1024]{1,0:T(8,128)(2,1)}, bf16[128,1024]{1,0:T(8,128)(2,1)}, u32[]{:S(2)}, u32[]{:S(2)}) collective-permute-start(bf16[128,1024]{1,0:T(8,128)(2,1)} %get-tuple-element.62), channel_id=1, source_target_pairs={{0,48},{16,0},{32,16},{48,32},{1,49},{17,1},{33,17},{49,33},{2,50}... | collective-permute-start | bytes 786440 | tf_op jit(solution)/shard_map/ppermute | solution.py:422
  134.1 1.2 copy-start.9
  135.7 14.0 %collective-permute-start.8 = (bf16[32,4096]{1,0:T(8,128)(2,1)S(1)}, bf16[32,4096]{1,0:T(8,128)(2,1)S(1)}, u32[]{:S(2)}, u32[]{:S(2)}) collective-permute-start(bf16[32,4096]{1,0:T(8,128)(2,1)S(1)} %rms_back.1.own_ref), channel_id=1, source_target_pairs={{0,1},{1,2},{2,3},{3,0},{4,5},{5,6},{6,7},{7,4},{8,9},{9,10},{10,1... | collective-permute-start | bytes 786440 | tf_op jit(solution)/shard_map/ppermute | solution.py:422
  137.2 1.2 copy-start.5
  140.1 17.4 %collective-permute-start.24 = (bf16[256,1024]{1,0:T(8,128)(2,1)S(1)}, bf16[256,1024]{1,0:T(8,128)(2,1)S(1)}, u32[]{:S(2)}, u32[]{:S(2)}) collective-permute-start(bf16[256,1024]{1,0:T(8,128)(2,1)S(1)} %get-tuple-element.69), channel_id=1, source_target_pairs={{0,4},{4,8},{8,12},{12,0},{1,5},{5,9},{9,13},{13,1},{2,6},{6,10},{... | collective-permute-start | bytes 1572872 | tf_op jit(solution)/shard_map/ppermute | solution.py:422
  141.4 18.0 %collective-permute-start.25 = (bf16[256,1024]{1,0:T(8,128)(2,1)S(1)}, bf16[256,1024]{1,0:T(8,128)(2,1)S(1)}, u32[]{:S(2)}, u32[]{:S(2)}) collective-permute-start(bf16[256,1024]{1,0:T(8,128)(2,1)S(1)} %get-tuple-element.70), channel_id=1, source_target_pairs={{0,12},{4,0},{8,4},{12,8},{1,13},{5,1},{9,5},{13,9},{2,14},{6,2},{... | collective-permute-start | bytes 1572872 | tf_op jit(solution)/shard_map/ppermute | solution.py:422
  143.5 1.2 copy-start.7
  146.4 14.4 %collective-permute-start.17 = (bf16[256,1024]{1,0:T(8,128)(2,1)S(1)}, bf16[256,1024]{1,0:T(8,128)(2,1)S(1)}, u32[]{:S(2)}, u32[]{:S(2)}) collective-permute-start(bf16[256,1024]{1,0:T(8,128)(2,1)S(1)} %get-tuple-element.63), channel_id=1, source_target_pairs={{0,16},{16,32},{32,48},{48,0},{1,17},{17,33},{33,49},{49,1},{2,18}... | collective-permute-start | bytes 1572872 | tf_op jit(solution)/shard_map/ppermute | solution.py:422
  146.4 14.4 %collective-permute-start.18 = (bf16[256,1024]{1,0:T(8,128)(2,1)S(1)}, bf16[256,1024]{1,0:T(8,128)(2,1)S(1)}, u32[]{:S(2)}, u32[]{:S(2)}) collective-permute-start(bf16[256,1024]{1,0:T(8,128)(2,1)S(1)} %get-tuple-element.64), channel_id=1, source_target_pairs={{0,48},{16,0},{32,16},{48,32},{1,49},{17,1},{33,17},{49,33},{2,50}... | collective-permute-start | bytes 1572872 | tf_op jit(solution)/shard_map/ppermute | solution.py:422
  149.7 6.4 %collective-permute-start.9 = (bf16[32,4096]{1,0:T(8,128)(2,1)S(1)}, bf16[32,4096]{1,0:T(8,128)(2,1)S(1)}, u32[]{:S(2)}, u32[]{:S(2)}) collective-permute-start(bf16[32,4096]{1,0:T(8,128)(2,1)S(1)} %rms_back.1.own_ref), channel_id=1, source_target_pairs={{0,3},{1,0},{2,1},{3,2},{4,7},{5,4},{6,5},{7,6},{8,11},{9,8},{10,9... | collective-permute-start | bytes 786440 | tf_op jit(solution)/shard_map/ppermute | solution.py:422
  156.0 6.2 %collective-permute-start.10 = (bf16[16,4096]{1,0:T(8,128)(2,1)S(1)}, bf16[16,4096]{1,0:T(8,128)(2,1)S(1)}, u32[]{:S(2)}, u32[]{:S(2)}) collective-permute-start(bf16[16,4096]{1,0:T(8,128)(2,1)S(1)} %slice.8), channel_id=1, source_target_pairs={{0,1},{1,2},{2,3},{3,0},{4,5},{5,6},{6,7},{7,4},{8,9},{9,10},{10,1... | collective-permute-start | bytes 393224 | tf_op jit(solution)/shard_map/ppermute | solution.py:422
  157.5 5.0 %collective-permute-start.11 = (bf16[16,4096]{1,0:T(8,128)(2,1)S(1)}, bf16[16,4096]{1,0:T(8,128)(2,1)S(1)}, u32[]{:S(2)}, u32[]{:S(2)}) collective-permute-start(bf16[16,4096]{1,0:T(8,128)(2,1)S(1)} %slice.9), channel_id=1, source_target_pairs={{0,3},{1,0},{2,1},{3,2},{4,7},{5,4},{6,5},{7,6},{8,11},{9,8},{10,9... | collective-permute-start | bytes 393224 | tf_op jit(solution)/shard_map/ppermute | solution.py:422
  (12 other events, 9.2 us)

commit v3 on v2

--- a/solution.py
+++ b/solution.py
@@ -24,6 +24,10 @@
 
 def total(value, axis):
     return jnp.sum(value.astype(F32), axis=axis, keepdims=True)
+
+
+def in_hbm(value):
+    return pltpu.with_memory_space_constraint(value, pltpu.HBM)
 
 
 def cost(flops, nbytes):
@@ -77,11 +81,21 @@
 
 
 def forward_kernel(
-    x_ref, gain_ref, cot_ref, a_hbm, b_hbm, keep_ref, send_ref, *rest
+    x_hbm, gain_hbm, cot_hbm, a_hbm, b_hbm, keep_ref, send_ref, *rest
 ):
     by_x, by_z = rest[:RING], rest[RING : 2 * RING]
-    a_buf, b_buf, normed_ref, left_ref, a_sem, b_sem = rest[2 * RING :]
+    x_ref, gain_ref, a_buf, b_buf, normed_ref, left_ref, in_sem, a_sem, b_sem, out_sem = rest[2 * RING :]
     count, step, cols = a_buf.shape
+    core = lax.axis_index("section")
+    get_x = pltpu.make_async_copy(x_hbm, x_ref, in_sem.at[0])
+    get_gain = pltpu.make_async_copy(gain_hbm, gain_ref, in_sem.at[1])
+    get_left = pltpu.make_async_copy(cot_hbm, left_ref, in_sem.at[2])
+    get_x.start()
+    get_gain.start()
+
+    @pl.when(core != 0)
+    def _():
+        get_left.start()
 
     def fetch(k):
         rows = pl.ds(k * step, step)
@@ -93,10 +107,11 @@
     for k in range(count):
         for copy in fetch(k):
             copy.start()
+    get_x.wait()
+    get_gain.wait()
     xf = x_ref[...].astype(F32)
     scale = lax.rsqrt(jnp.mean(xf * xf, axis=-1, keepdims=True) + EPS)
     normed_ref[...] = (xf * scale * gain_ref[...]).astype(BF16)
-    core = lax.axis_index("section")
 
     @pl.when(core == 0)
     def _():
@@ -104,7 +119,25 @@
 
     @pl.when(core != 0)
     def _():
-        left_ref[...] = cot_ref[...]
+        get_left.wait()
+
+    z, x = lax.axis_index("z"), lax.axis_index("x")
+    block = cols // RING
+    copies = []
+    for k in range(RING):
+        for j in range(RING):
+            to = slice(j * block, (j + 1) * block)
+            at_x = ((z + j) % RING * RING + (x + k) % RING) * block
+            at_z = ((z + k) % RING * RING + (x + j) % RING) * block
+            for source, at, out in ((normed_ref, at_x, by_x[k]), (left_ref, at_z, by_z[k])):
+                copies.append(
+                    pltpu.make_async_copy(
+                        source.at[:, pl.ds(pl.multiple_of(at, block), block)],
+                        out.at[:, to],
+                        out_sem.at[len(copies)],
+                    )
+                )
+                copies[-1].start()
 
     acc_a = acc_b = None
     for k in range(count):
@@ -132,15 +165,8 @@
         put(keep_ref, parts[1])
         put(send_ref, parts[0])
 
-    z, x = lax.axis_index("z"), lax.axis_index("x")
-    block = cols // RING
-    for k in range(RING):
-        for j in range(RING):
-            to = slice(j * block, (j + 1) * block)
-            at = ((z + j) % RING * RING + (x + k) % RING) * block
-            by_x[k][:, to] = normed_ref[:, pl.ds(pl.multiple_of(at, block), block)]
-            at = ((z + k) % RING * RING + (x + j) % RING) * block
-            by_z[k][:, to] = left_ref[:, pl.ds(pl.multiple_of(at, block), block)]
+    for copy in copies:
+        copy.wait()
 
 
 def forward(x, gain, cot, weight_a, weight_b):
@@ -151,16 +177,19 @@
     half = jax.ShapeDtypeStruct((rows, cols), BF16)
     outs = pl.pallas_call(
         forward_kernel,
-        in_specs=[VMEM] * 3 + [HBM] * 2,
-        out_specs=[VMEM] * (2 + 2 * RING),
-        out_shape=[half] * (2 + 2 * RING),
-        scratch_shapes=[pltpu.VMEM((count, step, cols), BF16)] * 2
+        in_specs=[HBM] * 5,
+        out_specs=[VMEM] * 2 + [HBM] * (2 * RING),
+        out_shape=[half] * 2 + [pltpu.HBM((rows, cols), BF16)] * (2 * RING),
+        scratch_shapes=[pltpu.VMEM((rows, width), BF16), pltpu.VMEM((1, width), F32)]
+        + [pltpu.VMEM((count, step, cols), BF16)] * 2
         + [pltpu.VMEM((rows, width), BF16)] * 2
-        + [pltpu.SemaphoreType.DMA((count,))] * 2,
+        + [pltpu.SemaphoreType.DMA((3,))]
+        + [pltpu.SemaphoreType.DMA((count,))] * 2
+        + [pltpu.SemaphoreType.DMA((2 * RING * RING,))],
         compiler_params=params(32),
         cost_estimate=cost(4 * rows * width * cols, 4 * width * cols),
         name="forward",
-    )(x, gain, cot, weight_a, weight_b)
+    )(in_hbm(x), in_hbm(gain), in_hbm(cot), in_hbm(weight_a), in_hbm(weight_b))
     return outs[0], outs[1], outs[2 : 2 + RING], outs[2 + RING :]
 
 
@@ -362,17 +391,20 @@
         compiler_params=params(24),
         cost_estimate=cost(4 * rows * width * cols, 4 * width * cols),
         name="dnorm",
-    )(first, second, weight_a, weight_b)
-
-
-def rms_back_kernel(x_ref, gain_ref, parts_ref, out_ref):
+    )(first, second, in_hbm(weight_a), in_hbm(weight_b))
+
+
+def rms_back_kernel(x_hbm, gain_ref, parts_ref, out_ref, x_ref, sem):
     rows = out_ref.shape[0]
     mine = pl.multiple_of(lax.axis_index("mp") * rows, rows)
-    xf = x_ref[pl.ds(mine, rows), :].astype(F32)
-    scale = lax.rsqrt(jnp.mean(xf * xf, axis=-1, keepdims=True) + EPS)
+    get_x = pltpu.make_async_copy(x_hbm.at[pl.ds(mine, rows), :], x_ref, sem)
+    get_x.start()
     dnorm = parts_ref[0].astype(F32)
     for i in range(1, RING):
         dnorm += parts_ref[i].astype(F32)
+    get_x.wait()
+    xf = x_ref[...].astype(F32)
+    scale = lax.rsqrt(jnp.mean(xf * xf, axis=-1, keepdims=True) + EPS)
     upper = gain_ref[...] * dnorm
     inner = jnp.mean(xf * upper, axis=-1, keepdims=True)
     out_ref[...] = (scale * upper - xf * (scale * scale * scale * inner)).astype(BF16)
@@ -382,34 +414,28 @@
     rows, width = parts.shape[1:]
     return pl.pallas_call(
         rms_back_kernel,
-        in_specs=[VMEM] * 3,
+        in_specs=[HBM] + [VMEM] * 2,
         out_specs=VMEM,
         out_shape=jax.ShapeDtypeStruct((rows, width), BF16),
+        scratch_shapes=[pltpu.VMEM((rows, width), BF16), pltpu.SemaphoreType.DMA],
         compiler_params=params(),
         cost_estimate=cost(10 * rows * width, 12 * rows * width),
         name="rms_back",
-    )(x, gain, parts)
-
-
-def place_kernel(own_ref, left_ref, right_ref, far_a_ref, far_b_ref, out_ref):
+    )(in_hbm(x), gain, parts)
+
+
+def place_kernel(own_ref, left_ref, right_ref, far_ref, out_ref):
     rows = own_ref.shape[0]
-    half = rows // 2
-
-    def at(k):
-        return pl.multiple_of(((lax.axis_index("mp") + k) % RING) * rows, rows)
-
-    out_ref[pl.ds(at(0), rows), :] = own_ref[...]
-    out_ref[pl.ds(at(3), rows), :] = left_ref[...]
-    out_ref[pl.ds(at(1), rows), :] = right_ref[...]
-    out_ref[pl.ds(at(2), half), :] = far_a_ref[...]
-    out_ref[pl.ds(pl.multiple_of(at(2) + half, half), half), :] = far_b_ref[...]
+    for k, ref in ((0, own_ref), (3, left_ref), (1, right_ref), (2, far_ref)):
+        at = (lax.axis_index("mp") + k) % RING * rows
+        out_ref[pl.ds(pl.multiple_of(at, rows), rows), :] = ref[...]
 
 
 def place(pieces):
     rows, width = pieces[0].shape
     return pl.pallas_call(
         place_kernel,
-        in_specs=[VMEM] * 5,
+        in_specs=[VMEM] * 4,
         out_specs=VMEM,
         out_shape=jax.ShapeDtypeStruct((RING * rows, width), BF16),
         compiler_params=params(),
@@ -423,10 +449,8 @@
 
 
 def gathered(block, axis):
-    half = block.shape[0] // 2
-    left, right = shift(block, axis, 1), shift(block, axis, 3)
-    far_a, far_b = shift(left[:half], axis, 1), shift(right[half:], axis, 3)
-    return [block, left, right, far_a, far_b]
+    left = shift(block, axis, 1)
+    return [block, left, shift(block, axis, 3), shift(left, axis, 1)]
 
 
 def spread(block, axis):
@@ -435,101 +459,129 @@
 
 
 def exchanged(slices, axis):
-    far = shift(slices[2], axis, 2)
-    return [slices[0], shift(slices[1], axis, 1), shift(slices[3], axis, 3), far]
+    return [shift(slices[1], axis, 1), shift(slices[3], axis, 3)], shift(slices[2], axis, 2)
 
 
 def turn_kernel(*refs):
-    pieces, out_ref = refs[:-1], refs[-1]
-    block, rows = out_ref.shape[1], pieces[0].shape[0]
+    pieces, (out_hbm, in_buf, out_buf, in_sem, out_sem) = refs[:RING], refs[RING:]
+    block, rows = out_buf.shape[1], pieces[0].shape[0]
+    loads = [pltpu.make_async_copy(pieces[p], in_buf.at[p], in_sem.at[p]) for p in range(RING)]
+    for load in loads:
+        load.start()
+    for load in loads:
+        load.wait()
+    stores = []
     for k in range(RING):
-        for p, piece in enumerate(pieces):
-            out_ref[k, :, p * rows : (p + 1) * rows] = piece[:, k * block : (k + 1) * block].T
+        for p in range(RING):
+            turned_block = in_buf[p, :, k * block : (k + 1) * block].T
+            out_buf[k, :, p * rows : (p + 1) * rows] = turned_block
+        stores.append(pltpu.make_async_copy(out_buf.at[k], out_hbm.at[k], out_sem.at[k]))
+        stores[-1].start()
+    for store in stores:
+        store.wait()
 
 
 def turned(pieces):
     rows, width = pieces[0].shape
+    shape = (RING, width // RING, RING * rows)
     return pl.pallas_call(
         turn_kernel,
-        in_specs=[VMEM] * RING,
-        out_specs=VMEM,
-        out_shape=jax.ShapeDtypeStruct((RING, width // RING, RING * rows), BF16),
+        in_specs=[HBM] * RING,
+        out_specs=HBM,
+        out_shape=pltpu.HBM(shape, BF16),
+        scratch_shapes=[pltpu.VMEM((RING, rows, width), BF16), pltpu.VMEM(shape, BF16)]
+        + [pltpu.SemaphoreType.DMA((RING,))] * 2,
         compiler_params=params(),
         cost_estimate=cost(0, 4 * RING * rows * width),
         name="turn",
-    )(*pieces)
-
-
-def far_kernel(left_ref, own_ref, near_ref, next_ref, far_ref, top_ref, low_ref, rows_ref):
+    )(*[in_hbm(piece) for piece in pieces])
+
+
+def far_kernel(left_hbm, own_ref, near_ref, next_ref, far_ref, top_ref, low_ref, rows_ref, left, sem):
+    load = pltpu.make_async_copy(left_hbm.at[2], left, sem)
+    load.start()
     rows = own_ref.shape[0]
     for p, piece in enumerate((own_ref, near_ref, next_ref, far_ref)):
         rows_ref[p * rows : (p + 1) * rows, :] = piece[...]
+    load.wait()
     half = top_ref.shape[0]
     for i, out in enumerate((top_ref, low_ref)):
         out[...] = jnp.dot(
-            left_ref[2, i * half : (i + 1) * half, :], rows_ref[...], preferred_element_type=F32
+            left[i * half : (i + 1) * half, :], rows_ref[...], preferred_element_type=F32
         ).astype(BF16)
 
 
 def far_block(left, pieces):
     rows, cols = pieces[0].shape
-    block = left.shape[1]
+    _, block, depth = left.shape
     half = jax.ShapeDtypeStruct((block // 2, cols), BF16)
     return pl.pallas_call(
         far_kernel,
-        in_specs=[VMEM] * (1 + RING),
+        in_specs=[HBM] + [VMEM] * RING,
         out_specs=[VMEM] * 3,
         out_shape=[half, half, jax.ShapeDtypeStruct((RING * rows, cols), BF16)],
+        scratch_shapes=[pltpu.VMEM((block, depth), BF16), pltpu.SemaphoreType.DMA],
         compiler_params=params(),
         cost_estimate=cost(2 * RING * rows * block * cols, 8 * RING * rows * cols),
         name="far",
-    )(left, *pieces)
-
-
-def side_kernel(left_ref, rows_ref, from_left_ref, from_right_ref, right_out, left_out):
+    )(in_hbm(left), *pieces)
+
+
+def side_kernel(left_hbm, rows_ref, from_left_ref, from_right_ref, right_out, left_out, left, sems):
+    loads = [pltpu.make_async_copy(left_hbm.at[k], left.at[i], sems.at[i]) for i, k in enumerate((1, 3))]
+    for load in loads:
+        load.start()
     half = from_left_ref.shape[0]
 
-    def product(k):
-        return jnp.dot(left_ref[k], rows_ref[...], preferred_element_type=F32)
-
-    block = product(1)
+    def product(i):
+        loads[i].wait()
+        return jnp.dot(left[i], rows_ref[...], preferred_element_type=F32)
+
+    block = product(0)
     right_out[:half, :] = (block[:half] + from_left_ref[...].astype(F32)).astype(BF16)
     right_out[half:, :] = block[half:].astype(BF16)
-    block = product(3)
+    block = product(1)
     left_out[:half, :] = block[:half].astype(BF16)
     left_out[half:, :] = (block[half:] + from_right_ref[...].astype(F32)).astype(BF16)
 
 
 def side_blocks(left, rows, from_left, from_right):
-    block, cols = left.shape[1], rows.shape[1]
+    _, block, depth = left.shape
+    cols = rows.shape[1]
     shape = jax.ShapeDtypeStruct((block, cols), BF16)
     return pl.pallas_call(
         side_kernel,
-        in_specs=[VMEM] * 4,
+        in_specs=[HBM] + [VMEM] * 3,
         out_specs=[VMEM] * 2,
         out_shape=[shape, shape],
+        scratch_shapes=[pltpu.VMEM((2, block, depth), BF16), pltpu.SemaphoreType.DMA((2,))],
         compiler_params=params(),
         cost_estimate=cost(4 * rows.shape[0] * block * cols, 4 * rows.size),
         name="side",
-    )(left, rows, from_left, from_right)
-
-
-def own_kernel(left_ref, rows_ref, a_ref, b_ref, out_ref):
-    block = jnp.dot(left_ref[0], rows_ref[...], preferred_element_type=F32)
+    )(in_hbm(left), rows, from_left, from_right)
+
+
+def own_kernel(left_hbm, rows_ref, a_ref, b_ref, out_ref, left, sem):
+    load = pltpu.make_async_copy(left_hbm.at[0], left, sem)
+    load.start()
+    load.wait()
+    block = jnp.dot(left[...], rows_ref[...], preferred_element_type=F32)
     out_ref[...] = block + a_ref[...].astype(F32) + b_ref[...].astype(F32)
 
 
 def own_block(left, rows, a, b):
-    block, cols = left.shape[1], rows.shape[1]
+    _, block, depth = left.shape
+    cols = rows.shape[1]
     return pl.pallas_call(
         own_kernel,
-        in_specs=[VMEM] * 4,
+        in_specs=[HBM] + [VMEM] * 3,
         out_specs=VMEM,
         out_shape=jax.ShapeDtypeStruct((block, cols), F32),
+        scratch_shapes=[pltpu.VMEM((block, depth), BF16), pltpu.SemaphoreType.DMA],
         compiler_params=params(),
         cost_estimate=cost(2 * rows.shape[0] * block * cols, 8 * rows.size),
         name="own",
-    )(left, rows, a, b)
+    )(in_hbm(left), rows, a, b)
 
 
 def reduced(left, pieces, axis):
@@ -540,7 +592,8 @@
 
 
 def per_device(states, gains, proj_a, proj_b, cotangent, src_len, tgt_len, dest):
-    weight_a, weight_b = proj_a[0], proj_b[0]
+    weight_a = proj_a[0]
+    weight_b = proj_b[0]
     rows = states[0]
     keep, send, by_x, by_z = forward(rows, gains, cotangent, weight_a, weight_b)
     swap = [(0, 1), (1, 0)]
@@ -550,12 +603,12 @@
     slots = slots.reshape(SEQ_DEV, MAXLEN, width)
     slots = lax.all_to_all(slots, ("z", "x"), split_axis=0, concat_axis=0, tiled=True)
     slots = slots.reshape(SLOTS, width)
-    lefts_a, lefts_b = exchanged(by_x, "x"), exchanged(by_z, "z")
-    slots, lefts_a = lax.optimization_barrier((slots, lefts_a))
+    (near_a, far_a), (near_b, far_b) = exchanged(by_x, "x"), exchanged(by_z, "z")
+    slots, near_a, near_b = lax.optimization_barrier((slots, near_a, near_b))
     front, back = attend(keep, got, slots, src_len, tgt_len, dest)
     back = back.reshape(SEQ_DEV, MAXLEN, width)
     back = lax.all_to_all(back, ("z", "x"), split_axis=0, concat_axis=0, tiled=True)
-    left_a, left_b = turned(lefts_a), turned(lefts_b)
+    left_a, left_b = turned([by_x[0], *near_a, far_a]), turned([by_z[0], *near_b, far_b])
     back, left_a, left_b = lax.optimization_barrier((back, left_a, left_b))
     keep, send = unpack(back.reshape(SLOTS, width), front, src_len, dest)
     got = lax.ppermute(send, "section", swap)

time: 165 us -> 138 us (0.84)
  local copies, waits for them, and re-layouts: 31.8 us -> 1.41 us
  Pallas kernels: 30.3 us -> 45.2 us
  waiting for transfers between devices: 40.3 us -> 34.2 us
  starting transfers between devices: 60.3 us -> 55.7 us
    unnamed x62 -> x20, local copies, waits for them, and re-layouts: 31.8 us -> 1.41 us
    pallas_call x11, Pallas kernels: 16.6 us -> 31.2 us  [the longest x1 8.96 us: forward(): pl.pallas_call(forward_kernel, in_specs=[HBM] * 5, out_specs=[VMEM] * 2 +...]
    ppermute x24 -> x23, waiting for transfers between devices: 37.3 us -> 31.2 us  [shift(): return lax.ppermute(value, axis, [(i, (i + k) % RING) for i in range(RING)])]
    ppermute x24 -> x23, starting transfers between devices: 43 us -> 38.1 us  [shift(): return lax.ppermute(value, axis, [(i, (i + k) % RING) for i in range(RING)])]
  transfers between devices with their start and end apart: 29 -> 28, of which waited for: 10 -> 9; matrix products, arithmetic and copies ran while one was open for 0% -> 0% of each run, Pallas kernels for 6% -> 22%
where the time goes in v3:
time: 138 us; the launch traced here: 137 us
  starting transfers between devices  55.7 us (40%)
  Pallas kernels  45.2 us (33%)
  waiting for transfers between devices  34.2 us (25%)
  local copies, waits for them, and re-layouts  1.41 us (1%)
    ppermute x23, starting transfers between devices, shift(): return lax.ppermute(value, axis, [(i, (i + k) % RING) for i in range(RING)])  38.1 us
    ppermute x23, waiting for transfers between devices, shift(): return lax.ppermute(value, axis, [(i, (i + k) % RING) for i in range(RING)])  31.2 us
    pallas_call x1, Pallas kernels, dnorm_partial(): pl.pallas_call(dnorm_kernel, in_specs=[VMEM] * 2 + [HBM] * 2, out_specs=V...  9.5 us
    pallas_call x1, Pallas kernels, forward(): pl.pallas_call(forward_kernel, in_specs=[HBM] * 5, out_specs=[VMEM] * 2 +...  8.96 us
    all_to_all x1, starting transfers between devices, per_device(): lax.all_to_all(slots, ('z', 'x'), split_axis=0, concat_axis=0, tiled=True)  8.4 us
    pallas_call x2, Pallas kernels, own_block(): pl.pallas_call(own_kernel, in_specs=[HBM] + [VMEM] * 3, out_specs=VMEM, o...  7.14 us
    pallas_call x2, Pallas kernels, side_blocks(): pl.pallas_call(side_kernel, in_specs=[HBM] + [VMEM] * 3, out_specs=[VMEM]...  5.32 us
    pallas_call x2, Pallas kernels, turned(): pl.pallas_call(turn_kernel, in_specs=[HBM] * RING, out_specs=HBM, out_sha...  4.67 us
  transfers between devices with their start and end apart: 28, of which 9 were waited for; matrix products, arithmetic and copies ran while one was open for 0% of the time, Pallas kernels for 22%

profile of v3, /device:TPU:0, one launch (start us, length us, event | category | flops | bytes accessed | tf_op | source)
XLA Modules:
  0.0 137.4 jit_solution(11695709038119990546)
XLA Ops:
  0.7 9.0 %forward.1 = (bf16[128,1024]{1,0:T(8,128)(2,1)S(1)}, bf16[128,1024]{1,0:T(8,128)(2,1)S(1)}, bf16[128,1024]{1,0:T(8,128)(2,1)}, bf16[128,1024]{1,0:T(8,128)(2,1)}...) custom-call(bf16[128,4096]{1,0:T(8,128)(2,1)} %bitcast.17, ...), custom_call_target="tpu_custom_call" | custom-call | flops 2147483648 | bytes 16777216 | tf_op jit(solution)/shard_map/forward/pallas_call | solution.py:178
  9.7 1.5 %collective-permute-done.got_ref = bf16[128,1024]{1,0:T(8,128)(2,1)S(1)} collective-permute-done((bf16[128,1024]{1,0:T(8,128)(2,1)S(1)}, bf16[128,1024]{1,0:T(8,128)(2,1)S(1)}, u32[]{:S(2)}, u32[]{:S(2)}) %collective-permute-start) | collective-permute-done | bytes 262176 | tf_op jit(solution)/shard_map/ppermute | solution.py:600
  11.3 1.2 pack.1
  12.4 8.4 %all-to-all-start = ((bf16[16,16,1024]{2,1,0:T(8,128)(2,1)}), bf16[16,16,1024]{2,1,0:T(8,128)(2,1)S(1)}, u32[]{:S(2)}, u32[]{:S(2)}) async-start(bf16[16,16,1024]{2,1,0:T(8,128)(2,1)} %bitcast.3), calls=%async_computation | async-start | bytes 1048576 | tf_op jit(solution)/shard_map/all_to_all | solution.py:604
  20.8 1.9 %collective-permute-start.1 = (bf16[128,1024]{1,0:T(8,128)(2,1)}, bf16[128,1024]{1,0:T(8,128)(2,1)S(1)}, u32[]{:S(2)}, u32[]{:S(2)}) collective-permute-start(bf16[128,1024]{1,0:T(8,128)(2,1)} %get-tuple-element.39), channel_id=1, source_target_pairs={{0,4},{4,8},{8,12},{12,0},{1,5},{5,9},{9,13},{13,1},{2,6},{6,10},{... | collective-permute-start | bytes 786440 | tf_op jit(solution)/shard_map/ppermute | solution.py:448
  22.8 1.4 %collective-permute-start.2 = (bf16[128,1024]{1,0:T(8,128)(2,1)}, bf16[128,1024]{1,0:T(8,128)(2,1)S(1)}, u32[]{:S(2)}, u32[]{:S(2)}) collective-permute-start(bf16[128,1024]{1,0:T(8,128)(2,1)} %get-tuple-element.40), channel_id=1, source_target_pairs={{0,12},{4,0},{8,4},{12,8},{1,13},{5,1},{9,5},{13,9},{2,14},{6,2},{... | collective-permute-start | bytes 786440 | tf_op jit(solution)/shard_map/ppermute | solution.py:448
  24.1 1.9 %collective-permute-start.3 = (bf16[128,1024]{1,0:T(8,128)(2,1)}, bf16[128,1024]{1,0:T(8,128)(2,1)S(1)}, u32[]{:S(2)}, u32[]{:S(2)}) collective-permute-start(bf16[128,1024]{1,0:T(8,128)(2,1)} %get-tuple-element.41), channel_id=1, source_target_pairs={{0,16},{16,32},{32,48},{48,0},{1,17},{17,33},{33,49},{49,1},{2,18}... | collective-permute-start | bytes 786440 | tf_op jit(solution)/shard_map/ppermute | solution.py:448
  26.0 1.4 %collective-permute-start.4 = (bf16[128,1024]{1,0:T(8,128)(2,1)}, bf16[128,1024]{1,0:T(8,128)(2,1)S(1)}, u32[]{:S(2)}, u32[]{:S(2)}) collective-permute-start(bf16[128,1024]{1,0:T(8,128)(2,1)} %get-tuple-element.42), channel_id=1, source_target_pairs={{0,48},{16,0},{32,16},{48,32},{1,49},{17,1},{33,17},{49,33},{2,50}... | collective-permute-start | bytes 786440 | tf_op jit(solution)/shard_map/ppermute | solution.py:448
  27.4 8.7 %collective-permute-done.1.refs_1_ = bf16[128,1024]{1,0:T(8,128)(2,1)S(1)} collective-permute-done((bf16[128,1024]{1,0:T(8,128)(2,1)}, bf16[128,1024]{1,0:T(8,128)(2,1)S(1)}, u32[]{:S(2)}, u32[]{:S(2)}) %collective-permute-start.1) | collective-permute-done | bytes 262176 | tf_op jit(solution)/shard_map/ppermute | solution.py:448
  36.1 0.7 collective-permute-done.3.refs_1_
  36.8 3.0 %attend.1 = (bf16[128,1024]{1,0:T(8,128)(2,1)S(1)}, bf16[256,1024]{1,0:T(8,128)(2,1)}) custom-call(bf16[128,1024]{1,0:T(8,128)(2,1)S(1)} %get-tuple-element.37.keep_ref, bf16[128,1024]{1,0:T(8,128)(2,1)S(1)} %collective-permute-done.got_ref, bf16[256,1024]{1,0:T(8,128)(2,1)S(1)} %bitcast.12, s32[16,16]{1,0:T(8,128)S(1)} %copy-done.1, ...), custom_call_target="tpu_custom_call" | custom-call | flops 805306368 | bytes 2097152 | tf_op jit(solution)/shard_map/attend/pallas_call | solution.py:277
  39.8 4.6 %all-to-all-start.1 = ((bf16[16,16,1024]{2,1,0:T(8,128)(2,1)}), bf16[16,16,1024]{2,1,0:T(8,128)(2,1)S(1)}, u32[]{:S(2)}, u32[]{:S(2)}) async-start(bf16[16,16,1024]{2,1,0:T(8,128)(2,1)} %bitcast.5), calls=%async_computation.1 | async-start | bytes 1048576 | tf_op jit(solution)/shard_map/all_to_all | solution.py:610
  44.4 3.4 %collective-permute-start.6 = (bf16[128,1024]{1,0:T(8,128)(2,1)}, bf16[128,1024]{1,0:T(8,128)(2,1)S(1)}, u32[]{:S(2)}, u32[]{:S(2)}) collective-permute-start(bf16[128,1024]{1,0:T(8,128)(2,1)} %get-tuple-element.52), channel_id=1, source_target_pairs={{0,32},{16,48},{32,0},{48,16},{1,33},{17,49},{33,1},{49,17},{2,34}... | collective-permute-start | bytes 786440 | tf_op jit(solution)/shard_map/ppermute | solution.py:448
  47.8 3.0 %collective-permute-start.5 = (bf16[128,1024]{1,0:T(8,128)(2,1)}, bf16[128,1024]{1,0:T(8,128)(2,1)S(1)}, u32[]{:S(2)}, u32[]{:S(2)}) collective-permute-start(bf16[128,1024]{1,0:T(8,128)(2,1)} %get-tuple-element.48), channel_id=1, source_target_pairs={{0,8},{4,12},{8,0},{12,4},{1,9},{5,13},{9,1},{13,5},{2,10},{6,14},... | collective-permute-start | bytes 786440 | tf_op jit(solution)/shard_map/ppermute | solution.py:448
  50.8 8.6 %collective-permute-done.6.refs_3_ = bf16[128,1024]{1,0:T(8,128)(2,1)S(1)} collective-permute-done((bf16[128,1024]{1,0:T(8,128)(2,1)}, bf16[128,1024]{1,0:T(8,128)(2,1)S(1)}, u32[]{:S(2)}, u32[]{:S(2)}) %collective-permute-start.6) | collective-permute-done | bytes 262176 | tf_op jit(solution)/shard_map/ppermute | solution.py:448
  59.4 0.7 copy-done.9
  60.1 2.3 %turn.3.left_hbm = bf16[4,256,512]{2,1,0:T(8,128)(2,1)} custom-call(bf16[128,1024]{1,0:T(8,128)(2,1)} %get-tuple-element.49.refs_0_, bf16[128,1024]{1,0:T(8,128)(2,1)} %copy-done.6, bf16[128,1024]{1,0:T(8,128)(2,1)} %copy-done.7, bf16[128,1024]{1,0:T(8,128)(2,1)} %copy-done.9), custom_call_target="tpu_custom_call" | custom-call | bytes 2097152 | tf_op jit(solution)/shard_map/turn/pallas_call | solution.py:487
  62.5 0.7 copy-done.8
  63.1 2.3 %turn.2.left_hbm = bf16[4,256,512]{2,1,0:T(8,128)(2,1)} custom-call(bf16[128,1024]{1,0:T(8,128)(2,1)} %get-tuple-element.45.refs_0_, bf16[128,1024]{1,0:T(8,128)(2,1)} %copy-done.4, bf16[128,1024]{1,0:T(8,128)(2,1)} %copy-done.5, bf16[128,1024]{1,0:T(8,128)(2,1)} %copy-done.8), custom_call_target="tpu_custom_call" | custom-call | bytes 2097152 | tf_op jit(solution)/shard_map/turn/pallas_call | solution.py:487
  66.0 1.5 %collective-permute-done.7.got_ref = bf16[128,1024]{1,0:T(8,128)(2,1)S(1)} collective-permute-done((bf16[128,1024]{1,0:T(8,128)(2,1)S(1)}, bf16[128,1024]{1,0:T(8,128)(2,1)S(1)}, u32[]{:S(2)}, u32[]{:S(2)}) %collective-permute-start.7) | collective-permute-done | bytes 262176 | tf_op jit(solution)/shard_map/ppermute | solution.py:614
  67.6 1.1 collective-permute-start.18
  68.7 2.2 %collective-permute-start.19 = (bf16[128,1024]{1,0:T(8,128)(2,1)S(1)}, bf16[128,1024]{1,0:T(8,128)(2,1)S(1)}, u32[]{:S(2)}, u32[]{:S(2)}) collective-permute-start(bf16[128,1024]{1,0:T(8,128)(2,1)S(1)} %get-tuple-element.58.second_ref.own_ref), channel_id=1, source_target_pairs={{0,48},{16,0},{32,16},{48,32},{1,49},{17,1},{33,17},{49,33},{2,50}... | collective-permute-start | bytes 786440 | tf_op jit(solution)/shard_map/ppermute | solution.py:448
  71.0 9.5 %dnorm.1 = bf16[128,4096]{1,0:T(8,128)(2,1)} custom-call(bf16[128,1024]{1,0:T(8,128)(2,1)S(1)} %get-tuple-element.57.first_ref.own_ref, bf16[128,1024]{1,0:T(8,128)(2,1)S(1)} %get-tuple-element.58.second_ref.own_ref, bf16[4096,1024]{1,0:T(8,128)(2,1)} %bitcast.14, bf16[4096,1024]{1,0:T(8,128)(2,1)} %bitcast.16), custom_call_target="tpu_custom_call" | custom-call | flops 2147483648 | bytes 16777216 | tf_op jit(solution)/shard_map/dnorm/pallas_call | solution.py:384
  80.5 4.5 %all-to-all-start.2 = ((bf16[4,32,4096]{2,1,0:T(8,128)(2,1)}), bf16[4,32,4096]{2,1,0:T(8,128)(2,1)S(1)}, u32[]{:S(2)}, u32[]{:S(2)}) async-start(bf16[4,32,4096]{2,1,0:T(8,128)(2,1)} %bitcast.7), calls=%async_computation.2 | async-start | bytes 2097152 | tf_op jit(solution)/shard_map/all_to_all | solution.py:619
  85.0 1.4 %collective-permute-start.11 = (bf16[128,1024]{1,0:T(8,128)(2,1)S(1)}, bf16[128,1024]{1,0:T(8,128)(2,1)S(1)}, u32[]{:S(2)}, u32[]{:S(2)}) collective-permute-start(bf16[128,1024]{1,0:T(8,128)(2,1)S(1)} %get-tuple-element.57.first_ref.own_ref), channel_id=1, source_target_pairs={{0,4},{4,8},{8,12},{12,0},{1,5},{5,9},{9,13},{13,1},{2,6},{6,10},{... | collective-permute-start | bytes 786440 | tf_op jit(solution)/shard_map/ppermute | solution.py:448
  86.4 1.8 %collective-permute-start.12 = (bf16[128,1024]{1,0:T(8,128)(2,1)S(1)}, bf16[128,1024]{1,0:T(8,128)(2,1)S(1)}, u32[]{:S(2)}, u32[]{:S(2)}) collective-permute-start(bf16[128,1024]{1,0:T(8,128)(2,1)S(1)} %get-tuple-element.57.first_ref.own_ref), channel_id=1, source_target_pairs={{0,12},{4,0},{8,4},{12,8},{1,13},{5,1},{9,5},{13,9},{2,14},{6,2},{... | collective-permute-start | bytes 786440 | tf_op jit(solution)/shard_map/ppermute | solution.py:448
  88.2 1.7 %collective-permute-start.13 = (bf16[128,1024]{1,0:T(8,128)(2,1)S(1)}, bf16[128,1024]{1,0:T(8,128)(2,1)S(1)}, u32[]{:S(2)}, u32[]{:S(2)}) collective-permute-start(bf16[128,1024]{1,0:T(8,128)(2,1)S(1)} %get-tuple-element.57.first_ref.own_ref), channel_id=1, source_target_pairs={{0,8},{4,12},{8,0},{12,4},{1,9},{5,13},{9,1},{13,5},{2,10},{6,14},... | collective-permute-start | bytes 786440 | tf_op jit(solution)/shard_map/ppermute | solution.py:448
  89.9 1.4 %far.3 = (bf16[128,1024]{1,0:T(8,128)(2,1)S(1)}, bf16[128,1024]{1,0:T(8,128)(2,1)S(1)}, bf16[512,1024]{1,0:T(8,128)(2,1)S(1)}) custom-call(bf16[4,256,512]{2,1,0:T(8,128)(2,1)} %turn.3.left_hbm, bf16[128,1024]{1,0:T(8,128)(2,1)S(1)} %get-tuple-element.58.second_ref.own_ref, bf16[128,1024]{1,0:T(8,128)(2,1)S(1)} %collective-permute-done.18.near_ref, ...), custom_call_target="tpu_custom_call" | custom-call | flops 268435456 | bytes 4194304 | tf_op jit(solution)/shard_map/far/pallas_call | solution.py:518
  91.3 0.6 collective-permute-start.21
  91.9 2.7 %collective-permute-start.22 = (bf16[128,1024]{1,0:T(8,128)(2,1)S(1)}, bf16[128,1024]{1,0:T(8,128)(2,1)S(1)}, u32[]{:S(2)}, u32[]{:S(2)}) collective-permute-start(bf16[128,1024]{1,0:T(8,128)(2,1)S(1)} %get-tuple-element.68), channel_id=1, source_target_pairs={{0,12},{4,0},{8,4},{12,8},{1,13},{5,1},{9,5},{13,9},{2,14},{6,2},{... | collective-permute-start | bytes 786440 | tf_op jit(solution)/shard_map/ppermute | solution.py:448
  94.6 4.1 %collective-permute-done.11.near_ref = bf16[128,1024]{1,0:T(8,128)(2,1)S(1)} collective-permute-done((bf16[128,1024]{1,0:T(8,128)(2,1)S(1)}, bf16[128,1024]{1,0:T(8,128)(2,1)S(1)}, u32[]{:S(2)}, u32[]{:S(2)}) %collective-permute-start.11) | collective-permute-done | bytes 262176 | tf_op jit(solution)/shard_map/ppermute | solution.py:448
  98.7 2.2 %collective-permute-done.13.far_ref = bf16[128,1024]{1,0:T(8,128)(2,1)S(1)} collective-permute-done((bf16[128,1024]{1,0:T(8,128)(2,1)S(1)}, bf16[128,1024]{1,0:T(8,128)(2,1)S(1)}, u32[]{:S(2)}, u32[]{:S(2)}) %collective-permute-start.13) | collective-permute-done | bytes 262176 | tf_op jit(solution)/shard_map/ppermute | solution.py:448
  100.9 1.4 %far.2 = (bf16[128,1024]{1,0:T(8,128)(2,1)S(1)}, bf16[128,1024]{1,0:T(8,128)(2,1)S(1)}, bf16[512,1024]{1,0:T(8,128)(2,1)S(1)}) custom-call(bf16[4,256,512]{2,1,0:T(8,128)(2,1)} %turn.2.left_hbm, bf16[128,1024]{1,0:T(8,128)(2,1)S(1)} %get-tuple-element.57.first_ref.own_ref, bf16[128,1024]{1,0:T(8,128)(2,1)S(1)} %collective-permute-done.11.near_ref, ...), custom_call_target="tpu_custom_call" | custom-call | flops 268435456 | bytes 4194304 | tf_op jit(solution)/shard_map/far/pallas_call | solution.py:518
  102.3 0.9 collective-permute-start.14
  103.3 2.4 %collective-permute-start.15 = (bf16[128,1024]{1,0:T(8,128)(2,1)S(1)}, bf16[128,1024]{1,0:T(8,128)(2,1)S(1)}, u32[]{:S(2)}, u32[]{:S(2)}) collective-permute-start(bf16[128,1024]{1,0:T(8,128)(2,1)S(1)} %get-tuple-element.62), channel_id=1, source_target_pairs={{0,48},{16,0},{32,16},{48,32},{1,49},{17,1},{33,17},{49,33},{2,50}... | collective-permute-start | bytes 786440 | tf_op jit(solution)/shard_map/ppermute | solution.py:448
  105.7 2.6 %side.3 = (bf16[256,1024]{1,0:T(8,128)(2,1)}, bf16[256,1024]{1,0:T(8,128)(2,1)}) custom-call(bf16[4,256,512]{2,1,0:T(8,128)(2,1)} %turn.3.left_hbm, bf16[512,1024]{1,0:T(8,128)(2,1)S(1)} %get-tuple-element.66.rows_ref, bf16[128,1024]{1,0:T(8,128)(2,1)S(1)} %collective-permute-done.21.from_left_ref, bf16[128,1024]{1,0:T(8,128)(2,1)S(1)} %collective-permute-done.22.from_right_ref), custom_call_target="tpu_custom_call" | custom-call | flops 536870912 | bytes 2097152 | tf_op jit(solution)/shard_map/side/pallas_call | solution.py:552
  108.3 1.2 collective-permute-start.23
  109.5 2.1 %collective-permute-start.24 = (bf16[256,1024]{1,0:T(8,128)(2,1)}, bf16[256,1024]{1,0:T(8,128)(2,1)}, u32[]{:S(2)}, u32[]{:S(2)}) collective-permute-start(bf16[256,1024]{1,0:T(8,128)(2,1)} %get-tuple-element.70), channel_id=1, source_target_pairs={{0,12},{4,0},{8,4},{12,8},{1,13},{5,1},{9,5},{13,9},{2,14},{6,2},{... | collective-permute-start | bytes 1572872 | tf_op jit(solution)/shard_map/ppermute | solution.py:448
  111.6 2.7 %side.2 = (bf16[256,1024]{1,0:T(8,128)(2,1)}, bf16[256,1024]{1,0:T(8,128)(2,1)}) custom-call(bf16[4,256,512]{2,1,0:T(8,128)(2,1)} %turn.2.left_hbm, bf16[512,1024]{1,0:T(8,128)(2,1)S(1)} %get-tuple-element.60.rows_ref, bf16[128,1024]{1,0:T(8,128)(2,1)S(1)} %collective-permute-done.14.from_left_ref, bf16[128,1024]{1,0:T(8,128)(2,1)S(1)} %collective-permute-done.15.from_right_ref), custom_call_target="tpu_custom_call" | custom-call | flops 536870912 | bytes 2097152 | tf_op jit(solution)/shard_map/side/pallas_call | solution.py:552
  114.3 0.4 collective-permute-start.16
  114.7 2.9 %collective-permute-start.17 = (bf16[256,1024]{1,0:T(8,128)(2,1)}, bf16[256,1024]{1,0:T(8,128)(2,1)}, u32[]{:S(2)}, u32[]{:S(2)}) collective-permute-start(bf16[256,1024]{1,0:T(8,128)(2,1)} %get-tuple-element.64), channel_id=1, source_target_pairs={{0,48},{16,0},{32,16},{48,32},{1,49},{17,1},{33,17},{49,33},{2,50}... | collective-permute-start | bytes 1572872 | tf_op jit(solution)/shard_map/ppermute | solution.py:448
  117.6 1.2 rms_back.1.own_ref
  118.8 1.8 %collective-permute-start.8 = (bf16[32,4096]{1,0:T(8,128)(2,1)S(1)}, bf16[32,4096]{1,0:T(8,128)(2,1)S(1)}, u32[]{:S(2)}, u32[]{:S(2)}) collective-permute-start(bf16[32,4096]{1,0:T(8,128)(2,1)S(1)} %rms_back.1.own_ref), channel_id=1, source_target_pairs={{0,1},{1,2},{2,3},{3,0},{4,5},{5,6},{6,7},{7,4},{8,9},{9,10},{10,1... | collective-permute-start | bytes 786440 | tf_op jit(solution)/shard_map/ppermute | solution.py:448
  120.6 1.6 %collective-permute-start.9 = (bf16[32,4096]{1,0:T(8,128)(2,1)S(1)}, bf16[32,4096]{1,0:T(8,128)(2,1)S(1)}, u32[]{:S(2)}, u32[]{:S(2)}) collective-permute-start(bf16[32,4096]{1,0:T(8,128)(2,1)S(1)} %rms_back.1.own_ref), channel_id=1, source_target_pairs={{0,3},{1,0},{2,1},{3,2},{4,7},{5,4},{6,5},{7,6},{8,11},{9,8},{10,9... | collective-permute-start | bytes 786440 | tf_op jit(solution)/shard_map/ppermute | solution.py:448
  122.3 6.5 %collective-permute-done.8.left_ref = bf16[32,4096]{1,0:T(8,128)(2,1)S(1)} collective-permute-done((bf16[32,4096]{1,0:T(8,128)(2,1)S(1)}, bf16[32,4096]{1,0:T(8,128)(2,1)S(1)}, u32[]{:S(2)}, u32[]{:S(2)}) %collective-permute-start.8) | collective-permute-done | bytes 262176 | tf_op jit(solution)/shard_map/ppermute | solution.py:448
  128.9 3.6 %own.3 = f32[256,1024]{1,0:T(8,128)} custom-call(bf16[4,256,512]{2,1,0:T(8,128)(2,1)} %turn.3.left_hbm, bf16[512,1024]{1,0:T(8,128)(2,1)S(1)} %get-tuple-element.66.rows_ref, bf16[256,1024]{1,0:T(8,128)(2,1)} %collective-permute-done.23.a_ref, bf16[256,1024]{1,0:T(8,128)(2,1)} %collective-permute-done.24.b_ref), custom_call_target="tpu_custom_call" | custom-call | flops 268435456 | bytes 4194304 | tf_op jit(solution)/shard_map/own/pallas_call | solution.py:575
  132.5 3.6 %own.2 = f32[256,1024]{1,0:T(8,128)} custom-call(bf16[4,256,512]{2,1,0:T(8,128)(2,1)} %turn.2.left_hbm, bf16[512,1024]{1,0:T(8,128)(2,1)S(1)} %get-tuple-element.60.rows_ref, bf16[256,1024]{1,0:T(8,128)(2,1)} %collective-permute-done.16.a_ref, bf16[256,1024]{1,0:T(8,128)(2,1)} %collective-permute-done.17.b_ref), custom_call_target="tpu_custom_call" | custom-call | flops 268435456 | bytes 4194304 | tf_op jit(solution)/shard_map/own/pallas_call | solution.py:575
  136.4 1.0 place.1
  (44 shorter events, 1.2 us)
Async XLA Ops:
  0.6 10.6 %copy-start.1 = (s32[16,16]{1,0:T(8,128)S(1)}, s32[16,16]{1,0:T(8,128)}, u32[]{:S(2)}) copy-start(s32[16,16]{1,0:T(8,128)} %src_ref.5) | copy-start | bytes 3076
  0.6 10.6 %copy-start.2 = (s32[16,16]{1,0:T(8,128)S(1)}, s32[16,16]{1,0:T(8,128)}, u32[]{:S(2)}) copy-start(s32[16,16]{1,0:T(8,128)} %dest_ref.5) | copy-start | bytes 3076
  0.7 36.2 %copy-start.3 = (s32[16,16]{1,0:T(8,128)S(1)}, s32[16,16]{1,0:T(8,128)}, u32[]{:S(2)}) copy-start(s32[16,16]{1,0:T(8,128)} %tgt_ref.1) | copy-start | bytes 3076
  9.6 1.6 %collective-permute-start = (bf16[128,1024]{1,0:T(8,128)(2,1)S(1)}, bf16[128,1024]{1,0:T(8,128)(2,1)S(1)}, u32[]{:S(2)}, u32[]{:S(2)}) collective-permute-start(bf16[128,1024]{1,0:T(8,128)(2,1)S(1)} %get-tuple-element.38), channel_id=1, source_target_pairs={{0,64},{64,0},{1,65},{65,1},{2,66},{66,2},{3,67},{67,3},{4,68},{68... | collective-permute-start | bytes 786440 | tf_op jit(solution)/shard_map/ppermute | solution.py:600
  12.4 24.4 %all-to-all-start = ((bf16[16,16,1024]{2,1,0:T(8,128)(2,1)}), bf16[16,16,1024]{2,1,0:T(8,128)(2,1)S(1)}, u32[]{:S(2)}, u32[]{:S(2)}) async-start(bf16[16,16,1024]{2,1,0:T(8,128)(2,1)} %bitcast.3), calls=%async_computation | async-start | bytes 1048576 | tf_op jit(solution)/shard_map/all_to_all | solution.py:604
  20.8 15.2 %collective-permute-start.1 = (bf16[128,1024]{1,0:T(8,128)(2,1)}, bf16[128,1024]{1,0:T(8,128)(2,1)S(1)}, u32[]{:S(2)}, u32[]{:S(2)}) collective-permute-start(bf16[128,1024]{1,0:T(8,128)(2,1)} %get-tuple-element.39), channel_id=1, source_target_pairs={{0,4},{4,8},{8,12},{12,0},{1,5},{5,9},{9,13},{13,1},{2,6},{6,10},{... | collective-permute-start | bytes 786440 | tf_op jit(solution)/shard_map/ppermute | solution.py:448
  22.8 13.3 %collective-permute-start.2 = (bf16[128,1024]{1,0:T(8,128)(2,1)}, bf16[128,1024]{1,0:T(8,128)(2,1)S(1)}, u32[]{:S(2)}, u32[]{:S(2)}) collective-permute-start(bf16[128,1024]{1,0:T(8,128)(2,1)} %get-tuple-element.40), channel_id=1, source_target_pairs={{0,12},{4,0},{8,4},{12,8},{1,13},{5,1},{9,5},{13,9},{2,14},{6,2},{... | collective-permute-start | bytes 786440 | tf_op jit(solution)/shard_map/ppermute | solution.py:448
  24.1 12.7 %collective-permute-start.3 = (bf16[128,1024]{1,0:T(8,128)(2,1)}, bf16[128,1024]{1,0:T(8,128)(2,1)S(1)}, u32[]{:S(2)}, u32[]{:S(2)}) collective-permute-start(bf16[128,1024]{1,0:T(8,128)(2,1)} %get-tuple-element.41), channel_id=1, source_target_pairs={{0,16},{16,32},{32,48},{48,0},{1,17},{17,33},{33,49},{49,1},{2,18}... | collective-permute-start | bytes 786440 | tf_op jit(solution)/shard_map/ppermute | solution.py:448
  26.0 10.8 %collective-permute-start.4 = (bf16[128,1024]{1,0:T(8,128)(2,1)}, bf16[128,1024]{1,0:T(8,128)(2,1)S(1)}, u32[]{:S(2)}, u32[]{:S(2)}) collective-permute-start(bf16[128,1024]{1,0:T(8,128)(2,1)} %get-tuple-element.42), channel_id=1, source_target_pairs={{0,48},{16,0},{32,16},{48,32},{1,49},{17,1},{33,17},{49,33},{2,50}... | collective-permute-start | bytes 786440 | tf_op jit(solution)/shard_map/ppermute | solution.py:448
  36.1 26.4 %copy-start.4 = (bf16[128,1024]{1,0:T(8,128)(2,1)}, bf16[128,1024]{1,0:T(8,128)(2,1)S(1)}, u32[]{:S(2)}) copy-start(bf16[128,1024]{1,0:T(8,128)(2,1)S(1)} %collective-permute-done.1.refs_1_) | copy-start | bytes 786436
  36.1 26.4 %copy-start.5 = (bf16[128,1024]{1,0:T(8,128)(2,1)}, bf16[128,1024]{1,0:T(8,128)(2,1)S(1)}, u32[]{:S(2)}) copy-start(bf16[128,1024]{1,0:T(8,128)(2,1)S(1)} %collective-permute-done.2.refs_2_) | copy-start | bytes 786436
  36.8 22.6 %copy-start.6 = (bf16[128,1024]{1,0:T(8,128)(2,1)}, bf16[128,1024]{1,0:T(8,128)(2,1)S(1)}, u32[]{:S(2)}) copy-start(bf16[128,1024]{1,0:T(8,128)(2,1)S(1)} %collective-permute-done.3.refs_1_) | copy-start | bytes 786436
  36.8 22.6 %copy-start.7 = (bf16[128,1024]{1,0:T(8,128)(2,1)}, bf16[128,1024]{1,0:T(8,128)(2,1)S(1)}, u32[]{:S(2)}) copy-start(bf16[128,1024]{1,0:T(8,128)(2,1)S(1)} %collective-permute-done.4.refs_2_) | copy-start | bytes 786436
  39.8 25.7 %all-to-all-start.1 = ((bf16[16,16,1024]{2,1,0:T(8,128)(2,1)}), bf16[16,16,1024]{2,1,0:T(8,128)(2,1)S(1)}, u32[]{:S(2)}, u32[]{:S(2)}) async-start(bf16[16,16,1024]{2,1,0:T(8,128)(2,1)} %bitcast.5), calls=%async_computation.1 | async-start | bytes 1048576 | tf_op jit(solution)/shard_map/all_to_all | solution.py:610
  44.4 15.0 %collective-permute-start.6 = (bf16[128,1024]{1,0:T(8,128)(2,1)}, bf16[128,1024]{1,0:T(8,128)(2,1)S(1)}, u32[]{:S(2)}, u32[]{:S(2)}) collective-permute-start(bf16[128,1024]{1,0:T(8,128)(2,1)} %get-tuple-element.52), channel_id=1, source_target_pairs={{0,32},{16,48},{32,0},{48,16},{1,33},{17,49},{33,1},{49,17},{2,34}... | collective-permute-start | bytes 786440 | tf_op jit(solution)/shard_map/ppermute | solution.py:448
  47.8 14.6 %collective-permute-start.5 = (bf16[128,1024]{1,0:T(8,128)(2,1)}, bf16[128,1024]{1,0:T(8,128)(2,1)S(1)}, u32[]{:S(2)}, u32[]{:S(2)}) collective-permute-start(bf16[128,1024]{1,0:T(8,128)(2,1)} %get-tuple-element.48), channel_id=1, source_target_pairs={{0,8},{4,12},{8,0},{12,4},{1,9},{5,13},{9,1},{13,5},{2,10},{6,14},... | collective-permute-start | bytes 786440 | tf_op jit(solution)/shard_map/ppermute | solution.py:448
  59.4 0.7 copy-start.9
  62.4 0.7 copy-start.8
  65.9 1.6 %collective-permute-start.7 = (bf16[128,1024]{1,0:T(8,128)(2,1)S(1)}, bf16[128,1024]{1,0:T(8,128)(2,1)S(1)}, u32[]{:S(2)}, u32[]{:S(2)}) collective-permute-start(bf16[128,1024]{1,0:T(8,128)(2,1)S(1)} %get-tuple-element.56), channel_id=1, source_target_pairs={{0,64},{64,0},{1,65},{65,1},{2,66},{66,2},{3,67},{67,3},{4,68},{68... | collective-permute-start | bytes 786440 | tf_op jit(solution)/shard_map/ppermute | solution.py:614
  67.6 20.6 %collective-permute-start.18 = (bf16[128,1024]{1,0:T(8,128)(2,1)S(1)}, bf16[128,1024]{1,0:T(8,128)(2,1)S(1)}, u32[]{:S(2)}, u32[]{:S(2)}) collective-permute-start(bf16[128,1024]{1,0:T(8,128)(2,1)S(1)} %get-tuple-element.58.second_ref.own_ref), channel_id=1, source_target_pairs={{0,16},{16,32},{32,48},{48,0},{1,17},{17,33},{33,49},{49,1},{2,18}... | collective-permute-start | bytes 786440 | tf_op jit(solution)/shard_map/ppermute | solution.py:448
  68.7 21.2 %collective-permute-start.19 = (bf16[128,1024]{1,0:T(8,128)(2,1)S(1)}, bf16[128,1024]{1,0:T(8,128)(2,1)S(1)}, u32[]{:S(2)}, u32[]{:S(2)}) collective-permute-start(bf16[128,1024]{1,0:T(8,128)(2,1)S(1)} %get-tuple-element.58.second_ref.own_ref), channel_id=1, source_target_pairs={{0,48},{16,0},{32,16},{48,32},{1,49},{17,1},{33,17},{49,33},{2,50}... | collective-permute-start | bytes 786440 | tf_op jit(solution)/shard_map/ppermute | solution.py:448
  70.9 19.0 %collective-permute-start.20 = (bf16[128,1024]{1,0:T(8,128)(2,1)S(1)}, bf16[128,1024]{1,0:T(8,128)(2,1)S(1)}, u32[]{:S(2)}, u32[]{:S(2)}) collective-permute-start(bf16[128,1024]{1,0:T(8,128)(2,1)S(1)} %get-tuple-element.58.second_ref.own_ref), channel_id=1, source_target_pairs={{0,32},{16,48},{32,0},{48,16},{1,33},{17,49},{33,1},{49,17},{2,34}... | collective-permute-start | bytes 786440 | tf_op jit(solution)/shard_map/ppermute | solution.py:448
  80.5 37.1 %copy-start = (f32[1,4096]{1,0:T(1,128)S(1)}, f32[1,4096]{1,0:T(1,128)}, u32[]{:S(2)}) copy-start(f32[1,4096]{1,0:T(1,128)} %gain_ref.1) | copy-start | bytes 49156
  80.5 37.1 %all-to-all-start.2 = ((bf16[4,32,4096]{2,1,0:T(8,128)(2,1)}), bf16[4,32,4096]{2,1,0:T(8,128)(2,1)S(1)}, u32[]{:S(2)}, u32[]{:S(2)}) async-start(bf16[4,32,4096]{2,1,0:T(8,128)(2,1)} %bitcast.7), calls=%async_computation.2 | async-start | bytes 2097152 | tf_op jit(solution)/shard_map/all_to_all | solution.py:619
  85.0 13.8 %collective-permute-start.11 = (bf16[128,1024]{1,0:T(8,128)(2,1)S(1)}, bf16[128,1024]{1,0:T(8,128)(2,1)S(1)}, u32[]{:S(2)}, u32[]{:S(2)}) collective-permute-start(bf16[128,1024]{1,0:T(8,128)(2,1)S(1)} %get-tuple-element.57.first_ref.own_ref), channel_id=1, source_target_pairs={{0,4},{4,8},{8,12},{12,0},{1,5},{5,9},{9,13},{13,1},{2,6},{6,10},{... | collective-permute-start | bytes 786440 | tf_op jit(solution)/shard_map/ppermute | solution.py:448
  86.4 12.4 %collective-permute-start.12 = (bf16[128,1024]{1,0:T(8,128)(2,1)S(1)}, bf16[128,1024]{1,0:T(8,128)(2,1)S(1)}, u32[]{:S(2)}, u32[]{:S(2)}) collective-permute-start(bf16[128,1024]{1,0:T(8,128)(2,1)S(1)} %get-tuple-element.57.first_ref.own_ref), channel_id=1, source_target_pairs={{0,12},{4,0},{8,4},{12,8},{1,13},{5,1},{9,5},{13,9},{2,14},{6,2},{... | collective-permute-start | bytes 786440 | tf_op jit(solution)/shard_map/ppermute | solution.py:448
  88.2 12.7 %collective-permute-start.13 = (bf16[128,1024]{1,0:T(8,128)(2,1)S(1)}, bf16[128,1024]{1,0:T(8,128)(2,1)S(1)}, u32[]{:S(2)}, u32[]{:S(2)}) collective-permute-start(bf16[128,1024]{1,0:T(8,128)(2,1)S(1)} %get-tuple-element.57.first_ref.own_ref), channel_id=1, source_target_pairs={{0,8},{4,12},{8,0},{12,4},{1,9},{5,13},{9,1},{13,5},{2,10},{6,14},... | collective-permute-start | bytes 786440 | tf_op jit(solution)/shard_map/ppermute | solution.py:448
  91.3 14.3 %collective-permute-start.21 = (bf16[128,1024]{1,0:T(8,128)(2,1)S(1)}, bf16[128,1024]{1,0:T(8,128)(2,1)S(1)}, u32[]{:S(2)}, u32[]{:S(2)}) collective-permute-start(bf16[128,1024]{1,0:T(8,128)(2,1)S(1)} %get-tuple-element.67), channel_id=1, source_target_pairs={{0,4},{4,8},{8,12},{12,0},{1,5},{5,9},{9,13},{13,1},{2,6},{6,10},{... | collective-permute-start | bytes 786440 | tf_op jit(solution)/shard_map/ppermute | solution.py:448
  91.9 13.7 %collective-permute-start.22 = (bf16[128,1024]{1,0:T(8,128)(2,1)S(1)}, bf16[128,1024]{1,0:T(8,128)(2,1)S(1)}, u32[]{:S(2)}, u32[]{:S(2)}) collective-permute-start(bf16[128,1024]{1,0:T(8,128)(2,1)S(1)} %get-tuple-element.68), channel_id=1, source_target_pairs={{0,12},{4,0},{8,4},{12,8},{1,13},{5,1},{9,5},{13,9},{2,14},{6,2},{... | collective-permute-start | bytes 786440 | tf_op jit(solution)/shard_map/ppermute | solution.py:448
  102.3 9.3 %collective-permute-start.14 = (bf16[128,1024]{1,0:T(8,128)(2,1)S(1)}, bf16[128,1024]{1,0:T(8,128)(2,1)S(1)}, u32[]{:S(2)}, u32[]{:S(2)}) collective-permute-start(bf16[128,1024]{1,0:T(8,128)(2,1)S(1)} %get-tuple-element.61), channel_id=1, source_target_pairs={{0,16},{16,32},{32,48},{48,0},{1,17},{17,33},{33,49},{49,1},{2,18}... | collective-permute-start | bytes 786440 | tf_op jit(solution)/shard_map/ppermute | solution.py:448
  103.3 8.3 %collective-permute-start.15 = (bf16[128,1024]{1,0:T(8,128)(2,1)S(1)}, bf16[128,1024]{1,0:T(8,128)(2,1)S(1)}, u32[]{:S(2)}, u32[]{:S(2)}) collective-permute-start(bf16[128,1024]{1,0:T(8,128)(2,1)S(1)} %get-tuple-element.62), channel_id=1, source_target_pairs={{0,48},{16,0},{32,16},{48,32},{1,49},{17,1},{33,17},{49,33},{2,50}... | collective-permute-start | bytes 786440 | tf_op jit(solution)/shard_map/ppermute | solution.py:448
  108.3 12.3 %collective-permute-start.23 = (bf16[256,1024]{1,0:T(8,128)(2,1)}, bf16[256,1024]{1,0:T(8,128)(2,1)}, u32[]{:S(2)}, u32[]{:S(2)}) collective-permute-start(bf16[256,1024]{1,0:T(8,128)(2,1)} %get-tuple-element.69), channel_id=1, source_target_pairs={{0,4},{4,8},{8,12},{12,0},{1,5},{5,9},{9,13},{13,1},{2,6},{6,10},{... | collective-permute-start | bytes 1572872 | tf_op jit(solution)/shard_map/ppermute | solution.py:448
  109.5 19.4 %collective-permute-start.24 = (bf16[256,1024]{1,0:T(8,128)(2,1)}, bf16[256,1024]{1,0:T(8,128)(2,1)}, u32[]{:S(2)}, u32[]{:S(2)}) collective-permute-start(bf16[256,1024]{1,0:T(8,128)(2,1)} %get-tuple-element.70), channel_id=1, source_target_pairs={{0,12},{4,0},{8,4},{12,8},{1,13},{5,1},{9,5},{13,9},{2,14},{6,2},{... | collective-permute-start | bytes 1572872 | tf_op jit(solution)/shard_map/ppermute | solution.py:448
  114.3 18.2 %collective-permute-start.16 = (bf16[256,1024]{1,0:T(8,128)(2,1)}, bf16[256,1024]{1,0:T(8,128)(2,1)}, u32[]{:S(2)}, u32[]{:S(2)}) collective-permute-start(bf16[256,1024]{1,0:T(8,128)(2,1)} %get-tuple-element.63), channel_id=1, source_target_pairs={{0,16},{16,32},{32,48},{48,0},{1,17},{17,33},{33,49},{49,1},{2,18}... | collective-permute-start | bytes 1572872 | tf_op jit(solution)/shard_map/ppermute | solution.py:448
  114.7 17.8 %collective-permute-start.17 = (bf16[256,1024]{1,0:T(8,128)(2,1)}, bf16[256,1024]{1,0:T(8,128)(2,1)}, u32[]{:S(2)}, u32[]{:S(2)}) collective-permute-start(bf16[256,1024]{1,0:T(8,128)(2,1)} %get-tuple-element.64), channel_id=1, source_target_pairs={{0,48},{16,0},{32,16},{48,32},{1,49},{17,1},{33,17},{49,33},{2,50}... | collective-permute-start | bytes 1572872 | tf_op jit(solution)/shard_map/ppermute | solution.py:448
  118.8 10.0 %collective-permute-start.8 = (bf16[32,4096]{1,0:T(8,128)(2,1)S(1)}, bf16[32,4096]{1,0:T(8,128)(2,1)S(1)}, u32[]{:S(2)}, u32[]{:S(2)}) collective-permute-start(bf16[32,4096]{1,0:T(8,128)(2,1)S(1)} %rms_back.1.own_ref), channel_id=1, source_target_pairs={{0,1},{1,2},{2,3},{3,0},{4,5},{5,6},{6,7},{7,4},{8,9},{9,10},{10,1... | collective-permute-start | bytes 786440 | tf_op jit(solution)/shard_map/ppermute | solution.py:448
  120.6 15.5 %collective-permute-start.9 = (bf16[32,4096]{1,0:T(8,128)(2,1)S(1)}, bf16[32,4096]{1,0:T(8,128)(2,1)S(1)}, u32[]{:S(2)}, u32[]{:S(2)}) collective-permute-start(bf16[32,4096]{1,0:T(8,128)(2,1)S(1)} %rms_back.1.own_ref), channel_id=1, source_target_pairs={{0,3},{1,0},{2,1},{3,2},{4,7},{5,4},{6,5},{7,6},{8,11},{9,8},{10,9... | collective-permute-start | bytes 786440 | tf_op jit(solution)/shard_map/ppermute | solution.py:448
  128.8 7.6 %collective-permute-start.10 = (bf16[32,4096]{1,0:T(8,128)(2,1)S(1)}, bf16[32,4096]{1,0:T(8,128)(2,1)S(1)}, u32[]{:S(2)}, u32[]{:S(2)}) collective-permute-start(bf16[32,4096]{1,0:T(8,128)(2,1)S(1)} %collective-permute-done.8.left_ref), channel_id=1, source_target_pairs={{0,1},{1,2},{2,3},{3,0},{4,5},{5,6},{6,7},{7,4},{8,9},{9,10},{10,1... | collective-permute-start | bytes 786440 | tf_op jit(solution)/shard_map/ppermute | solution.py:448

commit v4 on v3

--- a/solution.py
+++ b/solution.py
@@ -11,10 +11,13 @@
 TOK = 128
 SLOTS = 256
 RING = 4
+QUARTER = TOK // RING
+ORDER = (0, 3, 1, 2)
 EPS = 1e-06
 F32 = jnp.float32
 BF16 = jnp.bfloat16
 VMEM = pl.BlockSpec(memory_space=pltpu.VMEM)
+ANY = pl.BlockSpec(memory_space=pl.ANY)
 HBM = pl.BlockSpec(memory_space=pltpu.HBM)
 
 
@@ -122,6 +125,7 @@
         get_left.wait()
 
     z, x = lax.axis_index("z"), lax.axis_index("x")
+    quarter = pl.ds(pl.multiple_of(lax.axis_index("mp") * QUARTER, QUARTER), QUARTER)
     block = cols // RING
     copies = []
     for k in range(RING):
@@ -132,7 +136,7 @@
             for source, at, out in ((normed_ref, at_x, by_x[k]), (left_ref, at_z, by_z[k])):
                 copies.append(
                     pltpu.make_async_copy(
-                        source.at[:, pl.ds(pl.multiple_of(at, block), block)],
+                        source.at[quarter, pl.ds(pl.multiple_of(at, block), block)],
                         out.at[:, to],
                         out_sem.at[len(copies)],
                     )
@@ -179,7 +183,7 @@
         forward_kernel,
         in_specs=[HBM] * 5,
         out_specs=[VMEM] * 2 + [HBM] * (2 * RING),
-        out_shape=[half] * 2 + [pltpu.HBM((rows, cols), BF16)] * (2 * RING),
+        out_shape=[half] * 2 + [pltpu.HBM((QUARTER, cols), BF16)] * (2 * RING),
         scratch_shapes=[pltpu.VMEM((rows, width), BF16), pltpu.VMEM((1, width), F32)]
         + [pltpu.VMEM((count, step, cols), BF16)] * 2
         + [pltpu.VMEM((rows, width), BF16)] * 2
@@ -424,20 +428,26 @@
     )(in_hbm(x), gain, parts)
 
 
-def place_kernel(own_ref, left_ref, right_ref, far_ref, out_ref):
-    rows = own_ref.shape[0]
-    for k, ref in ((0, own_ref), (3, left_ref), (1, right_ref), (2, far_ref)):
-        at = (lax.axis_index("mp") + k) % RING * rows
-        out_ref[pl.ds(pl.multiple_of(at, rows), rows), :] = ref[...]
+def place_kernel(*refs):
+    pieces, (out_hbm, sems) = refs[:RING], refs[RING:]
+    rows = pieces[0].shape[0]
+    copies = []
+    for i, k in enumerate(ORDER):
+        at = pl.multiple_of((lax.axis_index("mp") + k) % RING * rows, rows)
+        copies.append(pltpu.make_async_copy(pieces[i], out_hbm.at[pl.ds(at, rows), :], sems.at[i]))
+        copies[-1].start()
+    for copy in copies:
+        copy.wait()
 
 
 def place(pieces):
     rows, width = pieces[0].shape
     return pl.pallas_call(
         place_kernel,
-        in_specs=[VMEM] * 4,
-        out_specs=VMEM,
-        out_shape=jax.ShapeDtypeStruct((RING * rows, width), BF16),
+        in_specs=[ANY] * RING,
+        out_specs=HBM,
+        out_shape=pltpu.HBM((RING * rows, width), BF16),
+        scratch_shapes=[pltpu.SemaphoreType.DMA((RING,))],
         compiler_params=params(),
         cost_estimate=cost(0, 4 * RING * rows * width),
         name="place",
@@ -459,136 +469,189 @@
 
 
 def exchanged(slices, axis):
-    return [shift(slices[1], axis, 1), shift(slices[3], axis, 3)], shift(slices[2], axis, 2)
-
-
-def turn_kernel(*refs):
-    pieces, (out_hbm, in_buf, out_buf, in_sem, out_sem) = refs[:RING], refs[RING:]
-    block, rows = out_buf.shape[1], pieces[0].shape[0]
-    loads = [pltpu.make_async_copy(pieces[p], in_buf.at[p], in_sem.at[p]) for p in range(RING)]
-    for load in loads:
-        load.start()
-    for load in loads:
-        load.wait()
-    stores = []
-    for k in range(RING):
-        for p in range(RING):
-            turned_block = in_buf[p, :, k * block : (k + 1) * block].T
-            out_buf[k, :, p * rows : (p + 1) * rows] = turned_block
-        stores.append(pltpu.make_async_copy(out_buf.at[k], out_hbm.at[k], out_sem.at[k]))
-        stores[-1].start()
-    for store in stores:
-        store.wait()
-
-
-def turned(pieces):
-    rows, width = pieces[0].shape
-    shape = (RING, width // RING, RING * rows)
-    return pl.pallas_call(
-        turn_kernel,
-        in_specs=[HBM] * RING,
+    far = shift(slices[2], axis, 2)
+    return [slices[0], shift(slices[1], axis, 1), shift(slices[3], axis, 3), far]
+
+
+def stack_kernel(*refs):
+    pieces, (out_hbm, sems) = refs[:-2], refs[-2:]
+    rows = pieces[0].shape[0]
+    copies = [
+        pltpu.make_async_copy(piece, out_hbm.at[pl.ds(i * rows, rows), :], sems.at[i])
+        for i, piece in enumerate(pieces)
+    ]
+    for copy in copies:
+        copy.start()
+    for copy in copies:
+        copy.wait()
+
+
+def stacked(pieces):
+    rows, cols = pieces[0].shape
+    count = len(pieces)
+    return pl.pallas_call(
+        stack_kernel,
+        in_specs=[ANY] * count,
         out_specs=HBM,
-        out_shape=pltpu.HBM(shape, BF16),
-        scratch_shapes=[pltpu.VMEM((RING, rows, width), BF16), pltpu.VMEM(shape, BF16)]
-        + [pltpu.SemaphoreType.DMA((RING,))] * 2,
-        compiler_params=params(),
-        cost_estimate=cost(0, 4 * RING * rows * width),
-        name="turn",
-    )(*[in_hbm(piece) for piece in pieces])
-
-
-def far_kernel(left_hbm, own_ref, near_ref, next_ref, far_ref, top_ref, low_ref, rows_ref, left, sem):
-    load = pltpu.make_async_copy(left_hbm.at[2], left, sem)
-    load.start()
-    rows = own_ref.shape[0]
-    for p, piece in enumerate((own_ref, near_ref, next_ref, far_ref)):
-        rows_ref[p * rows : (p + 1) * rows, :] = piece[...]
-    load.wait()
-    half = top_ref.shape[0]
-    for i, out in enumerate((top_ref, low_ref)):
-        out[...] = jnp.dot(
-            left[i * half : (i + 1) * half, :], rows_ref[...], preferred_element_type=F32
-        ).astype(BF16)
-
-
-def far_block(left, pieces):
-    rows, cols = pieces[0].shape
-    _, block, depth = left.shape
+        out_shape=pltpu.HBM((count * rows, cols), BF16),
+        scratch_shapes=[pltpu.SemaphoreType.DMA((count,))],
+        compiler_params=params(),
+        cost_estimate=cost(0, 4 * count * rows * cols),
+        name="stack",
+    )(*pieces)
+
+
+def tn(left, right):
+    return lax.dot_general(left, right, (((0,), (0,)), ((), ())), preferred_element_type=F32)
+
+
+def left_loads(lefts, buf, sems, ks):
+    block = buf.shape[-1]
+    mine = lax.axis_index("mp")
+    loads = [[[] for _ in ks] for _ in range(2)]
+    for f in range(2):
+        for i, k in enumerate(ks):
+            for j, (left, distance) in enumerate(zip(lefts, ORDER, strict=True)):
+                at = pl.multiple_of((mine + distance) % RING * QUARTER, QUARTER)
+                loads[f][i].append(
+                    pltpu.make_async_copy(
+                        left.at[f, :, :, pl.ds(k * block, block)],
+                        buf.at[f, i, :, pl.ds(at, QUARTER), :],
+                        sems.at[f, i, j],
+                    )
+                )
+                loads[f][i][-1].start()
+    return loads
+
+
+def left_scratch(block, count):
+    return [
+        pltpu.VMEM((2, count, RING, TOK, block), BF16),
+        pltpu.SemaphoreType.DMA((2, count, RING)),
+    ]
+
+
+def flat(value):
+    return value.reshape(RING * TOK, value.shape[-1])
+
+
+def wait_all(copies):
+    for copy in copies:
+        copy.wait()
+
+
+def far_kernel(*refs):
+    lefts, pieces, outs = refs[:RING], refs[RING : 3 * RING], refs[3 * RING : 3 * RING + 4]
+    rows_refs, (buf, sems, row_sems) = refs[3 * RING + 4 : 3 * RING + 6], refs[3 * RING + 6 :]
+    gets = [
+        pltpu.make_async_copy(
+            piece, rows_refs[i // RING].at[pl.ds(i % RING * TOK, TOK), :], row_sems.at[i]
+        )
+        for i, piece in enumerate(pieces)
+    ]
+    for get in gets:
+        get.start()
+    loads = left_loads(lefts, buf, sems, (2,))
+    half = outs[0].shape[0]
+    for f in range(2):
+        wait_all(gets[f * RING : (f + 1) * RING])
+        wait_all(loads[f][0])
+        block = tn(flat(buf[f, 0]), rows_refs[f][...]).astype(BF16)
+        outs[2 * f][...] = block[:half]
+        outs[2 * f + 1][...] = block[half:]
+
+
+def far_blocks(lefts, pieces_a, pieces_b):
+    rows, cols = pieces_a[0].shape
+    block = lefts[0].shape[-1] // RING
     half = jax.ShapeDtypeStruct((block // 2, cols), BF16)
+    tall = jax.ShapeDtypeStruct((RING * rows, cols), BF16)
     return pl.pallas_call(
         far_kernel,
-        in_specs=[HBM] + [VMEM] * RING,
-        out_specs=[VMEM] * 3,
-        out_shape=[half, half, jax.ShapeDtypeStruct((RING * rows, cols), BF16)],
-        scratch_shapes=[pltpu.VMEM((block, depth), BF16), pltpu.SemaphoreType.DMA],
-        compiler_params=params(),
-        cost_estimate=cost(2 * RING * rows * block * cols, 8 * RING * rows * cols),
+        in_specs=[HBM] * (3 * RING),
+        out_specs=[VMEM] * 6,
+        out_shape=[half] * 4 + [tall] * 2,
+        scratch_shapes=left_scratch(block, 1) + [pltpu.SemaphoreType.DMA((2 * RING,))],
+        compiler_params=params(),
+        cost_estimate=cost(4 * RING * rows * block * cols, 16 * RING * rows * cols),
         name="far",
-    )(in_hbm(left), *pieces)
-
-
-def side_kernel(left_hbm, rows_ref, from_left_ref, from_right_ref, right_out, left_out, left, sems):
-    loads = [pltpu.make_async_copy(left_hbm.at[k], left.at[i], sems.at[i]) for i, k in enumerate((1, 3))]
-    for load in loads:
-        load.start()
-    half = from_left_ref.shape[0]
-
-    def product(i):
-        loads[i].wait()
-        return jnp.dot(left[i], rows_ref[...], preferred_element_type=F32)
-
-    block = product(0)
-    right_out[:half, :] = (block[:half] + from_left_ref[...].astype(F32)).astype(BF16)
-    right_out[half:, :] = block[half:].astype(BF16)
-    block = product(1)
-    left_out[:half, :] = block[:half].astype(BF16)
-    left_out[half:, :] = (block[half:] + from_right_ref[...].astype(F32)).astype(BF16)
-
-
-def side_blocks(left, rows, from_left, from_right):
-    _, block, depth = left.shape
-    cols = rows.shape[1]
+    )(*[in_hbm(value) for value in (*lefts, *pieces_a, *pieces_b)])
+
+
+def side_kernel(*refs):
+    lefts, rows_refs, near, outs = refs[:RING], refs[RING : RING + 2], refs[RING + 2 : RING + 6], refs[RING + 6 : RING + 10]
+    buf, sems = refs[RING + 10 :]
+    loads = left_loads(lefts, buf, sems, (1, 3))
+    half = near[0].shape[0]
+    for f in range(2):
+        from_left, from_right = near[2 * f : 2 * f + 2]
+        to_right, to_left = outs[2 * f : 2 * f + 2]
+        wait_all(loads[f][0])
+        block = tn(flat(buf[f, 0]), rows_refs[f][...])
+        to_right[:half, :] = (block[:half] + from_left[...].astype(F32)).astype(BF16)
+        to_right[half:, :] = block[half:].astype(BF16)
+        wait_all(loads[f][1])
+        block = tn(flat(buf[f, 1]), rows_refs[f][...])
+        to_left[:half, :] = block[:half].astype(BF16)
+        to_left[half:, :] = (block[half:] + from_right[...].astype(F32)).astype(BF16)
+
+
+def side_blocks(lefts, rows, near):
+    depth, cols = rows[0].shape
+    block = lefts[0].shape[-1] // RING
     shape = jax.ShapeDtypeStruct((block, cols), BF16)
     return pl.pallas_call(
         side_kernel,
-        in_specs=[HBM] + [VMEM] * 3,
-        out_specs=[VMEM] * 2,
-        out_shape=[shape, shape],
-        scratch_shapes=[pltpu.VMEM((2, block, depth), BF16), pltpu.SemaphoreType.DMA((2,))],
-        compiler_params=params(),
-        cost_estimate=cost(4 * rows.shape[0] * block * cols, 4 * rows.size),
+        in_specs=[HBM] * RING + [VMEM] * 6,
+        out_specs=[VMEM] * 4,
+        out_shape=[shape] * 4,
+        scratch_shapes=left_scratch(block, 2),
+        compiler_params=params(),
+        cost_estimate=cost(8 * depth * block * cols, 8 * depth * cols),
         name="side",
-    )(in_hbm(left), rows, from_left, from_right)
-
-
-def own_kernel(left_hbm, rows_ref, a_ref, b_ref, out_ref, left, sem):
-    load = pltpu.make_async_copy(left_hbm.at[0], left, sem)
-    load.start()
-    load.wait()
-    block = jnp.dot(left[...], rows_ref[...], preferred_element_type=F32)
-    out_ref[...] = block + a_ref[...].astype(F32) + b_ref[...].astype(F32)
-
-
-def own_block(left, rows, a, b):
-    _, block, depth = left.shape
-    cols = rows.shape[1]
+    )(*[in_hbm(left) for left in lefts], *rows, *near)
+
+
+def own_kernel(*refs):
+    lefts, rows_refs, parts, outs = refs[:RING], refs[RING : RING + 2], refs[RING + 2 : RING + 6], refs[RING + 6 : RING + 8]
+    buf, sems, part_buf, part_sems, out_buf, out_sems = refs[RING + 8 :]
+    gets = [pltpu.make_async_copy(parts[i], part_buf.at[i], part_sems.at[i]) for i in range(4)]
+    for get in gets:
+        get.start()
+    loads = left_loads(lefts, buf, sems, (0,))
+    chunks = out_sems.shape[1]
+    puts = []
+    for f in range(2):
+        wait_all(loads[f][0])
+        block = tn(flat(buf[f, 0]), rows_refs[f][...])
+        wait_all(gets[2 * f : 2 * f + 2])
+        size = block.shape[0] // chunks
+        for c in range(chunks):
+            at = slice(c * size, (c + 1) * size)
+            out_buf[f, at] = (
+                block[at] + part_buf[2 * f, at].astype(F32) + part_buf[2 * f + 1, at].astype(F32)
+            )
+            put = pltpu.make_async_copy(out_buf.at[f, at], outs[f].at[at], out_sems.at[f, c])
+            put.start()
+            puts.append(put)
+    wait_all(puts)
+
+
+def own_blocks(lefts, rows, parts):
+    depth, cols = rows[0].shape
+    block = lefts[0].shape[-1] // RING
     return pl.pallas_call(
         own_kernel,
-        in_specs=[HBM] + [VMEM] * 3,
-        out_specs=VMEM,
-        out_shape=jax.ShapeDtypeStruct((block, cols), F32),
-        scratch_shapes=[pltpu.VMEM((block, depth), BF16), pltpu.SemaphoreType.DMA],
-        compiler_params=params(),
-        cost_estimate=cost(2 * rows.shape[0] * block * cols, 8 * rows.size),
+        in_specs=[HBM] * RING + [VMEM] * 2 + [ANY] * 4,
+        out_specs=[HBM] * 2,
+        out_shape=[pltpu.HBM((block, cols), F32)] * 2,
+        scratch_shapes=left_scratch(block, 1)
+        + [pltpu.VMEM((4, block, cols), BF16), pltpu.SemaphoreType.DMA((4,))]
+        + [pltpu.VMEM((2, block, cols), F32), pltpu.SemaphoreType.DMA((2, 4))],
+        compiler_params=params(),
+        cost_estimate=cost(4 * depth * block * cols, 16 * depth * cols),
         name="own",
-    )(in_hbm(left), rows, a, b)
-
-
-def reduced(left, pieces, axis):
-    top, low, rows = far_block(left, pieces)
-    from_left, from_right = shift(top, axis, 1), shift(low, axis, 3)
-    to_right, to_left = side_blocks(left, rows, from_left, from_right)
-    return own_block(left, rows, shift(to_right, axis, 1), shift(to_left, axis, 3))
+    )(*[in_hbm(left) for left in lefts], *rows, *parts)
 
 
 def per_device(states, gains, proj_a, proj_b, cotangent, src_len, tgt_len, dest):
@@ -603,15 +666,16 @@
     slots = slots.reshape(SEQ_DEV, MAXLEN, width)
     slots = lax.all_to_all(slots, ("z", "x"), split_axis=0, concat_axis=0, tiled=True)
     slots = slots.reshape(SLOTS, width)
-    (near_a, far_a), (near_b, far_b) = exchanged(by_x, "x"), exchanged(by_z, "z")
-    slots, near_a, near_b = lax.optimization_barrier((slots, near_a, near_b))
+    pieces = exchanged(by_x, "x") + exchanged(by_z, "z")
+    slots, pieces = lax.optimization_barrier((slots, pieces))
+    pieces[0], pieces[RING] = in_hbm(pieces[0]), in_hbm(pieces[RING])
+    lefts = gathered(stacked(pieces).reshape(2, RING, QUARTER, width), "mp")
     front, back = attend(keep, got, slots, src_len, tgt_len, dest)
     back = back.reshape(SEQ_DEV, MAXLEN, width)
     back = lax.all_to_all(back, ("z", "x"), split_axis=0, concat_axis=0, tiled=True)
-    left_a, left_b = turned([by_x[0], *near_a, far_a]), turned([by_z[0], *near_b, far_b])
-    back, left_a, left_b = lax.optimization_barrier((back, left_a, left_b))
     keep, send = unpack(back.reshape(SLOTS, width), front, src_len, dest)
     got = lax.ppermute(send, "section", swap)
+    got, lefts[1], lefts[2] = lax.optimization_barrier((got, lefts[1], lefts[2]))
     first, second = join(keep, got)
 
     rights_a, rights_b = spread(first, "x"), spread(second, "z")
@@ -622,8 +686,11 @@
     quarter = rms_back(rows, gains, parts)
     grad_states = place(gathered(quarter, "mp"))
 
-    grad_a = reduced(left_a, rights_a, "z")
-    grad_b = reduced(left_b, rights_b, "x")
+    outs = far_blocks(lefts, rights_a, rights_b)
+    near = [shift(out, axis, k) for out, axis, k in zip(outs[:4], "zzxx", (1, 3, 1, 3), strict=True)]
+    sides = side_blocks(lefts, outs[4:], near)
+    sides = [shift(out, axis, k) for out, axis, k in zip(sides, "zzxx", (1, 3, 1, 3), strict=True)]
+    grad_a, grad_b = own_blocks(lefts, outs[4:], sides)
     return (grad_states[None], grad_a[None], grad_b[None])
 
 

time: 138 us -> 139 us (level)
  starting transfers between devices: 55.7 us -> 63.7 us
  Pallas kernels: 45.2 us -> 40.4 us
  waiting for transfers between devices: 34.2 us -> 32.8 us
    ppermute x23 -> x26, starting transfers between devices: 38.1 us -> 46 us  [shift(): return lax.ppermute(value, axis, [(i, (i + k) % RING) for i in range(RING)])]
    pallas_call x9 -> x5, Pallas kernels: 21 us -> 16.4 us  [the longest x1 5.15 us: stacked(): pl.pallas_call(stack_kernel, in_specs=[ANY] * count, out_specs=HBM, out_s...]
    all_to_all x1, waiting for transfers between devices: 0.01 us -> 2.12 us  [per_device(): lax.all_to_all(back, ('z', 'x'), split_axis=0, concat_axis=0, tiled=True)]
    ppermute x23 -> x26, waiting for transfers between devices: 31.2 us -> 29.2 us  [shift(): return lax.ppermute(value, axis, [(i, (i + k) % RING) for i in range(RING)])]
    ppermute x2, waiting for transfers between devices: 3.03 us -> 1.51 us  [per_device(): got = lax.ppermute(send, 'section', swap)]
  transfers between devices with their start and end apart: 28 -> 31, of which waited for: 9 -> 10; matrix products, arithmetic and copies ran while one was open for 0% -> 0% of each run, Pallas kernels for 22% -> 19%
where the time goes in v4:
time: 139 us; the launch traced here: 138 us
  starting transfers between devices  63.7 us (46%)
  Pallas kernels  40.4 us (29%)
  waiting for transfers between devices  32.8 us (24%)
    ppermute x26, starting transfers between devices, shift(): return lax.ppermute(value, axis, [(i, (i + k) % RING) for i in range(RING)])  46 us
    ppermute x26, waiting for transfers between devices, shift(): return lax.ppermute(value, axis, [(i, (i + k) % RING) for i in range(RING)])  29.2 us
    pallas_call x1, Pallas kernels, dnorm_partial(): pl.pallas_call(dnorm_kernel, in_specs=[VMEM] * 2 + [HBM] * 2, out_specs=V...  9.32 us
    pallas_call x1, Pallas kernels, forward(): pl.pallas_call(forward_kernel, in_specs=[HBM] * 5, out_specs=[VMEM] * 2 +...  8.98 us
    all_to_all x1, starting transfers between devices, per_device(): lax.all_to_all(slots, ('z', 'x'), split_axis=0, concat_axis=0, tiled=True)  8.38 us
    pallas_call x1, Pallas kernels, stacked(): pl.pallas_call(stack_kernel, in_specs=[ANY] * count, out_specs=HBM, out_s...  5.15 us
    all_to_all x1, starting transfers between devices, per_device(): lax.all_to_all(back, ('z', 'x'), split_axis=0, concat_axis=0, tiled=True)  4.86 us
    all_to_all x1, starting transfers between devices, per_device(): lax.all_to_all(partial.reshape(RING, TOK // RING, -1), 'mp', split_axis=0...  4.24 us
  transfers between devices with their start and end apart: 31, of which 10 were waited for; matrix products, arithmetic and copies ran while one was open for 0% of the time, Pallas kernels for 19%

profile of v4, /device:TPU:0, one launch (start us, length us, event | category | flops | bytes accessed | tf_op | source)
XLA Modules:
  0.0 138.0 jit_solution(8680904213693447725)
XLA Ops:
  0.7 9.0 %forward.1 = (bf16[128,1024]{1,0:T(8,128)(2,1)S(1)}, bf16[128,1024]{1,0:T(8,128)(2,1)S(1)}, bf16[32,1024]{1,0:T(8,128)(2,1)}, bf16[32,1024]{1,0:T(8,128)(2,1)}, ...) custom-call(bf16[128,4096]{1,0:T(8,128)(2,1)} %bitcast.23, ...), custom_call_target="tpu_custom_call" | custom-call | flops 2147483648 | bytes 16777216 | tf_op jit(solution)/shard_map/forward/pallas_call | solution.py:182
  9.8 1.5 %collective-permute-done.got_ref = bf16[128,1024]{1,0:T(8,128)(2,1)S(1)} collective-permute-done((bf16[128,1024]{1,0:T(8,128)(2,1)S(1)}, bf16[128,1024]{1,0:T(8,128)(2,1)S(1)}, u32[]{:S(2)}, u32[]{:S(2)}) %collective-permute-start) | collective-permute-done | bytes 262176 | tf_op jit(solution)/shard_map/ppermute | solution.py:663
  11.3 1.2 pack.1
  12.4 8.4 %all-to-all-start = ((bf16[16,16,1024]{2,1,0:T(8,128)(2,1)}), bf16[16,16,1024]{2,1,0:T(8,128)(2,1)S(1)}, u32[]{:S(2)}, u32[]{:S(2)}) async-start(bf16[16,16,1024]{2,1,0:T(8,128)(2,1)} %bitcast.3), calls=%async_computation | async-start | bytes 1048576 | tf_op jit(solution)/shard_map/all_to_all | solution.py:667
  20.8 1.9 %collective-permute-start.1 = (bf16[32,1024]{1,0:T(8,128)(2,1)}, bf16[32,1024]{1,0:T(8,128)(2,1)S(1)}, u32[]{:S(2)}, u32[]{:S(2)}) collective-permute-start(bf16[32,1024]{1,0:T(8,128)(2,1)} %get-tuple-element.46), channel_id=1, source_target_pairs={{0,4},{4,8},{8,12},{12,0},{1,5},{5,9},{9,13},{13,1},{2,6},{6,10},{... | collective-permute-start | bytes 196616 | tf_op jit(solution)/shard_map/ppermute | solution.py:458
  22.8 1.4 collective-permute-start.2
  24.1 2.2 %collective-permute-start.3 = (bf16[32,1024]{1,0:T(8,128)(2,1)}, bf16[32,1024]{1,0:T(8,128)(2,1)S(1)}, u32[]{:S(2)}, u32[]{:S(2)}) collective-permute-start(bf16[32,1024]{1,0:T(8,128)(2,1)} %get-tuple-element.48), channel_id=1, source_target_pairs={{0,8},{4,12},{8,0},{12,4},{1,9},{5,13},{9,1},{13,5},{2,10},{6,14},... | collective-permute-start | bytes 196616 | tf_op jit(solution)/shard_map/ppermute | solution.py:458
  26.3 1.5 %collective-permute-start.4 = (bf16[32,1024]{1,0:T(8,128)(2,1)}, bf16[32,1024]{1,0:T(8,128)(2,1)S(1)}, u32[]{:S(2)}, u32[]{:S(2)}) collective-permute-start(bf16[32,1024]{1,0:T(8,128)(2,1)} %get-tuple-element.50), channel_id=1, source_target_pairs={{0,16},{16,32},{32,48},{48,0},{1,17},{17,33},{33,49},{49,1},{2,18}... | collective-permute-start | bytes 196616 | tf_op jit(solution)/shard_map/ppermute | solution.py:458
  27.8 1.8 %collective-permute-start.5 = (bf16[32,1024]{1,0:T(8,128)(2,1)}, bf16[32,1024]{1,0:T(8,128)(2,1)S(1)}, u32[]{:S(2)}, u32[]{:S(2)}) collective-permute-start(bf16[32,1024]{1,0:T(8,128)(2,1)} %get-tuple-element.51), channel_id=1, source_target_pairs={{0,48},{16,0},{32,16},{48,32},{1,49},{17,1},{33,17},{49,33},{2,50}... | collective-permute-start | bytes 196616 | tf_op jit(solution)/shard_map/ppermute | solution.py:458
  29.5 2.9 %collective-permute-done.1.refs_1_ = bf16[32,1024]{1,0:T(8,128)(2,1)S(1)} collective-permute-done((bf16[32,1024]{1,0:T(8,128)(2,1)}, bf16[32,1024]{1,0:T(8,128)(2,1)S(1)}, u32[]{:S(2)}, u32[]{:S(2)}) %collective-permute-start.1) | collective-permute-done | bytes 65568 | tf_op jit(solution)/shard_map/ppermute | solution.py:458
  32.4 3.0 %collective-permute-start.6 = (bf16[32,1024]{1,0:T(8,128)(2,1)}, bf16[32,1024]{1,0:T(8,128)(2,1)S(1)}, u32[]{:S(2)}, u32[]{:S(2)}) collective-permute-start(bf16[32,1024]{1,0:T(8,128)(2,1)} %get-tuple-element.52), channel_id=1, source_target_pairs={{0,32},{16,48},{32,0},{48,16},{1,33},{17,49},{33,1},{49,17},{2,34}... | collective-permute-start | bytes 196616 | tf_op jit(solution)/shard_map/ppermute | solution.py:458
  35.4 3.0 %collective-permute-done.6.refs_7_ = bf16[32,1024]{1,0:T(8,128)(2,1)S(1)} collective-permute-done((bf16[32,1024]{1,0:T(8,128)(2,1)}, bf16[32,1024]{1,0:T(8,128)(2,1)S(1)}, u32[]{:S(2)}, u32[]{:S(2)}) %collective-permute-start.6) | collective-permute-done | bytes 65568 | tf_op jit(solution)/shard_map/ppermute | solution.py:458
  38.4 2.9 %attend.1 = (bf16[128,1024]{1,0:T(8,128)(2,1)S(1)}, bf16[256,1024]{1,0:T(8,128)(2,1)}) custom-call(bf16[128,1024]{1,0:T(8,128)(2,1)S(1)} %get-tuple-element.43.keep_ref, bf16[128,1024]{1,0:T(8,128)(2,1)S(1)} %collective-permute-done.got_ref, bf16[256,1024]{1,0:T(8,128)(2,1)S(1)} %bitcast.13, s32[16,16]{1,0:T(8,128)S(1)} %copy-done.3, ...), custom_call_target="tpu_custom_call" | custom-call | flops 805306368 | bytes 2097152 | tf_op jit(solution)/shard_map/attend/pallas_call | solution.py:281
  41.3 4.9 %all-to-all-start.1 = ((bf16[16,16,1024]{2,1,0:T(8,128)(2,1)}), bf16[16,16,1024]{2,1,0:T(8,128)(2,1)S(1)}, u32[]{:S(2)}, u32[]{:S(2)}) async-start(bf16[16,16,1024]{2,1,0:T(8,128)(2,1)} %bitcast.5), calls=%async_computation.1 | async-start | bytes 1048576 | tf_op jit(solution)/shard_map/all_to_all | solution.py:675
  46.2 5.2 %stack.1 = bf16[256,1024]{1,0:T(8,128)(2,1)} custom-call(bf16[32,1024]{1,0:T(8,128)(2,1)} %get-tuple-element.58.refs_0_, bf16[32,1024]{1,0:T(8,128)(2,1)S(1)} %collective-permute-done.1.refs_1_, bf16[32,1024]{1,0:T(8,128)(2,1)S(1)} %collective-permute-done.2.refs_2_, bf16[32,1024]{1,0:T(8,128)(2,1)S(1)} %collective-permute-done.3.refs_3_, ...), custom_call_target="tpu_custom_call" | custom-call | bytes 1048576 | tf_op jit(solution)/shard_map/stack/pallas_call | solution.py:492
  51.3 1.6 %collective-permute-start.8 = (bf16[2,4,32,1024]{3,2,1,0:T(8,128)(2,1)}, bf16[2,4,32,1024]{3,2,1,0:T(8,128)(2,1)S(1)}, u32[]{:S(2)}, u32[]{:S(2)}) collective-permute-start(bf16[2,4,32,1024]{3,2,1,0:T(8,128)(2,1)} %bitcast.18), channel_id=1, source_target_pairs={{0,1},{1,2},{2,3},{3,0},{4,5},{5,6},{6,7},{7,4},{8,9},{9,10},{10,1... | collective-permute-start | bytes 1572872 | tf_op jit(solution)/shard_map/ppermute | solution.py:458
  53.0 1.7 %collective-permute-start.9 = (bf16[2,4,32,1024]{3,2,1,0:T(8,128)(2,1)}, bf16[2,4,32,1024]{3,2,1,0:T(8,128)(2,1)S(1)}, u32[]{:S(2)}, u32[]{:S(2)}) collective-permute-start(bf16[2,4,32,1024]{3,2,1,0:T(8,128)(2,1)} %bitcast.19), channel_id=1, source_target_pairs={{0,3},{1,0},{2,1},{3,2},{4,7},{5,4},{6,5},{7,6},{8,11},{9,8},{10,9... | collective-permute-start | bytes 1572872 | tf_op jit(solution)/shard_map/ppermute | solution.py:458
  54.6 2.1 %all-to-all-done.1 = bf16[16,16,1024]{2,1,0:T(8,128)(2,1)S(1)} async-done(((bf16[16,16,1024]{2,1,0:T(8,128)(2,1)}), bf16[16,16,1024]{2,1,0:T(8,128)(2,1)S(1)}, u32[]{:S(2)}, u32[]{:S(2)}) %all-to-all-start.1) | async-done | bytes 524320 | tf_op jit(solution)/shard_map/all_to_all | solution.py:675
  56.8 0.4 unpack.1
  57.3 8.0 %collective-permute-done.8.refs_1_ = bf16[2,4,32,1024]{3,2,1,0:T(8,128)(2,1)S(1)} collective-permute-done((bf16[2,4,32,1024]{3,2,1,0:T(8,128)(2,1)}, bf16[2,4,32,1024]{3,2,1,0:T(8,128)(2,1)S(1)}, u32[]{:S(2)}, u32[]{:S(2)}) %collective-permute-start.8) | collective-permute-done | bytes 524320 | tf_op jit(solution)/shard_map/ppermute | solution.py:458
  65.4 1.7 %collective-permute-start.14 = (bf16[128,1024]{1,0:T(8,128)(2,1)S(1)}, bf16[128,1024]{1,0:T(8,128)(2,1)S(1)}, u32[]{:S(2)}, u32[]{:S(2)}) collective-permute-start(bf16[128,1024]{1,0:T(8,128)(2,1)S(1)} %get-tuple-element.67.first_ref.refs_4_), channel_id=1, source_target_pairs={{0,4},{4,8},{8,12},{12,0},{1,5},{5,9},{9,13},{13,1},{2,6},{6,10},{... | collective-permute-start | bytes 786440 | tf_op jit(solution)/shard_map/ppermute | solution.py:458
  67.1 1.6 %collective-permute-start.15 = (bf16[128,1024]{1,0:T(8,128)(2,1)S(1)}, bf16[128,1024]{1,0:T(8,128)(2,1)S(1)}, u32[]{:S(2)}, u32[]{:S(2)}) collective-permute-start(bf16[128,1024]{1,0:T(8,128)(2,1)S(1)} %get-tuple-element.67.first_ref.refs_4_), channel_id=1, source_target_pairs={{0,12},{4,0},{8,4},{12,8},{1,13},{5,1},{9,5},{13,9},{2,14},{6,2},{... | collective-permute-start | bytes 786440 | tf_op jit(solution)/shard_map/ppermute | solution.py:458
  68.7 1.6 %collective-permute-start.13 = (bf16[2,4,32,1024]{3,2,1,0:T(8,128)(2,1)S(1)}, bf16[2,4,32,1024]{3,2,1,0:T(8,128)(2,1)}, u32[]{:S(2)}, u32[]{:S(2)}) collective-permute-start(bf16[2,4,32,1024]{3,2,1,0:T(8,128)(2,1)S(1)} %collective-permute-done.8.refs_1_), channel_id=1, source_target_pairs={{0,1},{1,2},{2,3},{3,0},{4,5},{5,6},{6,7},{7,4},{8,9},{9,10},{10,1... | collective-permute-start | bytes 1572872 | tf_op jit(solution)/shard_map/ppermute | solution.py:458
  70.3 1.9 %collective-permute-start.16 = (bf16[128,1024]{1,0:T(8,128)(2,1)S(1)}, bf16[128,1024]{1,0:T(8,128)(2,1)}, u32[]{:S(2)}, u32[]{:S(2)}) collective-permute-start(bf16[128,1024]{1,0:T(8,128)(2,1)S(1)} %get-tuple-element.67.first_ref.refs_4_), channel_id=1, source_target_pairs={{0,8},{4,12},{8,0},{12,4},{1,9},{5,13},{9,1},{13,5},{2,10},{6,14},... | collective-permute-start | bytes 786440 | tf_op jit(solution)/shard_map/ppermute | solution.py:458
  72.2 1.5 %collective-permute-start.17 = (bf16[128,1024]{1,0:T(8,128)(2,1)S(1)}, bf16[128,1024]{1,0:T(8,128)(2,1)}, u32[]{:S(2)}, u32[]{:S(2)}) collective-permute-start(bf16[128,1024]{1,0:T(8,128)(2,1)S(1)} %get-tuple-element.68.second_ref.refs_8_), channel_id=1, source_target_pairs={{0,16},{16,32},{32,48},{48,0},{1,17},{17,33},{33,49},{49,1},{2,18}... | collective-permute-start | bytes 786440 | tf_op jit(solution)/shard_map/ppermute | solution.py:458
  73.7 1.9 %collective-permute-done.14.refs_5_ = bf16[128,1024]{1,0:T(8,128)(2,1)S(1)} collective-permute-done((bf16[128,1024]{1,0:T(8,128)(2,1)S(1)}, bf16[128,1024]{1,0:T(8,128)(2,1)S(1)}, u32[]{:S(2)}, u32[]{:S(2)}) %collective-permute-start.14) | collective-permute-done | bytes 262176 | tf_op jit(solution)/shard_map/ppermute | solution.py:458
  75.5 3.2 %collective-permute-start.18 = (bf16[128,1024]{1,0:T(8,128)(2,1)S(1)}, bf16[128,1024]{1,0:T(8,128)(2,1)}, u32[]{:S(2)}, u32[]{:S(2)}) collective-permute-start(bf16[128,1024]{1,0:T(8,128)(2,1)S(1)} %get-tuple-element.68.second_ref.refs_8_), channel_id=1, source_target_pairs={{0,48},{16,0},{32,16},{48,32},{1,49},{17,1},{33,17},{49,33},{2,50}... | collective-permute-start | bytes 786440 | tf_op jit(solution)/shard_map/ppermute | solution.py:458
  78.7 0.9 collective-permute-start.19
  79.6 9.3 %dnorm.1 = bf16[128,4096]{1,0:T(8,128)(2,1)} custom-call(bf16[128,1024]{1,0:T(8,128)(2,1)S(1)} %get-tuple-element.67.first_ref.refs_4_, bf16[128,1024]{1,0:T(8,128)(2,1)S(1)} %get-tuple-element.68.second_ref.refs_8_, bf16[4096,1024]{1,0:T(8,128)(2,1)} %bitcast.15, bf16[4096,1024]{1,0:T(8,128)(2,1)} %bitcast.17), custom_call_target="tpu_custom_call" | custom-call | flops 2147483648 | bytes 16777216 | tf_op jit(solution)/shard_map/dnorm/pallas_call | solution.py:388
  89.0 4.2 %all-to-all-start.2 = ((bf16[4,32,4096]{2,1,0:T(8,128)(2,1)}), bf16[4,32,4096]{2,1,0:T(8,128)(2,1)S(1)}, u32[]{:S(2)}, u32[]{:S(2)}) async-start(bf16[4,32,4096]{2,1,0:T(8,128)(2,1)} %bitcast.8), calls=%async_computation.2 | async-start | bytes 2097152 | tf_op jit(solution)/shard_map/all_to_all | solution.py:683
  93.2 2.6 %far.1 = (bf16[128,1024]{1,0:T(8,128)(2,1)S(1)}, bf16[128,1024]{1,0:T(8,128)(2,1)S(1)}, bf16[128,1024]{1,0:T(8,128)(2,1)S(1)}, bf16[128,1024]{1,0:T(8,128)(2,1)S...) custom-call(bf16[2,4,32,1024]{3,2,1,0:T(8,128)(2,1)} %bitcast.20, bf16[2,4,32,1024]{3,2,1,0:T(8,128)(2,1)} %copy-done.6, ...), custom_call_target="tpu_custom_call" | custom-call | flops 536870912 | bytes 8388608 | tf_op jit(solution)/shard_map/far/pallas_call | solution.py:569
  95.9 0.9 collective-permute-start.20
  96.8 2.4 %collective-permute-start.21 = (bf16[128,1024]{1,0:T(8,128)(2,1)S(1)}, bf16[128,1024]{1,0:T(8,128)(2,1)S(1)}, u32[]{:S(2)}, u32[]{:S(2)}) collective-permute-start(bf16[128,1024]{1,0:T(8,128)(2,1)S(1)} %get-tuple-element.74), channel_id=1, source_target_pairs={{0,48},{16,0},{32,16},{48,32},{1,49},{17,1},{33,17},{49,33},{2,50}... | collective-permute-start | bytes 786440 | tf_op jit(solution)/shard_map/ppermute | solution.py:458
  99.2 0.6 collective-permute-start.22
  99.8 3.7 %collective-permute-start.23 = (bf16[128,1024]{1,0:T(8,128)(2,1)S(1)}, bf16[128,1024]{1,0:T(8,128)(2,1)S(1)}, u32[]{:S(2)}, u32[]{:S(2)}) collective-permute-start(bf16[128,1024]{1,0:T(8,128)(2,1)S(1)} %get-tuple-element.76), channel_id=1, source_target_pairs={{0,12},{4,0},{8,4},{12,8},{1,13},{5,1},{9,5},{13,9},{2,14},{6,2},{... | collective-permute-start | bytes 786440 | tf_op jit(solution)/shard_map/ppermute | solution.py:458
  103.5 4.3 %collective-permute-done.22.refs_8_ = bf16[128,1024]{1,0:T(8,128)(2,1)S(1)} collective-permute-done((bf16[128,1024]{1,0:T(8,128)(2,1)S(1)}, bf16[128,1024]{1,0:T(8,128)(2,1)S(1)}, u32[]{:S(2)}, u32[]{:S(2)}) %collective-permute-start.22) | collective-permute-done | bytes 262176 | tf_op jit(solution)/shard_map/ppermute | solution.py:458
  107.8 3.8 %side.1 = (bf16[256,1024]{1,0:T(8,128)(2,1)}, bf16[256,1024]{1,0:T(8,128)(2,1)}, bf16[256,1024]{1,0:T(8,128)(2,1)}, bf16[256,1024]{1,0:T(8,128)(2,1)}) custom-call(bf16[2,4,32,1024]{3,2,1,0:T(8,128)(2,1)} %bitcast.21, bf16[2,4,32,1024]{3,2,1,0:T(8,128)(2,1)} %copy-done.6, bf16[2,4,32,1024]{3,2,1,0:T(8,128)(2,1)} %copy-done.7, ...), custom_call_target="tpu_custom_call" | custom-call | flops 1073741824 | bytes 4194304 | tf_op jit(solution)/shard_map/side/pallas_call | solution.py:603
  111.8 3.2 %collective-permute-start.25 = (bf16[256,1024]{1,0:T(8,128)(2,1)}, bf16[256,1024]{1,0:T(8,128)(2,1)}, u32[]{:S(2)}, u32[]{:S(2)}) collective-permute-start(bf16[256,1024]{1,0:T(8,128)(2,1)} %get-tuple-element.78), channel_id=1, source_target_pairs={{0,48},{16,0},{32,16},{48,32},{1,49},{17,1},{33,17},{49,33},{2,50}... | collective-permute-start | bytes 1572872 | tf_op jit(solution)/shard_map/ppermute | solution.py:458
  115.0 1.4 %collective-permute-start.26 = (bf16[256,1024]{1,0:T(8,128)(2,1)}, bf16[256,1024]{1,0:T(8,128)(2,1)}, u32[]{:S(2)}, u32[]{:S(2)}) collective-permute-start(bf16[256,1024]{1,0:T(8,128)(2,1)} %get-tuple-element.79), channel_id=1, source_target_pairs={{0,4},{4,8},{8,12},{12,0},{1,5},{5,9},{9,13},{13,1},{2,6},{6,10},{... | collective-permute-start | bytes 1572872 | tf_op jit(solution)/shard_map/ppermute | solution.py:458
  116.4 2.0 %collective-permute-start.27 = (bf16[256,1024]{1,0:T(8,128)(2,1)}, bf16[256,1024]{1,0:T(8,128)(2,1)}, u32[]{:S(2)}, u32[]{:S(2)}) collective-permute-start(bf16[256,1024]{1,0:T(8,128)(2,1)} %get-tuple-element.80), channel_id=1, source_target_pairs={{0,12},{4,0},{8,4},{12,8},{1,13},{5,1},{9,5},{13,9},{2,14},{6,2},{... | collective-permute-start | bytes 1572872 | tf_op jit(solution)/shard_map/ppermute | solution.py:458
  118.4 1.2 rms_back.1.refs_0_
  119.6 2.4 %collective-permute-start.10 = (bf16[32,4096]{1,0:T(8,128)(2,1)S(1)}, bf16[32,4096]{1,0:T(8,128)(2,1)S(1)}, u32[]{:S(2)}, u32[]{:S(2)}) collective-permute-start(bf16[32,4096]{1,0:T(8,128)(2,1)S(1)} %rms_back.1.refs_0_), channel_id=1, source_target_pairs={{0,1},{1,2},{2,3},{3,0},{4,5},{5,6},{6,7},{7,4},{8,9},{9,10},{10,1... | collective-permute-start | bytes 786440 | tf_op jit(solution)/shard_map/ppermute | solution.py:458
  122.0 5.3 %collective-permute-done.10.refs_1_ = bf16[32,4096]{1,0:T(8,128)(2,1)S(1)} collective-permute-done((bf16[32,4096]{1,0:T(8,128)(2,1)S(1)}, bf16[32,4096]{1,0:T(8,128)(2,1)S(1)}, u32[]{:S(2)}, u32[]{:S(2)}) %collective-permute-start.10) | collective-permute-done | bytes 262176 | tf_op jit(solution)/shard_map/ppermute | solution.py:458
  127.3 2.0 %collective-permute-start.11 = (bf16[32,4096]{1,0:T(8,128)(2,1)S(1)}, bf16[32,4096]{1,0:T(8,128)(2,1)S(1)}, u32[]{:S(2)}, u32[]{:S(2)}) collective-permute-start(bf16[32,4096]{1,0:T(8,128)(2,1)S(1)} %rms_back.1.refs_0_), channel_id=1, source_target_pairs={{0,3},{1,0},{2,1},{3,2},{4,7},{5,4},{6,5},{7,6},{8,11},{9,8},{10,9... | collective-permute-start | bytes 786440 | tf_op jit(solution)/shard_map/ppermute | solution.py:458
  129.3 3.8 %own.1 = (f32[256,1024]{1,0:T(8,128)}, f32[256,1024]{1,0:T(8,128)}) custom-call(bf16[2,4,32,1024]{3,2,1,0:T(8,128)(2,1)} %bitcast.22, bf16[2,4,32,1024]{3,2,1,0:T(8,128)(2,1)} %copy-done.6, bf16[2,4,32,1024]{3,2,1,0:T(8,128)(2,1)} %copy-done.7, bf16[2,4,32,1024]{3,2,1,0:T(8,128)(2,1)} %collective-permute-done.13.refs_3_, ...), custom_call_target="tpu_custom_call" | custom-call | flops 536870912 | bytes 8388608 | tf_op jit(solution)/shard_map/own/pallas_call | solution.py:643
  133.1 0.5 collective-permute-done.11.refs_2_
  133.6 3.2 %collective-permute-done.12.refs_3_ = bf16[32,4096]{1,0:T(8,128)(2,1)S(1)} collective-permute-done((bf16[32,4096]{1,0:T(8,128)(2,1)S(1)}, bf16[32,4096]{1,0:T(8,128)(2,1)S(1)}, u32[]{:S(2)}, u32[]{:S(2)}) %collective-permute-start.12) | collective-permute-done | bytes 262176 | tf_op jit(solution)/shard_map/ppermute | solution.py:458
  136.9 1.0 place.1
  (46 shorter events, 0.5 us)
Async XLA Ops:
  0.6 10.6 %copy-start.3 = (s32[16,16]{1,0:T(8,128)S(1)}, s32[16,16]{1,0:T(8,128)}, u32[]{:S(2)}) copy-start(s32[16,16]{1,0:T(8,128)} %src_ref.5) | copy-start | bytes 3076
  0.6 10.6 %copy-start.4 = (s32[16,16]{1,0:T(8,128)S(1)}, s32[16,16]{1,0:T(8,128)}, u32[]{:S(2)}) copy-start(s32[16,16]{1,0:T(8,128)} %dest_ref.5) | copy-start | bytes 3076
  0.7 37.7 %copy-start.5 = (s32[16,16]{1,0:T(8,128)S(1)}, s32[16,16]{1,0:T(8,128)}, u32[]{:S(2)}) copy-start(s32[16,16]{1,0:T(8,128)} %tgt_ref.1) | copy-start | bytes 3076
  9.6 1.6 %collective-permute-start = (bf16[128,1024]{1,0:T(8,128)(2,1)S(1)}, bf16[128,1024]{1,0:T(8,128)(2,1)S(1)}, u32[]{:S(2)}, u32[]{:S(2)}) collective-permute-start(bf16[128,1024]{1,0:T(8,128)(2,1)S(1)} %get-tuple-element.44), channel_id=1, source_target_pairs={{0,64},{64,0},{1,65},{65,1},{2,66},{66,2},{3,67},{67,3},{4,68},{68... | collective-permute-start | bytes 786440 | tf_op jit(solution)/shard_map/ppermute | solution.py:663
  12.4 25.9 %all-to-all-start = ((bf16[16,16,1024]{2,1,0:T(8,128)(2,1)}), bf16[16,16,1024]{2,1,0:T(8,128)(2,1)S(1)}, u32[]{:S(2)}, u32[]{:S(2)}) async-start(bf16[16,16,1024]{2,1,0:T(8,128)(2,1)} %bitcast.3), calls=%async_computation | async-start | bytes 1048576 | tf_op jit(solution)/shard_map/all_to_all | solution.py:667
  20.8 11.5 %collective-permute-start.1 = (bf16[32,1024]{1,0:T(8,128)(2,1)}, bf16[32,1024]{1,0:T(8,128)(2,1)S(1)}, u32[]{:S(2)}, u32[]{:S(2)}) collective-permute-start(bf16[32,1024]{1,0:T(8,128)(2,1)} %get-tuple-element.46), channel_id=1, source_target_pairs={{0,4},{4,8},{8,12},{12,0},{1,5},{5,9},{9,13},{13,1},{2,6},{6,10},{... | collective-permute-start | bytes 196616 | tf_op jit(solution)/shard_map/ppermute | solution.py:458
  22.8 12.6 %collective-permute-start.2 = (bf16[32,1024]{1,0:T(8,128)(2,1)}, bf16[32,1024]{1,0:T(8,128)(2,1)S(1)}, u32[]{:S(2)}, u32[]{:S(2)}) collective-permute-start(bf16[32,1024]{1,0:T(8,128)(2,1)} %get-tuple-element.47), channel_id=1, source_target_pairs={{0,12},{4,0},{8,4},{12,8},{1,13},{5,1},{9,5},{13,9},{2,14},{6,2},{... | collective-permute-start | bytes 196616 | tf_op jit(solution)/shard_map/ppermute | solution.py:458
  24.1 11.2 %collective-permute-start.3 = (bf16[32,1024]{1,0:T(8,128)(2,1)}, bf16[32,1024]{1,0:T(8,128)(2,1)S(1)}, u32[]{:S(2)}, u32[]{:S(2)}) collective-permute-start(bf16[32,1024]{1,0:T(8,128)(2,1)} %get-tuple-element.48), channel_id=1, source_target_pairs={{0,8},{4,12},{8,0},{12,4},{1,9},{5,13},{9,1},{13,5},{2,10},{6,14},... | collective-permute-start | bytes 196616 | tf_op jit(solution)/shard_map/ppermute | solution.py:458
  26.3 9.1 %collective-permute-start.4 = (bf16[32,1024]{1,0:T(8,128)(2,1)}, bf16[32,1024]{1,0:T(8,128)(2,1)S(1)}, u32[]{:S(2)}, u32[]{:S(2)}) collective-permute-start(bf16[32,1024]{1,0:T(8,128)(2,1)} %get-tuple-element.50), channel_id=1, source_target_pairs={{0,16},{16,32},{32,48},{48,0},{1,17},{17,33},{33,49},{49,1},{2,18}... | collective-permute-start | bytes 196616 | tf_op jit(solution)/shard_map/ppermute | solution.py:458
  27.8 7.6 %collective-permute-start.5 = (bf16[32,1024]{1,0:T(8,128)(2,1)}, bf16[32,1024]{1,0:T(8,128)(2,1)S(1)}, u32[]{:S(2)}, u32[]{:S(2)}) collective-permute-start(bf16[32,1024]{1,0:T(8,128)(2,1)} %get-tuple-element.51), channel_id=1, source_target_pairs={{0,48},{16,0},{32,16},{48,32},{1,49},{17,1},{33,17},{49,33},{2,50}... | collective-permute-start | bytes 196616 | tf_op jit(solution)/shard_map/ppermute | solution.py:458
  32.4 6.0 %collective-permute-start.6 = (bf16[32,1024]{1,0:T(8,128)(2,1)}, bf16[32,1024]{1,0:T(8,128)(2,1)S(1)}, u32[]{:S(2)}, u32[]{:S(2)}) collective-permute-start(bf16[32,1024]{1,0:T(8,128)(2,1)} %get-tuple-element.52), channel_id=1, source_target_pairs={{0,32},{16,48},{32,0},{48,16},{1,33},{17,49},{33,1},{49,17},{2,34}... | collective-permute-start | bytes 196616 | tf_op jit(solution)/shard_map/ppermute | solution.py:458
  41.3 15.5 %all-to-all-start.1 = ((bf16[16,16,1024]{2,1,0:T(8,128)(2,1)}), bf16[16,16,1024]{2,1,0:T(8,128)(2,1)S(1)}, u32[]{:S(2)}, u32[]{:S(2)}) async-start(bf16[16,16,1024]{2,1,0:T(8,128)(2,1)} %bitcast.5), calls=%async_computation.1 | async-start | bytes 1048576 | tf_op jit(solution)/shard_map/all_to_all | solution.py:675
  51.3 13.9 %collective-permute-start.8 = (bf16[2,4,32,1024]{3,2,1,0:T(8,128)(2,1)}, bf16[2,4,32,1024]{3,2,1,0:T(8,128)(2,1)S(1)}, u32[]{:S(2)}, u32[]{:S(2)}) collective-permute-start(bf16[2,4,32,1024]{3,2,1,0:T(8,128)(2,1)} %bitcast.18), channel_id=1, source_target_pairs={{0,1},{1,2},{2,3},{3,0},{4,5},{5,6},{6,7},{7,4},{8,9},{9,10},{10,1... | collective-permute-start | bytes 1572872 | tf_op jit(solution)/shard_map/ppermute | solution.py:458
  53.0 12.3 %collective-permute-start.9 = (bf16[2,4,32,1024]{3,2,1,0:T(8,128)(2,1)}, bf16[2,4,32,1024]{3,2,1,0:T(8,128)(2,1)S(1)}, u32[]{:S(2)}, u32[]{:S(2)}) collective-permute-start(bf16[2,4,32,1024]{3,2,1,0:T(8,128)(2,1)} %bitcast.19), channel_id=1, source_target_pairs={{0,3},{1,0},{2,1},{3,2},{4,7},{5,4},{6,5},{7,6},{8,11},{9,8},{10,9... | collective-permute-start | bytes 1572872 | tf_op jit(solution)/shard_map/ppermute | solution.py:458
  57.2 8.1 %collective-permute-start.7 = (bf16[128,1024]{1,0:T(8,128)(2,1)S(1)}, bf16[128,1024]{1,0:T(8,128)(2,1)S(1)}, u32[]{:S(2)}, u32[]{:S(2)}) collective-permute-start(bf16[128,1024]{1,0:T(8,128)(2,1)S(1)} %get-tuple-element.57), channel_id=1, source_target_pairs={{0,64},{64,0},{1,65},{65,1},{2,66},{66,2},{3,67},{67,3},{4,68},{68... | collective-permute-start | bytes 786440 | tf_op jit(solution)/shard_map/ppermute | solution.py:677
  65.3 23.6 %copy-start.6 = (bf16[2,4,32,1024]{3,2,1,0:T(8,128)(2,1)}, bf16[2,4,32,1024]{3,2,1,0:T(8,128)(2,1)S(1)}, u32[]{:S(2)}) copy-start(bf16[2,4,32,1024]{3,2,1,0:T(8,128)(2,1)S(1)} %collective-permute-done.8.refs_1_) | copy-start | bytes 1572868
  65.3 23.6 %copy-start.7 = (bf16[2,4,32,1024]{3,2,1,0:T(8,128)(2,1)}, bf16[2,4,32,1024]{3,2,1,0:T(8,128)(2,1)S(1)}, u32[]{:S(2)}) copy-start(bf16[2,4,32,1024]{3,2,1,0:T(8,128)(2,1)S(1)} %collective-permute-done.9.refs_2_) | copy-start | bytes 1572868
  65.4 23.5 %copy-start = (bf16[128,1024]{1,0:T(8,128)(2,1)}, bf16[128,1024]{1,0:T(8,128)(2,1)S(1)}, u32[]{:S(2)}) copy-start(bf16[128,1024]{1,0:T(8,128)(2,1)S(1)} %get-tuple-element.67.first_ref.refs_4_) | copy-start | bytes 786436
  65.4 23.5 %copy-start.1 = (bf16[128,1024]{1,0:T(8,128)(2,1)}, bf16[128,1024]{1,0:T(8,128)(2,1)S(1)}, u32[]{:S(2)}) copy-start(bf16[128,1024]{1,0:T(8,128)(2,1)S(1)} %get-tuple-element.68.second_ref.refs_8_) | copy-start | bytes 786436
  65.4 10.1 %collective-permute-start.14 = (bf16[128,1024]{1,0:T(8,128)(2,1)S(1)}, bf16[128,1024]{1,0:T(8,128)(2,1)S(1)}, u32[]{:S(2)}, u32[]{:S(2)}) collective-permute-start(bf16[128,1024]{1,0:T(8,128)(2,1)S(1)} %get-tuple-element.67.first_ref.refs_4_), channel_id=1, source_target_pairs={{0,4},{4,8},{8,12},{12,0},{1,5},{5,9},{9,13},{13,1},{2,6},{6,10},{... | collective-permute-start | bytes 786440 | tf_op jit(solution)/shard_map/ppermute | solution.py:458
  67.1 11.6 %collective-permute-start.15 = (bf16[128,1024]{1,0:T(8,128)(2,1)S(1)}, bf16[128,1024]{1,0:T(8,128)(2,1)S(1)}, u32[]{:S(2)}, u32[]{:S(2)}) collective-permute-start(bf16[128,1024]{1,0:T(8,128)(2,1)S(1)} %get-tuple-element.67.first_ref.refs_4_), channel_id=1, source_target_pairs={{0,12},{4,0},{8,4},{12,8},{1,13},{5,1},{9,5},{13,9},{2,14},{6,2},{... | collective-permute-start | bytes 786440 | tf_op jit(solution)/shard_map/ppermute | solution.py:458
  68.7 24.5 %collective-permute-start.13 = (bf16[2,4,32,1024]{3,2,1,0:T(8,128)(2,1)S(1)}, bf16[2,4,32,1024]{3,2,1,0:T(8,128)(2,1)}, u32[]{:S(2)}, u32[]{:S(2)}) collective-permute-start(bf16[2,4,32,1024]{3,2,1,0:T(8,128)(2,1)S(1)} %collective-permute-done.8.refs_1_), channel_id=1, source_target_pairs={{0,1},{1,2},{2,3},{3,0},{4,5},{5,6},{6,7},{7,4},{8,9},{9,10},{10,1... | collective-permute-start | bytes 1572872 | tf_op jit(solution)/shard_map/ppermute | solution.py:458
  70.3 22.9 %collective-permute-start.16 = (bf16[128,1024]{1,0:T(8,128)(2,1)S(1)}, bf16[128,1024]{1,0:T(8,128)(2,1)}, u32[]{:S(2)}, u32[]{:S(2)}) collective-permute-start(bf16[128,1024]{1,0:T(8,128)(2,1)S(1)} %get-tuple-element.67.first_ref.refs_4_), channel_id=1, source_target_pairs={{0,8},{4,12},{8,0},{12,4},{1,9},{5,13},{9,1},{13,5},{2,10},{6,14},... | collective-permute-start | bytes 786440 | tf_op jit(solution)/shard_map/ppermute | solution.py:458
  72.2 21.0 %collective-permute-start.17 = (bf16[128,1024]{1,0:T(8,128)(2,1)S(1)}, bf16[128,1024]{1,0:T(8,128)(2,1)}, u32[]{:S(2)}, u32[]{:S(2)}) collective-permute-start(bf16[128,1024]{1,0:T(8,128)(2,1)S(1)} %get-tuple-element.68.second_ref.refs_8_), channel_id=1, source_target_pairs={{0,16},{16,32},{32,48},{48,0},{1,17},{17,33},{33,49},{49,1},{2,18}... | collective-permute-start | bytes 786440 | tf_op jit(solution)/shard_map/ppermute | solution.py:458
  75.5 13.4 %copy-start.8 = (bf16[128,1024]{1,0:T(8,128)(2,1)}, bf16[128,1024]{1,0:T(8,128)(2,1)S(1)}, u32[]{:S(2)}) copy-start(bf16[128,1024]{1,0:T(8,128)(2,1)S(1)} %collective-permute-done.14.refs_5_) | copy-start | bytes 786436
  75.5 17.7 %collective-permute-start.18 = (bf16[128,1024]{1,0:T(8,128)(2,1)S(1)}, bf16[128,1024]{1,0:T(8,128)(2,1)}, u32[]{:S(2)}, u32[]{:S(2)}) collective-permute-start(bf16[128,1024]{1,0:T(8,128)(2,1)S(1)} %get-tuple-element.68.second_ref.refs_8_), channel_id=1, source_target_pairs={{0,48},{16,0},{32,16},{48,32},{1,49},{17,1},{33,17},{49,33},{2,50}... | collective-permute-start | bytes 786440 | tf_op jit(solution)/shard_map/ppermute | solution.py:458
  78.7 10.2 %copy-start.9 = (bf16[128,1024]{1,0:T(8,128)(2,1)}, bf16[128,1024]{1,0:T(8,128)(2,1)S(1)}, u32[]{:S(2)}) copy-start(bf16[128,1024]{1,0:T(8,128)(2,1)S(1)} %collective-permute-done.15.refs_6_) | copy-start | bytes 786436
  78.7 14.5 %collective-permute-start.19 = (bf16[128,1024]{1,0:T(8,128)(2,1)S(1)}, bf16[128,1024]{1,0:T(8,128)(2,1)}, u32[]{:S(2)}, u32[]{:S(2)}) collective-permute-start(bf16[128,1024]{1,0:T(8,128)(2,1)S(1)} %get-tuple-element.68.second_ref.refs_8_), channel_id=1, source_target_pairs={{0,32},{16,48},{32,0},{48,16},{1,33},{17,49},{33,1},{49,17},{2,34}... | collective-permute-start | bytes 786440 | tf_op jit(solution)/shard_map/ppermute | solution.py:458
  89.0 29.5 %copy-start.2 = (f32[1,4096]{1,0:T(1,128)S(1)}, f32[1,4096]{1,0:T(1,128)}, u32[]{:S(2)}) copy-start(f32[1,4096]{1,0:T(1,128)} %gain_ref.1) | copy-start | bytes 49156
  89.0 29.5 %all-to-all-start.2 = ((bf16[4,32,4096]{2,1,0:T(8,128)(2,1)}), bf16[4,32,4096]{2,1,0:T(8,128)(2,1)S(1)}, u32[]{:S(2)}, u32[]{:S(2)}) async-start(bf16[4,32,4096]{2,1,0:T(8,128)(2,1)} %bitcast.8), calls=%async_computation.2 | async-start | bytes 2097152 | tf_op jit(solution)/shard_map/all_to_all | solution.py:683
  95.9 7.7 %collective-permute-start.20 = (bf16[128,1024]{1,0:T(8,128)(2,1)S(1)}, bf16[128,1024]{1,0:T(8,128)(2,1)S(1)}, u32[]{:S(2)}, u32[]{:S(2)}) collective-permute-start(bf16[128,1024]{1,0:T(8,128)(2,1)S(1)} %get-tuple-element.73), channel_id=1, source_target_pairs={{0,16},{16,32},{32,48},{48,0},{1,17},{17,33},{33,49},{49,1},{2,18}... | collective-permute-start | bytes 786440 | tf_op jit(solution)/shard_map/ppermute | solution.py:458
  96.8 6.7 %collective-permute-start.21 = (bf16[128,1024]{1,0:T(8,128)(2,1)S(1)}, bf16[128,1024]{1,0:T(8,128)(2,1)S(1)}, u32[]{:S(2)}, u32[]{:S(2)}) collective-permute-start(bf16[128,1024]{1,0:T(8,128)(2,1)S(1)} %get-tuple-element.74), channel_id=1, source_target_pairs={{0,48},{16,0},{32,16},{48,32},{1,49},{17,1},{33,17},{49,33},{2,50}... | collective-permute-start | bytes 786440 | tf_op jit(solution)/shard_map/ppermute | solution.py:458
  99.2 8.7 %collective-permute-start.22 = (bf16[128,1024]{1,0:T(8,128)(2,1)S(1)}, bf16[128,1024]{1,0:T(8,128)(2,1)S(1)}, u32[]{:S(2)}, u32[]{:S(2)}) collective-permute-start(bf16[128,1024]{1,0:T(8,128)(2,1)S(1)} %get-tuple-element.75), channel_id=1, source_target_pairs={{0,4},{4,8},{8,12},{12,0},{1,5},{5,9},{9,13},{13,1},{2,6},{6,10},{... | collective-permute-start | bytes 786440 | tf_op jit(solution)/shard_map/ppermute | solution.py:458
  99.8 8.1 %collective-permute-start.23 = (bf16[128,1024]{1,0:T(8,128)(2,1)S(1)}, bf16[128,1024]{1,0:T(8,128)(2,1)S(1)}, u32[]{:S(2)}, u32[]{:S(2)}) collective-permute-start(bf16[128,1024]{1,0:T(8,128)(2,1)S(1)} %get-tuple-element.76), channel_id=1, source_target_pairs={{0,12},{4,0},{8,4},{12,8},{1,13},{5,1},{9,5},{13,9},{2,14},{6,2},{... | collective-permute-start | bytes 786440 | tf_op jit(solution)/shard_map/ppermute | solution.py:458
  111.7 17.6 %collective-permute-start.24 = (bf16[256,1024]{1,0:T(8,128)(2,1)}, bf16[256,1024]{1,0:T(8,128)(2,1)}, u32[]{:S(2)}, u32[]{:S(2)}) collective-permute-start(bf16[256,1024]{1,0:T(8,128)(2,1)} %get-tuple-element.77), channel_id=1, source_target_pairs={{0,16},{16,32},{32,48},{48,0},{1,17},{17,33},{33,49},{49,1},{2,18}... | collective-permute-start | bytes 1572872 | tf_op jit(solution)/shard_map/ppermute | solution.py:458
  111.8 17.5 %collective-permute-start.25 = (bf16[256,1024]{1,0:T(8,128)(2,1)}, bf16[256,1024]{1,0:T(8,128)(2,1)}, u32[]{:S(2)}, u32[]{:S(2)}) collective-permute-start(bf16[256,1024]{1,0:T(8,128)(2,1)} %get-tuple-element.78), channel_id=1, source_target_pairs={{0,48},{16,0},{32,16},{48,32},{1,49},{17,1},{33,17},{49,33},{2,50}... | collective-permute-start | bytes 1572872 | tf_op jit(solution)/shard_map/ppermute | solution.py:458
  115.0 14.3 %collective-permute-start.26 = (bf16[256,1024]{1,0:T(8,128)(2,1)}, bf16[256,1024]{1,0:T(8,128)(2,1)}, u32[]{:S(2)}, u32[]{:S(2)}) collective-permute-start(bf16[256,1024]{1,0:T(8,128)(2,1)} %get-tuple-element.79), channel_id=1, source_target_pairs={{0,4},{4,8},{8,12},{12,0},{1,5},{5,9},{9,13},{13,1},{2,6},{6,10},{... | collective-permute-start | bytes 1572872 | tf_op jit(solution)/shard_map/ppermute | solution.py:458
  116.4 12.9 %collective-permute-start.27 = (bf16[256,1024]{1,0:T(8,128)(2,1)}, bf16[256,1024]{1,0:T(8,128)(2,1)}, u32[]{:S(2)}, u32[]{:S(2)}) collective-permute-start(bf16[256,1024]{1,0:T(8,128)(2,1)} %get-tuple-element.80), channel_id=1, source_target_pairs={{0,12},{4,0},{8,4},{12,8},{1,13},{5,1},{9,5},{13,9},{2,14},{6,2},{... | collective-permute-start | bytes 1572872 | tf_op jit(solution)/shard_map/ppermute | solution.py:458
  119.6 7.7 %collective-permute-start.10 = (bf16[32,4096]{1,0:T(8,128)(2,1)S(1)}, bf16[32,4096]{1,0:T(8,128)(2,1)S(1)}, u32[]{:S(2)}, u32[]{:S(2)}) collective-permute-start(bf16[32,4096]{1,0:T(8,128)(2,1)S(1)} %rms_back.1.refs_0_), channel_id=1, source_target_pairs={{0,1},{1,2},{2,3},{3,0},{4,5},{5,6},{6,7},{7,4},{8,9},{9,10},{10,1... | collective-permute-start | bytes 786440 | tf_op jit(solution)/shard_map/ppermute | solution.py:458
  127.3 6.4 %collective-permute-start.11 = (bf16[32,4096]{1,0:T(8,128)(2,1)S(1)}, bf16[32,4096]{1,0:T(8,128)(2,1)S(1)}, u32[]{:S(2)}, u32[]{:S(2)}) collective-permute-start(bf16[32,4096]{1,0:T(8,128)(2,1)S(1)} %rms_back.1.refs_0_), channel_id=1, source_target_pairs={{0,3},{1,0},{2,1},{3,2},{4,7},{5,4},{6,5},{7,6},{8,11},{9,8},{10,9... | collective-permute-start | bytes 786440 | tf_op jit(solution)/shard_map/ppermute | solution.py:458
  129.3 7.6 %collective-permute-start.12 = (bf16[32,4096]{1,0:T(8,128)(2,1)S(1)}, bf16[32,4096]{1,0:T(8,128)(2,1)S(1)}, u32[]{:S(2)}, u32[]{:S(2)}) collective-permute-start(bf16[32,4096]{1,0:T(8,128)(2,1)S(1)} %collective-permute-done.10.refs_1_), channel_id=1, source_target_pairs={{0,1},{1,2},{2,3},{3,0},{4,5},{5,6},{6,7},{7,4},{8,9},{9,10},{10,1... | collective-permute-start | bytes 786440 | tf_op jit(solution)/shard_map/ppermute | solution.py:458

commit v5 on v4

--- a/solution.py
+++ b/solution.py
@@ -27,6 +27,10 @@
 
 def total(value, axis):
     return jnp.sum(value.astype(F32), axis=axis, keepdims=True)
+
+
+def tn(left, right):
+    return lax.dot_general(left, right, (((0,), (0,)), ((), ())), preferred_element_type=F32)
 
 
 def in_hbm(value):
@@ -86,8 +90,8 @@
 def forward_kernel(
     x_hbm, gain_hbm, cot_hbm, a_hbm, b_hbm, keep_ref, send_ref, *rest
 ):
-    by_x, by_z = rest[:RING], rest[RING : 2 * RING]
-    x_ref, gain_ref, a_buf, b_buf, normed_ref, left_ref, in_sem, a_sem, b_sem, out_sem = rest[2 * RING :]
+    mine_hbm, other_hbm = rest[:2]
+    x_ref, gain_ref, a_buf, b_buf, normed_ref, left_ref, in_sem, a_sem, b_sem, out_sem = rest[2:]
     count, step, cols = a_buf.shape
     core = lax.axis_index("section")
     get_x = pltpu.make_async_copy(x_hbm, x_ref, in_sem.at[0])
@@ -133,11 +137,13 @@
             to = slice(j * block, (j + 1) * block)
             at_x = ((z + j) % RING * RING + (x + k) % RING) * block
             at_z = ((z + k) % RING * RING + (x + j) % RING) * block
-            for source, at, out in ((normed_ref, at_x, by_x[k]), (left_ref, at_z, by_z[k])):
+            at_mine = jnp.where(core == 0, at_x, at_z)
+            at_other = jnp.where(core == 0, at_z, at_x)
+            for source, at, out in ((left_ref, at_mine, mine_hbm), (normed_ref, at_other, other_hbm)):
                 copies.append(
                     pltpu.make_async_copy(
                         source.at[quarter, pl.ds(pl.multiple_of(at, block), block)],
-                        out.at[:, to],
+                        out.at[k, :, to],
                         out_sem.at[len(copies)],
                     )
                 )
@@ -179,11 +185,11 @@
     step = 512
     count = width // step
     half = jax.ShapeDtypeStruct((rows, cols), BF16)
-    outs = pl.pallas_call(
+    return pl.pallas_call(
         forward_kernel,
         in_specs=[HBM] * 5,
-        out_specs=[VMEM] * 2 + [HBM] * (2 * RING),
-        out_shape=[half] * 2 + [pltpu.HBM((QUARTER, cols), BF16)] * (2 * RING),
+        out_specs=[VMEM] * 2 + [HBM] * 2,
+        out_shape=[half] * 2 + [pltpu.HBM((RING, QUARTER, cols), BF16)] * 2,
         scratch_shapes=[pltpu.VMEM((rows, width), BF16), pltpu.VMEM((1, width), F32)]
         + [pltpu.VMEM((count, step, cols), BF16)] * 2
         + [pltpu.VMEM((rows, width), BF16)] * 2
@@ -194,10 +200,29 @@
         cost_estimate=cost(4 * rows * width * cols, 4 * width * cols),
         name="forward",
     )(in_hbm(x), in_hbm(gain), in_hbm(cot), in_hbm(weight_a), in_hbm(weight_b))
-    return outs[0], outs[1], outs[2 : 2 + RING], outs[2 + RING :]
-
-
-def pack_kernel(keep_ref, got_ref, src_ref, dest_ref, out_ref):
+
+
+def placed(places, refs, sems):
+    copies = [
+        pltpu.make_async_copy(refs[source].at[at], refs[out].at[to], sems.at[i])
+        for i, (source, at, out, to) in enumerate(places)
+    ]
+    for copy in copies:
+        copy.start()
+    return copies
+
+
+def wait_all(copies):
+    for copy in copies:
+        copy.wait()
+
+
+PAIRS = [(m, (k,), 2 + i, (m,)) for i, k in enumerate((0, 1, 3, 2)) for m in range(2)]
+STACK = [(p, (m,), RING, (m, p)) for p in range(RING) for m in range(2)]
+
+
+def pack_kernel(keep_ref, got_ref, src_ref, dest_ref, mine_ref, other_ref, out_ref, *rest):
+    copies = placed(PAIRS, (mine_ref, other_ref, *rest[:RING]), rest[RING])
     spread = slot_onehot(member_index(), src_ref, dest_ref)
 
     @pl.when(lax.axis_index("section") == 0)
@@ -208,23 +233,31 @@
     def _():
         out_ref[...] = jnp.dot(spread, got_ref[...], preferred_element_type=F32).astype(BF16)
 
-
-def pack(keep, got, src_len, dest):
+    wait_all(copies)
+
+
+def pack(keep, got, src_len, dest, mine, other):
     width = keep.shape[1]
-    return pl.pallas_call(
+    _, rows, cols = mine.shape
+    outs = pl.pallas_call(
         pack_kernel,
-        in_specs=[VMEM] * 4,
-        out_specs=VMEM,
-        out_shape=jax.ShapeDtypeStruct((SLOTS, width), BF16),
+        in_specs=[VMEM] * 4 + [HBM, ANY],
+        out_specs=[VMEM] + [HBM] * RING,
+        out_shape=[jax.ShapeDtypeStruct((SLOTS, width), BF16)]
+        + [pltpu.HBM((2, rows, cols), BF16)] * RING,
+        scratch_shapes=[pltpu.SemaphoreType.DMA((len(PAIRS),))],
         compiler_params=params(),
         cost_estimate=cost(2 * SLOTS * TOK * width, 2 * SLOTS * width),
         name="pack",
-    )(keep, got, src_len, dest)
+    )(keep, got, src_len, dest, in_hbm(mine), other)
+    return outs[0], outs[1:]
 
 
 def attend_kernel(
-    keep_ref, got_ref, slots_ref, src_ref, tgt_ref, dest_ref, front_ref, back_ref, own_ref
+    keep_ref, got_ref, slots_ref, src_ref, tgt_ref, dest_ref, *rest
 ):
+    front_ref, back_ref, stack_ref, own_ref, sems = rest[RING:]
+    copies = placed(STACK, (*rest[:RING], stack_ref), sems)
     mask = pair_mask(member_index(), src_ref, tgt_ref, dest_ref)
 
     @pl.when(lax.axis_index("section") == 0)
@@ -247,9 +280,6 @@
 
     def nt(left, right):
         return lax.dot_general(left, right, (((1,), (1,)), ((), ())), preferred_element_type=F32)
-
-    def tn(left, right):
-        return lax.dot_general(left, right, (((0,), (0,)), ((), ())), preferred_element_type=F32)
 
     def one(score, dweight):
         expo = jnp.where(mask, jnp.exp(score), 0.0)
@@ -274,40 +304,47 @@
         front_ref[:, second] = jnp.dot(weight, values, preferred_element_type=F32).astype(BF16)
         back_ref[:, first] = fold(tn(dscore, query))
         back_ref[:, second] = fold(tn(weight, dout))
-
-
-def attend(keep, got, slots, src_len, tgt_len, dest):
+    wait_all(copies)
+
+
+def attend(keep, got, slots, src_len, tgt_len, dest, pieces):
     rows, width = keep.shape
+    _, quarter, cols = pieces[0].shape
     return pl.pallas_call(
         attend_kernel,
-        in_specs=[VMEM] * 6,
-        out_specs=[VMEM] * 2,
+        in_specs=[VMEM] * 6 + [HBM] + [ANY] * (RING - 1),
+        out_specs=[VMEM] * 2 + [HBM],
         out_shape=[
             jax.ShapeDtypeStruct((rows, width), BF16),
             jax.ShapeDtypeStruct((SLOTS, width), BF16),
+            pltpu.HBM((2, RING, quarter, cols), BF16),
         ],
-        scratch_shapes=[pltpu.VMEM((rows, width), BF16)],
+        scratch_shapes=[pltpu.VMEM((rows, width), BF16), pltpu.SemaphoreType.DMA((len(STACK),))],
         compiler_params=params(),
         cost_estimate=cost(24 * rows * SLOTS * width, 8 * SLOTS * width),
         name="attend",
-    )(keep, got, slots, src_len, tgt_len, dest)
+    )(keep, got, slots, src_len, tgt_len, dest, in_hbm(pieces[0]), *pieces[1:])
 
 
 def unpack_kernel(back_ref, front_ref, src_ref, dest_ref, keep_ref, send_ref):
     spread = slot_onehot(member_index(), src_ref, dest_ref)
-    rows = lax.dot_general(
-        spread, back_ref[...], (((0,), (0,)), ((), ())), preferred_element_type=F32
-    ).astype(BF16)
-
-    @pl.when(lax.axis_index("section") == 0)
-    def _():
-        keep_ref[...] = rows
-        send_ref[...] = front_ref[...]
-
-    @pl.when(lax.axis_index("section") != 0)
-    def _():
-        keep_ref[...] = front_ref[...]
-        send_ref[...] = rows
+    rows = tn(spread, back_ref[...]).astype(BF16)
+    half = rows.shape[1] // 2
+    core = lax.axis_index("section")
+
+    @pl.when(core == 0)
+    def _():
+        keep_ref[:, :half] = rows[:, :half]
+        keep_ref[:, half:] = front_ref[:, :half]
+        send_ref[:, :half] = front_ref[:, half:]
+        send_ref[:, half:] = rows[:, half:]
+
+    @pl.when(core != 0)
+    def _():
+        keep_ref[:, :half] = front_ref[:, half:]
+        keep_ref[:, half:] = rows[:, half:]
+        send_ref[:, :half] = rows[:, :half]
+        send_ref[:, half:] = front_ref[:, :half]
 
 
 def unpack(back, front, src_len, dest):
@@ -324,78 +361,84 @@
     )(back, front, src_len, dest)
 
 
-def join_kernel(keep_ref, got_ref, first_ref, second_ref):
-    half = keep_ref.shape[1] // 2
-    mine = pl.multiple_of(lax.axis_index("section") * half, half)
-    other = pl.multiple_of((1 - lax.axis_index("section")) * half, half)
-    first_ref[:, pl.ds(mine, half)] = keep_ref[:, :half]
-    first_ref[:, pl.ds(other, half)] = got_ref[:, :half]
-    second_ref[:, pl.ds(mine, half)] = keep_ref[:, half:]
-    second_ref[:, pl.ds(other, half)] = got_ref[:, half:]
+def join_kernel(keep_ref, got_ref, rows_ref, other_ref):
+    width = keep_ref.shape[1]
+    half = width // 2
+    core = lax.axis_index("section")
+    mine = pl.multiple_of(core * half, half)
+    theirs = pl.multiple_of((1 - core) * half, half)
+    for ref, at in ((keep_ref, mine), (got_ref, theirs)):
+        rows_ref[:, pl.ds(at, half)] = ref[:, :half]
+        rows_ref[:, pl.ds(pl.multiple_of(width + at, half), half)] = ref[:, half:]
+        other_ref[:, pl.ds(at, half)] = ref[:, half:]
 
 
 def join(keep, got):
-    shape = jax.ShapeDtypeStruct(keep.shape, BF16)
+    rows, width = keep.shape
     return pl.pallas_call(
         join_kernel,
         in_specs=[VMEM, VMEM],
         out_specs=[VMEM] * 2,
-        out_shape=[shape, shape],
+        out_shape=[
+            jax.ShapeDtypeStruct((rows, 2 * width), BF16),
+            jax.ShapeDtypeStruct((rows, width), BF16),
+        ],
         compiler_params=params(),
         cost_estimate=cost(0, 8 * keep.size),
         name="join",
     )(keep, got)
 
 
-def dnorm_kernel(first_ref, second_ref, a_hbm, b_hbm, out_ref, a_buf, b_buf, a_sem, b_sem):
-    count, step, _ = a_buf.shape
-    source = lax.axis_index("section") == 0
+def dnorm_kernel(rows_ref, got_ref, a_hbm, b_hbm, out_ref, a_buf, b_buf, a_sem, b_sem):
+    count, step, cols = a_buf.shape
+    core = lax.axis_index("section")
 
     def nt(left, right):
         return lax.dot_general(left, right, (((1,), (1,)), ((), ())), preferred_element_type=F32)
 
-    def fetch(k):
-        rows = pl.ds(k * step, step)
-        return (
-            pltpu.make_async_copy(a_hbm.at[rows, :], a_buf.at[k], a_sem.at[k]),
-            pltpu.make_async_copy(b_hbm.at[rows, :], b_buf.at[k], b_sem.at[k]),
-        )
-
-    for k in range(count):
-        for copy in fetch(k):
-            copy.start()
-    for k in range(count):
-        at = slice(k * step, (k + 1) * step)
-        for copy in fetch(k):
-            copy.wait()
-
-        @pl.when(source)
-        def _(k=k, at=at):
-            out_ref[:, at] = (
-                nt(first_ref[...], a_buf[k]) + nt(second_ref[...], b_buf[k])
-            ).astype(BF16)
-
-        @pl.when(jnp.logical_not(source))
-        def _(k=k, at=at):
-            out_ref[:, at] = nt(first_ref[...], a_buf[k]).astype(BF16)
-
-
-def dnorm_partial(first, second, weight_a, weight_b):
-    rows, cols = first.shape
-    width = weight_a.shape[0]
+    def fetches(hbm, buf, sem):
+        return [
+            pltpu.make_async_copy(hbm.at[pl.ds(k * step, step), :], buf.at[k], sem.at[k])
+            for k in range(count)
+        ]
+
+    get_a, get_b = fetches(a_hbm, a_buf, a_sem), fetches(b_hbm, b_buf, b_sem)
+
+    @pl.when(core == 0)
+    def _():
+        for k in range(count):
+            get_a[k].start()
+            get_b[k].start()
+        for k in range(count):
+            get_a[k].wait()
+            get_b[k].wait()
+            block = nt(rows_ref[:, :cols], a_buf[k]) + nt(got_ref[...], b_buf[k])
+            out_ref[:, k * step : (k + 1) * step] = block.astype(BF16)
+
+    @pl.when(core != 0)
+    def _():
+        for k in range(count):
+            get_a[k].start()
+        for k in range(count):
+            get_a[k].wait()
+            out_ref[:, k * step : (k + 1) * step] = nt(got_ref[...], a_buf[k]).astype(BF16)
+
+
+def dnorm_partial(rows, got, weight_a, weight_b):
+    width, cols = weight_a.shape
     step = 512
     count = width // step
     return pl.pallas_call(
         dnorm_kernel,
         in_specs=[VMEM] * 2 + [HBM] * 2,
         out_specs=VMEM,
-        out_shape=jax.ShapeDtypeStruct((rows, width), BF16),
+        out_shape=jax.ShapeDtypeStruct((TOK, width), BF16),
         scratch_shapes=[pltpu.VMEM((count, step, cols), BF16)] * 2
         + [pltpu.SemaphoreType.DMA((count,))] * 2,
         compiler_params=params(24),
-        cost_estimate=cost(4 * rows * width * cols, 4 * width * cols),
+        cost_estimate=cost(4 * TOK * width * cols, 4 * width * cols),
         name="dnorm",
-    )(first, second, in_hbm(weight_a), in_hbm(weight_b))
+    )(rows, got, in_hbm(weight_a), in_hbm(weight_b))
 
 
 def rms_back_kernel(x_hbm, gain_ref, parts_ref, out_ref, x_ref, sem):
@@ -463,46 +506,25 @@
     return [block, left, shift(block, axis, 3), shift(left, axis, 1)]
 
 
-def spread(block, axis):
-    far = shift(block, axis, 2)
-    return [block, shift(block, axis, 1), shift(block, axis, 3), far]
-
-
-def exchanged(slices, axis):
-    far = shift(slices[2], axis, 2)
-    return [slices[0], shift(slices[1], axis, 1), shift(slices[3], axis, 3), far]
-
-
-def stack_kernel(*refs):
-    pieces, (out_hbm, sems) = refs[:-2], refs[-2:]
-    rows = pieces[0].shape[0]
-    copies = [
-        pltpu.make_async_copy(piece, out_hbm.at[pl.ds(i * rows, rows), :], sems.at[i])
-        for i, piece in enumerate(pieces)
-    ]
-    for copy in copies:
-        copy.start()
-    for copy in copies:
-        copy.wait()
-
-
-def stacked(pieces):
-    rows, cols = pieces[0].shape
-    count = len(pieces)
-    return pl.pallas_call(
-        stack_kernel,
-        in_specs=[ANY] * count,
-        out_specs=HBM,
-        out_shape=pltpu.HBM((count * rows, cols), BF16),
-        scratch_shapes=[pltpu.SemaphoreType.DMA((count,))],
-        compiler_params=params(),
-        cost_estimate=cost(0, 4 * count * rows * cols),
-        name="stack",
-    )(*pieces)
-
-
-def tn(left, right):
-    return lax.dot_general(left, right, (((0,), (0,)), ((), ())), preferred_element_type=F32)
+def moved(value, k, along, across=False):
+    pairs = []
+    for core in range(2):
+        for z in range(RING):
+            for x in range(RING):
+                to = {"z": z, "x": x}
+                to[along[core]] = (to[along[core]] + k) % RING
+                target = (1 - core if across else core, to["z"], to["x"])
+                pairs.append(
+                    ((core * RING + z) * RING + x, (target[0] * RING + target[1]) * RING + target[2])
+                )
+    return lax.ppermute(value, ("section", "z", "x"), pairs)
+
+
+GATHER, REDUCE = "xz", "zx"
+
+
+def fetched(own, others):
+    return [own] + [moved(others[k], k, GATHER) for k in (1, 3, 2)]
 
 
 def left_loads(lefts, buf, sems, ks):
@@ -535,162 +557,196 @@
     return value.reshape(RING * TOK, value.shape[-1])
 
 
-def wait_all(copies):
-    for copy in copies:
-        copy.wait()
-
-
 def far_kernel(*refs):
-    lefts, pieces, outs = refs[:RING], refs[RING : 3 * RING], refs[3 * RING : 3 * RING + 4]
-    rows_refs, (buf, sems, row_sems) = refs[3 * RING + 4 : 3 * RING + 6], refs[3 * RING + 6 :]
+    lefts, pieces = refs[:RING], refs[RING : 2 * RING]
+    top_ref, low_ref, rows_ref, buf, sems, row_sems = refs[2 * RING :]
     gets = [
-        pltpu.make_async_copy(
-            piece, rows_refs[i // RING].at[pl.ds(i % RING * TOK, TOK), :], row_sems.at[i]
-        )
+        pltpu.make_async_copy(piece, rows_ref.at[pl.ds(i * TOK, TOK), :], row_sems.at[i])
         for i, piece in enumerate(pieces)
     ]
     for get in gets:
         get.start()
     loads = left_loads(lefts, buf, sems, (2,))
-    half = outs[0].shape[0]
-    for f in range(2):
-        wait_all(gets[f * RING : (f + 1) * RING])
-        wait_all(loads[f][0])
-        block = tn(flat(buf[f, 0]), rows_refs[f][...]).astype(BF16)
-        outs[2 * f][...] = block[:half]
-        outs[2 * f + 1][...] = block[half:]
-
-
-def far_blocks(lefts, pieces_a, pieces_b):
-    rows, cols = pieces_a[0].shape
+    wait_all(gets)
+    half, cols = top_ref.shape[0], top_ref.shape[1] // 2
+    for m in range(2):
+        at = slice(m * cols, (m + 1) * cols)
+        wait_all(loads[m][0])
+        block = tn(flat(buf[m, 0]), rows_ref[:, at]).astype(BF16)
+        top_ref[:, at] = block[:half]
+        low_ref[:, at] = block[half:]
+
+
+def far_block(lefts, pieces):
+    rows, cols = pieces[0].shape
     block = lefts[0].shape[-1] // RING
     half = jax.ShapeDtypeStruct((block // 2, cols), BF16)
-    tall = jax.ShapeDtypeStruct((RING * rows, cols), BF16)
     return pl.pallas_call(
         far_kernel,
-        in_specs=[HBM] * (3 * RING),
-        out_specs=[VMEM] * 6,
-        out_shape=[half] * 4 + [tall] * 2,
-        scratch_shapes=left_scratch(block, 1) + [pltpu.SemaphoreType.DMA((2 * RING,))],
+        in_specs=[HBM] * (2 * RING),
+        out_specs=[VMEM] * 3,
+        out_shape=[half, half, jax.ShapeDtypeStruct((RING * rows, cols), BF16)],
+        scratch_shapes=left_scratch(block, 1) + [pltpu.SemaphoreType.DMA((RING,))],
         compiler_params=params(),
-        cost_estimate=cost(4 * RING * rows * block * cols, 16 * RING * rows * cols),
+        cost_estimate=cost(2 * RING * rows * block * cols, 8 * RING * rows * cols),
         name="far",
-    )(*[in_hbm(value) for value in (*lefts, *pieces_a, *pieces_b)])
+    )(*[in_hbm(value) for value in (*lefts, *pieces)])
 
 
 def side_kernel(*refs):
-    lefts, rows_refs, near, outs = refs[:RING], refs[RING : RING + 2], refs[RING + 2 : RING + 6], refs[RING + 6 : RING + 10]
-    buf, sems = refs[RING + 10 :]
-    loads = left_loads(lefts, buf, sems, (1, 3))
-    half = near[0].shape[0]
-    for f in range(2):
-        from_left, from_right = near[2 * f : 2 * f + 2]
-        to_right, to_left = outs[2 * f : 2 * f + 2]
-        wait_all(loads[f][0])
-        block = tn(flat(buf[f, 0]), rows_refs[f][...])
-        to_right[:half, :] = (block[:half] + from_left[...].astype(F32)).astype(BF16)
-        to_right[half:, :] = block[half:].astype(BF16)
-        wait_all(loads[f][1])
-        block = tn(flat(buf[f, 1]), rows_refs[f][...])
-        to_left[:half, :] = block[:half].astype(BF16)
-        to_left[half:, :] = (block[half:] + from_right[...].astype(F32)).astype(BF16)
-
-
-def side_blocks(lefts, rows, near):
-    depth, cols = rows[0].shape
+    lefts, (rows_ref, from_left, from_right) = refs[:RING], refs[RING : RING + 3]
+    rights, to_lefts, other_ref, buf, sems = refs[RING + 3 : RING + 5], refs[RING + 5 : RING + 7], *refs[RING + 7 :]
+    loads = left_loads(lefts, buf, sems, (1, 3, 0))
+    half, cols = from_left.shape[0], other_ref.shape[1]
+    for m in range(2):
+        at = slice(m * cols, (m + 1) * cols)
+
+        def product(i, m=m, at=at):
+            wait_all(loads[m][i])
+            return tn(flat(buf[m, i]), rows_ref[:, at])
+
+        block = product(0)
+        rights[m][:half, :] = (block[:half] + from_left[:, at].astype(F32)).astype(BF16)
+        rights[m][half:, :] = block[half:].astype(BF16)
+        block = product(1)
+        to_lefts[m][:half, :] = block[:half].astype(BF16)
+        to_lefts[m][half:, :] = (block[half:] + from_right[:, at].astype(F32)).astype(BF16)
+    wait_all(loads[0][2])
+    wait_all(loads[1][2])
+    other_ref[...] = tn(flat(buf[1, 2]), rows_ref[:, cols:]).astype(BF16)
+
+
+def side_blocks(lefts, rows, from_left, from_right):
+    depth, cols = rows.shape
     block = lefts[0].shape[-1] // RING
-    shape = jax.ShapeDtypeStruct((block, cols), BF16)
+    shape = jax.ShapeDtypeStruct((block, cols // 2), BF16)
     return pl.pallas_call(
         side_kernel,
-        in_specs=[HBM] * RING + [VMEM] * 6,
-        out_specs=[VMEM] * 4,
-        out_shape=[shape] * 4,
-        scratch_shapes=left_scratch(block, 2),
-        compiler_params=params(),
-        cost_estimate=cost(8 * depth * block * cols, 8 * depth * cols),
+        in_specs=[HBM] * RING + [VMEM] * 3,
+        out_specs=[VMEM] * 5,
+        out_shape=[shape] * 5,
+        scratch_shapes=left_scratch(block, 3),
+        compiler_params=params(16),
+        cost_estimate=cost(5 * depth * block * cols, 4 * depth * cols),
         name="side",
-    )(*[in_hbm(left) for left in lefts], *rows, *near)
+    )(*[in_hbm(left) for left in lefts], rows, from_left, from_right)
 
 
 def own_kernel(*refs):
-    lefts, rows_refs, parts, outs = refs[:RING], refs[RING : RING + 2], refs[RING + 2 : RING + 6], refs[RING + 6 : RING + 8]
+    lefts, rows_ref, parts, outs = refs[:RING], refs[RING], refs[RING + 1 : RING + 6], refs[RING + 6 : RING + 8]
     buf, sems, part_buf, part_sems, out_buf, out_sems = refs[RING + 8 :]
-    gets = [pltpu.make_async_copy(parts[i], part_buf.at[i], part_sems.at[i]) for i in range(4)]
+    gets = [pltpu.make_async_copy(parts[i], part_buf.at[i], part_sems.at[i]) for i in range(5)]
     for get in gets:
         get.start()
-    loads = left_loads(lefts, buf, sems, (0,))
+    mine = lax.axis_index("mp")
+    loads = []
+    for j, (left, distance) in enumerate(zip(lefts, ORDER, strict=True)):
+        at = pl.multiple_of((mine + distance) % RING * QUARTER, QUARTER)
+        loads.append(
+            pltpu.make_async_copy(
+                left.at[0, :, :, pl.ds(0, buf.shape[-1])],
+                buf.at[:, pl.ds(at, QUARTER), :],
+                sems.at[j],
+            )
+        )
+        loads[-1].start()
+    core = lax.axis_index("section")
     chunks = out_sems.shape[1]
-    puts = []
-    for f in range(2):
-        wait_all(loads[f][0])
-        block = tn(flat(buf[f, 0]), rows_refs[f][...])
-        wait_all(gets[2 * f : 2 * f + 2])
-        size = block.shape[0] // chunks
+    size = out_buf.shape[1] // chunks
+
+    def put(m, c, out):
+        at = slice(c * size, (c + 1) * size)
+        return pltpu.make_async_copy(out_buf.at[m, at], out.at[at], out_sems.at[m, c])
+
+    def write(m, c):
+        @pl.when(core == m)
+        def _():
+            put(m, c, outs[0]).start()
+
+        @pl.when(core != m)
+        def _():
+            put(m, c, outs[1]).start()
+
+    wait_all(loads)
+    block = tn(flat(buf[...]), rows_ref[:, : out_buf.shape[2]])
+    wait_all(gets[:2])
+    for c in range(chunks):
+        at = slice(c * size, (c + 1) * size)
+        out_buf[0, at] = block[at] + part_buf[0, at].astype(F32) + part_buf[1, at].astype(F32)
+        write(0, c)
+    wait_all(gets[2:])
+    for c in range(chunks):
+        at = slice(c * size, (c + 1) * size)
+        out_buf[1, at] = (
+            part_buf[4, at].astype(F32) + part_buf[2, at].astype(F32) + part_buf[3, at].astype(F32)
+        )
+        write(1, c)
+    for m in range(2):
         for c in range(chunks):
-            at = slice(c * size, (c + 1) * size)
-            out_buf[f, at] = (
-                block[at] + part_buf[2 * f, at].astype(F32) + part_buf[2 * f + 1, at].astype(F32)
-            )
-            put = pltpu.make_async_copy(out_buf.at[f, at], outs[f].at[at], out_sems.at[f, c])
-            put.start()
-            puts.append(put)
-    wait_all(puts)
+            put(m, c, outs[0]).wait()
 
 
 def own_blocks(lefts, rows, parts):
-    depth, cols = rows[0].shape
+    depth, cols = rows.shape
+    cols = cols // 2
     block = lefts[0].shape[-1] // RING
     return pl.pallas_call(
         own_kernel,
-        in_specs=[HBM] * RING + [VMEM] * 2 + [ANY] * 4,
+        in_specs=[HBM] * RING + [VMEM] + [ANY] * 5,
         out_specs=[HBM] * 2,
         out_shape=[pltpu.HBM((block, cols), F32)] * 2,
-        scratch_shapes=left_scratch(block, 1)
-        + [pltpu.VMEM((4, block, cols), BF16), pltpu.SemaphoreType.DMA((4,))]
+        scratch_shapes=[pltpu.VMEM((RING, TOK, block), BF16), pltpu.SemaphoreType.DMA((RING,))]
+        + [pltpu.VMEM((5, block, cols), BF16), pltpu.SemaphoreType.DMA((5,))]
         + [pltpu.VMEM((2, block, cols), F32), pltpu.SemaphoreType.DMA((2, 4))],
-        compiler_params=params(),
-        cost_estimate=cost(4 * depth * block * cols, 16 * depth * cols),
+        compiler_params=params(16),
+        cost_estimate=cost(2 * depth * block * cols, 16 * depth * cols),
         name="own",
-    )(*[in_hbm(left) for left in lefts], *rows, *parts)
+    )(*[in_hbm(left) for left in lefts], rows, *parts)
 
 
 def per_device(states, gains, proj_a, proj_b, cotangent, src_len, tgt_len, dest):
     weight_a = proj_a[0]
     weight_b = proj_b[0]
     rows = states[0]
-    keep, send, by_x, by_z = forward(rows, gains, cotangent, weight_a, weight_b)
+    keep, send, mine, other = forward(rows, gains, cotangent, weight_a, weight_b)
     swap = [(0, 1), (1, 0)]
     got = lax.ppermute(send, "section", swap)
-    slots = pack(keep, got, src_len, dest)
+    slots, slices = pack(keep, got, src_len, dest, mine, lax.ppermute(other, "section", swap))
     width = slots.shape[1]
     slots = slots.reshape(SEQ_DEV, MAXLEN, width)
     slots = lax.all_to_all(slots, ("z", "x"), split_axis=0, concat_axis=0, tiled=True)
     slots = slots.reshape(SLOTS, width)
-    pieces = exchanged(by_x, "x") + exchanged(by_z, "z")
-    slots, pieces = lax.optimization_barrier((slots, pieces))
-    pieces[0], pieces[RING] = in_hbm(pieces[0]), in_hbm(pieces[RING])
-    lefts = gathered(stacked(pieces).reshape(2, RING, QUARTER, width), "mp")
-    front, back = attend(keep, got, slots, src_len, tgt_len, dest)
+    pieces = fetched(slices[0], {1: slices[1], 3: slices[2], 2: slices[3]})
+    front, back, own = attend(keep, got, slots, src_len, tgt_len, dest, pieces)
+    lefts = gathered(own, "mp")
     back = back.reshape(SEQ_DEV, MAXLEN, width)
     back = lax.all_to_all(back, ("z", "x"), split_axis=0, concat_axis=0, tiled=True)
     keep, send = unpack(back.reshape(SLOTS, width), front, src_len, dest)
     got = lax.ppermute(send, "section", swap)
-    got, lefts[1], lefts[2] = lax.optimization_barrier((got, lefts[1], lefts[2]))
-    first, second = join(keep, got)
-
-    rights_a, rights_b = spread(first, "x"), spread(second, "z")
-    partial = dnorm_partial(first, second, weight_a, weight_b)
+    kind, others = join(keep, got)
+
+    rights = fetched(kind, {k: kind for k in (1, 2, 3)})
+    others = lax.ppermute(others, "section", swap)
+    others, lefts[1], lefts[2] = lax.optimization_barrier((others, lefts[1], lefts[2]))
+    partial = dnorm_partial(kind, others, weight_a, weight_b)
+    partial, rights[1], rights[2] = lax.optimization_barrier((partial, rights[1], rights[2]))
     parts = lax.all_to_all(
         partial.reshape(RING, TOK // RING, -1), "mp", split_axis=0, concat_axis=0, tiled=True
     )
     quarter = rms_back(rows, gains, parts)
     grad_states = place(gathered(quarter, "mp"))
 
-    outs = far_blocks(lefts, rights_a, rights_b)
-    near = [shift(out, axis, k) for out, axis, k in zip(outs[:4], "zzxx", (1, 3, 1, 3), strict=True)]
-    sides = side_blocks(lefts, outs[4:], near)
-    sides = [shift(out, axis, k) for out, axis, k in zip(sides, "zzxx", (1, 3, 1, 3), strict=True)]
-    grad_a, grad_b = own_blocks(lefts, outs[4:], sides)
+    top, low, stack = far_block(lefts, rights)
+    from_left, from_right = moved(top, 1, REDUCE), moved(low, 3, REDUCE)
+    right, right_other, left, left_other, own_other = side_blocks(lefts, stack, from_left, from_right)
+    sums = [
+        moved(right, 1, REDUCE),
+        moved(left, 3, REDUCE),
+        moved(right_other, 1, REDUCE, True),
+        moved(left_other, 3, REDUCE, True),
+        lax.ppermute(own_other, "section", swap),
+    ]
+    grad_a, grad_b = own_blocks(lefts, stack, sums)
     return (grad_states[None], grad_a[None], grad_b[None])
 
 

time: 139 us -> 133 us (0.957)
  starting transfers between devices: 63.7 us -> 42.9 us
  Pallas kernels: 40.4 us -> 48.1 us
  waiting for transfers between devices: 32.8 us -> 39.5 us
    ppermute x26 -> x6, starting transfers between devices: 46 us -> 8.26 us  [shift(): return lax.ppermute(value, axis, [(i, (i + k) % RING) for i in range(RING)])]
    ppermute x26 -> x6, waiting for transfers between devices: 29.2 us -> 1.99 us  [shift(): return lax.ppermute(value, axis, [(i, (i + k) % RING) for i in range(RING)])]
    ppermute x0 -> x15, waiting for transfers between devices: none -> 19 us  [the longest x12 18.4 us: moved(): return lax.ppermute(value, ('section', 'z', 'x'), pairs)]
    ppermute x0 -> x15, starting transfers between devices: none -> 16.6 us  [the longest x12 15.1 us: moved(): return lax.ppermute(value, ('section', 'z', 'x'), pairs)]
    all_to_all x1, waiting for transfers between devices: 0.01 us -> 7.78 us  [per_device(): lax.all_to_all(partial.reshape(RING, TOK // RING, -1), 'mp', split_axis=0...]
    pallas_call x6 -> x5, Pallas kernels: 19.5 us -> 27.1 us  [the longest x1 9.91 us: pack(): pl.pallas_call(pack_kernel, in_specs=[VMEM] * 4 + [HBM, ANY], out_specs=[...]
    all_to_all x1, waiting for transfers between devices: 2.12 us -> 8.17 us  [per_device(): lax.all_to_all(back, ('z', 'x'), split_axis=0, concat_axis=0, tiled=True)]
  transfers between devices with their start and end apart: 31 -> 26, of which waited for: 10 -> 11; matrix products, arithmetic and copies ran while one was open for 0% -> 0% of each run, Pallas kernels for 19% -> 17%
where the time goes in v5:
time: 133 us; the launch traced here: 132 us
  Pallas kernels  48.1 us (36%)
  starting transfers between devices  42.9 us (32%)
  waiting for transfers between devices  39.5 us (30%)
    ppermute x12, waiting for transfers between devices, moved(): return lax.ppermute(value, ('section', 'z', 'x'), pairs)  18.4 us
    ppermute x12, starting transfers between devices, moved(): return lax.ppermute(value, ('section', 'z', 'x'), pairs)  15.1 us
    pallas_call x1, Pallas kernels, pack(): pl.pallas_call(pack_kernel, in_specs=[VMEM] * 4 + [HBM, ANY], out_specs=[...  9.91 us
    pallas_call x1, Pallas kernels, dnorm_partial(): pl.pallas_call(dnorm_kernel, in_specs=[VMEM] * 2 + [HBM] * 2, out_specs=V...  9.32 us
    pallas_call x1, Pallas kernels, forward(): pl.pallas_call(forward_kernel, in_specs=[HBM] * 5, out_specs=[VMEM] * 2 +...  8.98 us
    all_to_all x1, starting transfers between devices, per_device(): lax.all_to_all(slots, ('z', 'x'), split_axis=0, concat_axis=0, tiled=True)  8.37 us
    ppermute x6, starting transfers between devices, shift(): return lax.ppermute(value, axis, [(i, (i + k) % RING) for i in range(RING)])  8.26 us
    all_to_all x1, waiting for transfers between devices, per_device(): lax.all_to_all(back, ('z', 'x'), split_axis=0, concat_axis=0, tiled=True)  8.17 us
  transfers between devices with their start and end apart: 26, of which 11 were waited for; matrix products, arithmetic and copies ran while one was open for 0% of the time, Pallas kernels for 17%

profile of v5, /device:TPU:0, one launch (start us, length us, event | category | flops | bytes accessed | tf_op | source)
XLA Modules:
  0.0 132.3 jit_solution(4739398065095024371)
XLA Ops:
  0.7 9.0 %forward.1 = (bf16[128,1024]{1,0:T(8,128)(2,1)S(1)}, bf16[128,1024]{1,0:T(8,128)(2,1)S(1)}, bf16[4,32,1024]{2,1,0:T(8,128)(2,1)}, bf16[4,32,1024]{2,1,0:T(8,128)(2,1)}) custom-call(bf16[128,4096]{1,0:T(8,128)(2,1)} %bitcast.17, f32[1,4096]{1,0:T(1,128)} %gain_ref.1, bf16[128,4096]{1,0:T(8,128)(2,1)} %cot_hbm.1, bf16[4096,1024]{1,0:T(8,128)(2,1)} %bitcast.13, ...), custom_call_target="tpu_custom_call" | custom-call | flops 2147483648 | bytes 16777216 | tf_op jit(solution)/shard_map/forward/pallas_call | solution.py:188
  9.6 0.1 collective-permute-start
  9.8 0.5 collective-permute-start.1
  10.2 1.0 collective-permute-done.got_ref
  11.3 0.6 collective-permute-done.1.other_ref
  11.9 9.9 %pack.1 = (bf16[256,1024]{1,0:T(8,128)(2,1)}, bf16[2,32,1024]{2,1,0:T(8,128)(2,1)}, bf16[2,32,1024]{2,1,0:T(8,128)(2,1)}, bf16[2,32,1024]{2,1,0:T(8,128)(2,1)}, bf16[2,32,1024]{2,1,0:T(8,128)(2,1)}) custom-call(bf16[128,1024]{1,0:T(8,128)(2,1)S(1)} %get-tuple-element.35.keep_ref, bf16[128,1024]{1,0:T(8,128)(2,1)S(1)} %collective-permute-done.got_ref, ...), custom_call_target="tpu_custom_call" | custom-call | flops 67108864 | bytes 524288 | tf_op jit(solution)/shard_map/pack/pallas_call | solution.py:242
  21.8 8.4 %all-to-all-start = ((bf16[16,16,1024]{2,1,0:T(8,128)(2,1)}), bf16[16,16,1024]{2,1,0:T(8,128)(2,1)S(1)}, u32[]{:S(2)}, u32[]{:S(2)}) async-start(bf16[16,16,1024]{2,1,0:T(8,128)(2,1)} %bitcast.3), calls=%async_computation | async-start | bytes 1048576 | tf_op jit(solution)/shard_map/all_to_all | solution.py:717
  30.1 1.9 %collective-permute-start.2 = (bf16[2,32,1024]{2,1,0:T(8,128)(2,1)}, bf16[2,32,1024]{2,1,0:T(8,128)(2,1)S(1)}, u32[]{:S(2)}, u32[]{:S(2)}) collective-permute-start(bf16[2,32,1024]{2,1,0:T(8,128)(2,1)} %get-tuple-element.41), channel_id=1, source_target_pairs={{0,4},{4,8},{8,12},{12,0},{16,20},{20,24},{24,28},{28,16},{32,36},... | collective-permute-start | bytes 393224 | tf_op jit(solution)/shard_map/ppermute | solution.py:520
  32.1 1.4 %collective-permute-start.3 = (bf16[2,32,1024]{2,1,0:T(8,128)(2,1)}, bf16[2,32,1024]{2,1,0:T(8,128)(2,1)S(1)}, u32[]{:S(2)}, u32[]{:S(2)}) collective-permute-start(bf16[2,32,1024]{2,1,0:T(8,128)(2,1)} %get-tuple-element.42), channel_id=1, source_target_pairs={{0,12},{4,0},{8,4},{12,8},{16,28},{20,16},{24,20},{28,24},{32,44},... | collective-permute-start | bytes 393224 | tf_op jit(solution)/shard_map/ppermute | solution.py:520
  33.5 2.2 %collective-permute-start.4 = (bf16[2,32,1024]{2,1,0:T(8,128)(2,1)}, bf16[2,32,1024]{2,1,0:T(8,128)(2,1)S(1)}, u32[]{:S(2)}, u32[]{:S(2)}) collective-permute-start(bf16[2,32,1024]{2,1,0:T(8,128)(2,1)} %get-tuple-element.43), channel_id=1, source_target_pairs={{0,8},{4,12},{8,0},{12,4},{16,24},{20,28},{24,16},{28,20},{32,40},... | collective-permute-start | bytes 393224 | tf_op jit(solution)/shard_map/ppermute | solution.py:520
  35.6 5.6 %collective-permute-done.2.rest_1_ = bf16[2,32,1024]{2,1,0:T(8,128)(2,1)S(1)} collective-permute-done((bf16[2,32,1024]{2,1,0:T(8,128)(2,1)}, bf16[2,32,1024]{2,1,0:T(8,128)(2,1)S(1)}, u32[]{:S(2)}, u32[]{:S(2)}) %collective-permute-start.2) | collective-permute-done | bytes 131104 | tf_op jit(solution)/shard_map/ppermute | solution.py:520
  41.2 1.7 %collective-permute-done.4.rest_3_ = bf16[2,32,1024]{2,1,0:T(8,128)(2,1)S(1)} collective-permute-done((bf16[2,32,1024]{2,1,0:T(8,128)(2,1)}, bf16[2,32,1024]{2,1,0:T(8,128)(2,1)S(1)}, u32[]{:S(2)}, u32[]{:S(2)}) %collective-permute-start.4) | collective-permute-done | bytes 131104 | tf_op jit(solution)/shard_map/ppermute | solution.py:520
  42.9 0.0 all-to-all-done
  42.9 5.9 %attend.1 = (bf16[128,1024]{1,0:T(8,128)(2,1)S(1)}, bf16[256,1024]{1,0:T(8,128)(2,1)}, bf16[2,4,32,1024]{3,2,1,0:T(8,128)(2,1)}) custom-call(bf16[128,1024]{1,0:T(8,128)(2,1)S(1)} %get-tuple-element.35.keep_ref, bf16[128,1024]{1,0:T(8,128)(2,1)S(1)} %collective-permute-done.got_ref, bf16[256,1024]{1,0:T(8,128)(2,1)S(1)} %bitcast.12, s32[16,16]{1,0:T(8,128)S(1)} %copy-done.2, ...), custom_call_target="tpu_custom_call" | custom-call | flops 805306368 | bytes 2097152 | tf_op jit(solution)/shard_map/attend/pallas_call | solution.py:313
  48.9 5.0 %all-to-all-start.1 = ((bf16[16,16,1024]{2,1,0:T(8,128)(2,1)}), bf16[16,16,1024]{2,1,0:T(8,128)(2,1)S(1)}, u32[]{:S(2)}, u32[]{:S(2)}) async-start(bf16[16,16,1024]{2,1,0:T(8,128)(2,1)} %bitcast.5), calls=%async_computation.1 | async-start | bytes 1048576 | tf_op jit(solution)/shard_map/all_to_all | solution.py:723
  53.8 1.6 %collective-permute-start.7 = (bf16[2,4,32,1024]{3,2,1,0:T(8,128)(2,1)}, bf16[2,4,32,1024]{3,2,1,0:T(8,128)(2,1)S(1)}, u32[]{:S(2)}, u32[]{:S(2)}) collective-permute-start(bf16[2,4,32,1024]{3,2,1,0:T(8,128)(2,1)} %get-tuple-element.50.refs_0_), channel_id=1, source_target_pairs={{0,1},{1,2},{2,3},{3,0},{4,5},{5,6},{6,7},{7,4},{8,9},{9,10},{10,1... | collective-permute-start | bytes 1572872 | tf_op jit(solution)/shard_map/ppermute | solution.py:501
  55.5 1.7 %collective-permute-start.8 = (bf16[2,4,32,1024]{3,2,1,0:T(8,128)(2,1)}, bf16[2,4,32,1024]{3,2,1,0:T(8,128)(2,1)S(1)}, u32[]{:S(2)}, u32[]{:S(2)}) collective-permute-start(bf16[2,4,32,1024]{3,2,1,0:T(8,128)(2,1)} %get-tuple-element.50.refs_0_), channel_id=1, source_target_pairs={{0,3},{1,0},{2,1},{3,2},{4,7},{5,4},{6,5},{7,6},{8,11},{9,8},{10,9... | collective-permute-start | bytes 1572872 | tf_op jit(solution)/shard_map/ppermute | solution.py:501
  57.1 8.2 %all-to-all-done.1 = bf16[16,16,1024]{2,1,0:T(8,128)(2,1)S(1)} async-done(((bf16[16,16,1024]{2,1,0:T(8,128)(2,1)}), bf16[16,16,1024]{2,1,0:T(8,128)(2,1)S(1)}, u32[]{:S(2)}, u32[]{:S(2)}) %all-to-all-start.1) | async-done | bytes 524320 | tf_op jit(solution)/shard_map/all_to_all | solution.py:723
  65.3 0.4 unpack.1
  65.7 0.1 collective-permute-start.5
  65.8 1.5 %collective-permute-done.5.got_ref = bf16[128,1024]{1,0:T(8,128)(2,1)S(1)} collective-permute-done((bf16[128,1024]{1,0:T(8,128)(2,1)S(1)}, bf16[128,1024]{1,0:T(8,128)(2,1)S(1)}, u32[]{:S(2)}, u32[]{:S(2)}) %collective-permute-start.5) | collective-permute-done | bytes 262176 | tf_op jit(solution)/shard_map/ppermute | solution.py:725
  67.3 0.1 join.1
  67.4 0.0 copy-start
  67.4 0.6 collective-permute-start.10
  68.0 1.5 %collective-permute-start.9 = (bf16[128,2048]{1,0:T(8,128)(2,1)S(1)}, bf16[128,2048]{1,0:T(8,128)(2,1)S(1)}, u32[]{:S(2)}, u32[]{:S(2)}) collective-permute-start(bf16[128,2048]{1,0:T(8,128)(2,1)S(1)} %get-tuple-element.48.rows_ref.refs_4_), channel_id=1, source_target_pairs={{0,4},{4,8},{8,12},{12,0},{16,20},{20,24},{24,28},{28,16},{32,36},... | collective-permute-start | bytes 1572872 | tf_op jit(solution)/shard_map/ppermute | solution.py:520
  69.5 0.0 collective-permute-done.7.refs_1_
  69.5 1.6 %collective-permute-start.14 = (bf16[2,4,32,1024]{3,2,1,0:T(8,128)(2,1)S(1)}, bf16[2,4,32,1024]{3,2,1,0:T(8,128)(2,1)}, u32[]{:S(2)}, u32[]{:S(2)}) collective-permute-start(bf16[2,4,32,1024]{3,2,1,0:T(8,128)(2,1)S(1)} %collective-permute-done.7.refs_1_), channel_id=1, source_target_pairs={{0,1},{1,2},{2,3},{3,0},{4,5},{5,6},{6,7},{7,4},{8,9},{9,10},{10,1... | collective-permute-start | bytes 1572872 | tf_op jit(solution)/shard_map/ppermute | solution.py:501
  71.2 0.9 collective-permute-start.15
  72.1 9.3 %dnorm.1 = bf16[128,4096]{1,0:T(8,128)(2,1)} custom-call(bf16[128,2048]{1,0:T(8,128)(2,1)S(1)} %get-tuple-element.48.rows_ref.refs_4_, bf16[128,1024]{1,0:T(8,128)(2,1)S(1)} %collective-permute-done.6.got_ref, bf16[4096,1024]{1,0:T(8,128)(2,1)} %bitcast.14, bf16[4096,1024]{1,0:T(8,128)(2,1)} %bitcast.16), custom_call_target="tpu_custom_call" | custom-call | flops 2147483648 | bytes 16777216 | tf_op jit(solution)/shard_map/dnorm/pallas_call | solution.py:431
  81.5 2.5 %collective-permute-done.9.refs_5_ = bf16[128,2048]{1,0:T(8,128)(2,1)S(1)} collective-permute-done((bf16[128,2048]{1,0:T(8,128)(2,1)S(1)}, bf16[128,2048]{1,0:T(8,128)(2,1)S(1)}, u32[]{:S(2)}, u32[]{:S(2)}) %collective-permute-start.9) | collective-permute-done | bytes 524320 | tf_op jit(solution)/shard_map/ppermute | solution.py:520
  84.0 0.8 copy-done.8
  84.8 4.5 %all-to-all-start.2 = ((bf16[4,32,4096]{2,1,0:T(8,128)(2,1)}), bf16[4,32,4096]{2,1,0:T(8,128)(2,1)S(1)}, u32[]{:S(2)}, u32[]{:S(2)}) async-start(bf16[4,32,4096]{2,1,0:T(8,128)(2,1)} %bitcast.7), calls=%async_computation.2 | async-start | bytes 2097152 | tf_op jit(solution)/shard_map/all_to_all | solution.py:733
  89.3 3.5 %far.1 = (bf16[128,2048]{1,0:T(8,128)(2,1)}, bf16[128,2048]{1,0:T(8,128)(2,1)}, bf16[512,2048]{1,0:T(8,128)(2,1)S(1)}) custom-call(bf16[2,4,32,1024]{3,2,1,0:T(8,128)(2,1)} %get-tuple-element.50.refs_0_, bf16[2,4,32,1024]{3,2,1,0:T(8,128)(2,1)} %copy-done.5, bf16[2,4,32,1024]{3,2,1,0:T(8,128)(2,1)} %copy-done.6, ...), custom_call_target="tpu_custom_call" | custom-call | flops 536870912 | bytes 8388608 | tf_op jit(solution)/shard_map/far/pallas_call | solution.py:584
  92.8 0.6 collective-permute-start.16
  93.5 2.7 %collective-permute-start.17 = (bf16[128,2048]{1,0:T(8,128)(2,1)}, bf16[128,2048]{1,0:T(8,128)(2,1)}, u32[]{:S(2)}, u32[]{:S(2)}) collective-permute-start(bf16[128,2048]{1,0:T(8,128)(2,1)} %get-tuple-element.59), channel_id=1, source_target_pairs={{0,48},{4,52},{8,56},{12,60},{16,0},{20,4},{24,8},{28,12},{32,16},... | collective-permute-start | bytes 1572872 | tf_op jit(solution)/shard_map/ppermute | solution.py:520
  96.1 7.8 %all-to-all-done.2.parts_ref = bf16[4,32,4096]{2,1,0:T(8,128)(2,1)S(1)} async-done(((bf16[4,32,4096]{2,1,0:T(8,128)(2,1)}), bf16[4,32,4096]{2,1,0:T(8,128)(2,1)S(1)}, u32[]{:S(2)}, u32[]{:S(2)}) %all-to-all-start.2) | async-done | bytes 1048608 | tf_op jit(solution)/shard_map/all_to_all | solution.py:733
  103.9 1.2 rms_back.1.refs_0_
  105.1 0.6 collective-permute-start.11
  105.7 4.7 %side.1 = (bf16[256,1024]{1,0:T(8,128)(2,1)S(1)}, bf16[256,1024]{1,0:T(8,128)(2,1)S(1)}, bf16[256,1024]{1,0:T(8,128)(2,1)S(1)}, bf16[256,1024]{1,0:T(8,128)(2,1)S(1)}, bf16[256,1024]{1,0:T(8,128)(2,1)S(1)}) custom-call(bf16[2,4,32,1024]{3,2,1,0:T(8,128)(2,1)} %get-tuple-element.50.refs_0_, bf16[2,4,32,1024]{3,2,1,0:T(8,128)(2,1)} %copy-done.5, ...), custom_call_target="tpu_custom_call" | custom-call | flops 1342177280 | bytes 4194304 | tf_op jit(solution)/shard_map/side/pallas_call | solution.py:623
  110.4 0.1 collective-permute-start.18
  110.5 3.2 %collective-permute-start.19 = (bf16[256,1024]{1,0:T(8,128)(2,1)S(1)}, bf16[256,1024]{1,0:T(8,128)(2,1)S(1)}, u32[]{:S(2)}, u32[]{:S(2)}) collective-permute-start(bf16[256,1024]{1,0:T(8,128)(2,1)S(1)} %get-tuple-element.61), channel_id=1, source_target_pairs={{0,48},{4,52},{8,56},{12,60},{16,0},{20,4},{24,8},{28,12},{32,16},... | collective-permute-start | bytes 1572872 | tf_op jit(solution)/shard_map/ppermute | solution.py:520
  113.8 1.1 collective-permute-start.22
  114.8 6.1 %collective-permute-done.18.refs_5_ = bf16[256,1024]{1,0:T(8,128)(2,1)S(1)} collective-permute-done((bf16[256,1024]{1,0:T(8,128)(2,1)S(1)}, bf16[256,1024]{1,0:T(8,128)(2,1)S(1)}, u32[]{:S(2)}, u32[]{:S(2)}) %collective-permute-start.18) | collective-permute-done | bytes 524320 | tf_op jit(solution)/shard_map/ppermute | solution.py:520
  120.9 2.7 %collective-permute-start.12 = (bf16[32,4096]{1,0:T(8,128)(2,1)S(1)}, bf16[32,4096]{1,0:T(8,128)(2,1)S(1)}, u32[]{:S(2)}, u32[]{:S(2)}) collective-permute-start(bf16[32,4096]{1,0:T(8,128)(2,1)S(1)} %rms_back.1.refs_0_), channel_id=1, source_target_pairs={{0,3},{1,0},{2,1},{3,2},{4,7},{5,4},{6,5},{7,6},{8,11},{9,8},{10,9... | collective-permute-start | bytes 786440 | tf_op jit(solution)/shard_map/ppermute | solution.py:501
  123.6 2.5 %collective-permute-done.21.refs_8_ = bf16[256,1024]{1,0:T(8,128)(2,1)S(1)} collective-permute-done((bf16[256,1024]{1,0:T(8,128)(2,1)S(1)}, bf16[256,1024]{1,0:T(8,128)(2,1)S(1)}, u32[]{:S(2)}, u32[]{:S(2)}) %collective-permute-start.21) | collective-permute-done | bytes 524320 | tf_op jit(solution)/shard_map/ppermute | solution.py:520
  126.1 3.1 %own.1 = (f32[256,1024]{1,0:T(8,128)}, f32[256,1024]{1,0:T(8,128)}) custom-call(bf16[2,4,32,1024]{3,2,1,0:T(8,128)(2,1)} %get-tuple-element.50.refs_0_, bf16[2,4,32,1024]{3,2,1,0:T(8,128)(2,1)} %copy-done.5, bf16[2,4,32,1024]{3,2,1,0:T(8,128)(2,1)} %copy-done.6, bf16[2,4,32,1024]{3,2,1,0:T(8,128)(2,1)} %collective-permute-done.14.refs_3_, ...), custom_call_target="tpu_custom_call" | custom-call | flops 268435456 | bytes 8388608 | tf_op jit(solution)/shard_map/own/pallas_call | solution.py:693
  129.2 2.0 %collective-permute-done.13.refs_3_ = bf16[32,4096]{1,0:T(8,128)(2,1)S(1)} collective-permute-done((bf16[32,4096]{1,0:T(8,128)(2,1)S(1)}, bf16[32,4096]{1,0:T(8,128)(2,1)S(1)}, u32[]{:S(2)}, u32[]{:S(2)}) %collective-permute-start.13) | collective-permute-done | bytes 262176 | tf_op jit(solution)/shard_map/ppermute | solution.py:501
  131.2 1.0 place.1
  (33 shorter events, 0.1 us)
Async XLA Ops:
  0.6 11.2 %copy-start.2 = (s32[16,16]{1,0:T(8,128)S(1)}, s32[16,16]{1,0:T(8,128)}, u32[]{:S(2)}) copy-start(s32[16,16]{1,0:T(8,128)} %src_ref.5) | copy-start | bytes 3076
  0.6 11.2 %copy-start.3 = (s32[16,16]{1,0:T(8,128)S(1)}, s32[16,16]{1,0:T(8,128)}, u32[]{:S(2)}) copy-start(s32[16,16]{1,0:T(8,128)} %dest_ref.5) | copy-start | bytes 3076
  0.7 42.3 %copy-start.4 = (s32[16,16]{1,0:T(8,128)S(1)}, s32[16,16]{1,0:T(8,128)}, u32[]{:S(2)}) copy-start(s32[16,16]{1,0:T(8,128)} %tgt_ref.1) | copy-start | bytes 3076
  9.6 1.6 %collective-permute-start = (bf16[128,1024]{1,0:T(8,128)(2,1)S(1)}, bf16[128,1024]{1,0:T(8,128)(2,1)S(1)}, u32[]{:S(2)}, u32[]{:S(2)}) collective-permute-start(bf16[128,1024]{1,0:T(8,128)(2,1)S(1)} %get-tuple-element.36), channel_id=1, source_target_pairs={{0,64},{64,0},{1,65},{65,1},{2,66},{66,2},{3,67},{67,3},{4,68},{68... | collective-permute-start | bytes 786440 | tf_op jit(solution)/shard_map/ppermute | solution.py:713
  9.8 2.1 %collective-permute-start.1 = (bf16[4,32,1024]{2,1,0:T(8,128)(2,1)}, bf16[4,32,1024]{2,1,0:T(8,128)(2,1)S(1)}, u32[]{:S(2)}, u32[]{:S(2)}) collective-permute-start(bf16[4,32,1024]{2,1,0:T(8,128)(2,1)} %get-tuple-element.38), channel_id=1, source_target_pairs={{0,64},{64,0},{1,65},{65,1},{2,66},{66,2},{3,67},{67,3},{4,68},{68... | collective-permute-start | bytes 786440 | tf_op jit(solution)/shard_map/ppermute | solution.py:714
  21.8 21.1 %all-to-all-start = ((bf16[16,16,1024]{2,1,0:T(8,128)(2,1)}), bf16[16,16,1024]{2,1,0:T(8,128)(2,1)S(1)}, u32[]{:S(2)}, u32[]{:S(2)}) async-start(bf16[16,16,1024]{2,1,0:T(8,128)(2,1)} %bitcast.3), calls=%async_computation | async-start | bytes 1048576 | tf_op jit(solution)/shard_map/all_to_all | solution.py:717
  30.1 11.0 %collective-permute-start.2 = (bf16[2,32,1024]{2,1,0:T(8,128)(2,1)}, bf16[2,32,1024]{2,1,0:T(8,128)(2,1)S(1)}, u32[]{:S(2)}, u32[]{:S(2)}) collective-permute-start(bf16[2,32,1024]{2,1,0:T(8,128)(2,1)} %get-tuple-element.41), channel_id=1, source_target_pairs={{0,4},{4,8},{8,12},{12,0},{16,20},{20,24},{24,28},{28,16},{32,36},... | collective-permute-start | bytes 393224 | tf_op jit(solution)/shard_map/ppermute | solution.py:520
  32.1 9.1 %collective-permute-start.3 = (bf16[2,32,1024]{2,1,0:T(8,128)(2,1)}, bf16[2,32,1024]{2,1,0:T(8,128)(2,1)S(1)}, u32[]{:S(2)}, u32[]{:S(2)}) collective-permute-start(bf16[2,32,1024]{2,1,0:T(8,128)(2,1)} %get-tuple-element.42), channel_id=1, source_target_pairs={{0,12},{4,0},{8,4},{12,8},{16,28},{20,16},{24,20},{28,24},{32,44},... | collective-permute-start | bytes 393224 | tf_op jit(solution)/shard_map/ppermute | solution.py:520
  33.5 9.4 %collective-permute-start.4 = (bf16[2,32,1024]{2,1,0:T(8,128)(2,1)}, bf16[2,32,1024]{2,1,0:T(8,128)(2,1)S(1)}, u32[]{:S(2)}, u32[]{:S(2)}) collective-permute-start(bf16[2,32,1024]{2,1,0:T(8,128)(2,1)} %get-tuple-element.43), channel_id=1, source_target_pairs={{0,8},{4,12},{8,0},{12,4},{16,24},{20,28},{24,16},{28,20},{32,40},... | collective-permute-start | bytes 393224 | tf_op jit(solution)/shard_map/ppermute | solution.py:520
  48.9 16.5 %all-to-all-start.1 = ((bf16[16,16,1024]{2,1,0:T(8,128)(2,1)}), bf16[16,16,1024]{2,1,0:T(8,128)(2,1)S(1)}, u32[]{:S(2)}, u32[]{:S(2)}) async-start(bf16[16,16,1024]{2,1,0:T(8,128)(2,1)} %bitcast.5), calls=%async_computation.1 | async-start | bytes 1048576 | tf_op jit(solution)/shard_map/all_to_all | solution.py:723
  53.8 15.7 %collective-permute-start.7 = (bf16[2,4,32,1024]{3,2,1,0:T(8,128)(2,1)}, bf16[2,4,32,1024]{3,2,1,0:T(8,128)(2,1)S(1)}, u32[]{:S(2)}, u32[]{:S(2)}) collective-permute-start(bf16[2,4,32,1024]{3,2,1,0:T(8,128)(2,1)} %get-tuple-element.50.refs_0_), channel_id=1, source_target_pairs={{0,1},{1,2},{2,3},{3,0},{4,5},{5,6},{6,7},{7,4},{8,9},{9,10},{10,1... | collective-permute-start | bytes 1572872 | tf_op jit(solution)/shard_map/ppermute | solution.py:501
  55.5 15.7 %collective-permute-start.8 = (bf16[2,4,32,1024]{3,2,1,0:T(8,128)(2,1)}, bf16[2,4,32,1024]{3,2,1,0:T(8,128)(2,1)S(1)}, u32[]{:S(2)}, u32[]{:S(2)}) collective-permute-start(bf16[2,4,32,1024]{3,2,1,0:T(8,128)(2,1)} %get-tuple-element.50.refs_0_), channel_id=1, source_target_pairs={{0,3},{1,0},{2,1},{3,2},{4,7},{5,4},{6,5},{7,6},{8,11},{9,8},{10,9... | collective-permute-start | bytes 1572872 | tf_op jit(solution)/shard_map/ppermute | solution.py:501
  65.7 1.6 %collective-permute-start.5 = (bf16[128,1024]{1,0:T(8,128)(2,1)S(1)}, bf16[128,1024]{1,0:T(8,128)(2,1)S(1)}, u32[]{:S(2)}, u32[]{:S(2)}) collective-permute-start(bf16[128,1024]{1,0:T(8,128)(2,1)S(1)} %get-tuple-element.47), channel_id=1, source_target_pairs={{0,64},{64,0},{1,65},{65,1},{2,66},{66,2},{3,67},{67,3},{4,68},{68... | collective-permute-start | bytes 786440 | tf_op jit(solution)/shard_map/ppermute | solution.py:725
  67.4 14.0 %copy-start = (bf16[128,2048]{1,0:T(8,128)(2,1)}, bf16[128,2048]{1,0:T(8,128)(2,1)S(1)}, u32[]{:S(2)}) copy-start(bf16[128,2048]{1,0:T(8,128)(2,1)S(1)} %get-tuple-element.48.rows_ref.refs_4_) | copy-start | bytes 1572868
  67.4 14.1 %collective-permute-start.10 = (bf16[128,2048]{1,0:T(8,128)(2,1)S(1)}, bf16[128,2048]{1,0:T(8,128)(2,1)S(1)}, u32[]{:S(2)}, u32[]{:S(2)}) collective-permute-start(bf16[128,2048]{1,0:T(8,128)(2,1)S(1)} %get-tuple-element.48.rows_ref.refs_4_), channel_id=1, source_target_pairs={{0,12},{4,0},{8,4},{12,8},{16,28},{20,16},{24,20},{28,24},{32,44},... | collective-permute-start | bytes 1572872 | tf_op jit(solution)/shard_map/ppermute | solution.py:520
  68.0 16.0 %collective-permute-start.9 = (bf16[128,2048]{1,0:T(8,128)(2,1)S(1)}, bf16[128,2048]{1,0:T(8,128)(2,1)S(1)}, u32[]{:S(2)}, u32[]{:S(2)}) collective-permute-start(bf16[128,2048]{1,0:T(8,128)(2,1)S(1)} %get-tuple-element.48.rows_ref.refs_4_), channel_id=1, source_target_pairs={{0,4},{4,8},{8,12},{12,0},{16,20},{20,24},{24,28},{28,16},{32,36},... | collective-permute-start | bytes 1572872 | tf_op jit(solution)/shard_map/ppermute | solution.py:520
  69.5 34.4 %copy-start.1 = (f32[1,4096]{1,0:T(1,128)S(1)}, f32[1,4096]{1,0:T(1,128)}, u32[]{:S(2)}) copy-start(f32[1,4096]{1,0:T(1,128)} %gain_ref.1) | copy-start | bytes 49156
  69.5 2.6 %collective-permute-start.6 = (bf16[128,1024]{1,0:T(8,128)(2,1)S(1)}, bf16[128,1024]{1,0:T(8,128)(2,1)S(1)}, u32[]{:S(2)}, u32[]{:S(2)}) collective-permute-start(bf16[128,1024]{1,0:T(8,128)(2,1)S(1)} %get-tuple-element.49), channel_id=1, source_target_pairs={{0,64},{64,0},{1,65},{65,1},{2,66},{66,2},{3,67},{67,3},{4,68},{68... | collective-permute-start | bytes 786440 | tf_op jit(solution)/shard_map/ppermute | solution.py:729
  69.5 11.9 %copy-start.5 = (bf16[2,4,32,1024]{3,2,1,0:T(8,128)(2,1)}, bf16[2,4,32,1024]{3,2,1,0:T(8,128)(2,1)S(1)}, u32[]{:S(2)}) copy-start(bf16[2,4,32,1024]{3,2,1,0:T(8,128)(2,1)S(1)} %collective-permute-done.7.refs_1_) | copy-start | bytes 1572868
  69.5 19.8 %collective-permute-start.14 = (bf16[2,4,32,1024]{3,2,1,0:T(8,128)(2,1)S(1)}, bf16[2,4,32,1024]{3,2,1,0:T(8,128)(2,1)}, u32[]{:S(2)}, u32[]{:S(2)}) collective-permute-start(bf16[2,4,32,1024]{3,2,1,0:T(8,128)(2,1)S(1)} %collective-permute-done.7.refs_1_), channel_id=1, source_target_pairs={{0,1},{1,2},{2,3},{3,0},{4,5},{5,6},{6,7},{7,4},{8,9},{9,10},{10,1... | collective-permute-start | bytes 1572872 | tf_op jit(solution)/shard_map/ppermute | solution.py:501
  71.2 10.3 %copy-start.6 = (bf16[2,4,32,1024]{3,2,1,0:T(8,128)(2,1)}, bf16[2,4,32,1024]{3,2,1,0:T(8,128)(2,1)S(1)}, u32[]{:S(2)}) copy-start(bf16[2,4,32,1024]{3,2,1,0:T(8,128)(2,1)S(1)} %collective-permute-done.8.refs_2_) | copy-start | bytes 1572868
  71.2 18.1 %collective-permute-start.15 = (bf16[128,2048]{1,0:T(8,128)(2,1)S(1)}, bf16[128,2048]{1,0:T(8,128)(2,1)}, u32[]{:S(2)}, u32[]{:S(2)}) collective-permute-start(bf16[128,2048]{1,0:T(8,128)(2,1)S(1)} %get-tuple-element.48.rows_ref.refs_4_), channel_id=1, source_target_pairs={{0,8},{4,12},{8,0},{12,4},{16,24},{20,28},{24,16},{28,20},{32,40},... | collective-permute-start | bytes 1572872 | tf_op jit(solution)/shard_map/ppermute | solution.py:520
  81.5 2.5 %copy-start.7 = (bf16[128,2048]{1,0:T(8,128)(2,1)}, bf16[128,2048]{1,0:T(8,128)(2,1)S(1)}, u32[]{:S(2)}) copy-start(bf16[128,2048]{1,0:T(8,128)(2,1)S(1)} %collective-permute-done.10.refs_6_) | copy-start | bytes 1572868
  84.0 0.8 copy-start.8
  84.8 19.1 %all-to-all-start.2 = ((bf16[4,32,4096]{2,1,0:T(8,128)(2,1)}), bf16[4,32,4096]{2,1,0:T(8,128)(2,1)S(1)}, u32[]{:S(2)}, u32[]{:S(2)}) async-start(bf16[4,32,4096]{2,1,0:T(8,128)(2,1)} %bitcast.7), calls=%async_computation.2 | async-start | bytes 2097152 | tf_op jit(solution)/shard_map/all_to_all | solution.py:733
  92.8 12.9 %collective-permute-start.16 = (bf16[128,2048]{1,0:T(8,128)(2,1)}, bf16[128,2048]{1,0:T(8,128)(2,1)}, u32[]{:S(2)}, u32[]{:S(2)}) collective-permute-start(bf16[128,2048]{1,0:T(8,128)(2,1)} %get-tuple-element.58), channel_id=1, source_target_pairs={{0,16},{4,20},{8,24},{12,28},{16,32},{20,36},{24,40},{28,44},{32,4... | collective-permute-start | bytes 1572872 | tf_op jit(solution)/shard_map/ppermute | solution.py:520
  93.5 12.3 %collective-permute-start.17 = (bf16[128,2048]{1,0:T(8,128)(2,1)}, bf16[128,2048]{1,0:T(8,128)(2,1)}, u32[]{:S(2)}, u32[]{:S(2)}) collective-permute-start(bf16[128,2048]{1,0:T(8,128)(2,1)} %get-tuple-element.59), channel_id=1, source_target_pairs={{0,48},{4,52},{8,56},{12,60},{16,0},{20,4},{24,8},{28,12},{32,16},... | collective-permute-start | bytes 1572872 | tf_op jit(solution)/shard_map/ppermute | solution.py:520
  105.1 8.7 %collective-permute-start.11 = (bf16[32,4096]{1,0:T(8,128)(2,1)S(1)}, bf16[32,4096]{1,0:T(8,128)(2,1)S(1)}, u32[]{:S(2)}, u32[]{:S(2)}) collective-permute-start(bf16[32,4096]{1,0:T(8,128)(2,1)S(1)} %rms_back.1.refs_0_), channel_id=1, source_target_pairs={{0,1},{1,2},{2,3},{3,0},{4,5},{5,6},{6,7},{7,4},{8,9},{9,10},{10,1... | collective-permute-start | bytes 786440 | tf_op jit(solution)/shard_map/ppermute | solution.py:501
  110.4 10.5 %collective-permute-start.18 = (bf16[256,1024]{1,0:T(8,128)(2,1)S(1)}, bf16[256,1024]{1,0:T(8,128)(2,1)S(1)}, u32[]{:S(2)}, u32[]{:S(2)}) collective-permute-start(bf16[256,1024]{1,0:T(8,128)(2,1)S(1)} %get-tuple-element.60), channel_id=1, source_target_pairs={{0,16},{4,20},{8,24},{12,28},{16,32},{20,36},{24,40},{28,44},{32,4... | collective-permute-start | bytes 1572872 | tf_op jit(solution)/shard_map/ppermute | solution.py:520
  110.5 13.1 %collective-permute-start.19 = (bf16[256,1024]{1,0:T(8,128)(2,1)S(1)}, bf16[256,1024]{1,0:T(8,128)(2,1)S(1)}, u32[]{:S(2)}, u32[]{:S(2)}) collective-permute-start(bf16[256,1024]{1,0:T(8,128)(2,1)S(1)} %get-tuple-element.61), channel_id=1, source_target_pairs={{0,48},{4,52},{8,56},{12,60},{16,0},{20,4},{24,8},{28,12},{32,16},... | collective-permute-start | bytes 1572872 | tf_op jit(solution)/shard_map/ppermute | solution.py:520
  113.8 9.8 %collective-permute-start.20 = (bf16[256,1024]{1,0:T(8,128)(2,1)S(1)}, bf16[256,1024]{1,0:T(8,128)(2,1)S(1)}, u32[]{:S(2)}, u32[]{:S(2)}) collective-permute-start(bf16[256,1024]{1,0:T(8,128)(2,1)S(1)} %get-tuple-element.62), channel_id=1, source_target_pairs={{0,80},{4,84},{8,88},{12,92},{16,96},{20,100},{24,104},{28,108},{3... | collective-permute-start | bytes 1572872 | tf_op jit(solution)/shard_map/ppermute | solution.py:520
  113.8 12.3 %collective-permute-start.21 = (bf16[256,1024]{1,0:T(8,128)(2,1)S(1)}, bf16[256,1024]{1,0:T(8,128)(2,1)S(1)}, u32[]{:S(2)}, u32[]{:S(2)}) collective-permute-start(bf16[256,1024]{1,0:T(8,128)(2,1)S(1)} %get-tuple-element.63), channel_id=1, source_target_pairs={{0,112},{4,116},{8,120},{12,124},{16,64},{20,68},{24,72},{28,76},{... | collective-permute-start | bytes 1572872 | tf_op jit(solution)/shard_map/ppermute | solution.py:520
  113.8 12.3 %collective-permute-start.22 = (bf16[256,1024]{1,0:T(8,128)(2,1)S(1)}, bf16[256,1024]{1,0:T(8,128)(2,1)S(1)}, u32[]{:S(2)}, u32[]{:S(2)}) collective-permute-start(bf16[256,1024]{1,0:T(8,128)(2,1)S(1)} %get-tuple-element.64), channel_id=1, source_target_pairs={{0,64},{64,0},{1,65},{65,1},{2,66},{66,2},{3,67},{67,3},{4,68},{68... | collective-permute-start | bytes 1572872 | tf_op jit(solution)/shard_map/ppermute | solution.py:747
  120.9 8.3 %collective-permute-start.12 = (bf16[32,4096]{1,0:T(8,128)(2,1)S(1)}, bf16[32,4096]{1,0:T(8,128)(2,1)S(1)}, u32[]{:S(2)}, u32[]{:S(2)}) collective-permute-start(bf16[32,4096]{1,0:T(8,128)(2,1)S(1)} %rms_back.1.refs_0_), channel_id=1, source_target_pairs={{0,3},{1,0},{2,1},{3,2},{4,7},{5,4},{6,5},{7,6},{8,11},{9,8},{10,9... | collective-permute-start | bytes 786440 | tf_op jit(solution)/shard_map/ppermute | solution.py:501
  123.6 7.6 %collective-permute-start.13 = (bf16[32,4096]{1,0:T(8,128)(2,1)S(1)}, bf16[32,4096]{1,0:T(8,128)(2,1)S(1)}, u32[]{:S(2)}, u32[]{:S(2)}) collective-permute-start(bf16[32,4096]{1,0:T(8,128)(2,1)S(1)} %collective-permute-done.11.refs_1_), channel_id=1, source_target_pairs={{0,1},{1,2},{2,3},{3,0},{4,5},{5,6},{6,7},{7,4},{8,9},{9,10},{10,1... | collective-permute-start | bytes 786440 | tf_op jit(solution)/shard_map/ppermute | solution.py:501

commit v6 on v5

--- a/solution.py
+++ b/solution.py
@@ -90,7 +90,7 @@
 def forward_kernel(
     x_hbm, gain_hbm, cot_hbm, a_hbm, b_hbm, keep_ref, send_ref, *rest
 ):
-    mine_hbm, other_hbm = rest[:2]
+    mine_ref, other_ref = rest[:2]
     x_ref, gain_ref, a_buf, b_buf, normed_ref, left_ref, in_sem, a_sem, b_sem, out_sem = rest[2:]
     count, step, cols = a_buf.shape
     core = lax.axis_index("section")
@@ -139,7 +139,7 @@
             at_z = ((z + k) % RING * RING + (x + j) % RING) * block
             at_mine = jnp.where(core == 0, at_x, at_z)
             at_other = jnp.where(core == 0, at_z, at_x)
-            for source, at, out in ((left_ref, at_mine, mine_hbm), (normed_ref, at_other, other_hbm)):
+            for source, at, out in ((left_ref, at_mine, mine_ref), (normed_ref, at_other, other_ref)):
                 copies.append(
                     pltpu.make_async_copy(
                         source.at[quarter, pl.ds(pl.multiple_of(at, block), block)],
@@ -188,8 +188,8 @@
     return pl.pallas_call(
         forward_kernel,
         in_specs=[HBM] * 5,
-        out_specs=[VMEM] * 2 + [HBM] * 2,
-        out_shape=[half] * 2 + [pltpu.HBM((RING, QUARTER, cols), BF16)] * 2,
+        out_specs=[VMEM] * 4,
+        out_shape=[half] * 2 + [jax.ShapeDtypeStruct((RING, QUARTER, cols), BF16)] * 2,
         scratch_shapes=[pltpu.VMEM((rows, width), BF16), pltpu.VMEM((1, width), F32)]
         + [pltpu.VMEM((count, step, cols), BF16)] * 2
         + [pltpu.VMEM((rows, width), BF16)] * 2
@@ -202,27 +202,15 @@
     )(in_hbm(x), in_hbm(gain), in_hbm(cot), in_hbm(weight_a), in_hbm(weight_b))
 
 
-def placed(places, refs, sems):
-    copies = [
-        pltpu.make_async_copy(refs[source].at[at], refs[out].at[to], sems.at[i])
-        for i, (source, at, out, to) in enumerate(places)
-    ]
-    for copy in copies:
-        copy.start()
-    return copies
-
-
 def wait_all(copies):
     for copy in copies:
         copy.wait()
 
 
-PAIRS = [(m, (k,), 2 + i, (m,)) for i, k in enumerate((0, 1, 3, 2)) for m in range(2)]
-STACK = [(p, (m,), RING, (m, p)) for p in range(RING) for m in range(2)]
-
-
 def pack_kernel(keep_ref, got_ref, src_ref, dest_ref, mine_ref, other_ref, out_ref, *rest):
-    copies = placed(PAIRS, (mine_ref, other_ref, *rest[:RING]), rest[RING])
+    for out, k in zip(rest, (0, 1, 3, 2), strict=True):
+        out[0] = mine_ref[k]
+        out[1] = other_ref[k]
     spread = slot_onehot(member_index(), src_ref, dest_ref)
 
     @pl.when(lax.axis_index("section") == 0)
@@ -232,8 +220,6 @@
     @pl.when(lax.axis_index("section") != 0)
     def _():
         out_ref[...] = jnp.dot(spread, got_ref[...], preferred_element_type=F32).astype(BF16)
-
-    wait_all(copies)
 
 
 def pack(keep, got, src_len, dest, mine, other):
@@ -241,23 +227,24 @@
     _, rows, cols = mine.shape
     outs = pl.pallas_call(
         pack_kernel,
-        in_specs=[VMEM] * 4 + [HBM, ANY],
-        out_specs=[VMEM] + [HBM] * RING,
+        in_specs=[VMEM] * 6,
+        out_specs=[VMEM] * (1 + RING),
         out_shape=[jax.ShapeDtypeStruct((SLOTS, width), BF16)]
-        + [pltpu.HBM((2, rows, cols), BF16)] * RING,
-        scratch_shapes=[pltpu.SemaphoreType.DMA((len(PAIRS),))],
+        + [jax.ShapeDtypeStruct((2, rows, cols), BF16)] * RING,
         compiler_params=params(),
         cost_estimate=cost(2 * SLOTS * TOK * width, 2 * SLOTS * width),
         name="pack",
-    )(keep, got, src_len, dest, in_hbm(mine), other)
+    )(keep, got, src_len, dest, mine, other)
     return outs[0], outs[1:]
 
 
 def attend_kernel(
     keep_ref, got_ref, slots_ref, src_ref, tgt_ref, dest_ref, *rest
 ):
-    front_ref, back_ref, stack_ref, own_ref, sems = rest[RING:]
-    copies = placed(STACK, (*rest[:RING], stack_ref), sems)
+    front_ref, back_ref, stack_ref, own_ref = rest[RING:]
+    for p in range(RING):
+        for m in range(2):
+            stack_ref[m, p] = rest[p][m]
     mask = pair_mask(member_index(), src_ref, tgt_ref, dest_ref)
 
     @pl.when(lax.axis_index("section") == 0)
@@ -304,7 +291,6 @@
         front_ref[:, second] = jnp.dot(weight, values, preferred_element_type=F32).astype(BF16)
         back_ref[:, first] = fold(tn(dscore, query))
         back_ref[:, second] = fold(tn(weight, dout))
-    wait_all(copies)
 
 
 def attend(keep, got, slots, src_len, tgt_len, dest, pieces):
@@ -312,18 +298,18 @@
     _, quarter, cols = pieces[0].shape
     return pl.pallas_call(
         attend_kernel,
-        in_specs=[VMEM] * 6 + [HBM] + [ANY] * (RING - 1),
-        out_specs=[VMEM] * 2 + [HBM],
+        in_specs=[VMEM] * (6 + RING),
+        out_specs=[VMEM] * 3,
         out_shape=[
             jax.ShapeDtypeStruct((rows, width), BF16),
             jax.ShapeDtypeStruct((SLOTS, width), BF16),
-            pltpu.HBM((2, RING, quarter, cols), BF16),
+            jax.ShapeDtypeStruct((2, RING, quarter, cols), BF16),
         ],
-        scratch_shapes=[pltpu.VMEM((rows, width), BF16), pltpu.SemaphoreType.DMA((len(STACK),))],
+        scratch_shapes=[pltpu.VMEM((rows, width), BF16)],
         compiler_params=params(),
         cost_estimate=cost(24 * rows * SLOTS * width, 8 * SLOTS * width),
         name="attend",
-    )(keep, got, slots, src_len, tgt_len, dest, in_hbm(pieces[0]), *pieces[1:])
+    )(keep, got, slots, src_len, tgt_len, dest, *pieces)
 
 
 def unpack_kernel(back_ref, front_ref, src_ref, dest_ref, keep_ref, send_ref):
@@ -393,9 +379,6 @@
     count, step, cols = a_buf.shape
     core = lax.axis_index("section")
 
-    def nt(left, right):
-        return lax.dot_general(left, right, (((1,), (1,)), ((), ())), preferred_element_type=F32)
-
     def fetches(hbm, buf, sem):
         return [
             pltpu.make_async_copy(hbm.at[pl.ds(k * step, step), :], buf.at[k], sem.at[k])
@@ -404,24 +387,26 @@
 
     get_a, get_b = fetches(a_hbm, a_buf, a_sem), fetches(b_hbm, b_buf, b_sem)
 
+    def products(terms):
+        for k in range(count):
+            for copies, _, _ in terms:
+                copies[k].start()
+        turned = [rows.T for _, _, rows in terms]
+        for k in range(count):
+            block = None
+            for (copies, weight, _), right in zip(terms, turned, strict=True):
+                copies[k].wait()
+                part = jnp.dot(weight[k], right, preferred_element_type=F32)
+                block = part if block is None else block + part
+            out_ref[:, k * step : (k + 1) * step] = block.T.astype(BF16)
+
     @pl.when(core == 0)
     def _():
-        for k in range(count):
-            get_a[k].start()
-            get_b[k].start()
-        for k in range(count):
-            get_a[k].wait()
-            get_b[k].wait()
-            block = nt(rows_ref[:, :cols], a_buf[k]) + nt(got_ref[...], b_buf[k])
-            out_ref[:, k * step : (k + 1) * step] = block.astype(BF16)
+        products([(get_a, a_buf, rows_ref[:, :cols]), (get_b, b_buf, got_ref[...])])
 
     @pl.when(core != 0)
     def _():
-        for k in range(count):
-            get_a[k].start()
-        for k in range(count):
-            get_a[k].wait()
-            out_ref[:, k * step : (k + 1) * step] = nt(got_ref[...], a_buf[k]).astype(BF16)
+        products([(get_a, a_buf, got_ref[...])])
 
 
 def dnorm_partial(rows, got, weight_a, weight_b):
@@ -595,9 +580,9 @@
 
 def side_kernel(*refs):
     lefts, (rows_ref, from_left, from_right) = refs[:RING], refs[RING : RING + 3]
-    rights, to_lefts, other_ref, buf, sems = refs[RING + 3 : RING + 5], refs[RING + 5 : RING + 7], *refs[RING + 7 :]
-    loads = left_loads(lefts, buf, sems, (1, 3, 0))
-    half, cols = from_left.shape[0], other_ref.shape[1]
+    rights, to_lefts, buf, sems = refs[RING + 3 : RING + 5], refs[RING + 5 : RING + 7], *refs[RING + 7 :]
+    loads = left_loads(lefts, buf, sems, (1, 3))
+    half, cols = from_left.shape[0], rights[0].shape[1]
     for m in range(2):
         at = slice(m * cols, (m + 1) * cols)
 
@@ -611,9 +596,6 @@
         block = product(1)
         to_lefts[m][:half, :] = block[:half].astype(BF16)
         to_lefts[m][half:, :] = (block[half:] + from_right[:, at].astype(F32)).astype(BF16)
-    wait_all(loads[0][2])
-    wait_all(loads[1][2])
-    other_ref[...] = tn(flat(buf[1, 2]), rows_ref[:, cols:]).astype(BF16)
 
 
 def side_blocks(lefts, rows, from_left, from_right):
@@ -623,33 +605,52 @@
     return pl.pallas_call(
         side_kernel,
         in_specs=[HBM] * RING + [VMEM] * 3,
-        out_specs=[VMEM] * 5,
-        out_shape=[shape] * 5,
-        scratch_shapes=left_scratch(block, 3),
-        compiler_params=params(16),
-        cost_estimate=cost(5 * depth * block * cols, 4 * depth * cols),
+        out_specs=[VMEM] * 4,
+        out_shape=[shape] * 4,
+        scratch_shapes=left_scratch(block, 2),
+        compiler_params=params(),
+        cost_estimate=cost(4 * depth * block * cols, 4 * depth * cols),
         name="side",
     )(*[in_hbm(left) for left in lefts], rows, from_left, from_right)
 
 
-def own_kernel(*refs):
-    lefts, rows_ref, parts, outs = refs[:RING], refs[RING], refs[RING + 1 : RING + 6], refs[RING + 6 : RING + 8]
-    buf, sems, part_buf, part_sems, out_buf, out_sems = refs[RING + 8 :]
-    gets = [pltpu.make_async_copy(parts[i], part_buf.at[i], part_sems.at[i]) for i in range(5)]
-    for get in gets:
-        get.start()
-    mine = lax.axis_index("mp")
-    loads = []
-    for j, (left, distance) in enumerate(zip(lefts, ORDER, strict=True)):
-        at = pl.multiple_of((mine + distance) % RING * QUARTER, QUARTER)
-        loads.append(
-            pltpu.make_async_copy(
-                left.at[0, :, :, pl.ds(0, buf.shape[-1])],
-                buf.at[:, pl.ds(at, QUARTER), :],
-                sems.at[j],
-            )
-        )
-        loads[-1].start()
+def middle_kernel(*refs):
+    lefts, (rows_ref, own_hbm, other_ref, own_ref, buf, sems, out_sem) = refs[:RING], refs[RING:]
+    loads = left_loads(lefts, buf, sems, (0,))
+    cols = own_ref.shape[1]
+    wait_all(loads[0][0])
+    own_ref[...] = tn(flat(buf[0, 0]), rows_ref[:, :cols]).astype(BF16)
+    put = pltpu.make_async_copy(own_ref, own_hbm, out_sem)
+    put.start()
+    wait_all(loads[1][0])
+    other_ref[...] = tn(flat(buf[1, 0]), rows_ref[:, cols:]).astype(BF16)
+    put.wait()
+
+
+def middle_blocks(lefts, rows):
+    depth, cols = rows.shape
+    block = lefts[0].shape[-1] // RING
+    return pl.pallas_call(
+        middle_kernel,
+        in_specs=[HBM] * RING + [VMEM],
+        out_specs=[HBM, VMEM],
+        out_shape=[
+            pltpu.HBM((block, cols // 2), BF16),
+            jax.ShapeDtypeStruct((block, cols // 2), BF16),
+        ],
+        scratch_shapes=[pltpu.VMEM((block, cols // 2), BF16)]
+        + left_scratch(block, 1)
+        + [pltpu.SemaphoreType.DMA],
+        compiler_params=params(),
+        cost_estimate=cost(2 * depth * block * cols, 4 * depth * cols),
+        name="middle",
+    )(*[in_hbm(left) for left in lefts], rows)
+
+
+def own_kernel(own_hbm, other_ref, *refs):
+    parts, outs, (own_ref, out_buf, own_sem, out_sems) = refs[:4], refs[4:6], refs[6:]
+    get = pltpu.make_async_copy(own_hbm, own_ref, own_sem)
+    get.start()
     core = lax.axis_index("section")
     chunks = out_sems.shape[1]
     size = out_buf.shape[1] // chunks
@@ -667,41 +668,36 @@
         def _():
             put(m, c, outs[1]).start()
 
-    wait_all(loads)
-    block = tn(flat(buf[...]), rows_ref[:, : out_buf.shape[2]])
-    wait_all(gets[:2])
-    for c in range(chunks):
-        at = slice(c * size, (c + 1) * size)
-        out_buf[0, at] = block[at] + part_buf[0, at].astype(F32) + part_buf[1, at].astype(F32)
-        write(0, c)
-    wait_all(gets[2:])
-    for c in range(chunks):
-        at = slice(c * size, (c + 1) * size)
-        out_buf[1, at] = (
-            part_buf[4, at].astype(F32) + part_buf[2, at].astype(F32) + part_buf[3, at].astype(F32)
-        )
-        write(1, c)
+    for m, base in ((1, other_ref), (0, own_ref)):
+        if m == 0:
+            get.wait()
+        for c in range(chunks):
+            at = slice(c * size, (c + 1) * size)
+            total_of = base[at].astype(F32) + parts[2 * m][at].astype(F32)
+            out_buf[m, at] = total_of + parts[2 * m + 1][at].astype(F32)
+            write(m, c)
     for m in range(2):
         for c in range(chunks):
             put(m, c, outs[0]).wait()
 
 
-def own_blocks(lefts, rows, parts):
-    depth, cols = rows.shape
-    cols = cols // 2
-    block = lefts[0].shape[-1] // RING
+def own_blocks(own, other, parts):
+    block, cols = own.shape
     return pl.pallas_call(
         own_kernel,
-        in_specs=[HBM] * RING + [VMEM] + [ANY] * 5,
+        in_specs=[HBM] + [VMEM] * 5,
         out_specs=[HBM] * 2,
         out_shape=[pltpu.HBM((block, cols), F32)] * 2,
-        scratch_shapes=[pltpu.VMEM((RING, TOK, block), BF16), pltpu.SemaphoreType.DMA((RING,))]
-        + [pltpu.VMEM((5, block, cols), BF16), pltpu.SemaphoreType.DMA((5,))]
-        + [pltpu.VMEM((2, block, cols), F32), pltpu.SemaphoreType.DMA((2, 4))],
-        compiler_params=params(16),
-        cost_estimate=cost(2 * depth * block * cols, 16 * depth * cols),
+        scratch_shapes=[
+            pltpu.VMEM((block, cols), BF16),
+            pltpu.VMEM((2, block, cols), F32),
+            pltpu.SemaphoreType.DMA,
+            pltpu.SemaphoreType.DMA((2, 4)),
+        ],
+        compiler_params=params(),
+        cost_estimate=cost(4 * block * cols, 20 * block * cols),
         name="own",
-    )(*[in_hbm(left) for left in lefts], rows, *parts)
+    )(in_hbm(own), other, *parts)
 
 
 def per_device(states, gains, proj_a, proj_b, cotangent, src_len, tgt_len, dest):
@@ -733,20 +729,20 @@
     parts = lax.all_to_all(
         partial.reshape(RING, TOK // RING, -1), "mp", split_axis=0, concat_axis=0, tiled=True
     )
-    quarter = rms_back(rows, gains, parts)
-    grad_states = place(gathered(quarter, "mp"))
-
     top, low, stack = far_block(lefts, rights)
     from_left, from_right = moved(top, 1, REDUCE), moved(low, 3, REDUCE)
-    right, right_other, left, left_other, own_other = side_blocks(lefts, stack, from_left, from_right)
+    parts, _, _ = lax.optimization_barrier((parts, from_left, from_right))
+    right, right_other, left, left_other = side_blocks(lefts, stack, from_left, from_right)
+    own, own_other = middle_blocks(lefts, stack)
     sums = [
         moved(right, 1, REDUCE),
         moved(left, 3, REDUCE),
         moved(right_other, 1, REDUCE, True),
         moved(left_other, 3, REDUCE, True),
-        lax.ppermute(own_other, "section", swap),
     ]
-    grad_a, grad_b = own_blocks(lefts, stack, sums)
+    quarter = rms_back(rows, gains, parts)
+    grad_states = place(gathered(quarter, "mp"))
+    grad_a, grad_b = own_blocks(own, lax.ppermute(own_other, "section", swap), sums)
     return (grad_states[None], grad_a[None], grad_b[None])
 
 

time: 133 us -> 126 us (0.947)
  waiting for transfers between devices: 39.5 us -> 32.7 us
  Pallas kernels: 48.1 us -> 44.6 us
  starting transfers between devices: 42.9 us -> 44.9 us
    ppermute x12, waiting for transfers between devices: 18.4 us -> 7.41 us  [moved(): return lax.ppermute(value, ('section', 'z', 'x'), pairs)]
    ppermute x6, waiting for transfers between devices: 1.99 us -> 12.6 us  [shift(): return lax.ppermute(value, axis, [(i, (i + k) % RING) for i in range(RING)])]
    pallas_call x4 -> x5, Pallas kernels: 27.9 us -> 19.8 us  [the longest x1 9.11 us: forward(): pl.pallas_call(forward_kernel, in_specs=[HBM] * 5, out_specs=[VMEM] * 4,...]
    all_to_all x1, waiting for transfers between devices: 7.78 us -> 0.01 us  [per_device(): lax.all_to_all(partial.reshape(RING, TOK // RING, -1), 'mp', split_axis=0...]
    pallas_call x1, Pallas kernels: 9.32 us -> 13.6 us  [dnorm_partial(): pl.pallas_call(dnorm_kernel, in_specs=[VMEM] * 2 + [HBM] * 2, out_specs=V...]
    ppermute x12, starting transfers between devices: 15.1 us -> 18 us  [moved(): return lax.ppermute(value, ('section', 'z', 'x'), pairs)]
    ppermute x1, waiting for transfers between devices: 0.01 us -> 1.52 us  [per_device(): others = lax.ppermute(others, 'section', swap)]
  transfers between devices with their start and end apart: 26 -> 26, of which waited for: 11 -> 11; matrix products, arithmetic and copies ran while one was open for 0% -> 0% of each run, Pallas kernels for 17% -> 21%
where the time goes in v6:
time: 126 us; the launch traced here: 125 us
  starting transfers between devices  44.9 us (36%)
  Pallas kernels  44.6 us (35%)
  waiting for transfers between devices  32.7 us (26%)
  local copies, waits for them, and re-layouts  1.96 us (2%)
    ppermute x12, starting transfers between devices, moved(): return lax.ppermute(value, ('section', 'z', 'x'), pairs)  18 us
    pallas_call x1, Pallas kernels, dnorm_partial(): pl.pallas_call(dnorm_kernel, in_specs=[VMEM] * 2 + [HBM] * 2, out_specs=V...  13.6 us
    ppermute x6, waiting for transfers between devices, shift(): return lax.ppermute(value, axis, [(i, (i + k) % RING) for i in range(RING)])  12.6 us
    pallas_call x1, Pallas kernels, forward(): pl.pallas_call(forward_kernel, in_specs=[HBM] * 5, out_specs=[VMEM] * 4,...  9.11 us
    ppermute x6, starting transfers between devices, shift(): return lax.ppermute(value, axis, [(i, (i + k) % RING) for i in range(RING)])  8.58 us
    all_to_all x1, starting transfers between devices, per_device(): lax.all_to_all(slots, ('z', 'x'), split_axis=0, concat_axis=0, tiled=True)  8.42 us
    all_to_all x1, waiting for transfers between devices, per_device(): lax.all_to_all(back, ('z', 'x'), split_axis=0, concat_axis=0, tiled=True)  8.18 us
    ppermute x12, waiting for transfers between devices, moved(): return lax.ppermute(value, ('section', 'z', 'x'), pairs)  7.41 us
  transfers between devices with their start and end apart: 26, of which 11 were waited for; matrix products, arithmetic and copies ran while one was open for 0% of the time, Pallas kernels for 21%

profile of v6, /device:TPU:0, one launch (start us, length us, event | category | flops | bytes accessed | tf_op | source)
XLA Modules:
  0.0 125.3 jit_solution(738364475100781732)
XLA Ops:
  0.7 9.1 %forward.1 = (bf16[128,1024]{1,0:T(8,128)(2,1)S(1)}, bf16[128,1024]{1,0:T(8,128)(2,1)S(1)}, bf16[4,32,1024]{2,1,0:T(8,128)(2,1)S(1)}, bf16[4,32,1024]{2,1,0:T(8,128)(2,1)S(1)}) custom-call(bf16[128,4096]{1,0:T(8,128)(2,1)} %bitcast.17, f32[1,4096]{1,0:T(1,128)} %gain_ref.1, bf16[128,4096]{1,0:T(8,128)(2,1)} %cot_hbm.1, bf16[4096,1024]{1,0:T(8,128)(2,1)} %bitcast.13, ...), custom_call_target="tpu_custom_call" | custom-call | flops 2147483648 | bytes 16777216 | tf_op jit(solution)/shard_map/forward/pallas_call | solution.py:188
  9.8 0.2 collective-permute-start
  10.0 0.4 collective-permute-start.1
  10.4 1.0 collective-permute-done.got_ref
  11.4 0.4 collective-permute-done.1.other_ref
  11.8 1.2 pack.1
  13.0 8.4 %all-to-all-start = ((bf16[16,16,1024]{2,1,0:T(8,128)(2,1)}), bf16[16,16,1024]{2,1,0:T(8,128)(2,1)S(1)}, u32[]{:S(2)}, u32[]{:S(2)}) async-start(bf16[16,16,1024]{2,1,0:T(8,128)(2,1)} %bitcast.3), calls=%async_computation | async-start | bytes 1048576 | tf_op jit(solution)/shard_map/all_to_all | solution.py:713
  21.4 1.9 %collective-permute-start.2 = (bf16[2,32,1024]{2,1,0:T(8,128)(2,1)S(1)}, bf16[2,32,1024]{2,1,0:T(8,128)(2,1)S(1)}, u32[]{:S(2)}, u32[]{:S(2)}) collective-permute-start(bf16[2,32,1024]{2,1,0:T(8,128)(2,1)S(1)} %get-tuple-element.43), channel_id=1, source_target_pairs={{0,4},{4,8},{8,12},{12,0},{16,20},{20,24},{24,28},{28,16},{32,36},... | collective-permute-start | bytes 393224 | tf_op jit(solution)/shard_map/ppermute | solution.py:505
  23.3 1.4 %collective-permute-start.3 = (bf16[2,32,1024]{2,1,0:T(8,128)(2,1)S(1)}, bf16[2,32,1024]{2,1,0:T(8,128)(2,1)S(1)}, u32[]{:S(2)}, u32[]{:S(2)}) collective-permute-start(bf16[2,32,1024]{2,1,0:T(8,128)(2,1)S(1)} %get-tuple-element.44), channel_id=1, source_target_pairs={{0,12},{4,0},{8,4},{12,8},{16,28},{20,16},{24,20},{28,24},{32,44},... | collective-permute-start | bytes 393224 | tf_op jit(solution)/shard_map/ppermute | solution.py:505
  24.7 2.2 %collective-permute-start.4 = (bf16[2,32,1024]{2,1,0:T(8,128)(2,1)S(1)}, bf16[2,32,1024]{2,1,0:T(8,128)(2,1)S(1)}, u32[]{:S(2)}, u32[]{:S(2)}) collective-permute-start(bf16[2,32,1024]{2,1,0:T(8,128)(2,1)S(1)} %get-tuple-element.45), channel_id=1, source_target_pairs={{0,8},{4,12},{8,0},{12,4},{16,24},{20,28},{24,16},{28,20},{32,40},... | collective-permute-start | bytes 393224 | tf_op jit(solution)/shard_map/ppermute | solution.py:505
  26.8 5.6 %collective-permute-done.2.rest_1_ = bf16[2,32,1024]{2,1,0:T(8,128)(2,1)S(1)} collective-permute-done((bf16[2,32,1024]{2,1,0:T(8,128)(2,1)S(1)}, bf16[2,32,1024]{2,1,0:T(8,128)(2,1)S(1)}, u32[]{:S(2)}, u32[]{:S(2)}) %collective-permute-start.2) | collective-permute-done | bytes 131104 | tf_op jit(solution)/shard_map/ppermute | solution.py:505
  32.4 1.7 %collective-permute-done.4.rest_3_ = bf16[2,32,1024]{2,1,0:T(8,128)(2,1)S(1)} collective-permute-done((bf16[2,32,1024]{2,1,0:T(8,128)(2,1)S(1)}, bf16[2,32,1024]{2,1,0:T(8,128)(2,1)S(1)}, u32[]{:S(2)}, u32[]{:S(2)}) %collective-permute-start.4) | collective-permute-done | bytes 131104 | tf_op jit(solution)/shard_map/ppermute | solution.py:505
  34.2 2.9 %attend.1 = (bf16[128,1024]{1,0:T(8,128)(2,1)S(1)}, bf16[256,1024]{1,0:T(8,128)(2,1)}, bf16[2,4,32,1024]{3,2,1,0:T(8,128)(2,1)S(1)}) custom-call(bf16[128,1024]{1,0:T(8,128)(2,1)S(1)} %get-tuple-element.37.keep_ref, bf16[128,1024]{1,0:T(8,128)(2,1)S(1)} %collective-permute-done.got_ref, bf16[256,1024]{1,0:T(8,128)(2,1)S(1)} %bitcast.12, ...), custom_call_target="tpu_custom_call" | custom-call | flops 805306368 | bytes 2097152 | tf_op jit(solution)/shard_map/attend/pallas_call | solution.py:299
  37.1 5.0 %all-to-all-start.1 = ((bf16[16,16,1024]{2,1,0:T(8,128)(2,1)}), bf16[16,16,1024]{2,1,0:T(8,128)(2,1)S(1)}, u32[]{:S(2)}, u32[]{:S(2)}) async-start(bf16[16,16,1024]{2,1,0:T(8,128)(2,1)} %bitcast.5), calls=%async_computation.1 | async-start | bytes 1048576 | tf_op jit(solution)/shard_map/all_to_all | solution.py:719
  42.1 1.7 %collective-permute-start.7 = (bf16[2,4,32,1024]{3,2,1,0:T(8,128)(2,1)S(1)}, bf16[2,4,32,1024]{3,2,1,0:T(8,128)(2,1)S(1)}, u32[]{:S(2)}, u32[]{:S(2)}) collective-permute-start(bf16[2,4,32,1024]{3,2,1,0:T(8,128)(2,1)S(1)} %get-tuple-element.52.refs_0_), channel_id=1, source_target_pairs={{0,1},{1,2},{2,3},{3,0},{4,5},{5,6},{6,7},{7,4},{8,9},{9,10},{10,1... | collective-permute-start | bytes 1572872 | tf_op jit(solution)/shard_map/ppermute | solution.py:486
  43.7 1.6 %collective-permute-start.8 = (bf16[2,4,32,1024]{3,2,1,0:T(8,128)(2,1)S(1)}, bf16[2,4,32,1024]{3,2,1,0:T(8,128)(2,1)S(1)}, u32[]{:S(2)}, u32[]{:S(2)}) collective-permute-start(bf16[2,4,32,1024]{3,2,1,0:T(8,128)(2,1)S(1)} %get-tuple-element.52.refs_0_), channel_id=1, source_target_pairs={{0,3},{1,0},{2,1},{3,2},{4,7},{5,4},{6,5},{7,6},{8,11},{9,8},{10,9... | collective-permute-start | bytes 1572872 | tf_op jit(solution)/shard_map/ppermute | solution.py:486
  45.4 8.2 %all-to-all-done.1 = bf16[16,16,1024]{2,1,0:T(8,128)(2,1)S(1)} async-done(((bf16[16,16,1024]{2,1,0:T(8,128)(2,1)}), bf16[16,16,1024]{2,1,0:T(8,128)(2,1)S(1)}, u32[]{:S(2)}, u32[]{:S(2)}) %all-to-all-start.1) | async-done | bytes 524320 | tf_op jit(solution)/shard_map/all_to_all | solution.py:719
  53.6 0.4 unpack.1
  54.1 1.5 %collective-permute-done.5.got_ref = bf16[128,1024]{1,0:T(8,128)(2,1)S(1)} collective-permute-done((bf16[128,1024]{1,0:T(8,128)(2,1)S(1)}, bf16[128,1024]{1,0:T(8,128)(2,1)S(1)}, u32[]{:S(2)}, u32[]{:S(2)}) %collective-permute-start.5) | collective-permute-done | bytes 262176 | tf_op jit(solution)/shard_map/ppermute | solution.py:721
  55.7 0.6 collective-permute-start.9
  56.3 2.7 %collective-permute-start.10 = (bf16[128,2048]{1,0:T(8,128)(2,1)S(1)}, bf16[128,2048]{1,0:T(8,128)(2,1)S(1)}, u32[]{:S(2)}, u32[]{:S(2)}) collective-permute-start(bf16[128,2048]{1,0:T(8,128)(2,1)S(1)} %get-tuple-element.50.rows_ref.refs_4_), channel_id=1, source_target_pairs={{0,12},{4,0},{8,4},{12,8},{16,28},{20,16},{24,20},{28,24},{32,44},... | collective-permute-start | bytes 1572872 | tf_op jit(solution)/shard_map/ppermute | solution.py:505
  59.0 1.6 %collective-permute-start.11 = (bf16[2,4,32,1024]{3,2,1,0:T(8,128)(2,1)S(1)}, bf16[2,4,32,1024]{3,2,1,0:T(8,128)(2,1)S(1)}, u32[]{:S(2)}, u32[]{:S(2)}) collective-permute-start(bf16[2,4,32,1024]{3,2,1,0:T(8,128)(2,1)S(1)} %collective-permute-done.7.refs_1_), channel_id=1, source_target_pairs={{0,1},{1,2},{2,3},{3,0},{4,5},{5,6},{6,7},{7,4},{8,9},{9,10},{10,1... | collective-permute-start | bytes 1572872 | tf_op jit(solution)/shard_map/ppermute | solution.py:486
  60.7 1.5 %collective-permute-done.6.got_ref = bf16[128,1024]{1,0:T(8,128)(2,1)S(1)} collective-permute-done((bf16[128,1024]{1,0:T(8,128)(2,1)S(1)}, bf16[128,1024]{1,0:T(8,128)(2,1)S(1)}, u32[]{:S(2)}, u32[]{:S(2)}) %collective-permute-start.6) | collective-permute-done | bytes 262176 | tf_op jit(solution)/shard_map/ppermute | solution.py:725
  62.2 13.6 %dnorm.1 = bf16[128,4096]{1,0:T(8,128)(2,1)} custom-call(bf16[128,2048]{1,0:T(8,128)(2,1)S(1)} %get-tuple-element.50.rows_ref.refs_4_, bf16[128,1024]{1,0:T(8,128)(2,1)S(1)} %collective-permute-done.6.got_ref, bf16[4096,1024]{1,0:T(8,128)(2,1)} %bitcast.14, bf16[4096,1024]{1,0:T(8,128)(2,1)} %bitcast.16), custom_call_target="tpu_custom_call" | custom-call | flops 2147483648 | bytes 16777216 | tf_op jit(solution)/shard_map/dnorm/pallas_call | solution.py:416
  75.9 0.8 copy-done.9
  76.7 0.1 copy-done.10
  76.8 0.2 copy-done.8
  77.1 0.8 copy-done.11
  77.9 3.5 %far.1 = (bf16[128,2048]{1,0:T(8,128)(2,1)}, bf16[128,2048]{1,0:T(8,128)(2,1)}, bf16[512,2048]{1,0:T(8,128)(2,1)S(1)}) custom-call(bf16[2,4,32,1024]{3,2,1,0:T(8,128)(2,1)} %copy-done, bf16[2,4,32,1024]{3,2,1,0:T(8,128)(2,1)} %copy-done.6, bf16[2,4,32,1024]{3,2,1,0:T(8,128)(2,1)} %copy-done.7, bf16[2,4,32,1024]{3,2,1,0:T(8,128)(2,1)} %copy-done.8, ...), custom_call_target="tpu_custom_call" | custom-call | flops 536870912 | bytes 8388608 | tf_op jit(solution)/shard_map/far/pallas_call | solution.py:569
  81.4 1.0 collective-permute-start.13
  82.4 2.3 %collective-permute-start.14 = (bf16[128,2048]{1,0:T(8,128)(2,1)}, bf16[128,2048]{1,0:T(8,128)(2,1)}, u32[]{:S(2)}, u32[]{:S(2)}) collective-permute-start(bf16[128,2048]{1,0:T(8,128)(2,1)} %get-tuple-element.60), channel_id=1, source_target_pairs={{0,48},{4,52},{8,56},{12,60},{16,0},{20,4},{24,8},{28,12},{32,16},... | collective-permute-start | bytes 1572872 | tf_op jit(solution)/shard_map/ppermute | solution.py:505
  84.7 4.2 %all-to-all-start.2 = ((bf16[4,32,4096]{2,1,0:T(8,128)(2,1)}), bf16[4,32,4096]{2,1,0:T(8,128)(2,1)S(1)}, u32[]{:S(2)}, u32[]{:S(2)}) async-start(bf16[4,32,4096]{2,1,0:T(8,128)(2,1)} %bitcast.7), calls=%async_computation.2 | async-start | bytes 2097152 | tf_op jit(solution)/shard_map/all_to_all | solution.py:729
  88.9 3.1 %middle.1 = (bf16[256,1024]{1,0:T(8,128)(2,1)}, bf16[256,1024]{1,0:T(8,128)(2,1)}) custom-call(bf16[2,4,32,1024]{3,2,1,0:T(8,128)(2,1)} %copy-done, bf16[2,4,32,1024]{3,2,1,0:T(8,128)(2,1)} %copy-done.6, bf16[2,4,32,1024]{3,2,1,0:T(8,128)(2,1)} %copy-done.7, bf16[2,4,32,1024]{3,2,1,0:T(8,128)(2,1)} %copy-done.8, bf16[512,2048]{1,0:T(8,128)(2,1)S(1)} %get-tuple-element.62.refs_4_), custom_call_target="tpu_custom_call" | custom-call | flops 536870912 | bytes 4194304 | tf_op jit(solution)/shard_map/middle/pallas_call | solution.py:633
  92.0 0.1 collective-permute-start.18
  92.1 0.1 collective-permute-done.13.refs_5_
  92.2 5.1 %side.1 = (bf16[256,1024]{1,0:T(8,128)(2,1)}, bf16[256,1024]{1,0:T(8,128)(2,1)}, bf16[256,1024]{1,0:T(8,128)(2,1)}, bf16[256,1024]{1,0:T(8,128)(2,1)}) custom-call(bf16[2,4,32,1024]{3,2,1,0:T(8,128)(2,1)} %copy-done, bf16[2,4,32,1024]{3,2,1,0:T(8,128)(2,1)} %copy-done.6, bf16[2,4,32,1024]{3,2,1,0:T(8,128)(2,1)} %copy-done.7, ...), custom_call_target="tpu_custom_call" | custom-call | flops 1073741824 | bytes 4194304 | tf_op jit(solution)/shard_map/side/pallas_call | solution.py:605
  97.3 1.3 %collective-permute-start.19 = (bf16[256,1024]{1,0:T(8,128)(2,1)}, bf16[256,1024]{1,0:T(8,128)(2,1)S(1)}, u32[]{:S(2)}, u32[]{:S(2)}) collective-permute-start(bf16[256,1024]{1,0:T(8,128)(2,1)} %get-tuple-element.65), channel_id=1, source_target_pairs={{0,16},{4,20},{8,24},{12,28},{16,32},{20,36},{24,40},{28,44},{32,4... | collective-permute-start | bytes 1572872 | tf_op jit(solution)/shard_map/ppermute | solution.py:505
  98.6 2.1 %collective-permute-start.20 = (bf16[256,1024]{1,0:T(8,128)(2,1)}, bf16[256,1024]{1,0:T(8,128)(2,1)S(1)}, u32[]{:S(2)}, u32[]{:S(2)}) collective-permute-start(bf16[256,1024]{1,0:T(8,128)(2,1)} %get-tuple-element.66), channel_id=1, source_target_pairs={{0,48},{4,52},{8,56},{12,60},{16,0},{20,4},{24,8},{28,12},{32,16},... | collective-permute-start | bytes 1572872 | tf_op jit(solution)/shard_map/ppermute | solution.py:505
  100.7 2.5 %collective-permute-start.22 = (bf16[256,1024]{1,0:T(8,128)(2,1)}, bf16[256,1024]{1,0:T(8,128)(2,1)S(1)}, u32[]{:S(2)}, u32[]{:S(2)}) collective-permute-start(bf16[256,1024]{1,0:T(8,128)(2,1)} %get-tuple-element.68), channel_id=1, source_target_pairs={{0,112},{4,116},{8,120},{12,124},{16,64},{20,68},{24,72},{28,76},{... | collective-permute-start | bytes 1572872 | tf_op jit(solution)/shard_map/ppermute | solution.py:505
  103.2 1.2 rms_back.1.refs_0_
  104.4 1.6 %collective-permute-start.15 = (bf16[32,4096]{1,0:T(8,128)(2,1)S(1)}, bf16[32,4096]{1,0:T(8,128)(2,1)S(1)}, u32[]{:S(2)}, u32[]{:S(2)}) collective-permute-start(bf16[32,4096]{1,0:T(8,128)(2,1)S(1)} %rms_back.1.refs_0_), channel_id=1, source_target_pairs={{0,1},{1,2},{2,3},{3,0},{4,5},{5,6},{6,7},{7,4},{8,9},{9,10},{10,1... | collective-permute-start | bytes 786440 | tf_op jit(solution)/shard_map/ppermute | solution.py:486
  106.0 7.5 %collective-permute-done.15.refs_1_ = bf16[32,4096]{1,0:T(8,128)(2,1)S(1)} collective-permute-done((bf16[32,4096]{1,0:T(8,128)(2,1)S(1)}, bf16[32,4096]{1,0:T(8,128)(2,1)S(1)}, u32[]{:S(2)}, u32[]{:S(2)}) %collective-permute-start.15) | collective-permute-done | bytes 262176 | tf_op jit(solution)/shard_map/ppermute | solution.py:486
  113.5 1.7 %collective-permute-start.16 = (bf16[32,4096]{1,0:T(8,128)(2,1)S(1)}, bf16[32,4096]{1,0:T(8,128)(2,1)S(1)}, u32[]{:S(2)}, u32[]{:S(2)}) collective-permute-start(bf16[32,4096]{1,0:T(8,128)(2,1)S(1)} %rms_back.1.refs_0_), channel_id=1, source_target_pairs={{0,3},{1,0},{2,1},{3,2},{4,7},{5,4},{6,5},{7,6},{8,11},{9,8},{10,9... | collective-permute-start | bytes 786440 | tf_op jit(solution)/shard_map/ppermute | solution.py:486
  115.3 0.3 collective-permute-start.17
  115.6 3.4 %own.1 = (f32[256,1024]{1,0:T(8,128)}, f32[256,1024]{1,0:T(8,128)}) custom-call(bf16[256,1024]{1,0:T(8,128)(2,1)} %get-tuple-element.63.own_hbm, bf16[256,1024]{1,0:T(8,128)(2,1)} %collective-permute-done.18.other_ref, bf16[256,1024]{1,0:T(8,128)(2,1)S(1)} %collective-permute-done.19.refs_0_, bf16[256,1024]{1,0:T(8,128)(2,1)S(1)} %collective-permute-done.20.refs_1_, ...), custom_call_target="tpu_custom_call" | custom-call | flops 1048576 | bytes 5242880 | tf_op jit(solution)/shard_map/own/pallas_call | solution.py:686
  119.0 1.7 %collective-permute-done.16.refs_2_ = bf16[32,4096]{1,0:T(8,128)(2,1)S(1)} collective-permute-done((bf16[32,4096]{1,0:T(8,128)(2,1)S(1)}, bf16[32,4096]{1,0:T(8,128)(2,1)S(1)}, u32[]{:S(2)}, u32[]{:S(2)}) %collective-permute-start.16) | collective-permute-done | bytes 262176 | tf_op jit(solution)/shard_map/ppermute | solution.py:486
  120.7 3.4 %collective-permute-done.17.refs_3_ = bf16[32,4096]{1,0:T(8,128)(2,1)S(1)} collective-permute-done((bf16[32,4096]{1,0:T(8,128)(2,1)S(1)}, bf16[32,4096]{1,0:T(8,128)(2,1)S(1)}, u32[]{:S(2)}, u32[]{:S(2)}) %collective-permute-start.17) | collective-permute-done | bytes 262176 | tf_op jit(solution)/shard_map/ppermute | solution.py:486
  124.1 1.0 place.1
  (40 shorter events, 0.3 us)
Async XLA Ops:
  0.6 11.1 %copy-start.3 = (s32[16,16]{1,0:T(8,128)S(1)}, s32[16,16]{1,0:T(8,128)}, u32[]{:S(2)}) copy-start(s32[16,16]{1,0:T(8,128)} %src_ref.5) | copy-start | bytes 3076
  0.6 11.1 %copy-start.4 = (s32[16,16]{1,0:T(8,128)S(1)}, s32[16,16]{1,0:T(8,128)}, u32[]{:S(2)}) copy-start(s32[16,16]{1,0:T(8,128)} %dest_ref.5) | copy-start | bytes 3076
  0.7 33.5 %copy-start.5 = (s32[16,16]{1,0:T(8,128)S(1)}, s32[16,16]{1,0:T(8,128)}, u32[]{:S(2)}) copy-start(s32[16,16]{1,0:T(8,128)} %tgt_ref.1) | copy-start | bytes 3076
  9.8 1.6 %collective-permute-start = (bf16[128,1024]{1,0:T(8,128)(2,1)S(1)}, bf16[128,1024]{1,0:T(8,128)(2,1)S(1)}, u32[]{:S(2)}, u32[]{:S(2)}) collective-permute-start(bf16[128,1024]{1,0:T(8,128)(2,1)S(1)} %get-tuple-element.38), channel_id=1, source_target_pairs={{0,64},{64,0},{1,65},{65,1},{2,66},{66,2},{3,67},{67,3},{4,68},{68... | collective-permute-start | bytes 786440 | tf_op jit(solution)/shard_map/ppermute | solution.py:709
  10.0 1.8 %collective-permute-start.1 = (bf16[4,32,1024]{2,1,0:T(8,128)(2,1)S(1)}, bf16[4,32,1024]{2,1,0:T(8,128)(2,1)S(1)}, u32[]{:S(2)}, u32[]{:S(2)}) collective-permute-start(bf16[4,32,1024]{2,1,0:T(8,128)(2,1)S(1)} %get-tuple-element.40), channel_id=1, source_target_pairs={{0,64},{64,0},{1,65},{65,1},{2,66},{66,2},{3,67},{67,3},{4,68},{68... | collective-permute-start | bytes 786440 | tf_op jit(solution)/shard_map/ppermute | solution.py:710
  13.0 21.2 %all-to-all-start = ((bf16[16,16,1024]{2,1,0:T(8,128)(2,1)}), bf16[16,16,1024]{2,1,0:T(8,128)(2,1)S(1)}, u32[]{:S(2)}, u32[]{:S(2)}) async-start(bf16[16,16,1024]{2,1,0:T(8,128)(2,1)} %bitcast.3), calls=%async_computation | async-start | bytes 1048576 | tf_op jit(solution)/shard_map/all_to_all | solution.py:713
  21.4 11.0 %collective-permute-start.2 = (bf16[2,32,1024]{2,1,0:T(8,128)(2,1)S(1)}, bf16[2,32,1024]{2,1,0:T(8,128)(2,1)S(1)}, u32[]{:S(2)}, u32[]{:S(2)}) collective-permute-start(bf16[2,32,1024]{2,1,0:T(8,128)(2,1)S(1)} %get-tuple-element.43), channel_id=1, source_target_pairs={{0,4},{4,8},{8,12},{12,0},{16,20},{20,24},{24,28},{28,16},{32,36},... | collective-permute-start | bytes 393224 | tf_op jit(solution)/shard_map/ppermute | solution.py:505
  23.3 9.1 %collective-permute-start.3 = (bf16[2,32,1024]{2,1,0:T(8,128)(2,1)S(1)}, bf16[2,32,1024]{2,1,0:T(8,128)(2,1)S(1)}, u32[]{:S(2)}, u32[]{:S(2)}) collective-permute-start(bf16[2,32,1024]{2,1,0:T(8,128)(2,1)S(1)} %get-tuple-element.44), channel_id=1, source_target_pairs={{0,12},{4,0},{8,4},{12,8},{16,28},{20,16},{24,20},{28,24},{32,44},... | collective-permute-start | bytes 393224 | tf_op jit(solution)/shard_map/ppermute | solution.py:505
  24.7 9.4 %collective-permute-start.4 = (bf16[2,32,1024]{2,1,0:T(8,128)(2,1)S(1)}, bf16[2,32,1024]{2,1,0:T(8,128)(2,1)S(1)}, u32[]{:S(2)}, u32[]{:S(2)}) collective-permute-start(bf16[2,32,1024]{2,1,0:T(8,128)(2,1)S(1)} %get-tuple-element.45), channel_id=1, source_target_pairs={{0,8},{4,12},{8,0},{12,4},{16,24},{20,28},{24,16},{28,20},{32,40},... | collective-permute-start | bytes 393224 | tf_op jit(solution)/shard_map/ppermute | solution.py:505
  37.1 38.7 %copy-start = (bf16[2,4,32,1024]{3,2,1,0:T(8,128)(2,1)}, bf16[2,4,32,1024]{3,2,1,0:T(8,128)(2,1)S(1)}, u32[]{:S(2)}) copy-start(bf16[2,4,32,1024]{3,2,1,0:T(8,128)(2,1)S(1)} %get-tuple-element.52.refs_0_) | copy-start | bytes 1572868
  37.1 16.5 %all-to-all-start.1 = ((bf16[16,16,1024]{2,1,0:T(8,128)(2,1)}), bf16[16,16,1024]{2,1,0:T(8,128)(2,1)S(1)}, u32[]{:S(2)}, u32[]{:S(2)}) async-start(bf16[16,16,1024]{2,1,0:T(8,128)(2,1)} %bitcast.5), calls=%async_computation.1 | async-start | bytes 1048576 | tf_op jit(solution)/shard_map/all_to_all | solution.py:719
  42.1 16.9 %collective-permute-start.7 = (bf16[2,4,32,1024]{3,2,1,0:T(8,128)(2,1)S(1)}, bf16[2,4,32,1024]{3,2,1,0:T(8,128)(2,1)S(1)}, u32[]{:S(2)}, u32[]{:S(2)}) collective-permute-start(bf16[2,4,32,1024]{3,2,1,0:T(8,128)(2,1)S(1)} %get-tuple-element.52.refs_0_), channel_id=1, source_target_pairs={{0,1},{1,2},{2,3},{3,0},{4,5},{5,6},{6,7},{7,4},{8,9},{9,10},{10,1... | collective-permute-start | bytes 1572872 | tf_op jit(solution)/shard_map/ppermute | solution.py:486
  43.7 16.8 %collective-permute-start.8 = (bf16[2,4,32,1024]{3,2,1,0:T(8,128)(2,1)S(1)}, bf16[2,4,32,1024]{3,2,1,0:T(8,128)(2,1)S(1)}, u32[]{:S(2)}, u32[]{:S(2)}) collective-permute-start(bf16[2,4,32,1024]{3,2,1,0:T(8,128)(2,1)S(1)} %get-tuple-element.52.refs_0_), channel_id=1, source_target_pairs={{0,3},{1,0},{2,1},{3,2},{4,7},{5,4},{6,5},{7,6},{8,11},{9,8},{10,9... | collective-permute-start | bytes 1572872 | tf_op jit(solution)/shard_map/ppermute | solution.py:486
  54.0 1.6 %collective-permute-start.5 = (bf16[128,1024]{1,0:T(8,128)(2,1)S(1)}, bf16[128,1024]{1,0:T(8,128)(2,1)S(1)}, u32[]{:S(2)}, u32[]{:S(2)}) collective-permute-start(bf16[128,1024]{1,0:T(8,128)(2,1)S(1)} %get-tuple-element.49), channel_id=1, source_target_pairs={{0,64},{64,0},{1,65},{65,1},{2,66},{66,2},{3,67},{67,3},{4,68},{68... | collective-permute-start | bytes 786440 | tf_op jit(solution)/shard_map/ppermute | solution.py:721
  55.7 20.2 %copy-start.1 = (bf16[128,2048]{1,0:T(8,128)(2,1)}, bf16[128,2048]{1,0:T(8,128)(2,1)S(1)}, u32[]{:S(2)}) copy-start(bf16[128,2048]{1,0:T(8,128)(2,1)S(1)} %get-tuple-element.50.rows_ref.refs_4_) | copy-start | bytes 1572868
  55.7 20.2 %collective-permute-start.9 = (bf16[128,2048]{1,0:T(8,128)(2,1)S(1)}, bf16[128,2048]{1,0:T(8,128)(2,1)S(1)}, u32[]{:S(2)}, u32[]{:S(2)}) collective-permute-start(bf16[128,2048]{1,0:T(8,128)(2,1)S(1)} %get-tuple-element.50.rows_ref.refs_4_), channel_id=1, source_target_pairs={{0,4},{4,8},{8,12},{12,0},{16,20},{20,24},{24,28},{28,16},{32,36},... | collective-permute-start | bytes 1572872 | tf_op jit(solution)/shard_map/ppermute | solution.py:505
  56.3 19.6 %collective-permute-start.10 = (bf16[128,2048]{1,0:T(8,128)(2,1)S(1)}, bf16[128,2048]{1,0:T(8,128)(2,1)S(1)}, u32[]{:S(2)}, u32[]{:S(2)}) collective-permute-start(bf16[128,2048]{1,0:T(8,128)(2,1)S(1)} %get-tuple-element.50.rows_ref.refs_4_), channel_id=1, source_target_pairs={{0,12},{4,0},{8,4},{12,8},{16,28},{20,16},{24,20},{28,24},{32,44},... | collective-permute-start | bytes 1572872 | tf_op jit(solution)/shard_map/ppermute | solution.py:505
  59.0 16.9 %copy-start.6 = (bf16[2,4,32,1024]{3,2,1,0:T(8,128)(2,1)}, bf16[2,4,32,1024]{3,2,1,0:T(8,128)(2,1)S(1)}, u32[]{:S(2)}) copy-start(bf16[2,4,32,1024]{3,2,1,0:T(8,128)(2,1)S(1)} %collective-permute-done.7.refs_1_) | copy-start | bytes 1572868
  59.0 16.9 %collective-permute-start.11 = (bf16[2,4,32,1024]{3,2,1,0:T(8,128)(2,1)S(1)}, bf16[2,4,32,1024]{3,2,1,0:T(8,128)(2,1)S(1)}, u32[]{:S(2)}, u32[]{:S(2)}) collective-permute-start(bf16[2,4,32,1024]{3,2,1,0:T(8,128)(2,1)S(1)} %collective-permute-done.7.refs_1_), channel_id=1, source_target_pairs={{0,1},{1,2},{2,3},{3,0},{4,5},{5,6},{6,7},{7,4},{8,9},{9,10},{10,1... | collective-permute-start | bytes 1572872 | tf_op jit(solution)/shard_map/ppermute | solution.py:486
  60.6 15.3 %collective-permute-start.12 = (bf16[128,2048]{1,0:T(8,128)(2,1)S(1)}, bf16[128,2048]{1,0:T(8,128)(2,1)S(1)}, u32[]{:S(2)}, u32[]{:S(2)}) collective-permute-start(bf16[128,2048]{1,0:T(8,128)(2,1)S(1)} %get-tuple-element.50.rows_ref.refs_4_), channel_id=1, source_target_pairs={{0,8},{4,12},{8,0},{12,4},{16,24},{20,28},{24,16},{28,20},{32,40},... | collective-permute-start | bytes 1572872 | tf_op jit(solution)/shard_map/ppermute | solution.py:505
  60.6 15.3 %copy-start.7 = (bf16[2,4,32,1024]{3,2,1,0:T(8,128)(2,1)}, bf16[2,4,32,1024]{3,2,1,0:T(8,128)(2,1)S(1)}, u32[]{:S(2)}) copy-start(bf16[2,4,32,1024]{3,2,1,0:T(8,128)(2,1)S(1)} %collective-permute-done.8.refs_2_) | copy-start | bytes 1572868
  60.6 1.6 %collective-permute-start.6 = (bf16[128,1024]{1,0:T(8,128)(2,1)S(1)}, bf16[128,1024]{1,0:T(8,128)(2,1)S(1)}, u32[]{:S(2)}, u32[]{:S(2)}) collective-permute-start(bf16[128,1024]{1,0:T(8,128)(2,1)S(1)} %get-tuple-element.51), channel_id=1, source_target_pairs={{0,64},{64,0},{1,65},{65,1},{2,66},{66,2},{3,67},{67,3},{4,68},{68... | collective-permute-start | bytes 786440 | tf_op jit(solution)/shard_map/ppermute | solution.py:725
  75.8 27.3 %copy-start.2 = (f32[1,4096]{1,0:T(1,128)S(1)}, f32[1,4096]{1,0:T(1,128)}, u32[]{:S(2)}) copy-start(f32[1,4096]{1,0:T(1,128)} %gain_ref.1) | copy-start | bytes 49156
  75.9 0.8 copy-start.9
  75.9 0.9 copy-start.10
  75.9 1.2 copy-start.8
  77.1 0.8 copy-start.11
  81.4 10.8 %collective-permute-start.13 = (bf16[128,2048]{1,0:T(8,128)(2,1)}, bf16[128,2048]{1,0:T(8,128)(2,1)}, u32[]{:S(2)}, u32[]{:S(2)}) collective-permute-start(bf16[128,2048]{1,0:T(8,128)(2,1)} %get-tuple-element.59), channel_id=1, source_target_pairs={{0,16},{4,20},{8,24},{12,28},{16,32},{20,36},{24,40},{28,44},{32,4... | collective-permute-start | bytes 1572872 | tf_op jit(solution)/shard_map/ppermute | solution.py:505
  82.4 9.7 %collective-permute-start.14 = (bf16[128,2048]{1,0:T(8,128)(2,1)}, bf16[128,2048]{1,0:T(8,128)(2,1)}, u32[]{:S(2)}, u32[]{:S(2)}) collective-permute-start(bf16[128,2048]{1,0:T(8,128)(2,1)} %get-tuple-element.60), channel_id=1, source_target_pairs={{0,48},{4,52},{8,56},{12,60},{16,0},{20,4},{24,8},{28,12},{32,16},... | collective-permute-start | bytes 1572872 | tf_op jit(solution)/shard_map/ppermute | solution.py:505
  84.7 18.5 %all-to-all-start.2 = ((bf16[4,32,4096]{2,1,0:T(8,128)(2,1)}), bf16[4,32,4096]{2,1,0:T(8,128)(2,1)S(1)}, u32[]{:S(2)}, u32[]{:S(2)}) async-start(bf16[4,32,4096]{2,1,0:T(8,128)(2,1)} %bitcast.7), calls=%async_computation.2 | async-start | bytes 2097152 | tf_op jit(solution)/shard_map/all_to_all | solution.py:729
  92.0 12.4 %collective-permute-start.18 = (bf16[256,1024]{1,0:T(8,128)(2,1)}, bf16[256,1024]{1,0:T(8,128)(2,1)}, u32[]{:S(2)}, u32[]{:S(2)}) collective-permute-start(bf16[256,1024]{1,0:T(8,128)(2,1)} %get-tuple-element.64), channel_id=1, source_target_pairs={{0,64},{64,0},{1,65},{65,1},{2,66},{66,2},{3,67},{67,3},{4,68},{68... | collective-permute-start | bytes 1572872 | tf_op jit(solution)/shard_map/ppermute | solution.py:745
  97.3 18.0 %collective-permute-start.19 = (bf16[256,1024]{1,0:T(8,128)(2,1)}, bf16[256,1024]{1,0:T(8,128)(2,1)S(1)}, u32[]{:S(2)}, u32[]{:S(2)}) collective-permute-start(bf16[256,1024]{1,0:T(8,128)(2,1)} %get-tuple-element.65), channel_id=1, source_target_pairs={{0,16},{4,20},{8,24},{12,28},{16,32},{20,36},{24,40},{28,44},{32,4... | collective-permute-start | bytes 1572872 | tf_op jit(solution)/shard_map/ppermute | solution.py:505
  98.6 17.0 %collective-permute-start.20 = (bf16[256,1024]{1,0:T(8,128)(2,1)}, bf16[256,1024]{1,0:T(8,128)(2,1)S(1)}, u32[]{:S(2)}, u32[]{:S(2)}) collective-permute-start(bf16[256,1024]{1,0:T(8,128)(2,1)} %get-tuple-element.66), channel_id=1, source_target_pairs={{0,48},{4,52},{8,56},{12,60},{16,0},{20,4},{24,8},{28,12},{32,16},... | collective-permute-start | bytes 1572872 | tf_op jit(solution)/shard_map/ppermute | solution.py:505
  100.7 14.9 %collective-permute-start.21 = (bf16[256,1024]{1,0:T(8,128)(2,1)}, bf16[256,1024]{1,0:T(8,128)(2,1)S(1)}, u32[]{:S(2)}, u32[]{:S(2)}) collective-permute-start(bf16[256,1024]{1,0:T(8,128)(2,1)} %get-tuple-element.67), channel_id=1, source_target_pairs={{0,80},{4,84},{8,88},{12,92},{16,96},{20,100},{24,104},{28,108},{3... | collective-permute-start | bytes 1572872 | tf_op jit(solution)/shard_map/ppermute | solution.py:505
  100.7 14.9 %collective-permute-start.22 = (bf16[256,1024]{1,0:T(8,128)(2,1)}, bf16[256,1024]{1,0:T(8,128)(2,1)S(1)}, u32[]{:S(2)}, u32[]{:S(2)}) collective-permute-start(bf16[256,1024]{1,0:T(8,128)(2,1)} %get-tuple-element.68), channel_id=1, source_target_pairs={{0,112},{4,116},{8,120},{12,124},{16,64},{20,68},{24,72},{28,76},{... | collective-permute-start | bytes 1572872 | tf_op jit(solution)/shard_map/ppermute | solution.py:505
  104.4 9.2 %collective-permute-start.15 = (bf16[32,4096]{1,0:T(8,128)(2,1)S(1)}, bf16[32,4096]{1,0:T(8,128)(2,1)S(1)}, u32[]{:S(2)}, u32[]{:S(2)}) collective-permute-start(bf16[32,4096]{1,0:T(8,128)(2,1)S(1)} %rms_back.1.refs_0_), channel_id=1, source_target_pairs={{0,1},{1,2},{2,3},{3,0},{4,5},{5,6},{6,7},{7,4},{8,9},{9,10},{10,1... | collective-permute-start | bytes 786440 | tf_op jit(solution)/shard_map/ppermute | solution.py:486
  113.5 7.2 %collective-permute-start.16 = (bf16[32,4096]{1,0:T(8,128)(2,1)S(1)}, bf16[32,4096]{1,0:T(8,128)(2,1)S(1)}, u32[]{:S(2)}, u32[]{:S(2)}) collective-permute-start(bf16[32,4096]{1,0:T(8,128)(2,1)S(1)} %rms_back.1.refs_0_), channel_id=1, source_target_pairs={{0,3},{1,0},{2,1},{3,2},{4,7},{5,4},{6,5},{7,6},{8,11},{9,8},{10,9... | collective-permute-start | bytes 786440 | tf_op jit(solution)/shard_map/ppermute | solution.py:486
  115.3 8.8 %collective-permute-start.17 = (bf16[32,4096]{1,0:T(8,128)(2,1)S(1)}, bf16[32,4096]{1,0:T(8,128)(2,1)S(1)}, u32[]{:S(2)}, u32[]{:S(2)}) collective-permute-start(bf16[32,4096]{1,0:T(8,128)(2,1)S(1)} %collective-permute-done.15.refs_1_), channel_id=1, source_target_pairs={{0,1},{1,2},{2,3},{3,0},{4,5},{5,6},{6,7},{7,4},{8,9},{9,10},{10,1... | collective-permute-start | bytes 786440 | tf_op jit(solution)/shard_map/ppermute | solution.py:486

commit v7 on v6

--- a/solution.py
+++ b/solution.py
@@ -14,6 +14,7 @@
 QUARTER = TOK // RING
 ORDER = (0, 3, 1, 2)
 EPS = 1e-06
+SHARE = 16
 F32 = jnp.float32
 BF16 = jnp.bfloat16
 VMEM = pl.BlockSpec(memory_space=pltpu.VMEM)
@@ -38,7 +39,7 @@
 
 
 def cost(flops, nbytes):
-    return pl.CostEstimate(flops=flops, bytes_accessed=nbytes, transcendentals=0)
+    return pl.CostEstimate(flops=flops // SHARE, bytes_accessed=nbytes // SHARE, transcendentals=0)
 
 
 def params(mib=12, **more):
@@ -375,9 +376,12 @@
     )(keep, got)
 
 
-def dnorm_kernel(rows_ref, got_ref, a_hbm, b_hbm, out_ref, a_buf, b_buf, a_sem, b_sem):
+def dnorm_kernel(rows_ref, got_ref, a_hbm, b_hbm, out_hbm, a_buf, b_buf, out_buf, a_sem, b_sem, out_sem):
     count, step, cols = a_buf.shape
     core = lax.axis_index("section")
+
+    def nt(left, right):
+        return lax.dot_general(left, right, (((1,), (1,)), ((), ())), preferred_element_type=F32)
 
     def fetches(hbm, buf, sem):
         return [
@@ -387,26 +391,33 @@
 
     get_a, get_b = fetches(a_hbm, a_buf, a_sem), fetches(b_hbm, b_buf, b_sem)
 
-    def products(terms):
+    def put(k):
+        at = slice(k * step, (k + 1) * step)
+        return pltpu.make_async_copy(out_buf.at[:, at], out_hbm.at[:, at], out_sem.at[k])
+
+    @pl.when(core == 0)
+    def _():
         for k in range(count):
-            for copies, _, _ in terms:
-                copies[k].start()
-        turned = [rows.T for _, _, rows in terms]
+            get_a[k].start()
+            get_b[k].start()
         for k in range(count):
-            block = None
-            for (copies, weight, _), right in zip(terms, turned, strict=True):
-                copies[k].wait()
-                part = jnp.dot(weight[k], right, preferred_element_type=F32)
-                block = part if block is None else block + part
-            out_ref[:, k * step : (k + 1) * step] = block.T.astype(BF16)
-
-    @pl.when(core == 0)
-    def _():
-        products([(get_a, a_buf, rows_ref[:, :cols]), (get_b, b_buf, got_ref[...])])
+            get_a[k].wait()
+            get_b[k].wait()
+            block = nt(rows_ref[:, :cols], a_buf[k]) + nt(got_ref[...], b_buf[k])
+            out_buf[:, k * step : (k + 1) * step] = block.astype(BF16)
+            put(k).start()
 
     @pl.when(core != 0)
     def _():
-        products([(get_a, a_buf, got_ref[...])])
+        for k in range(count):
+            get_a[k].start()
+        for k in range(count):
+            get_a[k].wait()
+            out_buf[:, k * step : (k + 1) * step] = nt(got_ref[...], a_buf[k]).astype(BF16)
+            put(k).start()
+
+    for k in range(count):
+        put(k).wait()
 
 
 def dnorm_partial(rows, got, weight_a, weight_b):
@@ -416,10 +427,11 @@
     return pl.pallas_call(
         dnorm_kernel,
         in_specs=[VMEM] * 2 + [HBM] * 2,
-        out_specs=VMEM,
-        out_shape=jax.ShapeDtypeStruct((TOK, width), BF16),
+        out_specs=HBM,
+        out_shape=pltpu.HBM((TOK, width), BF16),
         scratch_shapes=[pltpu.VMEM((count, step, cols), BF16)] * 2
-        + [pltpu.SemaphoreType.DMA((count,))] * 2,
+        + [pltpu.VMEM((TOK, width), BF16)]
+        + [pltpu.SemaphoreType.DMA((count,))] * 3,
         compiler_params=params(24),
         cost_estimate=cost(4 * TOK * width * cols, 4 * width * cols),
         name="dnorm",
@@ -487,8 +499,8 @@
 
 
 def gathered(block, axis):
-    left = shift(block, axis, 1)
-    return [block, left, shift(block, axis, 3), shift(left, axis, 1)]
+    left, right = lax.optimization_barrier((shift(block, axis, 1), shift(block, axis, 3)))
+    return [block, left, right, shift(left, axis, 1)]
 
 
 def moved(value, k, along, across=False):
@@ -544,15 +556,10 @@
 
 def far_kernel(*refs):
     lefts, pieces = refs[:RING], refs[RING : 2 * RING]
-    top_ref, low_ref, rows_ref, buf, sems, row_sems = refs[2 * RING :]
-    gets = [
-        pltpu.make_async_copy(piece, rows_ref.at[pl.ds(i * TOK, TOK), :], row_sems.at[i])
-        for i, piece in enumerate(pieces)
-    ]
-    for get in gets:
-        get.start()
+    top_ref, low_ref, rows_ref, buf, sems = refs[2 * RING :]
     loads = left_loads(lefts, buf, sems, (2,))
-    wait_all(gets)
+    for i, piece in enumerate(pieces):
+        rows_ref[i * TOK : (i + 1) * TOK, :] = piece[...]
     half, cols = top_ref.shape[0], top_ref.shape[1] // 2
     for m in range(2):
         at = slice(m * cols, (m + 1) * cols)
@@ -568,14 +575,14 @@
     half = jax.ShapeDtypeStruct((block // 2, cols), BF16)
     return pl.pallas_call(
         far_kernel,
-        in_specs=[HBM] * (2 * RING),
+        in_specs=[HBM] * RING + [VMEM] * RING,
         out_specs=[VMEM] * 3,
         out_shape=[half, half, jax.ShapeDtypeStruct((RING * rows, cols), BF16)],
-        scratch_shapes=left_scratch(block, 1) + [pltpu.SemaphoreType.DMA((RING,))],
+        scratch_shapes=left_scratch(block, 1),
         compiler_params=params(),
         cost_estimate=cost(2 * RING * rows * block * cols, 8 * RING * rows * cols),
         name="far",
-    )(*[in_hbm(value) for value in (*lefts, *pieces)])
+    )(*[in_hbm(left) for left in lefts], *pieces)
 
 
 def side_kernel(*refs):
@@ -615,16 +622,17 @@
 
 
 def middle_kernel(*refs):
-    lefts, (rows_ref, own_hbm, other_ref, own_ref, buf, sems, out_sem) = refs[:RING], refs[RING:]
+    lefts, (rows_ref, own_hbm, other_hbm, out_buf, buf, sems, out_sems) = refs[:RING], refs[RING:]
     loads = left_loads(lefts, buf, sems, (0,))
-    cols = own_ref.shape[1]
-    wait_all(loads[0][0])
-    own_ref[...] = tn(flat(buf[0, 0]), rows_ref[:, :cols]).astype(BF16)
-    put = pltpu.make_async_copy(own_ref, own_hbm, out_sem)
-    put.start()
-    wait_all(loads[1][0])
-    other_ref[...] = tn(flat(buf[1, 0]), rows_ref[:, cols:]).astype(BF16)
-    put.wait()
+    cols = out_buf.shape[2]
+    puts = []
+    for m, out in enumerate((own_hbm, other_hbm)):
+        wait_all(loads[m][0])
+        at = slice(m * cols, (m + 1) * cols)
+        out_buf[m] = tn(flat(buf[m, 0]), rows_ref[:, at]).astype(BF16)
+        puts.append(pltpu.make_async_copy(out_buf.at[m], out, out_sems.at[m]))
+        puts[-1].start()
+    wait_all(puts)
 
 
 def middle_blocks(lefts, rows):
@@ -633,14 +641,11 @@
     return pl.pallas_call(
         middle_kernel,
         in_specs=[HBM] * RING + [VMEM],
-        out_specs=[HBM, VMEM],
-        out_shape=[
-            pltpu.HBM((block, cols // 2), BF16),
-            jax.ShapeDtypeStruct((block, cols // 2), BF16),
-        ],
-        scratch_shapes=[pltpu.VMEM((block, cols // 2), BF16)]
+        out_specs=[HBM] * 2,
+        out_shape=[pltpu.HBM((block, cols // 2), BF16)] * 2,
+        scratch_shapes=[pltpu.VMEM((2, block, cols // 2), BF16)]
         + left_scratch(block, 1)
-        + [pltpu.SemaphoreType.DMA],
+        + [pltpu.SemaphoreType.DMA((2,))],
         compiler_params=params(),
         cost_estimate=cost(2 * depth * block * cols, 4 * depth * cols),
         name="middle",
@@ -734,6 +739,7 @@
     parts, _, _ = lax.optimization_barrier((parts, from_left, from_right))
     right, right_other, left, left_other = side_blocks(lefts, stack, from_left, from_right)
     own, own_other = middle_blocks(lefts, stack)
+    own_other, _ = lax.optimization_barrier((own_other, right))
     sums = [
         moved(right, 1, REDUCE),
         moved(left, 3, REDUCE),

time: 126 us -> 117 us (0.929)
  Pallas kernels: 44.6 us -> 35.1 us
  starting transfers between devices: 44.9 us -> 46.2 us
    ppermute x12, waiting for transfers between devices: 7.41 us -> 19.6 us  [moved(): return lax.ppermute(value, ('section', 'z', 'x'), pairs)]
    ppermute x6, waiting for transfers between devices: 12.6 us -> 1.85 us  [shift(): return lax.ppermute(value, axis, [(i, (i + k) % RING) for i in range(RING)])]
    pallas_call x2, Pallas kernels: 17.1 us -> 11 us  [the longest x1 9.08 us: dnorm_partial(): pl.pallas_call(dnorm_kernel, in_specs=[VMEM] * 2 + [HBM] * 2, out_specs=H...]
    pallas_call x1, Pallas kernels: 5.11 us -> 2.94 us  [side_blocks(): pl.pallas_call(side_kernel, in_specs=[HBM] * RING + [VMEM] * 3, out_specs...]
    ppermute x1, waiting for transfers between devices: 1.52 us -> 0.01 us  [per_device(): others = lax.ppermute(others, 'section', swap)]
  transfers between devices with their start and end apart: 26 -> 26, of which waited for: 11 -> 11; matrix products, arithmetic and copies ran while one was open for 0% -> 0% of each run, Pallas kernels for 21% -> 17%
where the time goes in v7:
time: 117 us; the launch traced here: 116 us
  starting transfers between devices  46.2 us (39%)
  Pallas kernels  35.1 us (30%)
  waiting for transfers between devices  32.6 us (28%)
    ppermute x12, waiting for transfers between devices, moved(): return lax.ppermute(value, ('section', 'z', 'x'), pairs)  19.6 us
    ppermute x12, starting transfers between devices, moved(): return lax.ppermute(value, ('section', 'z', 'x'), pairs)  18.4 us
    pallas_call x1, Pallas kernels, forward(): pl.pallas_call(forward_kernel, in_specs=[HBM] * 5, out_specs=[VMEM] * 4,...  9.11 us
    pallas_call x1, Pallas kernels, dnorm_partial(): pl.pallas_call(dnorm_kernel, in_specs=[VMEM] * 2 + [HBM] * 2, out_specs=H...  9.08 us
    ppermute x6, starting transfers between devices, shift(): return lax.ppermute(value, axis, [(i, (i + k) % RING) for i in range(RING)])  9.07 us
    all_to_all x1, starting transfers between devices, per_device(): lax.all_to_all(slots, ('z', 'x'), split_axis=0, concat_axis=0, tiled=True)  8.42 us
    all_to_all x1, waiting for transfers between devices, per_device(): lax.all_to_all(back, ('z', 'x'), split_axis=0, concat_axis=0, tiled=True)  8.18 us
    all_to_all x1, starting transfers between devices, per_device(): lax.all_to_all(back, ('z', 'x'), split_axis=0, concat_axis=0, tiled=True)  4.96 us
  transfers between devices with their start and end apart: 26, of which 11 were waited for; matrix products, arithmetic and copies ran while one was open for 0% of the time, Pallas kernels for 17%

profile of v7, /device:TPU:0, one launch (start us, length us, event | category | flops | bytes accessed | tf_op | source)
XLA Modules:
  0.0 115.7 jit_solution(2430063795548459007)
XLA Ops:
  0.7 9.1 %forward.1 = (bf16[128,1024]{1,0:T(8,128)(2,1)S(1)}, bf16[128,1024]{1,0:T(8,128)(2,1)S(1)}, bf16[4,32,1024]{2,1,0:T(8,128)(2,1)S(1)}, bf16[4,32,1024]{2,1,0:T(8,128)(2,1)S(1)}) custom-call(bf16[128,4096]{1,0:T(8,128)(2,1)} %bitcast.18, f32[1,4096]{1,0:T(1,128)} %gain_ref.1, bf16[128,4096]{1,0:T(8,128)(2,1)} %cot_hbm.1, bf16[4096,1024]{1,0:T(8,128)(2,1)} %bitcast.13, ...), custom_call_target="tpu_custom_call" | custom-call | flops 134217728 | bytes 1048576 | tf_op jit(solution)/shard_map/forward/pallas_call | solution.py:189
  9.8 0.2 collective-permute-start
  10.0 0.4 collective-permute-start.1
  10.4 1.0 collective-permute-done.got_ref
  11.4 0.4 collective-permute-done.1.other_ref
  11.8 1.2 %pack.1 = (bf16[256,1024]{1,0:T(8,128)(2,1)}, bf16[2,32,1024]{2,1,0:T(8,128)(2,1)S(1)}, bf16[2,32,1024]{2,1,0:T(8,128)(2,1)S(1)}, bf16[2,32,1024]{2,1,0:T(8,128)(2,1)S(1)}, bf16[2,32,1024]{2,1,0:T(8,128)(2,1)S(1)}) custom-call(bf16[128,1024]{1,0:T(8,128)(2,1)S(1)} %get-tuple-element.42.keep_ref, bf16[128,1024]{1,0:T(8,128)(2,1)S(1)} %collective-permute-done.got_ref, ...), custom_call_target="tpu_custom_call" | custom-call | flops 4194304 | bytes 32768 | tf_op jit(solution)/shard_map/pack/pallas_call | solution.py:229
  13.0 8.4 %all-to-all-start = ((bf16[16,16,1024]{2,1,0:T(8,128)(2,1)}), bf16[16,16,1024]{2,1,0:T(8,128)(2,1)S(1)}, u32[]{:S(2)}, u32[]{:S(2)}) async-start(bf16[16,16,1024]{2,1,0:T(8,128)(2,1)} %bitcast.3), calls=%async_computation | async-start | bytes 1048576 | tf_op jit(solution)/shard_map/all_to_all | solution.py:718
  21.4 1.9 %collective-permute-start.2 = (bf16[2,32,1024]{2,1,0:T(8,128)(2,1)S(1)}, bf16[2,32,1024]{2,1,0:T(8,128)(2,1)S(1)}, u32[]{:S(2)}, u32[]{:S(2)}) collective-permute-start(bf16[2,32,1024]{2,1,0:T(8,128)(2,1)S(1)} %get-tuple-element.48), channel_id=1, source_target_pairs={{0,4},{4,8},{8,12},{12,0},{16,20},{20,24},{24,28},{28,16},{32,36},... | collective-permute-start | bytes 393224 | tf_op jit(solution)/shard_map/ppermute | solution.py:517
  23.3 1.4 %collective-permute-start.3 = (bf16[2,32,1024]{2,1,0:T(8,128)(2,1)S(1)}, bf16[2,32,1024]{2,1,0:T(8,128)(2,1)S(1)}, u32[]{:S(2)}, u32[]{:S(2)}) collective-permute-start(bf16[2,32,1024]{2,1,0:T(8,128)(2,1)S(1)} %get-tuple-element.49), channel_id=1, source_target_pairs={{0,12},{4,0},{8,4},{12,8},{16,28},{20,16},{24,20},{28,24},{32,44},... | collective-permute-start | bytes 393224 | tf_op jit(solution)/shard_map/ppermute | solution.py:517
  24.7 2.2 %collective-permute-start.4 = (bf16[2,32,1024]{2,1,0:T(8,128)(2,1)S(1)}, bf16[2,32,1024]{2,1,0:T(8,128)(2,1)S(1)}, u32[]{:S(2)}, u32[]{:S(2)}) collective-permute-start(bf16[2,32,1024]{2,1,0:T(8,128)(2,1)S(1)} %get-tuple-element.50), channel_id=1, source_target_pairs={{0,8},{4,12},{8,0},{12,4},{16,24},{20,28},{24,16},{28,20},{32,40},... | collective-permute-start | bytes 393224 | tf_op jit(solution)/shard_map/ppermute | solution.py:517
  26.8 5.6 %collective-permute-done.2.rest_1_ = bf16[2,32,1024]{2,1,0:T(8,128)(2,1)S(1)} collective-permute-done((bf16[2,32,1024]{2,1,0:T(8,128)(2,1)S(1)}, bf16[2,32,1024]{2,1,0:T(8,128)(2,1)S(1)}, u32[]{:S(2)}, u32[]{:S(2)}) %collective-permute-start.2) | collective-permute-done | bytes 131104 | tf_op jit(solution)/shard_map/ppermute | solution.py:517
  32.4 1.7 %collective-permute-done.4.rest_3_ = bf16[2,32,1024]{2,1,0:T(8,128)(2,1)S(1)} collective-permute-done((bf16[2,32,1024]{2,1,0:T(8,128)(2,1)S(1)}, bf16[2,32,1024]{2,1,0:T(8,128)(2,1)S(1)}, u32[]{:S(2)}, u32[]{:S(2)}) %collective-permute-start.4) | collective-permute-done | bytes 131104 | tf_op jit(solution)/shard_map/ppermute | solution.py:517
  34.2 2.9 %attend.1 = (bf16[128,1024]{1,0:T(8,128)(2,1)S(1)}, bf16[256,1024]{1,0:T(8,128)(2,1)}, bf16[2,4,32,1024]{3,2,1,0:T(8,128)(2,1)S(1)}) custom-call(bf16[128,1024]{1,0:T(8,128)(2,1)S(1)} %get-tuple-element.42.keep_ref, bf16[128,1024]{1,0:T(8,128)(2,1)S(1)} %collective-permute-done.got_ref, bf16[256,1024]{1,0:T(8,128)(2,1)S(1)} %bitcast.11, ...), custom_call_target="tpu_custom_call" | custom-call | flops 50331648 | bytes 131072 | tf_op jit(solution)/shard_map/attend/pallas_call | solution.py:300
  37.1 5.0 %all-to-all-start.1 = ((bf16[16,16,1024]{2,1,0:T(8,128)(2,1)}), bf16[16,16,1024]{2,1,0:T(8,128)(2,1)S(1)}, u32[]{:S(2)}, u32[]{:S(2)}) async-start(bf16[16,16,1024]{2,1,0:T(8,128)(2,1)} %bitcast.5), calls=%async_computation.1 | async-start | bytes 1048576 | tf_op jit(solution)/shard_map/all_to_all | solution.py:724
  42.1 1.7 %collective-permute-start.7 = (bf16[2,4,32,1024]{3,2,1,0:T(8,128)(2,1)S(1)}, bf16[2,4,32,1024]{3,2,1,0:T(8,128)(2,1)}, u32[]{:S(2)}, u32[]{:S(2)}) collective-permute-start(bf16[2,4,32,1024]{3,2,1,0:T(8,128)(2,1)S(1)} %get-tuple-element.57.refs_0_), channel_id=1, source_target_pairs={{0,1},{1,2},{2,3},{3,0},{4,5},{5,6},{6,7},{7,4},{8,9},{9,10},{10,1... | collective-permute-start | bytes 1572872 | tf_op jit(solution)/shard_map/ppermute | solution.py:498
  43.7 1.6 %collective-permute-start.8 = (bf16[2,4,32,1024]{3,2,1,0:T(8,128)(2,1)S(1)}, bf16[2,4,32,1024]{3,2,1,0:T(8,128)(2,1)S(1)}, u32[]{:S(2)}, u32[]{:S(2)}) collective-permute-start(bf16[2,4,32,1024]{3,2,1,0:T(8,128)(2,1)S(1)} %get-tuple-element.57.refs_0_), channel_id=1, source_target_pairs={{0,3},{1,0},{2,1},{3,2},{4,7},{5,4},{6,5},{7,6},{8,11},{9,8},{10,9... | collective-permute-start | bytes 1572872 | tf_op jit(solution)/shard_map/ppermute | solution.py:498
  45.4 8.2 %all-to-all-done.1 = bf16[16,16,1024]{2,1,0:T(8,128)(2,1)S(1)} async-done(((bf16[16,16,1024]{2,1,0:T(8,128)(2,1)}), bf16[16,16,1024]{2,1,0:T(8,128)(2,1)S(1)}, u32[]{:S(2)}, u32[]{:S(2)}) %all-to-all-start.1) | async-done | bytes 524320 | tf_op jit(solution)/shard_map/all_to_all | solution.py:724
  53.6 0.4 unpack.1
  54.0 0.1 collective-permute-start.5
  54.1 1.5 %collective-permute-done.5.got_ref = bf16[128,1024]{1,0:T(8,128)(2,1)S(1)} collective-permute-done((bf16[128,1024]{1,0:T(8,128)(2,1)S(1)}, bf16[128,1024]{1,0:T(8,128)(2,1)S(1)}, u32[]{:S(2)}, u32[]{:S(2)}) %collective-permute-start.5) | collective-permute-done | bytes 262176 | tf_op jit(solution)/shard_map/ppermute | solution.py:726
  55.6 0.1 join.1
  55.7 0.6 collective-permute-start.9
  56.3 2.7 %collective-permute-start.10 = (bf16[128,2048]{1,0:T(8,128)(2,1)S(1)}, bf16[128,2048]{1,0:T(8,128)(2,1)S(1)}, u32[]{:S(2)}, u32[]{:S(2)}) collective-permute-start(bf16[128,2048]{1,0:T(8,128)(2,1)S(1)} %get-tuple-element.55.rows_ref.refs_4_), channel_id=1, source_target_pairs={{0,12},{4,0},{8,4},{12,8},{16,28},{20,16},{24,20},{28,24},{32,44},... | collective-permute-start | bytes 1572872 | tf_op jit(solution)/shard_map/ppermute | solution.py:517
  59.0 0.8 copy-done.5
  59.8 1.6 %collective-permute-start.11 = (bf16[2,4,32,1024]{3,2,1,0:T(8,128)(2,1)}, bf16[2,4,32,1024]{3,2,1,0:T(8,128)(2,1)}, u32[]{:S(2)}, u32[]{:S(2)}) collective-permute-start(bf16[2,4,32,1024]{3,2,1,0:T(8,128)(2,1)} %collective-permute-done.7.refs_1_), channel_id=1, source_target_pairs={{0,1},{1,2},{2,3},{3,0},{4,5},{5,6},{6,7},{7,4},{8,9},{9,10},{10,1... | collective-permute-start | bytes 1572872 | tf_op jit(solution)/shard_map/ppermute | solution.py:498
  61.4 0.9 collective-permute-start.12
  62.3 9.1 %dnorm.1 = bf16[128,4096]{1,0:T(8,128)(2,1)} custom-call(bf16[128,2048]{1,0:T(8,128)(2,1)S(1)} %get-tuple-element.55.rows_ref.refs_4_, bf16[128,1024]{1,0:T(8,128)(2,1)S(1)} %collective-permute-done.6.got_ref, bf16[4096,1024]{1,0:T(8,128)(2,1)} %bitcast.14, bf16[4096,1024]{1,0:T(8,128)(2,1)} %bitcast.16), custom_call_target="tpu_custom_call" | custom-call | flops 134217728 | bytes 1048576 | tf_op jit(solution)/shard_map/dnorm/pallas_call | solution.py:427
  71.4 4.7 %all-to-all-start.2 = ((bf16[4,32,4096]{2,1,0:T(8,128)(2,1)}), bf16[4,32,4096]{2,1,0:T(8,128)(2,1)S(1)}, u32[]{:S(2)}, u32[]{:S(2)}) async-start(bf16[4,32,4096]{2,1,0:T(8,128)(2,1)} %bitcast.17), calls=%async_computation.2 | async-start | bytes 2097152 | tf_op jit(solution)/shard_map/all_to_all | solution.py:734
  76.1 2.0 %far.1 = (bf16[128,2048]{1,0:T(8,128)(2,1)S(1)}, bf16[128,2048]{1,0:T(8,128)(2,1)S(1)}, bf16[512,2048]{1,0:T(8,128)(2,1)S(1)}) custom-call(bf16[2,4,32,1024]{3,2,1,0:T(8,128)(2,1)} %copy-done, bf16[2,4,32,1024]{3,2,1,0:T(8,128)(2,1)} %collective-permute-done.7.refs_1_, bf16[2,4,32,1024]{3,2,1,0:T(8,128)(2,1)} %copy-done.5, ...), custom_call_target="tpu_custom_call" | custom-call | flops 33554432 | bytes 524288 | tf_op jit(solution)/shard_map/far/pallas_call | solution.py:576
  78.0 1.0 collective-permute-start.13
  79.1 2.3 %collective-permute-start.14 = (bf16[128,2048]{1,0:T(8,128)(2,1)S(1)}, bf16[128,2048]{1,0:T(8,128)(2,1)S(1)}, u32[]{:S(2)}, u32[]{:S(2)}) collective-permute-start(bf16[128,2048]{1,0:T(8,128)(2,1)S(1)} %get-tuple-element.67), channel_id=1, source_target_pairs={{0,48},{4,52},{8,56},{12,60},{16,0},{20,4},{24,8},{28,12},{32,16},... | collective-permute-start | bytes 1572872 | tf_op jit(solution)/shard_map/ppermute | solution.py:517
  81.3 2.7 %middle.1 = (bf16[256,1024]{1,0:T(8,128)(2,1)}, bf16[256,1024]{1,0:T(8,128)(2,1)}) custom-call(bf16[2,4,32,1024]{3,2,1,0:T(8,128)(2,1)} %copy-done, bf16[2,4,32,1024]{3,2,1,0:T(8,128)(2,1)} %collective-permute-done.7.refs_1_, bf16[2,4,32,1024]{3,2,1,0:T(8,128)(2,1)} %copy-done.5, bf16[2,4,32,1024]{3,2,1,0:T(8,128)(2,1)} %collective-permute-done.11.refs_3_, ...), custom_call_target="tpu_custom_call" | custom-call | flops 33554432 | bytes 262144 | tf_op jit(solution)/shard_map/middle/pallas_call | solution.py:641
  84.1 4.4 %collective-permute-done.13.refs_5_ = bf16[128,2048]{1,0:T(8,128)(2,1)S(1)} collective-permute-done((bf16[128,2048]{1,0:T(8,128)(2,1)S(1)}, bf16[128,2048]{1,0:T(8,128)(2,1)S(1)}, u32[]{:S(2)}, u32[]{:S(2)}) %collective-permute-start.13) | collective-permute-done | bytes 524320 | tf_op jit(solution)/shard_map/ppermute | solution.py:517
  88.5 2.9 %side.1 = (bf16[256,1024]{1,0:T(8,128)(2,1)S(1)}, bf16[256,1024]{1,0:T(8,128)(2,1)S(1)}, bf16[256,1024]{1,0:T(8,128)(2,1)S(1)}, bf16[256,1024]{1,0:T(8,128)(2,1)S(1)}) custom-call(bf16[2,4,32,1024]{3,2,1,0:T(8,128)(2,1)} %copy-done, bf16[2,4,32,1024]{3,2,1,0:T(8,128)(2,1)} %collective-permute-done.7.refs_1_, bf16[2,4,32,1024]{3,2,1,0:T(8,128)(2,1)} %copy-done.5, ...), custom_call_target="tpu_custom_call" | custom-call | flops 67108864 | bytes 262144 | tf_op jit(solution)/shard_map/side/pallas_call | solution.py:612
  91.5 1.2 %rms_back.1.refs_0_ = bf16[32,4096]{1,0:T(8,128)(2,1)S(1)} custom-call(bf16[128,4096]{1,0:T(8,128)(2,1)} %bitcast.19, f32[1,4096]{1,0:T(1,128)S(1)} %copy-done.3, bf16[4,32,4096]{2,1,0:T(8,128)(2,1)S(1)} %all-to-all-done.2.parts_ref), custom_call_target="tpu_custom_call" | custom-call | flops 81920 | bytes 98304 | tf_op jit(solution)/shard_map/rms_back/pallas_call | solution.py:459
  92.6 2.1 %collective-permute-start.15 = (bf16[32,4096]{1,0:T(8,128)(2,1)S(1)}, bf16[32,4096]{1,0:T(8,128)(2,1)S(1)}, u32[]{:S(2)}, u32[]{:S(2)}) collective-permute-start(bf16[32,4096]{1,0:T(8,128)(2,1)S(1)} %rms_back.1.refs_0_), channel_id=1, source_target_pairs={{0,1},{1,2},{2,3},{3,0},{4,5},{5,6},{6,7},{7,4},{8,9},{9,10},{10,1... | collective-permute-start | bytes 786440 | tf_op jit(solution)/shard_map/ppermute | solution.py:498
  94.7 1.3 %collective-permute-start.16 = (bf16[32,4096]{1,0:T(8,128)(2,1)S(1)}, bf16[32,4096]{1,0:T(8,128)(2,1)S(1)}, u32[]{:S(2)}, u32[]{:S(2)}) collective-permute-start(bf16[32,4096]{1,0:T(8,128)(2,1)S(1)} %rms_back.1.refs_0_), channel_id=1, source_target_pairs={{0,3},{1,0},{2,1},{3,2},{4,7},{5,4},{6,5},{7,6},{8,11},{9,8},{10,9... | collective-permute-start | bytes 786440 | tf_op jit(solution)/shard_map/ppermute | solution.py:498
  96.0 1.2 %collective-permute-start.19 = (bf16[256,1024]{1,0:T(8,128)(2,1)S(1)}, bf16[256,1024]{1,0:T(8,128)(2,1)S(1)}, u32[]{:S(2)}, u32[]{:S(2)}) collective-permute-start(bf16[256,1024]{1,0:T(8,128)(2,1)S(1)} %get-tuple-element.74), channel_id=1, source_target_pairs={{0,16},{4,20},{8,24},{12,28},{16,32},{20,36},{24,40},{28,44},{32,4... | collective-permute-start | bytes 1572872 | tf_op jit(solution)/shard_map/ppermute | solution.py:517
  97.2 2.0 %collective-permute-start.20 = (bf16[256,1024]{1,0:T(8,128)(2,1)S(1)}, bf16[256,1024]{1,0:T(8,128)(2,1)S(1)}, u32[]{:S(2)}, u32[]{:S(2)}) collective-permute-start(bf16[256,1024]{1,0:T(8,128)(2,1)S(1)} %get-tuple-element.76), channel_id=1, source_target_pairs={{0,48},{4,52},{8,56},{12,60},{16,0},{20,4},{24,8},{28,12},{32,16},... | collective-permute-start | bytes 1572872 | tf_op jit(solution)/shard_map/ppermute | solution.py:517
  99.3 1.5 %collective-permute-done.15.refs_1_ = bf16[32,4096]{1,0:T(8,128)(2,1)S(1)} collective-permute-done((bf16[32,4096]{1,0:T(8,128)(2,1)S(1)}, bf16[32,4096]{1,0:T(8,128)(2,1)S(1)}, u32[]{:S(2)}, u32[]{:S(2)}) %collective-permute-start.15) | collective-permute-done | bytes 262176 | tf_op jit(solution)/shard_map/ppermute | solution.py:498
  100.7 0.3 collective-permute-done.16.refs_2_
  101.1 2.2 %collective-permute-start.22 = (bf16[256,1024]{1,0:T(8,128)(2,1)S(1)}, bf16[256,1024]{1,0:T(8,128)(2,1)S(1)}, u32[]{:S(2)}, u32[]{:S(2)}) collective-permute-start(bf16[256,1024]{1,0:T(8,128)(2,1)S(1)} %get-tuple-element.78), channel_id=1, source_target_pairs={{0,112},{4,116},{8,120},{12,124},{16,64},{20,68},{24,72},{28,76},{... | collective-permute-start | bytes 1572872 | tf_op jit(solution)/shard_map/ppermute | solution.py:517
  103.3 0.8 collective-permute-start.17
  104.1 2.3 %collective-permute-done.19.refs_0_ = bf16[256,1024]{1,0:T(8,128)(2,1)S(1)} collective-permute-done((bf16[256,1024]{1,0:T(8,128)(2,1)S(1)}, bf16[256,1024]{1,0:T(8,128)(2,1)S(1)}, u32[]{:S(2)}, u32[]{:S(2)}) %collective-permute-start.19) | collective-permute-done | bytes 524320 | tf_op jit(solution)/shard_map/ppermute | solution.py:517
  106.4 0.0 collective-permute-done.20.refs_1_
  106.4 5.6 %collective-permute-done.21.refs_2_ = bf16[256,1024]{1,0:T(8,128)(2,1)S(1)} collective-permute-done((bf16[256,1024]{1,0:T(8,128)(2,1)S(1)}, bf16[256,1024]{1,0:T(8,128)(2,1)S(1)}, u32[]{:S(2)}, u32[]{:S(2)}) %collective-permute-start.21) | collective-permute-done | bytes 524320 | tf_op jit(solution)/shard_map/ppermute | solution.py:517
  112.0 2.5 %own.1 = (f32[256,1024]{1,0:T(8,128)}, f32[256,1024]{1,0:T(8,128)}) custom-call(bf16[256,1024]{1,0:T(8,128)(2,1)} %get-tuple-element.72.own_hbm, bf16[256,1024]{1,0:T(8,128)(2,1)S(1)} %collective-permute-done.18.other_ref, bf16[256,1024]{1,0:T(8,128)(2,1)S(1)} %collective-permute-done.19.refs_0_, bf16[256,1024]{1,0:T(8,128)(2,1)S(1)} %collective-permute-done.20.refs_1_, ...), custom_call_target="tpu_custom_call" | custom-call | flops 65536 | bytes 327680 | tf_op jit(solution)/shard_map/own/pallas_call | solution.py:691
  114.6 1.0 place.1
  (28 shorter events, 0.1 us)
Async XLA Ops:
  0.6 11.1 %copy-start.1 = (s32[16,16]{1,0:T(8,128)S(1)}, s32[16,16]{1,0:T(8,128)}, u32[]{:S(2)}) copy-start(s32[16,16]{1,0:T(8,128)} %src_ref.5) | copy-start | bytes 3076
  0.6 11.1 %copy-start.2 = (s32[16,16]{1,0:T(8,128)S(1)}, s32[16,16]{1,0:T(8,128)}, u32[]{:S(2)}) copy-start(s32[16,16]{1,0:T(8,128)} %dest_ref.5) | copy-start | bytes 3076
  0.7 33.5 %copy-start.4 = (s32[16,16]{1,0:T(8,128)S(1)}, s32[16,16]{1,0:T(8,128)}, u32[]{:S(2)}) copy-start(s32[16,16]{1,0:T(8,128)} %tgt_ref.1) | copy-start | bytes 3076
  9.8 1.6 %collective-permute-start = (bf16[128,1024]{1,0:T(8,128)(2,1)S(1)}, bf16[128,1024]{1,0:T(8,128)(2,1)S(1)}, u32[]{:S(2)}, u32[]{:S(2)}) collective-permute-start(bf16[128,1024]{1,0:T(8,128)(2,1)S(1)} %get-tuple-element.43), channel_id=1, source_target_pairs={{0,64},{64,0},{1,65},{65,1},{2,66},{66,2},{3,67},{67,3},{4,68},{68... | collective-permute-start | bytes 786440 | tf_op jit(solution)/shard_map/ppermute | solution.py:714
  10.0 1.8 %collective-permute-start.1 = (bf16[4,32,1024]{2,1,0:T(8,128)(2,1)S(1)}, bf16[4,32,1024]{2,1,0:T(8,128)(2,1)S(1)}, u32[]{:S(2)}, u32[]{:S(2)}) collective-permute-start(bf16[4,32,1024]{2,1,0:T(8,128)(2,1)S(1)} %get-tuple-element.45), channel_id=1, source_target_pairs={{0,64},{64,0},{1,65},{65,1},{2,66},{66,2},{3,67},{67,3},{4,68},{68... | collective-permute-start | bytes 786440 | tf_op jit(solution)/shard_map/ppermute | solution.py:715
  13.0 21.2 %all-to-all-start = ((bf16[16,16,1024]{2,1,0:T(8,128)(2,1)}), bf16[16,16,1024]{2,1,0:T(8,128)(2,1)S(1)}, u32[]{:S(2)}, u32[]{:S(2)}) async-start(bf16[16,16,1024]{2,1,0:T(8,128)(2,1)} %bitcast.3), calls=%async_computation | async-start | bytes 1048576 | tf_op jit(solution)/shard_map/all_to_all | solution.py:718
  21.4 11.0 %collective-permute-start.2 = (bf16[2,32,1024]{2,1,0:T(8,128)(2,1)S(1)}, bf16[2,32,1024]{2,1,0:T(8,128)(2,1)S(1)}, u32[]{:S(2)}, u32[]{:S(2)}) collective-permute-start(bf16[2,32,1024]{2,1,0:T(8,128)(2,1)S(1)} %get-tuple-element.48), channel_id=1, source_target_pairs={{0,4},{4,8},{8,12},{12,0},{16,20},{20,24},{24,28},{28,16},{32,36},... | collective-permute-start | bytes 393224 | tf_op jit(solution)/shard_map/ppermute | solution.py:517
  23.3 9.1 %collective-permute-start.3 = (bf16[2,32,1024]{2,1,0:T(8,128)(2,1)S(1)}, bf16[2,32,1024]{2,1,0:T(8,128)(2,1)S(1)}, u32[]{:S(2)}, u32[]{:S(2)}) collective-permute-start(bf16[2,32,1024]{2,1,0:T(8,128)(2,1)S(1)} %get-tuple-element.49), channel_id=1, source_target_pairs={{0,12},{4,0},{8,4},{12,8},{16,28},{20,16},{24,20},{28,24},{32,44},... | collective-permute-start | bytes 393224 | tf_op jit(solution)/shard_map/ppermute | solution.py:517
  24.7 9.4 %collective-permute-start.4 = (bf16[2,32,1024]{2,1,0:T(8,128)(2,1)S(1)}, bf16[2,32,1024]{2,1,0:T(8,128)(2,1)S(1)}, u32[]{:S(2)}, u32[]{:S(2)}) collective-permute-start(bf16[2,32,1024]{2,1,0:T(8,128)(2,1)S(1)} %get-tuple-element.50), channel_id=1, source_target_pairs={{0,8},{4,12},{8,0},{12,4},{16,24},{20,28},{24,16},{28,20},{32,40},... | collective-permute-start | bytes 393224 | tf_op jit(solution)/shard_map/ppermute | solution.py:517
  37.1 34.2 %copy-start = (bf16[2,4,32,1024]{3,2,1,0:T(8,128)(2,1)}, bf16[2,4,32,1024]{3,2,1,0:T(8,128)(2,1)S(1)}, u32[]{:S(2)}) copy-start(bf16[2,4,32,1024]{3,2,1,0:T(8,128)(2,1)S(1)} %get-tuple-element.57.refs_0_) | copy-start | bytes 1572868
  37.1 16.5 %all-to-all-start.1 = ((bf16[16,16,1024]{2,1,0:T(8,128)(2,1)}), bf16[16,16,1024]{2,1,0:T(8,128)(2,1)S(1)}, u32[]{:S(2)}, u32[]{:S(2)}) async-start(bf16[16,16,1024]{2,1,0:T(8,128)(2,1)} %bitcast.5), calls=%async_computation.1 | async-start | bytes 1048576 | tf_op jit(solution)/shard_map/all_to_all | solution.py:724
  42.1 16.9 %collective-permute-start.7 = (bf16[2,4,32,1024]{3,2,1,0:T(8,128)(2,1)S(1)}, bf16[2,4,32,1024]{3,2,1,0:T(8,128)(2,1)}, u32[]{:S(2)}, u32[]{:S(2)}) collective-permute-start(bf16[2,4,32,1024]{3,2,1,0:T(8,128)(2,1)S(1)} %get-tuple-element.57.refs_0_), channel_id=1, source_target_pairs={{0,1},{1,2},{2,3},{3,0},{4,5},{5,6},{6,7},{7,4},{8,9},{9,10},{10,1... | collective-permute-start | bytes 1572872 | tf_op jit(solution)/shard_map/ppermute | solution.py:498
  43.7 15.2 %collective-permute-start.8 = (bf16[2,4,32,1024]{3,2,1,0:T(8,128)(2,1)S(1)}, bf16[2,4,32,1024]{3,2,1,0:T(8,128)(2,1)S(1)}, u32[]{:S(2)}, u32[]{:S(2)}) collective-permute-start(bf16[2,4,32,1024]{3,2,1,0:T(8,128)(2,1)S(1)} %get-tuple-element.57.refs_0_), channel_id=1, source_target_pairs={{0,3},{1,0},{2,1},{3,2},{4,7},{5,4},{6,5},{7,6},{8,11},{9,8},{10,9... | collective-permute-start | bytes 1572872 | tf_op jit(solution)/shard_map/ppermute | solution.py:498
  54.0 1.6 %collective-permute-start.5 = (bf16[128,1024]{1,0:T(8,128)(2,1)S(1)}, bf16[128,1024]{1,0:T(8,128)(2,1)S(1)}, u32[]{:S(2)}, u32[]{:S(2)}) collective-permute-start(bf16[128,1024]{1,0:T(8,128)(2,1)S(1)} %get-tuple-element.54), channel_id=1, source_target_pairs={{0,64},{64,0},{1,65},{65,1},{2,66},{66,2},{3,67},{67,3},{4,68},{68... | collective-permute-start | bytes 786440 | tf_op jit(solution)/shard_map/ppermute | solution.py:726
  55.7 15.7 %collective-permute-start.9 = (bf16[128,2048]{1,0:T(8,128)(2,1)S(1)}, bf16[128,2048]{1,0:T(8,128)(2,1)S(1)}, u32[]{:S(2)}, u32[]{:S(2)}) collective-permute-start(bf16[128,2048]{1,0:T(8,128)(2,1)S(1)} %get-tuple-element.55.rows_ref.refs_4_), channel_id=1, source_target_pairs={{0,4},{4,8},{8,12},{12,0},{16,20},{20,24},{24,28},{28,16},{32,36},... | collective-permute-start | bytes 1572872 | tf_op jit(solution)/shard_map/ppermute | solution.py:517
  56.3 15.1 %collective-permute-start.10 = (bf16[128,2048]{1,0:T(8,128)(2,1)S(1)}, bf16[128,2048]{1,0:T(8,128)(2,1)S(1)}, u32[]{:S(2)}, u32[]{:S(2)}) collective-permute-start(bf16[128,2048]{1,0:T(8,128)(2,1)S(1)} %get-tuple-element.55.rows_ref.refs_4_), channel_id=1, source_target_pairs={{0,12},{4,0},{8,4},{12,8},{16,28},{20,16},{24,20},{28,24},{32,44},... | collective-permute-start | bytes 1572872 | tf_op jit(solution)/shard_map/ppermute | solution.py:517
  59.0 3.3 %collective-permute-start.6 = (bf16[128,1024]{1,0:T(8,128)(2,1)S(1)}, bf16[128,1024]{1,0:T(8,128)(2,1)S(1)}, u32[]{:S(2)}, u32[]{:S(2)}) collective-permute-start(bf16[128,1024]{1,0:T(8,128)(2,1)S(1)} %get-tuple-element.56), channel_id=1, source_target_pairs={{0,64},{64,0},{1,65},{65,1},{2,66},{66,2},{3,67},{67,3},{4,68},{68... | collective-permute-start | bytes 786440 | tf_op jit(solution)/shard_map/ppermute | solution.py:730
  59.0 0.8 copy-start.5
  59.8 16.3 %collective-permute-start.11 = (bf16[2,4,32,1024]{3,2,1,0:T(8,128)(2,1)}, bf16[2,4,32,1024]{3,2,1,0:T(8,128)(2,1)}, u32[]{:S(2)}, u32[]{:S(2)}) collective-permute-start(bf16[2,4,32,1024]{3,2,1,0:T(8,128)(2,1)} %collective-permute-done.7.refs_1_), channel_id=1, source_target_pairs={{0,1},{1,2},{2,3},{3,0},{4,5},{5,6},{6,7},{7,4},{8,9},{9,10},{10,1... | collective-permute-start | bytes 1572872 | tf_op jit(solution)/shard_map/ppermute | solution.py:498
  61.4 14.7 %collective-permute-start.12 = (bf16[128,2048]{1,0:T(8,128)(2,1)S(1)}, bf16[128,2048]{1,0:T(8,128)(2,1)S(1)}, u32[]{:S(2)}, u32[]{:S(2)}) collective-permute-start(bf16[128,2048]{1,0:T(8,128)(2,1)S(1)} %get-tuple-element.55.rows_ref.refs_4_), channel_id=1, source_target_pairs={{0,8},{4,12},{8,0},{12,4},{16,24},{20,28},{24,16},{28,20},{32,40},... | collective-permute-start | bytes 1572872 | tf_op jit(solution)/shard_map/ppermute | solution.py:517
  71.4 20.1 %copy-start.3 = (f32[1,4096]{1,0:T(1,128)S(1)}, f32[1,4096]{1,0:T(1,128)}, u32[]{:S(2)}) copy-start(f32[1,4096]{1,0:T(1,128)} %gain_ref.1) | copy-start | bytes 49156
  71.4 20.0 %all-to-all-start.2 = ((bf16[4,32,4096]{2,1,0:T(8,128)(2,1)}), bf16[4,32,4096]{2,1,0:T(8,128)(2,1)S(1)}, u32[]{:S(2)}, u32[]{:S(2)}) async-start(bf16[4,32,4096]{2,1,0:T(8,128)(2,1)} %bitcast.17), calls=%async_computation.2 | async-start | bytes 2097152 | tf_op jit(solution)/shard_map/all_to_all | solution.py:734
  78.0 10.5 %collective-permute-start.13 = (bf16[128,2048]{1,0:T(8,128)(2,1)S(1)}, bf16[128,2048]{1,0:T(8,128)(2,1)S(1)}, u32[]{:S(2)}, u32[]{:S(2)}) collective-permute-start(bf16[128,2048]{1,0:T(8,128)(2,1)S(1)} %get-tuple-element.66), channel_id=1, source_target_pairs={{0,16},{4,20},{8,24},{12,28},{16,32},{20,36},{24,40},{28,44},{32,4... | collective-permute-start | bytes 1572872 | tf_op jit(solution)/shard_map/ppermute | solution.py:517
  79.1 9.4 %collective-permute-start.14 = (bf16[128,2048]{1,0:T(8,128)(2,1)S(1)}, bf16[128,2048]{1,0:T(8,128)(2,1)S(1)}, u32[]{:S(2)}, u32[]{:S(2)}) collective-permute-start(bf16[128,2048]{1,0:T(8,128)(2,1)S(1)} %get-tuple-element.67), channel_id=1, source_target_pairs={{0,48},{4,52},{8,56},{12,60},{16,0},{20,4},{24,8},{28,12},{32,16},... | collective-permute-start | bytes 1572872 | tf_op jit(solution)/shard_map/ppermute | solution.py:517
  92.6 8.1 %collective-permute-start.15 = (bf16[32,4096]{1,0:T(8,128)(2,1)S(1)}, bf16[32,4096]{1,0:T(8,128)(2,1)S(1)}, u32[]{:S(2)}, u32[]{:S(2)}) collective-permute-start(bf16[32,4096]{1,0:T(8,128)(2,1)S(1)} %rms_back.1.refs_0_), channel_id=1, source_target_pairs={{0,1},{1,2},{2,3},{3,0},{4,5},{5,6},{6,7},{7,4},{8,9},{9,10},{10,1... | collective-permute-start | bytes 786440 | tf_op jit(solution)/shard_map/ppermute | solution.py:498
  94.7 6.4 %collective-permute-start.16 = (bf16[32,4096]{1,0:T(8,128)(2,1)S(1)}, bf16[32,4096]{1,0:T(8,128)(2,1)S(1)}, u32[]{:S(2)}, u32[]{:S(2)}) collective-permute-start(bf16[32,4096]{1,0:T(8,128)(2,1)S(1)} %rms_back.1.refs_0_), channel_id=1, source_target_pairs={{0,3},{1,0},{2,1},{3,2},{4,7},{5,4},{6,5},{7,6},{8,11},{9,8},{10,9... | collective-permute-start | bytes 786440 | tf_op jit(solution)/shard_map/ppermute | solution.py:498
  96.0 7.3 %collective-permute-start.18 = (bf16[256,1024]{1,0:T(8,128)(2,1)}, bf16[256,1024]{1,0:T(8,128)(2,1)S(1)}, u32[]{:S(2)}, u32[]{:S(2)}) collective-permute-start(bf16[256,1024]{1,0:T(8,128)(2,1)} %get-tuple-element.75), channel_id=1, source_target_pairs={{0,64},{64,0},{1,65},{65,1},{2,66},{66,2},{3,67},{67,3},{4,68},{68... | collective-permute-start | bytes 1572872 | tf_op jit(solution)/shard_map/ppermute | solution.py:751
  96.0 10.4 %collective-permute-start.19 = (bf16[256,1024]{1,0:T(8,128)(2,1)S(1)}, bf16[256,1024]{1,0:T(8,128)(2,1)S(1)}, u32[]{:S(2)}, u32[]{:S(2)}) collective-permute-start(bf16[256,1024]{1,0:T(8,128)(2,1)S(1)} %get-tuple-element.74), channel_id=1, source_target_pairs={{0,16},{4,20},{8,24},{12,28},{16,32},{20,36},{24,40},{28,44},{32,4... | collective-permute-start | bytes 1572872 | tf_op jit(solution)/shard_map/ppermute | solution.py:517
  97.2 9.2 %collective-permute-start.20 = (bf16[256,1024]{1,0:T(8,128)(2,1)S(1)}, bf16[256,1024]{1,0:T(8,128)(2,1)S(1)}, u32[]{:S(2)}, u32[]{:S(2)}) collective-permute-start(bf16[256,1024]{1,0:T(8,128)(2,1)S(1)} %get-tuple-element.76), channel_id=1, source_target_pairs={{0,48},{4,52},{8,56},{12,60},{16,0},{20,4},{24,8},{28,12},{32,16},... | collective-permute-start | bytes 1572872 | tf_op jit(solution)/shard_map/ppermute | solution.py:517
  100.7 11.3 %collective-permute-start.21 = (bf16[256,1024]{1,0:T(8,128)(2,1)S(1)}, bf16[256,1024]{1,0:T(8,128)(2,1)S(1)}, u32[]{:S(2)}, u32[]{:S(2)}) collective-permute-start(bf16[256,1024]{1,0:T(8,128)(2,1)S(1)} %get-tuple-element.77), channel_id=1, source_target_pairs={{0,80},{4,84},{8,88},{12,92},{16,96},{20,100},{24,104},{28,108},{3... | collective-permute-start | bytes 1572872 | tf_op jit(solution)/shard_map/ppermute | solution.py:517
  101.1 10.9 %collective-permute-start.22 = (bf16[256,1024]{1,0:T(8,128)(2,1)S(1)}, bf16[256,1024]{1,0:T(8,128)(2,1)S(1)}, u32[]{:S(2)}, u32[]{:S(2)}) collective-permute-start(bf16[256,1024]{1,0:T(8,128)(2,1)S(1)} %get-tuple-element.78), channel_id=1, source_target_pairs={{0,112},{4,116},{8,120},{12,124},{16,64},{20,68},{24,72},{28,76},{... | collective-permute-start | bytes 1572872 | tf_op jit(solution)/shard_map/ppermute | solution.py:517
  103.3 11.2 %collective-permute-start.17 = (bf16[32,4096]{1,0:T(8,128)(2,1)S(1)}, bf16[32,4096]{1,0:T(8,128)(2,1)S(1)}, u32[]{:S(2)}, u32[]{:S(2)}) collective-permute-start(bf16[32,4096]{1,0:T(8,128)(2,1)S(1)} %collective-permute-done.15.refs_1_), channel_id=1, source_target_pairs={{0,1},{1,2},{2,3},{3,0},{4,5},{5,6},{6,7},{7,4},{8,9},{9,10},{10,1... | collective-permute-start | bytes 786440 | tf_op jit(solution)/shard_map/ppermute | solution.py:498

commit v8 on v7

--- a/solution.py
+++ b/solution.py
@@ -503,17 +503,15 @@
     return [block, left, right, shift(left, axis, 1)]
 
 
-def moved(value, k, along, across=False):
+def moved(value, k, along):
     pairs = []
     for core in range(2):
         for z in range(RING):
             for x in range(RING):
                 to = {"z": z, "x": x}
                 to[along[core]] = (to[along[core]] + k) % RING
-                target = (1 - core if across else core, to["z"], to["x"])
-                pairs.append(
-                    ((core * RING + z) * RING + x, (target[0] * RING + target[1]) * RING + target[2])
-                )
+                base = core * RING
+                pairs.append(((base + z) * RING + x, (base + to["z"]) * RING + to["x"]))
     return lax.ppermute(value, ("section", "z", "x"), pairs)
 
 
@@ -586,10 +584,9 @@
 
 
 def side_kernel(*refs):
-    lefts, (rows_ref, from_left, from_right) = refs[:RING], refs[RING : RING + 3]
-    rights, to_lefts, buf, sems = refs[RING + 3 : RING + 5], refs[RING + 5 : RING + 7], *refs[RING + 7 :]
+    lefts, (rows_ref, from_left, from_right, right, left, buf, sems) = refs[:RING], refs[RING:]
     loads = left_loads(lefts, buf, sems, (1, 3))
-    half, cols = from_left.shape[0], rights[0].shape[1]
+    half, cols = from_left.shape[0], right.shape[1] // 2
     for m in range(2):
         at = slice(m * cols, (m + 1) * cols)
 
@@ -598,22 +595,22 @@
             return tn(flat(buf[m, i]), rows_ref[:, at])
 
         block = product(0)
-        rights[m][:half, :] = (block[:half] + from_left[:, at].astype(F32)).astype(BF16)
-        rights[m][half:, :] = block[half:].astype(BF16)
+        right[:half, at] = (block[:half] + from_left[:, at].astype(F32)).astype(BF16)
+        right[half:, at] = block[half:].astype(BF16)
         block = product(1)
-        to_lefts[m][:half, :] = block[:half].astype(BF16)
-        to_lefts[m][half:, :] = (block[half:] + from_right[:, at].astype(F32)).astype(BF16)
+        left[:half, at] = block[:half].astype(BF16)
+        left[half:, at] = (block[half:] + from_right[:, at].astype(F32)).astype(BF16)
 
 
 def side_blocks(lefts, rows, from_left, from_right):
     depth, cols = rows.shape
     block = lefts[0].shape[-1] // RING
-    shape = jax.ShapeDtypeStruct((block, cols // 2), BF16)
+    shape = jax.ShapeDtypeStruct((block, cols), BF16)
     return pl.pallas_call(
         side_kernel,
         in_specs=[HBM] * RING + [VMEM] * 3,
-        out_specs=[VMEM] * 4,
-        out_shape=[shape] * 4,
+        out_specs=[VMEM] * 2,
+        out_shape=[shape] * 2,
         scratch_shapes=left_scratch(block, 2),
         compiler_params=params(),
         cost_estimate=cost(4 * depth * block * cols, 4 * depth * cols),
@@ -652,57 +649,107 @@
     )(*[in_hbm(left) for left in lefts], rows)
 
 
-def own_kernel(own_hbm, other_ref, *refs):
-    parts, outs, (own_ref, out_buf, own_sem, out_sems) = refs[:4], refs[4:6], refs[6:]
-    get = pltpu.make_async_copy(own_hbm, own_ref, own_sem)
+def cross_kernel(own_hbm, a_ref, b_ref, out_ref, own_ref, sem):
+    get = pltpu.make_async_copy(own_hbm, own_ref, sem)
     get.start()
-    core = lax.axis_index("section")
-    chunks = out_sems.shape[1]
-    size = out_buf.shape[1] // chunks
-
-    def put(m, c, out):
+    cols = out_ref.shape[1]
+    both = a_ref[:, cols:].astype(F32) + b_ref[:, cols:].astype(F32)
+    get.wait()
+    out_ref[...] = (own_ref[...].astype(F32) + both).astype(BF16)
+
+
+def cross_sum(own, a, b):
+    block, cols = own.shape
+    return pl.pallas_call(
+        cross_kernel,
+        in_specs=[HBM] + [VMEM] * 2,
+        out_specs=VMEM,
+        out_shape=jax.ShapeDtypeStruct((block, cols), BF16),
+        scratch_shapes=[pltpu.VMEM((block, cols), BF16), pltpu.SemaphoreType.DMA],
+        compiler_params=params(),
+        cost_estimate=cost(2 * block * cols, 8 * block * cols),
+        name="cross",
+    )(in_hbm(own), a, b)
+
+
+CHUNKS = 4
+
+
+def write_out(values, first, second, buf, sems, is_first):
+    size = buf.shape[0] // CHUNKS
+
+    def put(c, out):
         at = slice(c * size, (c + 1) * size)
-        return pltpu.make_async_copy(out_buf.at[m, at], out.at[at], out_sems.at[m, c])
-
-    def write(m, c):
-        @pl.when(core == m)
-        def _():
-            put(m, c, outs[0]).start()
-
-        @pl.when(core != m)
-        def _():
-            put(m, c, outs[1]).start()
-
-    for m, base in ((1, other_ref), (0, own_ref)):
-        if m == 0:
-            get.wait()
-        for c in range(chunks):
-            at = slice(c * size, (c + 1) * size)
-            total_of = base[at].astype(F32) + parts[2 * m][at].astype(F32)
-            out_buf[m, at] = total_of + parts[2 * m + 1][at].astype(F32)
-            write(m, c)
-    for m in range(2):
-        for c in range(chunks):
-            put(m, c, outs[0]).wait()
-
-
-def own_blocks(own, other, parts):
+        return pltpu.make_async_copy(buf.at[at], out.at[at], sems.at[c])
+
+    for c in range(CHUNKS):
+        at = slice(c * size, (c + 1) * size)
+        buf[at] = values(at)
+
+        @pl.when(is_first)
+        def _(c=c):
+            put(c, first).start()
+
+        @pl.when(jnp.logical_not(is_first))
+        def _(c=c):
+            put(c, second).start()
+
+    for c in range(CHUNKS):
+        put(c, first).wait()
+
+
+def own_kernel(own_hbm, a_ref, b_ref, first, second, own_ref, buf, sem, sems):
+    get = pltpu.make_async_copy(own_hbm, own_ref, sem)
+    get.start()
+    cols = own_ref.shape[1]
+    get.wait()
+
+    def values(at):
+        both = a_ref[at, :cols].astype(F32) + b_ref[at, :cols].astype(F32)
+        return own_ref[at].astype(F32) + both
+
+    write_out(values, first, second, buf, sems, lax.axis_index("section") == 0)
+
+
+def own_sum(own, a, b):
     block, cols = own.shape
     return pl.pallas_call(
         own_kernel,
-        in_specs=[HBM] + [VMEM] * 5,
+        in_specs=[HBM] + [VMEM] * 2,
         out_specs=[HBM] * 2,
         out_shape=[pltpu.HBM((block, cols), F32)] * 2,
         scratch_shapes=[
             pltpu.VMEM((block, cols), BF16),
-            pltpu.VMEM((2, block, cols), F32),
+            pltpu.VMEM((block, cols), F32),
             pltpu.SemaphoreType.DMA,
-            pltpu.SemaphoreType.DMA((2, 4)),
+            pltpu.SemaphoreType.DMA((CHUNKS,)),
         ],
         compiler_params=params(),
-        cost_estimate=cost(4 * block * cols, 20 * block * cols),
+        cost_estimate=cost(2 * block * cols, 10 * block * cols),
         name="own",
-    )(in_hbm(own), other, *parts)
+    )(in_hbm(own), a, b)
+
+
+def last_kernel(got_ref, first_in, second_in, first, second, buf, sems):
+    def values(at):
+        return got_ref[at].astype(F32)
+
+    write_out(values, first, second, buf, sems, lax.axis_index("section") != 0)
+
+
+def last_write(got, first, second):
+    block, cols = got.shape
+    return pl.pallas_call(
+        last_kernel,
+        in_specs=[VMEM] + [HBM] * 2,
+        out_specs=[HBM] * 2,
+        out_shape=[pltpu.HBM((block, cols), F32)] * 2,
+        input_output_aliases={1: 0, 2: 1},
+        scratch_shapes=[pltpu.VMEM((block, cols), F32), pltpu.SemaphoreType.DMA((CHUNKS,))],
+        compiler_params=params(),
+        cost_estimate=cost(block * cols, 6 * block * cols),
+        name="last",
+    )(got, in_hbm(first), in_hbm(second))
 
 
 def per_device(states, gains, proj_a, proj_b, cotangent, src_len, tgt_len, dest):
@@ -736,19 +783,18 @@
     )
     top, low, stack = far_block(lefts, rights)
     from_left, from_right = moved(top, 1, REDUCE), moved(low, 3, REDUCE)
-    parts, _, _ = lax.optimization_barrier((parts, from_left, from_right))
-    right, right_other, left, left_other = side_blocks(lefts, stack, from_left, from_right)
     own, own_other = middle_blocks(lefts, stack)
-    own_other, _ = lax.optimization_barrier((own_other, right))
-    sums = [
-        moved(right, 1, REDUCE),
-        moved(left, 3, REDUCE),
-        moved(right_other, 1, REDUCE, True),
-        moved(left_other, 3, REDUCE, True),
-    ]
+    stack, own, own_other = lax.optimization_barrier((stack, own, own_other))
+    right, left = side_blocks(lefts, stack, from_left, from_right)
+    left, parts = lax.optimization_barrier((left, parts))
+    right, left = moved(right, 1, REDUCE), moved(left, 3, REDUCE)
     quarter = rms_back(rows, gains, parts)
-    grad_states = place(gathered(quarter, "mp"))
-    grad_a, grad_b = own_blocks(own, lax.ppermute(own_other, "section", swap), sums)
+    quarters = gathered(quarter, "mp")
+    crossed = lax.ppermute(cross_sum(own_other, right, left), "section", swap)
+    grad_a, grad_b = own_sum(own, right, left)
+    quarters[3], grad_a = lax.optimization_barrier((quarters[3], grad_a))
+    grad_states = place(quarters)
+    grad_a, grad_b = last_write(crossed, grad_a, grad_b)
     return (grad_states[None], grad_a[None], grad_b[None])
 
 

time: 117 us -> 125 us (1.068)
  waiting for transfers between devices: 32.6 us -> 39.7 us
  Pallas kernels: 35.1 us -> 38.4 us
  starting transfers between devices: 46.2 us -> 44.5 us
    ppermute x6, waiting for transfers between devices: 1.85 us -> 7.8 us  [shift(): return lax.ppermute(value, axis, [(i, (i + k) % RING) for i in range(RING)])]
    pallas_call x1 -> x3, Pallas kernels: 2.53 us -> 4.24 us  [the longest x1 2.09 us: own_sum(): pl.pallas_call(own_kernel, in_specs=[HBM] + [VMEM] * 2, out_specs=[HBM] *...]
    ppermute x12 -> x10, starting transfers between devices: 18.4 us -> 17.3 us  [moved(): return lax.ppermute(value, ('section', 'z', 'x'), pairs)]
    ppermute x12 -> x10, waiting for transfers between devices: 19.6 us -> 20.6 us  [moved(): return lax.ppermute(value, ('section', 'z', 'x'), pairs)]
  transfers between devices with their start and end apart: 26 -> 24, of which waited for: 11 -> 11; matrix products, arithmetic and copies ran while one was open for 0% -> 0% of each run, Pallas kernels for 17% -> 20%
where the time goes in v8:
time: 125 us; the launch traced here: 124 us
  starting transfers between devices  44.5 us (36%)
  waiting for transfers between devices  39.7 us (32%)
  Pallas kernels  38.4 us (31%)
    ppermute x10, waiting for transfers between devices, moved(): return lax.ppermute(value, ('section', 'z', 'x'), pairs)  20.6 us
    ppermute x10, starting transfers between devices, moved(): return lax.ppermute(value, ('section', 'z', 'x'), pairs)  17.3 us
    pallas_call x1, Pallas kernels, forward(): pl.pallas_call(forward_kernel, in_specs=[HBM] * 5, out_specs=[VMEM] * 4,...  9.11 us
    pallas_call x1, Pallas kernels, dnorm_partial(): pl.pallas_call(dnorm_kernel, in_specs=[VMEM] * 2 + [HBM] * 2, out_specs=H...  9.07 us
    ppermute x6, starting transfers between devices, shift(): return lax.ppermute(value, axis, [(i, (i + k) % RING) for i in range(RING)])  8.51 us
    all_to_all x1, starting transfers between devices, per_device(): lax.all_to_all(slots, ('z', 'x'), split_axis=0, concat_axis=0, tiled=True)  8.42 us
    all_to_all x1, waiting for transfers between devices, per_device(): lax.all_to_all(back, ('z', 'x'), split_axis=0, concat_axis=0, tiled=True)  8.38 us
    ppermute x6, waiting for transfers between devices, shift(): return lax.ppermute(value, axis, [(i, (i + k) % RING) for i in range(RING)])  7.8 us
  transfers between devices with their start and end apart: 24, of which 11 were waited for; matrix products, arithmetic and copies ran while one was open for 0% of the time, Pallas kernels for 20%

profile of v8, /device:TPU:0, one launch (start us, length us, event | category | flops | bytes accessed | tf_op | source)
XLA Modules:
  0.0 123.6 jit_solution(12815753582992983698)
XLA Ops:
  0.7 9.1 %forward.1 = (bf16[128,1024]{1,0:T(8,128)(2,1)S(1)}, bf16[128,1024]{1,0:T(8,128)(2,1)S(1)}, bf16[4,32,1024]{2,1,0:T(8,128)(2,1)S(1)}, bf16[4,32,1024]{2,1,0:T(8,128)(2,1)S(1)}) custom-call(bf16[128,4096]{1,0:T(8,128)(2,1)} %bitcast.18, f32[1,4096]{1,0:T(1,128)} %gain_ref.1, bf16[128,4096]{1,0:T(8,128)(2,1)} %cot_hbm.1, bf16[4096,1024]{1,0:T(8,128)(2,1)} %bitcast.13, ...), custom_call_target="tpu_custom_call" | custom-call | flops 134217728 | bytes 1048576 | tf_op jit(solution)/shard_map/forward/pallas_call | solution.py:189
  9.8 0.2 collective-permute-start
  10.0 0.4 collective-permute-start.1
  10.4 1.0 collective-permute-done.got_ref
  11.4 0.4 collective-permute-done.1.other_ref
  11.8 1.2 pack.1
  13.0 8.4 %all-to-all-start = ((bf16[16,16,1024]{2,1,0:T(8,128)(2,1)}), bf16[16,16,1024]{2,1,0:T(8,128)(2,1)S(1)}, u32[]{:S(2)}, u32[]{:S(2)}) async-start(bf16[16,16,1024]{2,1,0:T(8,128)(2,1)} %bitcast.3), calls=%async_computation | async-start | bytes 1048576 | tf_op jit(solution)/shard_map/all_to_all | solution.py:765
  21.4 1.9 %collective-permute-start.2 = (bf16[2,32,1024]{2,1,0:T(8,128)(2,1)S(1)}, bf16[2,32,1024]{2,1,0:T(8,128)(2,1)S(1)}, u32[]{:S(2)}, u32[]{:S(2)}) collective-permute-start(bf16[2,32,1024]{2,1,0:T(8,128)(2,1)S(1)} %get-tuple-element.53), channel_id=1, source_target_pairs={{0,4},{4,8},{8,12},{12,0},{16,20},{20,24},{24,28},{28,16},{32,36},... | collective-permute-start | bytes 393224 | tf_op jit(solution)/shard_map/ppermute | solution.py:515
  23.3 1.4 %collective-permute-start.3 = (bf16[2,32,1024]{2,1,0:T(8,128)(2,1)S(1)}, bf16[2,32,1024]{2,1,0:T(8,128)(2,1)S(1)}, u32[]{:S(2)}, u32[]{:S(2)}) collective-permute-start(bf16[2,32,1024]{2,1,0:T(8,128)(2,1)S(1)} %get-tuple-element.54), channel_id=1, source_target_pairs={{0,12},{4,0},{8,4},{12,8},{16,28},{20,16},{24,20},{28,24},{32,44},... | collective-permute-start | bytes 393224 | tf_op jit(solution)/shard_map/ppermute | solution.py:515
  24.7 2.2 %collective-permute-start.4 = (bf16[2,32,1024]{2,1,0:T(8,128)(2,1)S(1)}, bf16[2,32,1024]{2,1,0:T(8,128)(2,1)S(1)}, u32[]{:S(2)}, u32[]{:S(2)}) collective-permute-start(bf16[2,32,1024]{2,1,0:T(8,128)(2,1)S(1)} %get-tuple-element.55), channel_id=1, source_target_pairs={{0,8},{4,12},{8,0},{12,4},{16,24},{20,28},{24,16},{28,20},{32,40},... | collective-permute-start | bytes 393224 | tf_op jit(solution)/shard_map/ppermute | solution.py:515
  26.8 5.6 %collective-permute-done.2.rest_1_ = bf16[2,32,1024]{2,1,0:T(8,128)(2,1)S(1)} collective-permute-done((bf16[2,32,1024]{2,1,0:T(8,128)(2,1)S(1)}, bf16[2,32,1024]{2,1,0:T(8,128)(2,1)S(1)}, u32[]{:S(2)}, u32[]{:S(2)}) %collective-permute-start.2) | collective-permute-done | bytes 131104 | tf_op jit(solution)/shard_map/ppermute | solution.py:515
  32.4 1.7 %collective-permute-done.4.rest_3_ = bf16[2,32,1024]{2,1,0:T(8,128)(2,1)S(1)} collective-permute-done((bf16[2,32,1024]{2,1,0:T(8,128)(2,1)S(1)}, bf16[2,32,1024]{2,1,0:T(8,128)(2,1)S(1)}, u32[]{:S(2)}, u32[]{:S(2)}) %collective-permute-start.4) | collective-permute-done | bytes 131104 | tf_op jit(solution)/shard_map/ppermute | solution.py:515
  34.1 0.0 all-to-all-done
  34.2 3.0 %attend.1 = (bf16[128,1024]{1,0:T(8,128)(2,1)S(1)}, bf16[256,1024]{1,0:T(8,128)(2,1)}, bf16[2,4,32,1024]{3,2,1,0:T(8,128)(2,1)S(1)}) custom-call(bf16[128,1024]{1,0:T(8,128)(2,1)S(1)} %get-tuple-element.47.keep_ref, bf16[128,1024]{1,0:T(8,128)(2,1)S(1)} %collective-permute-done.got_ref, bf16[256,1024]{1,0:T(8,128)(2,1)S(1)} %bitcast.11, ...), custom_call_target="tpu_custom_call" | custom-call | flops 50331648 | bytes 131072 | tf_op jit(solution)/shard_map/attend/pallas_call | solution.py:300
  37.1 5.0 %all-to-all-start.1 = ((bf16[16,16,1024]{2,1,0:T(8,128)(2,1)}), bf16[16,16,1024]{2,1,0:T(8,128)(2,1)S(1)}, u32[]{:S(2)}, u32[]{:S(2)}) async-start(bf16[16,16,1024]{2,1,0:T(8,128)(2,1)} %bitcast.5), calls=%async_computation.1 | async-start | bytes 1048576 | tf_op jit(solution)/shard_map/all_to_all | solution.py:771
  42.1 3.1 %collective-permute-start.8 = (bf16[2,4,32,1024]{3,2,1,0:T(8,128)(2,1)S(1)}, bf16[2,4,32,1024]{3,2,1,0:T(8,128)(2,1)S(1)}, u32[]{:S(2)}, u32[]{:S(2)}) collective-permute-start(bf16[2,4,32,1024]{3,2,1,0:T(8,128)(2,1)S(1)} %get-tuple-element.56.refs_0_), channel_id=1, source_target_pairs={{0,3},{1,0},{2,1},{3,2},{4,7},{5,4},{6,5},{7,6},{8,11},{9,8},{10,9... | collective-permute-start | bytes 1572872 | tf_op jit(solution)/shard_map/ppermute | solution.py:498
  45.2 8.4 %all-to-all-done.1 = bf16[16,16,1024]{2,1,0:T(8,128)(2,1)S(1)} async-done(((bf16[16,16,1024]{2,1,0:T(8,128)(2,1)}), bf16[16,16,1024]{2,1,0:T(8,128)(2,1)S(1)}, u32[]{:S(2)}, u32[]{:S(2)}) %all-to-all-start.1) | async-done | bytes 524320 | tf_op jit(solution)/shard_map/all_to_all | solution.py:771
  53.6 0.4 unpack.1
  54.0 0.1 collective-permute-start.5
  54.1 1.5 %collective-permute-done.5.got_ref = bf16[128,1024]{1,0:T(8,128)(2,1)S(1)} collective-permute-done((bf16[128,1024]{1,0:T(8,128)(2,1)S(1)}, bf16[128,1024]{1,0:T(8,128)(2,1)S(1)}, u32[]{:S(2)}, u32[]{:S(2)}) %collective-permute-start.5) | collective-permute-done | bytes 262176 | tf_op jit(solution)/shard_map/ppermute | solution.py:773
  55.6 0.1 join.1
  55.7 0.6 collective-permute-start.11
  56.2 1.5 %collective-permute-start.10 = (bf16[128,2048]{1,0:T(8,128)(2,1)S(1)}, bf16[128,2048]{1,0:T(8,128)(2,1)S(1)}, u32[]{:S(2)}, u32[]{:S(2)}) collective-permute-start(bf16[128,2048]{1,0:T(8,128)(2,1)S(1)} %get-tuple-element.66.rows_ref.refs_4_), channel_id=1, source_target_pairs={{0,4},{4,8},{8,12},{12,0},{16,20},{20,24},{24,28},{28,16},{32,36},... | collective-permute-start | bytes 1572872 | tf_op jit(solution)/shard_map/ppermute | solution.py:515
  57.8 0.0 collective-permute-done.8.refs_2_
  57.8 1.8 %collective-permute-done.7.refs_1_ = bf16[2,4,32,1024]{3,2,1,0:T(8,128)(2,1)} collective-permute-done((bf16[2,4,32,1024]{3,2,1,0:T(8,128)(2,1)S(1)}, bf16[2,4,32,1024]{3,2,1,0:T(8,128)(2,1)}, u32[]{:S(2)}, u32[]{:S(2)}) %collective-permute-start.7) | collective-permute-done | bytes 524320 | tf_op jit(solution)/shard_map/ppermute | solution.py:498
  59.6 3.1 %collective-permute-start.12 = (bf16[128,2048]{1,0:T(8,128)(2,1)S(1)}, bf16[128,2048]{1,0:T(8,128)(2,1)}, u32[]{:S(2)}, u32[]{:S(2)}) collective-permute-start(bf16[128,2048]{1,0:T(8,128)(2,1)S(1)} %get-tuple-element.66.rows_ref.refs_4_), channel_id=1, source_target_pairs={{0,8},{4,12},{8,0},{12,4},{16,24},{20,28},{24,16},{28,20},{32,40},... | collective-permute-start | bytes 1572872 | tf_op jit(solution)/shard_map/ppermute | solution.py:515
  62.7 9.1 %dnorm.1 = bf16[128,4096]{1,0:T(8,128)(2,1)} custom-call(bf16[128,2048]{1,0:T(8,128)(2,1)S(1)} %get-tuple-element.66.rows_ref.refs_4_, bf16[128,1024]{1,0:T(8,128)(2,1)S(1)} %collective-permute-done.6.got_ref, bf16[4096,1024]{1,0:T(8,128)(2,1)} %bitcast.14, bf16[4096,1024]{1,0:T(8,128)(2,1)} %bitcast.16), custom_call_target="tpu_custom_call" | custom-call | flops 134217728 | bytes 1048576 | tf_op jit(solution)/shard_map/dnorm/pallas_call | solution.py:427
  71.8 0.0 copy-start.3
  71.8 0.5 collective-permute-done.10.refs_5_
  72.3 4.5 %all-to-all-start.2 = ((bf16[4,32,4096]{2,1,0:T(8,128)(2,1)}), bf16[4,32,4096]{2,1,0:T(8,128)(2,1)S(1)}, u32[]{:S(2)}, u32[]{:S(2)}) async-start(bf16[4,32,4096]{2,1,0:T(8,128)(2,1)} %bitcast.17), calls=%async_computation.2 | async-start | bytes 2097152 | tf_op jit(solution)/shard_map/all_to_all | solution.py:781
  76.8 3.0 %far.1 = (bf16[128,2048]{1,0:T(8,128)(2,1)S(1)}, bf16[128,2048]{1,0:T(8,128)(2,1)S(1)}, bf16[512,2048]{1,0:T(8,128)(2,1)S(1)}) custom-call(bf16[2,4,32,1024]{3,2,1,0:T(8,128)(2,1)} %copy-done, bf16[2,4,32,1024]{3,2,1,0:T(8,128)(2,1)} %collective-permute-done.7.refs_1_, bf16[2,4,32,1024]{3,2,1,0:T(8,128)(2,1)} %copy-done.5, ...), custom_call_target="tpu_custom_call" | custom-call | flops 33554432 | bytes 524288 | tf_op jit(solution)/shard_map/far/pallas_call | solution.py:574
  79.7 1.1 collective-permute-start.13
  80.8 2.2 %collective-permute-start.14 = (bf16[128,2048]{1,0:T(8,128)(2,1)S(1)}, bf16[128,2048]{1,0:T(8,128)(2,1)S(1)}, u32[]{:S(2)}, u32[]{:S(2)}) collective-permute-start(bf16[128,2048]{1,0:T(8,128)(2,1)S(1)} %get-tuple-element.75), channel_id=1, source_target_pairs={{0,48},{4,52},{8,56},{12,60},{16,0},{20,4},{24,8},{28,12},{32,16},... | collective-permute-start | bytes 1572872 | tf_op jit(solution)/shard_map/ppermute | solution.py:515
  83.1 2.7 %middle.1 = (bf16[256,1024]{1,0:T(8,128)(2,1)}, bf16[256,1024]{1,0:T(8,128)(2,1)}) custom-call(bf16[2,4,32,1024]{3,2,1,0:T(8,128)(2,1)} %copy-done, bf16[2,4,32,1024]{3,2,1,0:T(8,128)(2,1)} %collective-permute-done.7.refs_1_, bf16[2,4,32,1024]{3,2,1,0:T(8,128)(2,1)} %copy-done.5, bf16[2,4,32,1024]{3,2,1,0:T(8,128)(2,1)} %collective-permute-done.9.refs_3_, ...), custom_call_target="tpu_custom_call" | custom-call | flops 33554432 | bytes 262144 | tf_op jit(solution)/shard_map/middle/pallas_call | solution.py:638
  85.8 4.4 %collective-permute-done.13.refs_5_ = bf16[128,2048]{1,0:T(8,128)(2,1)S(1)} collective-permute-done((bf16[128,2048]{1,0:T(8,128)(2,1)S(1)}, bf16[128,2048]{1,0:T(8,128)(2,1)S(1)}, u32[]{:S(2)}, u32[]{:S(2)}) %collective-permute-start.13) | collective-permute-done | bytes 524320 | tf_op jit(solution)/shard_map/ppermute | solution.py:515
  90.2 3.5 %side.1 = (bf16[256,2048]{1,0:T(8,128)(2,1)}, bf16[256,2048]{1,0:T(8,128)(2,1)S(1)}) custom-call(bf16[2,4,32,1024]{3,2,1,0:T(8,128)(2,1)} %copy-done, bf16[2,4,32,1024]{3,2,1,0:T(8,128)(2,1)} %collective-permute-done.7.refs_1_, bf16[2,4,32,1024]{3,2,1,0:T(8,128)(2,1)} %copy-done.5, bf16[2,4,32,1024]{3,2,1,0:T(8,128)(2,1)} %collective-permute-done.9.refs_3_, ...), custom_call_target="tpu_custom_call" | custom-call | flops 67108864 | bytes 262144 | tf_op jit(solution)/shard_map/side/pallas_call | solution.py:609
  93.7 1.3 %collective-permute-start.18 = (bf16[256,2048]{1,0:T(8,128)(2,1)}, bf16[256,2048]{1,0:T(8,128)(2,1)S(1)}, u32[]{:S(2)}, u32[]{:S(2)}) collective-permute-start(bf16[256,2048]{1,0:T(8,128)(2,1)} %get-tuple-element.82), channel_id=1, source_target_pairs={{0,16},{4,20},{8,24},{12,28},{16,32},{20,36},{24,40},{28,44},{32,4... | collective-permute-start | bytes 3145736 | tf_op jit(solution)/shard_map/ppermute | solution.py:515
  95.0 2.1 %collective-permute-start.19 = (bf16[256,2048]{1,0:T(8,128)(2,1)S(1)}, bf16[256,2048]{1,0:T(8,128)(2,1)S(1)}, u32[]{:S(2)}, u32[]{:S(2)}) collective-permute-start(bf16[256,2048]{1,0:T(8,128)(2,1)S(1)} %get-tuple-element.83), channel_id=1, source_target_pairs={{0,48},{4,52},{8,56},{12,60},{16,0},{20,4},{24,8},{28,12},{32,16},... | collective-permute-start | bytes 3145736 | tf_op jit(solution)/shard_map/ppermute | solution.py:515
  97.1 1.2 rms_back.1.refs_0_
  98.3 3.3 %collective-permute-start.16 = (bf16[32,4096]{1,0:T(8,128)(2,1)S(1)}, bf16[32,4096]{1,0:T(8,128)(2,1)S(1)}, u32[]{:S(2)}, u32[]{:S(2)}) collective-permute-start(bf16[32,4096]{1,0:T(8,128)(2,1)S(1)} %rms_back.1.refs_0_), channel_id=1, source_target_pairs={{0,3},{1,0},{2,1},{3,2},{4,7},{5,4},{6,5},{7,6},{8,11},{9,8},{10,9... | collective-permute-start | bytes 786440 | tf_op jit(solution)/shard_map/ppermute | solution.py:498
  101.6 8.4 %collective-permute-done.18.a_ref = bf16[256,2048]{1,0:T(8,128)(2,1)S(1)} collective-permute-done((bf16[256,2048]{1,0:T(8,128)(2,1)}, bf16[256,2048]{1,0:T(8,128)(2,1)S(1)}, u32[]{:S(2)}, u32[]{:S(2)}) %collective-permute-start.18) | collective-permute-done | bytes 1048608 | tf_op jit(solution)/shard_map/ppermute | solution.py:515
  110.0 1.1 cross.1
  111.1 0.1 collective-permute-start.20
  111.2 2.1 %collective-permute-start.17 = (bf16[32,4096]{1,0:T(8,128)(2,1)S(1)}, bf16[32,4096]{1,0:T(8,128)(2,1)S(1)}, u32[]{:S(2)}, u32[]{:S(2)}) collective-permute-start(bf16[32,4096]{1,0:T(8,128)(2,1)S(1)} %collective-permute-done.15.refs_1_), channel_id=1, source_target_pairs={{0,1},{1,2},{2,3},{3,0},{4,5},{5,6},{6,7},{7,4},{8,9},{9,10},{10,1... | collective-permute-start | bytes 786440 | tf_op jit(solution)/shard_map/ppermute | solution.py:498
  113.3 2.1 %own.1 = (f32[256,1024]{1,0:T(8,128)}, f32[256,1024]{1,0:T(8,128)}) custom-call(bf16[256,1024]{1,0:T(8,128)(2,1)} %get-tuple-element.81.own_hbm, bf16[256,2048]{1,0:T(8,128)(2,1)S(1)} %collective-permute-done.18.a_ref, bf16[256,2048]{1,0:T(8,128)(2,1)S(1)} %collective-permute-done.19.b_ref), custom_call_target="tpu_custom_call" | custom-call | flops 32768 | bytes 163840 | tf_op jit(solution)/shard_map/own/pallas_call | solution.py:716
  115.4 6.0 %collective-permute-done.17.refs_3_ = bf16[32,4096]{1,0:T(8,128)(2,1)S(1)} collective-permute-done((bf16[32,4096]{1,0:T(8,128)(2,1)S(1)}, bf16[32,4096]{1,0:T(8,128)(2,1)S(1)}, u32[]{:S(2)}, u32[]{:S(2)}) %collective-permute-start.17) | collective-permute-done | bytes 262176 | tf_op jit(solution)/shard_map/ppermute | solution.py:498
  121.4 1.0 place.1
  122.4 1.0 last.1
  (26 shorter events, 0.1 us)
Async XLA Ops:
  0.6 11.1 %copy-start.1 = (s32[16,16]{1,0:T(8,128)S(1)}, s32[16,16]{1,0:T(8,128)}, u32[]{:S(2)}) copy-start(s32[16,16]{1,0:T(8,128)} %src_ref.5) | copy-start | bytes 3076
  0.6 11.1 %copy-start.2 = (s32[16,16]{1,0:T(8,128)S(1)}, s32[16,16]{1,0:T(8,128)}, u32[]{:S(2)}) copy-start(s32[16,16]{1,0:T(8,128)} %dest_ref.5) | copy-start | bytes 3076
  0.7 33.5 %copy-start.4 = (s32[16,16]{1,0:T(8,128)S(1)}, s32[16,16]{1,0:T(8,128)}, u32[]{:S(2)}) copy-start(s32[16,16]{1,0:T(8,128)} %tgt_ref.1) | copy-start | bytes 3076
  9.8 1.6 %collective-permute-start = (bf16[128,1024]{1,0:T(8,128)(2,1)S(1)}, bf16[128,1024]{1,0:T(8,128)(2,1)S(1)}, u32[]{:S(2)}, u32[]{:S(2)}) collective-permute-start(bf16[128,1024]{1,0:T(8,128)(2,1)S(1)} %get-tuple-element.48), channel_id=1, source_target_pairs={{0,64},{64,0},{1,65},{65,1},{2,66},{66,2},{3,67},{67,3},{4,68},{68... | collective-permute-start | bytes 786440 | tf_op jit(solution)/shard_map/ppermute | solution.py:761
  10.0 1.8 %collective-permute-start.1 = (bf16[4,32,1024]{2,1,0:T(8,128)(2,1)S(1)}, bf16[4,32,1024]{2,1,0:T(8,128)(2,1)S(1)}, u32[]{:S(2)}, u32[]{:S(2)}) collective-permute-start(bf16[4,32,1024]{2,1,0:T(8,128)(2,1)S(1)} %get-tuple-element.50), channel_id=1, source_target_pairs={{0,64},{64,0},{1,65},{65,1},{2,66},{66,2},{3,67},{67,3},{4,68},{68... | collective-permute-start | bytes 786440 | tf_op jit(solution)/shard_map/ppermute | solution.py:762
  13.0 21.2 %all-to-all-start = ((bf16[16,16,1024]{2,1,0:T(8,128)(2,1)}), bf16[16,16,1024]{2,1,0:T(8,128)(2,1)S(1)}, u32[]{:S(2)}, u32[]{:S(2)}) async-start(bf16[16,16,1024]{2,1,0:T(8,128)(2,1)} %bitcast.3), calls=%async_computation | async-start | bytes 1048576 | tf_op jit(solution)/shard_map/all_to_all | solution.py:765
  21.4 11.0 %collective-permute-start.2 = (bf16[2,32,1024]{2,1,0:T(8,128)(2,1)S(1)}, bf16[2,32,1024]{2,1,0:T(8,128)(2,1)S(1)}, u32[]{:S(2)}, u32[]{:S(2)}) collective-permute-start(bf16[2,32,1024]{2,1,0:T(8,128)(2,1)S(1)} %get-tuple-element.53), channel_id=1, source_target_pairs={{0,4},{4,8},{8,12},{12,0},{16,20},{20,24},{24,28},{28,16},{32,36},... | collective-permute-start | bytes 393224 | tf_op jit(solution)/shard_map/ppermute | solution.py:515
  23.3 9.1 %collective-permute-start.3 = (bf16[2,32,1024]{2,1,0:T(8,128)(2,1)S(1)}, bf16[2,32,1024]{2,1,0:T(8,128)(2,1)S(1)}, u32[]{:S(2)}, u32[]{:S(2)}) collective-permute-start(bf16[2,32,1024]{2,1,0:T(8,128)(2,1)S(1)} %get-tuple-element.54), channel_id=1, source_target_pairs={{0,12},{4,0},{8,4},{12,8},{16,28},{20,16},{24,20},{28,24},{32,44},... | collective-permute-start | bytes 393224 | tf_op jit(solution)/shard_map/ppermute | solution.py:515
  24.7 9.4 %collective-permute-start.4 = (bf16[2,32,1024]{2,1,0:T(8,128)(2,1)S(1)}, bf16[2,32,1024]{2,1,0:T(8,128)(2,1)S(1)}, u32[]{:S(2)}, u32[]{:S(2)}) collective-permute-start(bf16[2,32,1024]{2,1,0:T(8,128)(2,1)S(1)} %get-tuple-element.55), channel_id=1, source_target_pairs={{0,8},{4,12},{8,0},{12,4},{16,24},{20,28},{24,16},{28,20},{32,40},... | collective-permute-start | bytes 393224 | tf_op jit(solution)/shard_map/ppermute | solution.py:515
  37.1 34.6 %copy-start = (bf16[2,4,32,1024]{3,2,1,0:T(8,128)(2,1)}, bf16[2,4,32,1024]{3,2,1,0:T(8,128)(2,1)S(1)}, u32[]{:S(2)}) copy-start(bf16[2,4,32,1024]{3,2,1,0:T(8,128)(2,1)S(1)} %get-tuple-element.56.refs_0_) | copy-start | bytes 1572868
  37.1 16.5 %all-to-all-start.1 = ((bf16[16,16,1024]{2,1,0:T(8,128)(2,1)}), bf16[16,16,1024]{2,1,0:T(8,128)(2,1)S(1)}, u32[]{:S(2)}, u32[]{:S(2)}) async-start(bf16[16,16,1024]{2,1,0:T(8,128)(2,1)} %bitcast.5), calls=%async_computation.1 | async-start | bytes 1048576 | tf_op jit(solution)/shard_map/all_to_all | solution.py:771
  42.1 15.7 %collective-permute-start.8 = (bf16[2,4,32,1024]{3,2,1,0:T(8,128)(2,1)S(1)}, bf16[2,4,32,1024]{3,2,1,0:T(8,128)(2,1)S(1)}, u32[]{:S(2)}, u32[]{:S(2)}) collective-permute-start(bf16[2,4,32,1024]{3,2,1,0:T(8,128)(2,1)S(1)} %get-tuple-element.56.refs_0_), channel_id=1, source_target_pairs={{0,3},{1,0},{2,1},{3,2},{4,7},{5,4},{6,5},{7,6},{8,11},{9,8},{10,9... | collective-permute-start | bytes 1572872 | tf_op jit(solution)/shard_map/ppermute | solution.py:498
  45.2 14.4 %collective-permute-start.7 = (bf16[2,4,32,1024]{3,2,1,0:T(8,128)(2,1)S(1)}, bf16[2,4,32,1024]{3,2,1,0:T(8,128)(2,1)}, u32[]{:S(2)}, u32[]{:S(2)}) collective-permute-start(bf16[2,4,32,1024]{3,2,1,0:T(8,128)(2,1)S(1)} %get-tuple-element.56.refs_0_), channel_id=1, source_target_pairs={{0,1},{1,2},{2,3},{3,0},{4,5},{5,6},{6,7},{7,4},{8,9},{9,10},{10,1... | collective-permute-start | bytes 1572872 | tf_op jit(solution)/shard_map/ppermute | solution.py:498
  54.0 1.6 %collective-permute-start.5 = (bf16[128,1024]{1,0:T(8,128)(2,1)S(1)}, bf16[128,1024]{1,0:T(8,128)(2,1)S(1)}, u32[]{:S(2)}, u32[]{:S(2)}) collective-permute-start(bf16[128,1024]{1,0:T(8,128)(2,1)S(1)} %get-tuple-element.60), channel_id=1, source_target_pairs={{0,64},{64,0},{1,65},{65,1},{2,66},{66,2},{3,67},{67,3},{4,68},{68... | collective-permute-start | bytes 786440 | tf_op jit(solution)/shard_map/ppermute | solution.py:773
  55.7 16.1 %collective-permute-start.11 = (bf16[128,2048]{1,0:T(8,128)(2,1)S(1)}, bf16[128,2048]{1,0:T(8,128)(2,1)S(1)}, u32[]{:S(2)}, u32[]{:S(2)}) collective-permute-start(bf16[128,2048]{1,0:T(8,128)(2,1)S(1)} %get-tuple-element.66.rows_ref.refs_4_), channel_id=1, source_target_pairs={{0,12},{4,0},{8,4},{12,8},{16,28},{20,16},{24,20},{28,24},{32,44},... | collective-permute-start | bytes 1572872 | tf_op jit(solution)/shard_map/ppermute | solution.py:515
  56.2 16.0 %collective-permute-start.10 = (bf16[128,2048]{1,0:T(8,128)(2,1)S(1)}, bf16[128,2048]{1,0:T(8,128)(2,1)S(1)}, u32[]{:S(2)}, u32[]{:S(2)}) collective-permute-start(bf16[128,2048]{1,0:T(8,128)(2,1)S(1)} %get-tuple-element.66.rows_ref.refs_4_), channel_id=1, source_target_pairs={{0,4},{4,8},{8,12},{12,0},{16,20},{20,24},{24,28},{28,16},{32,36},... | collective-permute-start | bytes 1572872 | tf_op jit(solution)/shard_map/ppermute | solution.py:515
  57.8 4.9 %collective-permute-start.6 = (bf16[128,1024]{1,0:T(8,128)(2,1)S(1)}, bf16[128,1024]{1,0:T(8,128)(2,1)S(1)}, u32[]{:S(2)}, u32[]{:S(2)}) collective-permute-start(bf16[128,1024]{1,0:T(8,128)(2,1)S(1)} %get-tuple-element.61), channel_id=1, source_target_pairs={{0,64},{64,0},{1,65},{65,1},{2,66},{66,2},{3,67},{67,3},{4,68},{68... | collective-permute-start | bytes 786440 | tf_op jit(solution)/shard_map/ppermute | solution.py:777
  57.8 14.0 %copy-start.5 = (bf16[2,4,32,1024]{3,2,1,0:T(8,128)(2,1)}, bf16[2,4,32,1024]{3,2,1,0:T(8,128)(2,1)S(1)}, u32[]{:S(2)}) copy-start(bf16[2,4,32,1024]{3,2,1,0:T(8,128)(2,1)S(1)} %collective-permute-done.8.refs_2_) | copy-start | bytes 1572868
  59.6 17.2 %collective-permute-start.9 = (bf16[2,4,32,1024]{3,2,1,0:T(8,128)(2,1)}, bf16[2,4,32,1024]{3,2,1,0:T(8,128)(2,1)}, u32[]{:S(2)}, u32[]{:S(2)}) collective-permute-start(bf16[2,4,32,1024]{3,2,1,0:T(8,128)(2,1)} %collective-permute-done.7.refs_1_), channel_id=1, source_target_pairs={{0,1},{1,2},{2,3},{3,0},{4,5},{5,6},{6,7},{7,4},{8,9},{9,10},{10,1... | collective-permute-start | bytes 1572872 | tf_op jit(solution)/shard_map/ppermute | solution.py:498
  59.6 17.2 %collective-permute-start.12 = (bf16[128,2048]{1,0:T(8,128)(2,1)S(1)}, bf16[128,2048]{1,0:T(8,128)(2,1)}, u32[]{:S(2)}, u32[]{:S(2)}) collective-permute-start(bf16[128,2048]{1,0:T(8,128)(2,1)S(1)} %get-tuple-element.66.rows_ref.refs_4_), channel_id=1, source_target_pairs={{0,8},{4,12},{8,0},{12,4},{16,24},{20,28},{24,16},{28,20},{32,40},... | collective-permute-start | bytes 1572872 | tf_op jit(solution)/shard_map/ppermute | solution.py:515
  71.8 25.3 %copy-start.3 = (f32[1,4096]{1,0:T(1,128)S(1)}, f32[1,4096]{1,0:T(1,128)}, u32[]{:S(2)}) copy-start(f32[1,4096]{1,0:T(1,128)} %gain_ref.1) | copy-start | bytes 49156
  72.3 22.7 %all-to-all-start.2 = ((bf16[4,32,4096]{2,1,0:T(8,128)(2,1)}), bf16[4,32,4096]{2,1,0:T(8,128)(2,1)S(1)}, u32[]{:S(2)}, u32[]{:S(2)}) async-start(bf16[4,32,4096]{2,1,0:T(8,128)(2,1)} %bitcast.17), calls=%async_computation.2 | async-start | bytes 2097152 | tf_op jit(solution)/shard_map/all_to_all | solution.py:781
  79.7 10.5 %collective-permute-start.13 = (bf16[128,2048]{1,0:T(8,128)(2,1)S(1)}, bf16[128,2048]{1,0:T(8,128)(2,1)S(1)}, u32[]{:S(2)}, u32[]{:S(2)}) collective-permute-start(bf16[128,2048]{1,0:T(8,128)(2,1)S(1)} %get-tuple-element.74), channel_id=1, source_target_pairs={{0,16},{4,20},{8,24},{12,28},{16,32},{20,36},{24,40},{28,44},{32,4... | collective-permute-start | bytes 1572872 | tf_op jit(solution)/shard_map/ppermute | solution.py:515
  80.8 9.4 %collective-permute-start.14 = (bf16[128,2048]{1,0:T(8,128)(2,1)S(1)}, bf16[128,2048]{1,0:T(8,128)(2,1)S(1)}, u32[]{:S(2)}, u32[]{:S(2)}) collective-permute-start(bf16[128,2048]{1,0:T(8,128)(2,1)S(1)} %get-tuple-element.75), channel_id=1, source_target_pairs={{0,48},{4,52},{8,56},{12,60},{16,0},{20,4},{24,8},{28,12},{32,16},... | collective-permute-start | bytes 1572872 | tf_op jit(solution)/shard_map/ppermute | solution.py:515
  93.7 16.3 %collective-permute-start.18 = (bf16[256,2048]{1,0:T(8,128)(2,1)}, bf16[256,2048]{1,0:T(8,128)(2,1)S(1)}, u32[]{:S(2)}, u32[]{:S(2)}) collective-permute-start(bf16[256,2048]{1,0:T(8,128)(2,1)} %get-tuple-element.82), channel_id=1, source_target_pairs={{0,16},{4,20},{8,24},{12,28},{16,32},{20,36},{24,40},{28,44},{32,4... | collective-permute-start | bytes 3145736 | tf_op jit(solution)/shard_map/ppermute | solution.py:515
  95.0 15.0 %collective-permute-start.19 = (bf16[256,2048]{1,0:T(8,128)(2,1)S(1)}, bf16[256,2048]{1,0:T(8,128)(2,1)S(1)}, u32[]{:S(2)}, u32[]{:S(2)}) collective-permute-start(bf16[256,2048]{1,0:T(8,128)(2,1)S(1)} %get-tuple-element.83), channel_id=1, source_target_pairs={{0,48},{4,52},{8,56},{12,60},{16,0},{20,4},{24,8},{28,12},{32,16},... | collective-permute-start | bytes 3145736 | tf_op jit(solution)/shard_map/ppermute | solution.py:515
  98.3 12.9 %collective-permute-start.16 = (bf16[32,4096]{1,0:T(8,128)(2,1)S(1)}, bf16[32,4096]{1,0:T(8,128)(2,1)S(1)}, u32[]{:S(2)}, u32[]{:S(2)}) collective-permute-start(bf16[32,4096]{1,0:T(8,128)(2,1)S(1)} %rms_back.1.refs_0_), channel_id=1, source_target_pairs={{0,3},{1,0},{2,1},{3,2},{4,7},{5,4},{6,5},{7,6},{8,11},{9,8},{10,9... | collective-permute-start | bytes 786440 | tf_op jit(solution)/shard_map/ppermute | solution.py:498
  101.6 9.7 %collective-permute-start.15 = (bf16[32,4096]{1,0:T(8,128)(2,1)S(1)}, bf16[32,4096]{1,0:T(8,128)(2,1)S(1)}, u32[]{:S(2)}, u32[]{:S(2)}) collective-permute-start(bf16[32,4096]{1,0:T(8,128)(2,1)S(1)} %rms_back.1.refs_0_), channel_id=1, source_target_pairs={{0,1},{1,2},{2,3},{3,0},{4,5},{5,6},{6,7},{7,4},{8,9},{9,10},{10,1... | collective-permute-start | bytes 786440 | tf_op jit(solution)/shard_map/ppermute | solution.py:498
  111.1 11.3 %collective-permute-start.20 = (bf16[256,1024]{1,0:T(8,128)(2,1)S(1)}, bf16[256,1024]{1,0:T(8,128)(2,1)S(1)}, u32[]{:S(2)}, u32[]{:S(2)}) collective-permute-start(bf16[256,1024]{1,0:T(8,128)(2,1)S(1)} %cross.1), channel_id=1, source_target_pairs={{0,64},{64,0},{1,65},{65,1},{2,66},{66,2},{3,67},{67,3},{4,68},{68... | collective-permute-start | bytes 1572872 | tf_op jit(solution)/shard_map/ppermute | solution.py:793
  111.2 10.2 %collective-permute-start.17 = (bf16[32,4096]{1,0:T(8,128)(2,1)S(1)}, bf16[32,4096]{1,0:T(8,128)(2,1)S(1)}, u32[]{:S(2)}, u32[]{:S(2)}) collective-permute-start(bf16[32,4096]{1,0:T(8,128)(2,1)S(1)} %collective-permute-done.15.refs_1_), channel_id=1, source_target_pairs={{0,1},{1,2},{2,3},{3,0},{4,5},{5,6},{6,7},{7,4},{8,9},{9,10},{10,1... | collective-permute-start | bytes 786440 | tf_op jit(solution)/shard_map/ppermute | solution.py:498

commit v9 on v7

--- a/solution.py
+++ b/solution.py
@@ -556,8 +556,8 @@
 
 def far_kernel(*refs):
     lefts, pieces = refs[:RING], refs[RING : 2 * RING]
-    top_ref, low_ref, rows_ref, buf, sems = refs[2 * RING :]
-    loads = left_loads(lefts, buf, sems, (2,))
+    top_ref, low_ref, rows_ref, other_ref, buf, sems = refs[2 * RING :]
+    loads = left_loads(lefts, buf, sems, (2, 0))
     for i, piece in enumerate(pieces):
         rows_ref[i * TOK : (i + 1) * TOK, :] = piece[...]
     half, cols = top_ref.shape[0], top_ref.shape[1] // 2
@@ -567,6 +567,9 @@
         block = tn(flat(buf[m, 0]), rows_ref[:, at]).astype(BF16)
         top_ref[:, at] = block[:half]
         low_ref[:, at] = block[half:]
+    wait_all(loads[0][1])
+    wait_all(loads[1][1])
+    other_ref[...] = tn(flat(buf[1, 1]), rows_ref[:, cols:]).astype(BF16)
 
 
 def far_block(lefts, pieces):
@@ -576,11 +579,16 @@
     return pl.pallas_call(
         far_kernel,
         in_specs=[HBM] * RING + [VMEM] * RING,
-        out_specs=[VMEM] * 3,
-        out_shape=[half, half, jax.ShapeDtypeStruct((RING * rows, cols), BF16)],
-        scratch_shapes=left_scratch(block, 1),
-        compiler_params=params(),
-        cost_estimate=cost(2 * RING * rows * block * cols, 8 * RING * rows * cols),
+        out_specs=[VMEM] * 4,
+        out_shape=[
+            half,
+            half,
+            jax.ShapeDtypeStruct((RING * rows, cols), BF16),
+            jax.ShapeDtypeStruct((block, cols // 2), BF16),
+        ],
+        scratch_shapes=left_scratch(block, 2),
+        compiler_params=params(),
+        cost_estimate=cost(3 * RING * rows * block * cols, 8 * RING * rows * cols),
         name="far",
     )(*[in_hbm(left) for left in lefts], *pieces)
 
@@ -622,40 +630,41 @@
 
 
 def middle_kernel(*refs):
-    lefts, (rows_ref, own_hbm, other_hbm, out_buf, buf, sems, out_sems) = refs[:RING], refs[RING:]
+    lefts, (rows_ref, own_hbm, out_buf, buf, sems, out_sem) = refs[:RING], refs[RING:]
     loads = left_loads(lefts, buf, sems, (0,))
-    cols = out_buf.shape[2]
-    puts = []
-    for m, out in enumerate((own_hbm, other_hbm)):
-        wait_all(loads[m][0])
-        at = slice(m * cols, (m + 1) * cols)
-        out_buf[m] = tn(flat(buf[m, 0]), rows_ref[:, at]).astype(BF16)
-        puts.append(pltpu.make_async_copy(out_buf.at[m], out, out_sems.at[m]))
-        puts[-1].start()
-    wait_all(puts)
-
-
-def middle_blocks(lefts, rows):
+    wait_all(loads[0][0])
+    wait_all(loads[1][0])
+    out_buf[...] = tn(flat(buf[0, 0]), rows_ref[:, : out_buf.shape[1]]).astype(BF16)
+    put = pltpu.make_async_copy(out_buf, own_hbm, out_sem)
+    put.start()
+    put.wait()
+
+
+def middle_block(lefts, rows):
     depth, cols = rows.shape
     block = lefts[0].shape[-1] // RING
     return pl.pallas_call(
         middle_kernel,
         in_specs=[HBM] * RING + [VMEM],
-        out_specs=[HBM] * 2,
-        out_shape=[pltpu.HBM((block, cols // 2), BF16)] * 2,
-        scratch_shapes=[pltpu.VMEM((2, block, cols // 2), BF16)]
+        out_specs=HBM,
+        out_shape=pltpu.HBM((block, cols // 2), BF16),
+        scratch_shapes=[pltpu.VMEM((block, cols // 2), BF16)]
         + left_scratch(block, 1)
-        + [pltpu.SemaphoreType.DMA((2,))],
-        compiler_params=params(),
-        cost_estimate=cost(2 * depth * block * cols, 4 * depth * cols),
+        + [pltpu.SemaphoreType.DMA],
+        compiler_params=params(),
+        cost_estimate=cost(depth * block * cols, 4 * depth * cols),
         name="middle",
     )(*[in_hbm(left) for left in lefts], rows)
 
 
-def own_kernel(own_hbm, other_ref, *refs):
-    parts, outs, (own_ref, out_buf, own_sem, out_sems) = refs[:4], refs[4:6], refs[6:]
-    get = pltpu.make_async_copy(own_hbm, own_ref, own_sem)
-    get.start()
+def own_kernel(own_hbm, other_hbm, *refs):
+    parts, outs, (base_ref, out_buf, base_sems, out_sems) = refs[:4], refs[4:6], refs[6:]
+    gets = [
+        pltpu.make_async_copy(base, base_ref.at[m], base_sems.at[m])
+        for m, base in enumerate((own_hbm, other_hbm))
+    ]
+    for get in gets:
+        get.start()
     core = lax.axis_index("section")
     chunks = out_sems.shape[1]
     size = out_buf.shape[1] // chunks
@@ -673,12 +682,11 @@
         def _():
             put(m, c, outs[1]).start()
 
-    for m, base in ((1, other_ref), (0, own_ref)):
-        if m == 0:
-            get.wait()
+    for m in range(2):
+        gets[m].wait()
         for c in range(chunks):
             at = slice(c * size, (c + 1) * size)
-            total_of = base[at].astype(F32) + parts[2 * m][at].astype(F32)
+            total_of = base_ref[m, at].astype(F32) + parts[2 * m][at].astype(F32)
             out_buf[m, at] = total_of + parts[2 * m + 1][at].astype(F32)
             write(m, c)
     for m in range(2):
@@ -690,19 +698,19 @@
     block, cols = own.shape
     return pl.pallas_call(
         own_kernel,
-        in_specs=[HBM] + [VMEM] * 5,
+        in_specs=[HBM] * 2 + [VMEM] * 4,
         out_specs=[HBM] * 2,
         out_shape=[pltpu.HBM((block, cols), F32)] * 2,
         scratch_shapes=[
-            pltpu.VMEM((block, cols), BF16),
+            pltpu.VMEM((2, block, cols), BF16),
             pltpu.VMEM((2, block, cols), F32),
-            pltpu.SemaphoreType.DMA,
+            pltpu.SemaphoreType.DMA((2,)),
             pltpu.SemaphoreType.DMA((2, 4)),
         ],
         compiler_params=params(),
         cost_estimate=cost(4 * block * cols, 20 * block * cols),
         name="own",
-    )(in_hbm(own), other, *parts)
+    )(in_hbm(own), in_hbm(other), *parts)
 
 
 def per_device(states, gains, proj_a, proj_b, cotangent, src_len, tgt_len, dest):
@@ -734,12 +742,13 @@
     parts = lax.all_to_all(
         partial.reshape(RING, TOK // RING, -1), "mp", split_axis=0, concat_axis=0, tiled=True
     )
-    top, low, stack = far_block(lefts, rights)
+    top, low, stack, own_other = far_block(lefts, rights)
     from_left, from_right = moved(top, 1, REDUCE), moved(low, 3, REDUCE)
-    parts, _, _ = lax.optimization_barrier((parts, from_left, from_right))
+    own = middle_block(lefts, stack)
+    crossed = lax.ppermute(own_other, "section", swap)
+    stack, own, crossed = lax.optimization_barrier((stack, own, crossed))
     right, right_other, left, left_other = side_blocks(lefts, stack, from_left, from_right)
-    own, own_other = middle_blocks(lefts, stack)
-    own_other, _ = lax.optimization_barrier((own_other, right))
+    left_other, parts = lax.optimization_barrier((left_other, parts))
     sums = [
         moved(right, 1, REDUCE),
         moved(left, 3, REDUCE),
@@ -748,7 +757,7 @@
     ]
     quarter = rms_back(rows, gains, parts)
     grad_states = place(gathered(quarter, "mp"))
-    grad_a, grad_b = own_blocks(own, lax.ppermute(own_other, "section", swap), sums)
+    grad_a, grad_b = own_blocks(own, crossed, sums)
     return (grad_states[None], grad_a[None], grad_b[None])
 
 

time: 117 us -> 120 us (1.026)
  waiting for transfers between devices: 32.6 us -> 40 us
  starting transfers between devices: 46.2 us -> 42.2 us
    ppermute x6, waiting for transfers between devices: 1.85 us -> 16.2 us  [shift(): return lax.ppermute(value, axis, [(i, (i + k) % RING) for i in range(RING)])]
    ppermute x12, waiting for transfers between devices: 19.6 us -> 12.5 us  [moved(): return lax.ppermute(value, ('section', 'z', 'x'), pairs)]
    ppermute x6, starting transfers between devices: 9.07 us -> 6.99 us  [shift(): return lax.ppermute(value, axis, [(i, (i + k) % RING) for i in range(RING)])]
    ppermute x12, starting transfers between devices: 18.4 us -> 16.6 us  [moved(): return lax.ppermute(value, ('section', 'z', 'x'), pairs)]
  transfers between devices with their start and end apart: 26 -> 26, of which waited for: 11 -> 12; matrix products, arithmetic and copies ran while one was open for 0% -> 0% of each run, Pallas kernels for 17% -> 15%
where the time goes in v9:
time: 120 us; the launch traced here: 119 us
  starting transfers between devices  42.2 us (35%)
  waiting for transfers between devices  40 us (33%)
  Pallas kernels  35.3 us (29%)
    ppermute x12, starting transfers between devices, moved(): return lax.ppermute(value, ('section', 'z', 'x'), pairs)  16.6 us
    ppermute x6, waiting for transfers between devices, shift(): return lax.ppermute(value, axis, [(i, (i + k) % RING) for i in range(RING)])  16.2 us
    ppermute x12, waiting for transfers between devices, moved(): return lax.ppermute(value, ('section', 'z', 'x'), pairs)  12.5 us
    pallas_call x1, Pallas kernels, forward(): pl.pallas_call(forward_kernel, in_specs=[HBM] * 5, out_specs=[VMEM] * 4,...  9.11 us
    pallas_call x1, Pallas kernels, dnorm_partial(): pl.pallas_call(dnorm_kernel, in_specs=[VMEM] * 2 + [HBM] * 2, out_specs=H...  9.07 us
    all_to_all x1, starting transfers between devices, per_device(): lax.all_to_all(slots, ('z', 'x'), split_axis=0, concat_axis=0, tiled=True)  8.42 us
    all_to_all x1, waiting for transfers between devices, per_device(): lax.all_to_all(back, ('z', 'x'), split_axis=0, concat_axis=0, tiled=True)  8.37 us
    ppermute x6, starting transfers between devices, shift(): return lax.ppermute(value, axis, [(i, (i + k) % RING) for i in range(RING)])  6.99 us
  transfers between devices with their start and end apart: 26, of which 12 were waited for; matrix products, arithmetic and copies ran while one was open for 0% of the time, Pallas kernels for 15%

profile of v9, /device:TPU:0, one launch (start us, length us, event | category | flops | bytes accessed | tf_op | source)
XLA Modules:
  0.0 118.6 jit_solution(10195125591223357957)
XLA Ops:
  0.7 9.1 %forward.1 = (bf16[128,1024]{1,0:T(8,128)(2,1)S(1)}, bf16[128,1024]{1,0:T(8,128)(2,1)S(1)}, bf16[4,32,1024]{2,1,0:T(8,128)(2,1)S(1)}, bf16[4,32,1024]{2,1,0:T(8,128)(2,1)S(1)}) custom-call(bf16[128,4096]{1,0:T(8,128)(2,1)} %bitcast.18, f32[1,4096]{1,0:T(1,128)} %gain_ref.1, bf16[128,4096]{1,0:T(8,128)(2,1)} %cot_hbm.1, bf16[4096,1024]{1,0:T(8,128)(2,1)} %bitcast.13, ...), custom_call_target="tpu_custom_call" | custom-call | flops 134217728 | bytes 1048576 | tf_op jit(solution)/shard_map/forward/pallas_call | solution.py:189
  9.8 0.2 collective-permute-start
  10.0 0.4 collective-permute-start.1
  10.4 1.0 collective-permute-done.got_ref
  11.4 0.4 collective-permute-done.1.other_ref
  11.8 1.2 pack.1
  13.0 8.4 %all-to-all-start = ((bf16[16,16,1024]{2,1,0:T(8,128)(2,1)}), bf16[16,16,1024]{2,1,0:T(8,128)(2,1)S(1)}, u32[]{:S(2)}, u32[]{:S(2)}) async-start(bf16[16,16,1024]{2,1,0:T(8,128)(2,1)} %bitcast.3), calls=%async_computation | async-start | bytes 1048576 | tf_op jit(solution)/shard_map/all_to_all | solution.py:726
  21.4 1.9 %collective-permute-start.2 = (bf16[2,32,1024]{2,1,0:T(8,128)(2,1)S(1)}, bf16[2,32,1024]{2,1,0:T(8,128)(2,1)S(1)}, u32[]{:S(2)}, u32[]{:S(2)}) collective-permute-start(bf16[2,32,1024]{2,1,0:T(8,128)(2,1)S(1)} %get-tuple-element.50), channel_id=1, source_target_pairs={{0,4},{4,8},{8,12},{12,0},{16,20},{20,24},{24,28},{28,16},{32,36},... | collective-permute-start | bytes 393224 | tf_op jit(solution)/shard_map/ppermute | solution.py:517
  23.3 1.4 %collective-permute-start.3 = (bf16[2,32,1024]{2,1,0:T(8,128)(2,1)S(1)}, bf16[2,32,1024]{2,1,0:T(8,128)(2,1)S(1)}, u32[]{:S(2)}, u32[]{:S(2)}) collective-permute-start(bf16[2,32,1024]{2,1,0:T(8,128)(2,1)S(1)} %get-tuple-element.51), channel_id=1, source_target_pairs={{0,12},{4,0},{8,4},{12,8},{16,28},{20,16},{24,20},{28,24},{32,44},... | collective-permute-start | bytes 393224 | tf_op jit(solution)/shard_map/ppermute | solution.py:517
  24.7 2.2 %collective-permute-start.4 = (bf16[2,32,1024]{2,1,0:T(8,128)(2,1)S(1)}, bf16[2,32,1024]{2,1,0:T(8,128)(2,1)S(1)}, u32[]{:S(2)}, u32[]{:S(2)}) collective-permute-start(bf16[2,32,1024]{2,1,0:T(8,128)(2,1)S(1)} %get-tuple-element.52), channel_id=1, source_target_pairs={{0,8},{4,12},{8,0},{12,4},{16,24},{20,28},{24,16},{28,20},{32,40},... | collective-permute-start | bytes 393224 | tf_op jit(solution)/shard_map/ppermute | solution.py:517
  26.8 5.6 %collective-permute-done.2.rest_1_ = bf16[2,32,1024]{2,1,0:T(8,128)(2,1)S(1)} collective-permute-done((bf16[2,32,1024]{2,1,0:T(8,128)(2,1)S(1)}, bf16[2,32,1024]{2,1,0:T(8,128)(2,1)S(1)}, u32[]{:S(2)}, u32[]{:S(2)}) %collective-permute-start.2) | collective-permute-done | bytes 131104 | tf_op jit(solution)/shard_map/ppermute | solution.py:517
  32.4 1.7 %collective-permute-done.4.rest_3_ = bf16[2,32,1024]{2,1,0:T(8,128)(2,1)S(1)} collective-permute-done((bf16[2,32,1024]{2,1,0:T(8,128)(2,1)S(1)}, bf16[2,32,1024]{2,1,0:T(8,128)(2,1)S(1)}, u32[]{:S(2)}, u32[]{:S(2)}) %collective-permute-start.4) | collective-permute-done | bytes 131104 | tf_op jit(solution)/shard_map/ppermute | solution.py:517
  34.2 2.9 %attend.1 = (bf16[128,1024]{1,0:T(8,128)(2,1)S(1)}, bf16[256,1024]{1,0:T(8,128)(2,1)}, bf16[2,4,32,1024]{3,2,1,0:T(8,128)(2,1)S(1)}) custom-call(bf16[128,1024]{1,0:T(8,128)(2,1)S(1)} %get-tuple-element.44.keep_ref, bf16[128,1024]{1,0:T(8,128)(2,1)S(1)} %collective-permute-done.got_ref, bf16[256,1024]{1,0:T(8,128)(2,1)S(1)} %bitcast.11, ...), custom_call_target="tpu_custom_call" | custom-call | flops 50331648 | bytes 131072 | tf_op jit(solution)/shard_map/attend/pallas_call | solution.py:300
  37.1 5.0 %all-to-all-start.1 = ((bf16[16,16,1024]{2,1,0:T(8,128)(2,1)}), bf16[16,16,1024]{2,1,0:T(8,128)(2,1)S(1)}, u32[]{:S(2)}, u32[]{:S(2)}) async-start(bf16[16,16,1024]{2,1,0:T(8,128)(2,1)} %bitcast.5), calls=%async_computation.1 | async-start | bytes 1048576 | tf_op jit(solution)/shard_map/all_to_all | solution.py:732
  42.1 3.1 %collective-permute-start.8 = (bf16[2,4,32,1024]{3,2,1,0:T(8,128)(2,1)S(1)}, bf16[2,4,32,1024]{3,2,1,0:T(8,128)(2,1)S(1)}, u32[]{:S(2)}, u32[]{:S(2)}) collective-permute-start(bf16[2,4,32,1024]{3,2,1,0:T(8,128)(2,1)S(1)} %get-tuple-element.53.refs_0_), channel_id=1, source_target_pairs={{0,3},{1,0},{2,1},{3,2},{4,7},{5,4},{6,5},{7,6},{8,11},{9,8},{10,9... | collective-permute-start | bytes 1572872 | tf_op jit(solution)/shard_map/ppermute | solution.py:498
  45.2 8.4 %all-to-all-done.1 = bf16[16,16,1024]{2,1,0:T(8,128)(2,1)S(1)} async-done(((bf16[16,16,1024]{2,1,0:T(8,128)(2,1)}), bf16[16,16,1024]{2,1,0:T(8,128)(2,1)S(1)}, u32[]{:S(2)}, u32[]{:S(2)}) %all-to-all-start.1) | async-done | bytes 524320 | tf_op jit(solution)/shard_map/all_to_all | solution.py:732
  53.6 0.4 unpack.1
  54.0 0.1 collective-permute-start.5
  54.1 1.5 %collective-permute-done.5.got_ref = bf16[128,1024]{1,0:T(8,128)(2,1)S(1)} collective-permute-done((bf16[128,1024]{1,0:T(8,128)(2,1)S(1)}, bf16[128,1024]{1,0:T(8,128)(2,1)S(1)}, u32[]{:S(2)}, u32[]{:S(2)}) %collective-permute-start.5) | collective-permute-done | bytes 262176 | tf_op jit(solution)/shard_map/ppermute | solution.py:734
  55.6 0.1 join.1
  55.7 0.6 collective-permute-start.11
  56.2 1.5 %collective-permute-start.10 = (bf16[128,2048]{1,0:T(8,128)(2,1)S(1)}, bf16[128,2048]{1,0:T(8,128)(2,1)S(1)}, u32[]{:S(2)}, u32[]{:S(2)}) collective-permute-start(bf16[128,2048]{1,0:T(8,128)(2,1)S(1)} %get-tuple-element.63.rows_ref.refs_4_), channel_id=1, source_target_pairs={{0,4},{4,8},{8,12},{12,0},{16,20},{20,24},{24,28},{28,16},{32,36},... | collective-permute-start | bytes 1572872 | tf_op jit(solution)/shard_map/ppermute | solution.py:517
  57.8 1.8 %collective-permute-done.7.refs_1_ = bf16[2,4,32,1024]{3,2,1,0:T(8,128)(2,1)} collective-permute-done((bf16[2,4,32,1024]{3,2,1,0:T(8,128)(2,1)S(1)}, bf16[2,4,32,1024]{3,2,1,0:T(8,128)(2,1)}, u32[]{:S(2)}, u32[]{:S(2)}) %collective-permute-start.7) | collective-permute-done | bytes 524320 | tf_op jit(solution)/shard_map/ppermute | solution.py:498
  59.6 0.6 collective-permute-start.9
  60.2 2.5 %collective-permute-start.12 = (bf16[128,2048]{1,0:T(8,128)(2,1)S(1)}, bf16[128,2048]{1,0:T(8,128)(2,1)S(1)}, u32[]{:S(2)}, u32[]{:S(2)}) collective-permute-start(bf16[128,2048]{1,0:T(8,128)(2,1)S(1)} %get-tuple-element.63.rows_ref.refs_4_), channel_id=1, source_target_pairs={{0,8},{4,12},{8,0},{12,4},{16,24},{20,28},{24,16},{28,20},{32,40},... | collective-permute-start | bytes 1572872 | tf_op jit(solution)/shard_map/ppermute | solution.py:517
  62.6 0.0 collective-permute-done.6.got_ref
  62.7 9.1 %dnorm.1 = bf16[128,4096]{1,0:T(8,128)(2,1)} custom-call(bf16[128,2048]{1,0:T(8,128)(2,1)S(1)} %get-tuple-element.63.rows_ref.refs_4_, bf16[128,1024]{1,0:T(8,128)(2,1)S(1)} %collective-permute-done.6.got_ref, bf16[4096,1024]{1,0:T(8,128)(2,1)} %bitcast.14, bf16[4096,1024]{1,0:T(8,128)(2,1)} %bitcast.16), custom_call_target="tpu_custom_call" | custom-call | flops 134217728 | bytes 1048576 | tf_op jit(solution)/shard_map/dnorm/pallas_call | solution.py:427
  71.7 0.0 copy-start.3
  71.8 0.5 collective-permute-done.10.refs_5_
  72.2 4.5 %all-to-all-start.2 = ((bf16[4,32,4096]{2,1,0:T(8,128)(2,1)}), bf16[4,32,4096]{2,1,0:T(8,128)(2,1)S(1)}, u32[]{:S(2)}, u32[]{:S(2)}) async-start(bf16[4,32,4096]{2,1,0:T(8,128)(2,1)} %bitcast.17), calls=%async_computation.2 | async-start | bytes 2097152 | tf_op jit(solution)/shard_map/all_to_all | solution.py:742
  76.7 0.0 collective-permute-done.9.refs_3_
  76.7 0.0 collective-permute-done.12.refs_7_
  76.8 2.5 %far.1 = (bf16[128,2048]{1,0:T(8,128)(2,1)S(1)}, bf16[128,2048]{1,0:T(8,128)(2,1)S(1)}, bf16[512,2048]{1,0:T(8,128)(2,1)S(1)}, bf16[256,1024]{1,0:T(8,128)(2,1)S(1)}) custom-call(bf16[2,4,32,1024]{3,2,1,0:T(8,128)(2,1)} %copy-done, bf16[2,4,32,1024]{3,2,1,0:T(8,128)(2,1)} %collective-permute-done.7.refs_1_, bf16[2,4,32,1024]{3,2,1,0:T(8,128)(2,1)} %copy-done.5, ...), custom_call_target="tpu_custom_call" | custom-call | flops 50331648 | bytes 524288 | tf_op jit(solution)/shard_map/far/pallas_call | solution.py:579
  79.3 0.1 collective-permute-start.13
  79.4 1.1 collective-permute-start.14
  80.4 2.2 %collective-permute-start.15 = (bf16[128,2048]{1,0:T(8,128)(2,1)S(1)}, bf16[128,2048]{1,0:T(8,128)(2,1)S(1)}, u32[]{:S(2)}, u32[]{:S(2)}) collective-permute-start(bf16[128,2048]{1,0:T(8,128)(2,1)S(1)} %get-tuple-element.71), channel_id=1, source_target_pairs={{0,48},{4,52},{8,56},{12,60},{16,0},{20,4},{24,8},{28,12},{32,16},... | collective-permute-start | bytes 1572872 | tf_op jit(solution)/shard_map/ppermute | solution.py:517
  82.7 2.4 %middle.1.own_hbm = bf16[256,1024]{1,0:T(8,128)(2,1)} custom-call(bf16[2,4,32,1024]{3,2,1,0:T(8,128)(2,1)} %copy-done, bf16[2,4,32,1024]{3,2,1,0:T(8,128)(2,1)} %collective-permute-done.7.refs_1_, bf16[2,4,32,1024]{3,2,1,0:T(8,128)(2,1)} %copy-done.5, bf16[2,4,32,1024]{3,2,1,0:T(8,128)(2,1)} %collective-permute-done.9.refs_3_, ...), custom_call_target="tpu_custom_call" | custom-call | flops 16777216 | bytes 262144 | tf_op jit(solution)/shard_map/middle/pallas_call | solution.py:646
  85.1 4.7 %collective-permute-done.14.refs_5_ = bf16[128,2048]{1,0:T(8,128)(2,1)S(1)} collective-permute-done((bf16[128,2048]{1,0:T(8,128)(2,1)S(1)}, bf16[128,2048]{1,0:T(8,128)(2,1)S(1)}, u32[]{:S(2)}, u32[]{:S(2)}) %collective-permute-start.14) | collective-permute-done | bytes 524320 | tf_op jit(solution)/shard_map/ppermute | solution.py:517
  89.8 2.9 %side.1 = (bf16[256,1024]{1,0:T(8,128)(2,1)S(1)}, bf16[256,1024]{1,0:T(8,128)(2,1)S(1)}, bf16[256,1024]{1,0:T(8,128)(2,1)S(1)}, bf16[256,1024]{1,0:T(8,128)(2,1)S(1)}) custom-call(bf16[2,4,32,1024]{3,2,1,0:T(8,128)(2,1)} %copy-done, bf16[2,4,32,1024]{3,2,1,0:T(8,128)(2,1)} %collective-permute-done.7.refs_1_, bf16[2,4,32,1024]{3,2,1,0:T(8,128)(2,1)} %copy-done.5, ...), custom_call_target="tpu_custom_call" | custom-call | flops 67108864 | bytes 262144 | tf_op jit(solution)/shard_map/side/pallas_call | solution.py:620
  92.8 1.2 rms_back.1.refs_0_
  94.0 3.3 %collective-permute-start.17 = (bf16[32,4096]{1,0:T(8,128)(2,1)S(1)}, bf16[32,4096]{1,0:T(8,128)(2,1)S(1)}, u32[]{:S(2)}, u32[]{:S(2)}) collective-permute-start(bf16[32,4096]{1,0:T(8,128)(2,1)S(1)} %rms_back.1.refs_0_), channel_id=1, source_target_pairs={{0,3},{1,0},{2,1},{3,2},{4,7},{5,4},{6,5},{7,6},{8,11},{9,8},{10,9... | collective-permute-start | bytes 786440 | tf_op jit(solution)/shard_map/ppermute | solution.py:498
  97.3 1.3 %collective-permute-start.19 = (bf16[256,1024]{1,0:T(8,128)(2,1)S(1)}, bf16[256,1024]{1,0:T(8,128)(2,1)S(1)}, u32[]{:S(2)}, u32[]{:S(2)}) collective-permute-start(bf16[256,1024]{1,0:T(8,128)(2,1)S(1)} %get-tuple-element.79), channel_id=1, source_target_pairs={{0,16},{4,20},{8,24},{12,28},{16,32},{20,36},{24,40},{28,44},{32,4... | collective-permute-start | bytes 1572872 | tf_op jit(solution)/shard_map/ppermute | solution.py:517
  98.5 2.0 %collective-permute-start.20 = (bf16[256,1024]{1,0:T(8,128)(2,1)S(1)}, bf16[256,1024]{1,0:T(8,128)(2,1)S(1)}, u32[]{:S(2)}, u32[]{:S(2)}) collective-permute-start(bf16[256,1024]{1,0:T(8,128)(2,1)S(1)} %get-tuple-element.80), channel_id=1, source_target_pairs={{0,48},{4,52},{8,56},{12,60},{16,0},{20,4},{24,8},{28,12},{32,16},... | collective-permute-start | bytes 1572872 | tf_op jit(solution)/shard_map/ppermute | solution.py:517
  100.5 2.1 %collective-permute-done.17.refs_2_ = bf16[32,4096]{1,0:T(8,128)(2,1)S(1)} collective-permute-done((bf16[32,4096]{1,0:T(8,128)(2,1)S(1)}, bf16[32,4096]{1,0:T(8,128)(2,1)S(1)}, u32[]{:S(2)}, u32[]{:S(2)}) %collective-permute-start.17) | collective-permute-done | bytes 262176 | tf_op jit(solution)/shard_map/ppermute | solution.py:498
  102.6 3.4 %collective-permute-done.16.refs_1_ = bf16[32,4096]{1,0:T(8,128)(2,1)S(1)} collective-permute-done((bf16[32,4096]{1,0:T(8,128)(2,1)S(1)}, bf16[32,4096]{1,0:T(8,128)(2,1)S(1)}, u32[]{:S(2)}, u32[]{:S(2)}) %collective-permute-start.16) | collective-permute-done | bytes 262176 | tf_op jit(solution)/shard_map/ppermute | solution.py:498
  106.0 8.9 %collective-permute-done.18.refs_3_ = bf16[32,4096]{1,0:T(8,128)(2,1)S(1)} collective-permute-done((bf16[32,4096]{1,0:T(8,128)(2,1)S(1)}, bf16[32,4096]{1,0:T(8,128)(2,1)S(1)}, u32[]{:S(2)}, u32[]{:S(2)}) %collective-permute-start.18) | collective-permute-done | bytes 262176 | tf_op jit(solution)/shard_map/ppermute | solution.py:498
  114.9 1.0 place.1
  115.9 2.5 %own.1 = (f32[256,1024]{1,0:T(8,128)}, f32[256,1024]{1,0:T(8,128)}) custom-call(bf16[256,1024]{1,0:T(8,128)(2,1)} %middle.1.own_hbm, bf16[256,1024]{1,0:T(8,128)(2,1)} %copy-done.6, bf16[256,1024]{1,0:T(8,128)(2,1)S(1)} %collective-permute-done.19.refs_0_, bf16[256,1024]{1,0:T(8,128)(2,1)S(1)} %collective-permute-done.20.refs_1_, ...), custom_call_target="tpu_custom_call" | custom-call | flops 65536 | bytes 327680 | tf_op jit(solution)/shard_map/own/pallas_call | solution.py:699
  (30 shorter events, 0.1 us)
Async XLA Ops:
  0.6 11.1 %copy-start.1 = (s32[16,16]{1,0:T(8,128)S(1)}, s32[16,16]{1,0:T(8,128)}, u32[]{:S(2)}) copy-start(s32[16,16]{1,0:T(8,128)} %src_ref.5) | copy-start | bytes 3076
  0.6 11.1 %copy-start.2 = (s32[16,16]{1,0:T(8,128)S(1)}, s32[16,16]{1,0:T(8,128)}, u32[]{:S(2)}) copy-start(s32[16,16]{1,0:T(8,128)} %dest_ref.5) | copy-start | bytes 3076
  0.7 33.5 %copy-start.4 = (s32[16,16]{1,0:T(8,128)S(1)}, s32[16,16]{1,0:T(8,128)}, u32[]{:S(2)}) copy-start(s32[16,16]{1,0:T(8,128)} %tgt_ref.1) | copy-start | bytes 3076
  9.8 1.6 %collective-permute-start = (bf16[128,1024]{1,0:T(8,128)(2,1)S(1)}, bf16[128,1024]{1,0:T(8,128)(2,1)S(1)}, u32[]{:S(2)}, u32[]{:S(2)}) collective-permute-start(bf16[128,1024]{1,0:T(8,128)(2,1)S(1)} %get-tuple-element.45), channel_id=1, source_target_pairs={{0,64},{64,0},{1,65},{65,1},{2,66},{66,2},{3,67},{67,3},{4,68},{68... | collective-permute-start | bytes 786440 | tf_op jit(solution)/shard_map/ppermute | solution.py:722
  10.0 1.8 %collective-permute-start.1 = (bf16[4,32,1024]{2,1,0:T(8,128)(2,1)S(1)}, bf16[4,32,1024]{2,1,0:T(8,128)(2,1)S(1)}, u32[]{:S(2)}, u32[]{:S(2)}) collective-permute-start(bf16[4,32,1024]{2,1,0:T(8,128)(2,1)S(1)} %get-tuple-element.47), channel_id=1, source_target_pairs={{0,64},{64,0},{1,65},{65,1},{2,66},{66,2},{3,67},{67,3},{4,68},{68... | collective-permute-start | bytes 786440 | tf_op jit(solution)/shard_map/ppermute | solution.py:723
  13.0 21.2 %all-to-all-start = ((bf16[16,16,1024]{2,1,0:T(8,128)(2,1)}), bf16[16,16,1024]{2,1,0:T(8,128)(2,1)S(1)}, u32[]{:S(2)}, u32[]{:S(2)}) async-start(bf16[16,16,1024]{2,1,0:T(8,128)(2,1)} %bitcast.3), calls=%async_computation | async-start | bytes 1048576 | tf_op jit(solution)/shard_map/all_to_all | solution.py:726
  21.4 11.0 %collective-permute-start.2 = (bf16[2,32,1024]{2,1,0:T(8,128)(2,1)S(1)}, bf16[2,32,1024]{2,1,0:T(8,128)(2,1)S(1)}, u32[]{:S(2)}, u32[]{:S(2)}) collective-permute-start(bf16[2,32,1024]{2,1,0:T(8,128)(2,1)S(1)} %get-tuple-element.50), channel_id=1, source_target_pairs={{0,4},{4,8},{8,12},{12,0},{16,20},{20,24},{24,28},{28,16},{32,36},... | collective-permute-start | bytes 393224 | tf_op jit(solution)/shard_map/ppermute | solution.py:517
  23.3 9.1 %collective-permute-start.3 = (bf16[2,32,1024]{2,1,0:T(8,128)(2,1)S(1)}, bf16[2,32,1024]{2,1,0:T(8,128)(2,1)S(1)}, u32[]{:S(2)}, u32[]{:S(2)}) collective-permute-start(bf16[2,32,1024]{2,1,0:T(8,128)(2,1)S(1)} %get-tuple-element.51), channel_id=1, source_target_pairs={{0,12},{4,0},{8,4},{12,8},{16,28},{20,16},{24,20},{28,24},{32,44},... | collective-permute-start | bytes 393224 | tf_op jit(solution)/shard_map/ppermute | solution.py:517
  24.7 9.4 %collective-permute-start.4 = (bf16[2,32,1024]{2,1,0:T(8,128)(2,1)S(1)}, bf16[2,32,1024]{2,1,0:T(8,128)(2,1)S(1)}, u32[]{:S(2)}, u32[]{:S(2)}) collective-permute-start(bf16[2,32,1024]{2,1,0:T(8,128)(2,1)S(1)} %get-tuple-element.52), channel_id=1, source_target_pairs={{0,8},{4,12},{8,0},{12,4},{16,24},{20,28},{24,16},{28,20},{32,40},... | collective-permute-start | bytes 393224 | tf_op jit(solution)/shard_map/ppermute | solution.py:517
  37.1 34.6 %copy-start = (bf16[2,4,32,1024]{3,2,1,0:T(8,128)(2,1)}, bf16[2,4,32,1024]{3,2,1,0:T(8,128)(2,1)S(1)}, u32[]{:S(2)}) copy-start(bf16[2,4,32,1024]{3,2,1,0:T(8,128)(2,1)S(1)} %get-tuple-element.53.refs_0_) | copy-start | bytes 1572868
  37.1 16.5 %all-to-all-start.1 = ((bf16[16,16,1024]{2,1,0:T(8,128)(2,1)}), bf16[16,16,1024]{2,1,0:T(8,128)(2,1)S(1)}, u32[]{:S(2)}, u32[]{:S(2)}) async-start(bf16[16,16,1024]{2,1,0:T(8,128)(2,1)} %bitcast.5), calls=%async_computation.1 | async-start | bytes 1048576 | tf_op jit(solution)/shard_map/all_to_all | solution.py:732
  42.1 15.7 %collective-permute-start.8 = (bf16[2,4,32,1024]{3,2,1,0:T(8,128)(2,1)S(1)}, bf16[2,4,32,1024]{3,2,1,0:T(8,128)(2,1)S(1)}, u32[]{:S(2)}, u32[]{:S(2)}) collective-permute-start(bf16[2,4,32,1024]{3,2,1,0:T(8,128)(2,1)S(1)} %get-tuple-element.53.refs_0_), channel_id=1, source_target_pairs={{0,3},{1,0},{2,1},{3,2},{4,7},{5,4},{6,5},{7,6},{8,11},{9,8},{10,9... | collective-permute-start | bytes 1572872 | tf_op jit(solution)/shard_map/ppermute | solution.py:498
  45.2 14.4 %collective-permute-start.7 = (bf16[2,4,32,1024]{3,2,1,0:T(8,128)(2,1)S(1)}, bf16[2,4,32,1024]{3,2,1,0:T(8,128)(2,1)}, u32[]{:S(2)}, u32[]{:S(2)}) collective-permute-start(bf16[2,4,32,1024]{3,2,1,0:T(8,128)(2,1)S(1)} %get-tuple-element.53.refs_0_), channel_id=1, source_target_pairs={{0,1},{1,2},{2,3},{3,0},{4,5},{5,6},{6,7},{7,4},{8,9},{9,10},{10,1... | collective-permute-start | bytes 1572872 | tf_op jit(solution)/shard_map/ppermute | solution.py:498
  54.0 1.6 %collective-permute-start.5 = (bf16[128,1024]{1,0:T(8,128)(2,1)S(1)}, bf16[128,1024]{1,0:T(8,128)(2,1)S(1)}, u32[]{:S(2)}, u32[]{:S(2)}) collective-permute-start(bf16[128,1024]{1,0:T(8,128)(2,1)S(1)} %get-tuple-element.57), channel_id=1, source_target_pairs={{0,64},{64,0},{1,65},{65,1},{2,66},{66,2},{3,67},{67,3},{4,68},{68... | collective-permute-start | bytes 786440 | tf_op jit(solution)/shard_map/ppermute | solution.py:734
  55.7 16.1 %collective-permute-start.11 = (bf16[128,2048]{1,0:T(8,128)(2,1)S(1)}, bf16[128,2048]{1,0:T(8,128)(2,1)S(1)}, u32[]{:S(2)}, u32[]{:S(2)}) collective-permute-start(bf16[128,2048]{1,0:T(8,128)(2,1)S(1)} %get-tuple-element.63.rows_ref.refs_4_), channel_id=1, source_target_pairs={{0,12},{4,0},{8,4},{12,8},{16,28},{20,16},{24,20},{28,24},{32,44},... | collective-permute-start | bytes 1572872 | tf_op jit(solution)/shard_map/ppermute | solution.py:517
  56.2 16.0 %collective-permute-start.10 = (bf16[128,2048]{1,0:T(8,128)(2,1)S(1)}, bf16[128,2048]{1,0:T(8,128)(2,1)S(1)}, u32[]{:S(2)}, u32[]{:S(2)}) collective-permute-start(bf16[128,2048]{1,0:T(8,128)(2,1)S(1)} %get-tuple-element.63.rows_ref.refs_4_), channel_id=1, source_target_pairs={{0,4},{4,8},{8,12},{12,0},{16,20},{20,24},{24,28},{28,16},{32,36},... | collective-permute-start | bytes 1572872 | tf_op jit(solution)/shard_map/ppermute | solution.py:517
  57.7 4.9 %collective-permute-start.6 = (bf16[128,1024]{1,0:T(8,128)(2,1)S(1)}, bf16[128,1024]{1,0:T(8,128)(2,1)S(1)}, u32[]{:S(2)}, u32[]{:S(2)}) collective-permute-start(bf16[128,1024]{1,0:T(8,128)(2,1)S(1)} %get-tuple-element.58), channel_id=1, source_target_pairs={{0,64},{64,0},{1,65},{65,1},{2,66},{66,2},{3,67},{67,3},{4,68},{68... | collective-permute-start | bytes 786440 | tf_op jit(solution)/shard_map/ppermute | solution.py:738
  57.8 1.8 %copy-start.5 = (bf16[2,4,32,1024]{3,2,1,0:T(8,128)(2,1)}, bf16[2,4,32,1024]{3,2,1,0:T(8,128)(2,1)S(1)}, u32[]{:S(2)}) copy-start(bf16[2,4,32,1024]{3,2,1,0:T(8,128)(2,1)S(1)} %collective-permute-done.8.refs_2_) | copy-start | bytes 1572868
  59.6 17.2 %collective-permute-start.9 = (bf16[2,4,32,1024]{3,2,1,0:T(8,128)(2,1)}, bf16[2,4,32,1024]{3,2,1,0:T(8,128)(2,1)}, u32[]{:S(2)}, u32[]{:S(2)}) collective-permute-start(bf16[2,4,32,1024]{3,2,1,0:T(8,128)(2,1)} %collective-permute-done.7.refs_1_), channel_id=1, source_target_pairs={{0,1},{1,2},{2,3},{3,0},{4,5},{5,6},{6,7},{7,4},{8,9},{9,10},{10,1... | collective-permute-start | bytes 1572872 | tf_op jit(solution)/shard_map/ppermute | solution.py:498
  60.2 16.6 %collective-permute-start.12 = (bf16[128,2048]{1,0:T(8,128)(2,1)S(1)}, bf16[128,2048]{1,0:T(8,128)(2,1)S(1)}, u32[]{:S(2)}, u32[]{:S(2)}) collective-permute-start(bf16[128,2048]{1,0:T(8,128)(2,1)S(1)} %get-tuple-element.63.rows_ref.refs_4_), channel_id=1, source_target_pairs={{0,8},{4,12},{8,0},{12,4},{16,24},{20,28},{24,16},{28,20},{32,40},... | collective-permute-start | bytes 1572872 | tf_op jit(solution)/shard_map/ppermute | solution.py:517
  71.7 21.0 %copy-start.3 = (f32[1,4096]{1,0:T(1,128)S(1)}, f32[1,4096]{1,0:T(1,128)}, u32[]{:S(2)}) copy-start(f32[1,4096]{1,0:T(1,128)} %gain_ref.1) | copy-start | bytes 49156
  72.2 20.5 %all-to-all-start.2 = ((bf16[4,32,4096]{2,1,0:T(8,128)(2,1)}), bf16[4,32,4096]{2,1,0:T(8,128)(2,1)S(1)}, u32[]{:S(2)}, u32[]{:S(2)}) async-start(bf16[4,32,4096]{2,1,0:T(8,128)(2,1)} %bitcast.17), calls=%async_computation.2 | async-start | bytes 2097152 | tf_op jit(solution)/shard_map/all_to_all | solution.py:742
  79.3 5.8 %collective-permute-start.13 = (bf16[256,1024]{1,0:T(8,128)(2,1)S(1)}, bf16[256,1024]{1,0:T(8,128)(2,1)S(1)}, u32[]{:S(2)}, u32[]{:S(2)}) collective-permute-start(bf16[256,1024]{1,0:T(8,128)(2,1)S(1)} %get-tuple-element.68), channel_id=1, source_target_pairs={{0,64},{64,0},{1,65},{65,1},{2,66},{66,2},{3,67},{67,3},{4,68},{68... | collective-permute-start | bytes 1572872 | tf_op jit(solution)/shard_map/ppermute | solution.py:748
  79.4 10.5 %collective-permute-start.14 = (bf16[128,2048]{1,0:T(8,128)(2,1)S(1)}, bf16[128,2048]{1,0:T(8,128)(2,1)S(1)}, u32[]{:S(2)}, u32[]{:S(2)}) collective-permute-start(bf16[128,2048]{1,0:T(8,128)(2,1)S(1)} %get-tuple-element.70), channel_id=1, source_target_pairs={{0,16},{4,20},{8,24},{12,28},{16,32},{20,36},{24,40},{28,44},{32,4... | collective-permute-start | bytes 1572872 | tf_op jit(solution)/shard_map/ppermute | solution.py:517
  80.4 9.4 %collective-permute-start.15 = (bf16[128,2048]{1,0:T(8,128)(2,1)S(1)}, bf16[128,2048]{1,0:T(8,128)(2,1)S(1)}, u32[]{:S(2)}, u32[]{:S(2)}) collective-permute-start(bf16[128,2048]{1,0:T(8,128)(2,1)S(1)} %get-tuple-element.71), channel_id=1, source_target_pairs={{0,48},{4,52},{8,56},{12,60},{16,0},{20,4},{24,8},{28,12},{32,16},... | collective-permute-start | bytes 1572872 | tf_op jit(solution)/shard_map/ppermute | solution.py:517
  85.1 4.7 %copy-start.6 = (bf16[256,1024]{1,0:T(8,128)(2,1)}, bf16[256,1024]{1,0:T(8,128)(2,1)S(1)}, u32[]{:S(2)}) copy-start(bf16[256,1024]{1,0:T(8,128)(2,1)S(1)} %collective-permute-done.13.other_hbm) | copy-start | bytes 1572868
  94.0 8.6 %collective-permute-start.17 = (bf16[32,4096]{1,0:T(8,128)(2,1)S(1)}, bf16[32,4096]{1,0:T(8,128)(2,1)S(1)}, u32[]{:S(2)}, u32[]{:S(2)}) collective-permute-start(bf16[32,4096]{1,0:T(8,128)(2,1)S(1)} %rms_back.1.refs_0_), channel_id=1, source_target_pairs={{0,3},{1,0},{2,1},{3,2},{4,7},{5,4},{6,5},{7,6},{8,11},{9,8},{10,9... | collective-permute-start | bytes 786440 | tf_op jit(solution)/shard_map/ppermute | solution.py:498
  97.3 8.7 %collective-permute-start.16 = (bf16[32,4096]{1,0:T(8,128)(2,1)S(1)}, bf16[32,4096]{1,0:T(8,128)(2,1)S(1)}, u32[]{:S(2)}, u32[]{:S(2)}) collective-permute-start(bf16[32,4096]{1,0:T(8,128)(2,1)S(1)} %rms_back.1.refs_0_), channel_id=1, source_target_pairs={{0,1},{1,2},{2,3},{3,0},{4,5},{5,6},{6,7},{7,4},{8,9},{9,10},{10,1... | collective-permute-start | bytes 786440 | tf_op jit(solution)/shard_map/ppermute | solution.py:498
  97.3 18.6 %collective-permute-start.19 = (bf16[256,1024]{1,0:T(8,128)(2,1)S(1)}, bf16[256,1024]{1,0:T(8,128)(2,1)S(1)}, u32[]{:S(2)}, u32[]{:S(2)}) collective-permute-start(bf16[256,1024]{1,0:T(8,128)(2,1)S(1)} %get-tuple-element.79), channel_id=1, source_target_pairs={{0,16},{4,20},{8,24},{12,28},{16,32},{20,36},{24,40},{28,44},{32,4... | collective-permute-start | bytes 1572872 | tf_op jit(solution)/shard_map/ppermute | solution.py:517
  98.5 17.4 %collective-permute-start.20 = (bf16[256,1024]{1,0:T(8,128)(2,1)S(1)}, bf16[256,1024]{1,0:T(8,128)(2,1)S(1)}, u32[]{:S(2)}, u32[]{:S(2)}) collective-permute-start(bf16[256,1024]{1,0:T(8,128)(2,1)S(1)} %get-tuple-element.80), channel_id=1, source_target_pairs={{0,48},{4,52},{8,56},{12,60},{16,0},{20,4},{24,8},{28,12},{32,16},... | collective-permute-start | bytes 1572872 | tf_op jit(solution)/shard_map/ppermute | solution.py:517
  100.5 15.4 %collective-permute-start.21 = (bf16[256,1024]{1,0:T(8,128)(2,1)S(1)}, bf16[256,1024]{1,0:T(8,128)(2,1)S(1)}, u32[]{:S(2)}, u32[]{:S(2)}) collective-permute-start(bf16[256,1024]{1,0:T(8,128)(2,1)S(1)} %get-tuple-element.81), channel_id=1, source_target_pairs={{0,80},{4,84},{8,88},{12,92},{16,96},{20,100},{24,104},{28,108},{3... | collective-permute-start | bytes 1572872 | tf_op jit(solution)/shard_map/ppermute | solution.py:517
  102.6 13.4 %collective-permute-start.22 = (bf16[256,1024]{1,0:T(8,128)(2,1)S(1)}, bf16[256,1024]{1,0:T(8,128)(2,1)S(1)}, u32[]{:S(2)}, u32[]{:S(2)}) collective-permute-start(bf16[256,1024]{1,0:T(8,128)(2,1)S(1)} %get-tuple-element.82), channel_id=1, source_target_pairs={{0,112},{4,116},{8,120},{12,124},{16,64},{20,68},{24,72},{28,76},{... | collective-permute-start | bytes 1572872 | tf_op jit(solution)/shard_map/ppermute | solution.py:517
  106.0 8.9 %collective-permute-start.18 = (bf16[32,4096]{1,0:T(8,128)(2,1)S(1)}, bf16[32,4096]{1,0:T(8,128)(2,1)S(1)}, u32[]{:S(2)}, u32[]{:S(2)}) collective-permute-start(bf16[32,4096]{1,0:T(8,128)(2,1)S(1)} %collective-permute-done.16.refs_1_), channel_id=1, source_target_pairs={{0,1},{1,2},{2,3},{3,0},{4,5},{5,6},{6,7},{7,4},{8,9},{9,10},{10,1... | collective-permute-start | bytes 786440 | tf_op jit(solution)/shard_map/ppermute | solution.py:498

commit v10 on v9

--- a/solution.py
+++ b/solution.py
@@ -438,8 +438,8 @@
     )(rows, got, in_hbm(weight_a), in_hbm(weight_b))
 
 
-def rms_back_kernel(x_hbm, gain_ref, parts_ref, out_ref, x_ref, sem):
-    rows = out_ref.shape[0]
+def rms_back_kernel(x_hbm, gain_ref, parts_ref, out_hbm, x_ref, row_ref, sem, sems):
+    rows = row_ref.shape[0]
     mine = pl.multiple_of(lax.axis_index("mp") * rows, rows)
     get_x = pltpu.make_async_copy(x_hbm.at[pl.ds(mine, rows), :], x_ref, sem)
     get_x.start()
@@ -451,47 +451,27 @@
     scale = lax.rsqrt(jnp.mean(xf * xf, axis=-1, keepdims=True) + EPS)
     upper = gain_ref[...] * dnorm
     inner = jnp.mean(xf * upper, axis=-1, keepdims=True)
-    out_ref[...] = (scale * upper - xf * (scale * scale * scale * inner)).astype(BF16)
+    row_ref[...] = (scale * upper - xf * (scale * scale * scale * inner)).astype(BF16)
+    puts = [pltpu.make_async_copy(row_ref, out_hbm.at[i], sems.at[i]) for i in range(RING)]
+    for put in puts:
+        put.start()
+    for put in puts:
+        put.wait()
 
 
 def rms_back(x, gain, parts):
-    rows, width = parts.shape[1:]
+    _, rows, width = parts.shape
     return pl.pallas_call(
         rms_back_kernel,
         in_specs=[HBM] + [VMEM] * 2,
-        out_specs=VMEM,
-        out_shape=jax.ShapeDtypeStruct((rows, width), BF16),
-        scratch_shapes=[pltpu.VMEM((rows, width), BF16), pltpu.SemaphoreType.DMA],
+        out_specs=HBM,
+        out_shape=pltpu.HBM((RING, rows, width), BF16),
+        scratch_shapes=[pltpu.VMEM((rows, width), BF16)] * 2
+        + [pltpu.SemaphoreType.DMA, pltpu.SemaphoreType.DMA((RING,))],
         compiler_params=params(),
         cost_estimate=cost(10 * rows * width, 12 * rows * width),
         name="rms_back",
     )(in_hbm(x), gain, parts)
-
-
-def place_kernel(*refs):
-    pieces, (out_hbm, sems) = refs[:RING], refs[RING:]
-    rows = pieces[0].shape[0]
-    copies = []
-    for i, k in enumerate(ORDER):
-        at = pl.multiple_of((lax.axis_index("mp") + k) % RING * rows, rows)
-        copies.append(pltpu.make_async_copy(pieces[i], out_hbm.at[pl.ds(at, rows), :], sems.at[i]))
-        copies[-1].start()
-    for copy in copies:
-        copy.wait()
-
-
-def place(pieces):
-    rows, width = pieces[0].shape
-    return pl.pallas_call(
-        place_kernel,
-        in_specs=[ANY] * RING,
-        out_specs=HBM,
-        out_shape=pltpu.HBM((RING * rows, width), BF16),
-        scratch_shapes=[pltpu.SemaphoreType.DMA((RING,))],
-        compiler_params=params(),
-        cost_estimate=cost(0, 4 * RING * rows * width),
-        name="place",
-    )(*pieces)
 
 
 def shift(value, axis, k):
@@ -755,9 +735,10 @@
         moved(right_other, 1, REDUCE, True),
         moved(left_other, 3, REDUCE, True),
     ]
-    quarter = rms_back(rows, gains, parts)
-    grad_states = place(gathered(quarter, "mp"))
+    quarters = rms_back(rows, gains, parts)
+    quarters = lax.all_to_all(quarters, "mp", split_axis=0, concat_axis=0, tiled=True)
     grad_a, grad_b = own_blocks(own, crossed, sums)
+    grad_states = quarters.reshape(rows.shape)
     return (grad_states[None], grad_a[None], grad_b[None])
 
 

time: 120 us -> 121 us (level)
  waiting for transfers between devices: 40 us -> 36.1 us
  starting transfers between devices: 42.2 us -> 45.6 us
    ppermute x6 -> x3, waiting for transfers between devices: 16.2 us -> 1.8 us  [shift(): return lax.ppermute(value, axis, [(i, (i + k) % RING) for i in range(RING)])]
    ppermute x12, waiting for transfers between devices: 12.5 us -> 23 us  [moved(): return lax.ppermute(value, ('section', 'z', 'x'), pairs)]
    all_to_all x0 -> x1, starting transfers between devices: none -> 4.79 us  [per_device(): lax.all_to_all(quarters, 'mp', split_axis=0, concat_axis=0, tiled=True)]
    ppermute x6 -> x3, starting transfers between devices: 6.99 us -> 3.71 us  [shift(): return lax.ppermute(value, axis, [(i, (i + k) % RING) for i in range(RING)])]
    ppermute x12, starting transfers between devices: 16.6 us -> 18.4 us  [moved(): return lax.ppermute(value, ('section', 'z', 'x'), pairs)]
  transfers between devices with their start and end apart: 26 -> 24, of which waited for: 12 -> 13; matrix products, arithmetic and copies ran while one was open for 0% -> 0% of each run, Pallas kernels for 15% -> 17%
where the time goes in v10:
time: 121 us; the launch traced here: 119 us
  starting transfers between devices  45.6 us (38%)
  waiting for transfers between devices  36.1 us (30%)
  Pallas kernels  35.3 us (29%)
    ppermute x12, waiting for transfers between devices, moved(): return lax.ppermute(value, ('section', 'z', 'x'), pairs)  23 us
    ppermute x12, starting transfers between devices, moved(): return lax.ppermute(value, ('section', 'z', 'x'), pairs)  18.4 us
    pallas_call x1, Pallas kernels, forward(): pl.pallas_call(forward_kernel, in_specs=[HBM] * 5, out_specs=[VMEM] * 4,...  9.11 us
    pallas_call x1, Pallas kernels, dnorm_partial(): pl.pallas_call(dnorm_kernel, in_specs=[VMEM] * 2 + [HBM] * 2, out_specs=H...  9.07 us
    all_to_all x1, starting transfers between devices, per_device(): lax.all_to_all(slots, ('z', 'x'), split_axis=0, concat_axis=0, tiled=True)  8.42 us
    all_to_all x1, waiting for transfers between devices, per_device(): lax.all_to_all(back, ('z', 'x'), split_axis=0, concat_axis=0, tiled=True)  8.37 us
    all_to_all x1, starting transfers between devices, per_device(): lax.all_to_all(back, ('z', 'x'), split_axis=0, concat_axis=0, tiled=True)  4.96 us
    all_to_all x1, starting transfers between devices, per_device(): lax.all_to_all(quarters, 'mp', split_axis=0, concat_axis=0, tiled=True)  4.79 us
  transfers between devices with their start and end apart: 24, of which 13 were waited for; matrix products, arithmetic and copies ran while one was open for 0% of the time, Pallas kernels for 17%

profile of v10, /device:TPU:0, one launch (start us, length us, event | category | flops | bytes accessed | tf_op | source)
XLA Modules:
  0.0 118.8 jit_solution(9716788346839064839)
XLA Ops:
  0.7 9.1 %forward.1 = (bf16[128,1024]{1,0:T(8,128)(2,1)S(1)}, bf16[128,1024]{1,0:T(8,128)(2,1)S(1)}, bf16[4,32,1024]{2,1,0:T(8,128)(2,1)S(1)}, bf16[4,32,1024]{2,1,0:T(8,128)(2,1)S(1)}) custom-call(bf16[128,4096]{1,0:T(8,128)(2,1)} %bitcast.19, f32[1,4096]{1,0:T(1,128)} %gain_ref.1, bf16[128,4096]{1,0:T(8,128)(2,1)} %cot_hbm.1, bf16[4096,1024]{1,0:T(8,128)(2,1)} %bitcast.13, ...), custom_call_target="tpu_custom_call" | custom-call | flops 134217728 | bytes 1048576 | tf_op jit(solution)/shard_map/forward/pallas_call | solution.py:189
  9.8 0.2 collective-permute-start
  10.0 0.4 collective-permute-start.1
  10.4 1.0 collective-permute-done.got_ref
  11.4 0.4 collective-permute-done.1.other_ref
  11.8 1.2 pack.1
  13.0 8.4 %all-to-all-start = ((bf16[16,16,1024]{2,1,0:T(8,128)(2,1)}), bf16[16,16,1024]{2,1,0:T(8,128)(2,1)S(1)}, u32[]{:S(2)}, u32[]{:S(2)}) async-start(bf16[16,16,1024]{2,1,0:T(8,128)(2,1)} %bitcast.3), calls=%async_computation | async-start | bytes 1048576 | tf_op jit(solution)/shard_map/all_to_all | solution.py:706
  21.4 1.9 %collective-permute-start.2 = (bf16[2,32,1024]{2,1,0:T(8,128)(2,1)S(1)}, bf16[2,32,1024]{2,1,0:T(8,128)(2,1)S(1)}, u32[]{:S(2)}, u32[]{:S(2)}) collective-permute-start(bf16[2,32,1024]{2,1,0:T(8,128)(2,1)S(1)} %get-tuple-element.48), channel_id=1, source_target_pairs={{0,4},{4,8},{8,12},{12,0},{16,20},{20,24},{24,28},{28,16},{32,36},... | collective-permute-start | bytes 393224 | tf_op jit(solution)/shard_map/ppermute | solution.py:497
  23.3 1.4 %collective-permute-start.3 = (bf16[2,32,1024]{2,1,0:T(8,128)(2,1)S(1)}, bf16[2,32,1024]{2,1,0:T(8,128)(2,1)S(1)}, u32[]{:S(2)}, u32[]{:S(2)}) collective-permute-start(bf16[2,32,1024]{2,1,0:T(8,128)(2,1)S(1)} %get-tuple-element.49), channel_id=1, source_target_pairs={{0,12},{4,0},{8,4},{12,8},{16,28},{20,16},{24,20},{28,24},{32,44},... | collective-permute-start | bytes 393224 | tf_op jit(solution)/shard_map/ppermute | solution.py:497
  24.7 2.2 %collective-permute-start.4 = (bf16[2,32,1024]{2,1,0:T(8,128)(2,1)S(1)}, bf16[2,32,1024]{2,1,0:T(8,128)(2,1)S(1)}, u32[]{:S(2)}, u32[]{:S(2)}) collective-permute-start(bf16[2,32,1024]{2,1,0:T(8,128)(2,1)S(1)} %get-tuple-element.50), channel_id=1, source_target_pairs={{0,8},{4,12},{8,0},{12,4},{16,24},{20,28},{24,16},{28,20},{32,40},... | collective-permute-start | bytes 393224 | tf_op jit(solution)/shard_map/ppermute | solution.py:497
  26.8 5.6 %collective-permute-done.2.rest_1_ = bf16[2,32,1024]{2,1,0:T(8,128)(2,1)S(1)} collective-permute-done((bf16[2,32,1024]{2,1,0:T(8,128)(2,1)S(1)}, bf16[2,32,1024]{2,1,0:T(8,128)(2,1)S(1)}, u32[]{:S(2)}, u32[]{:S(2)}) %collective-permute-start.2) | collective-permute-done | bytes 131104 | tf_op jit(solution)/shard_map/ppermute | solution.py:497
  32.4 0.0 collective-permute-done.3.rest_2_
  32.4 1.7 %collective-permute-done.4.rest_3_ = bf16[2,32,1024]{2,1,0:T(8,128)(2,1)S(1)} collective-permute-done((bf16[2,32,1024]{2,1,0:T(8,128)(2,1)S(1)}, bf16[2,32,1024]{2,1,0:T(8,128)(2,1)S(1)}, u32[]{:S(2)}, u32[]{:S(2)}) %collective-permute-start.4) | collective-permute-done | bytes 131104 | tf_op jit(solution)/shard_map/ppermute | solution.py:497
  34.2 2.9 %attend.1 = (bf16[128,1024]{1,0:T(8,128)(2,1)S(1)}, bf16[256,1024]{1,0:T(8,128)(2,1)}, bf16[2,4,32,1024]{3,2,1,0:T(8,128)(2,1)S(1)}) custom-call(bf16[128,1024]{1,0:T(8,128)(2,1)S(1)} %get-tuple-element.42.keep_ref, bf16[128,1024]{1,0:T(8,128)(2,1)S(1)} %collective-permute-done.got_ref, bf16[256,1024]{1,0:T(8,128)(2,1)S(1)} %bitcast.11, ...), custom_call_target="tpu_custom_call" | custom-call | flops 50331648 | bytes 131072 | tf_op jit(solution)/shard_map/attend/pallas_call | solution.py:300
  37.1 5.0 %all-to-all-start.1 = ((bf16[16,16,1024]{2,1,0:T(8,128)(2,1)}), bf16[16,16,1024]{2,1,0:T(8,128)(2,1)S(1)}, u32[]{:S(2)}, u32[]{:S(2)}) async-start(bf16[16,16,1024]{2,1,0:T(8,128)(2,1)} %bitcast.5), calls=%async_computation.1 | async-start | bytes 1048576 | tf_op jit(solution)/shard_map/all_to_all | solution.py:712
  42.1 3.1 %collective-permute-start.8 = (bf16[2,4,32,1024]{3,2,1,0:T(8,128)(2,1)S(1)}, bf16[2,4,32,1024]{3,2,1,0:T(8,128)(2,1)S(1)}, u32[]{:S(2)}, u32[]{:S(2)}) collective-permute-start(bf16[2,4,32,1024]{3,2,1,0:T(8,128)(2,1)S(1)} %get-tuple-element.51.refs_0_), channel_id=1, source_target_pairs={{0,3},{1,0},{2,1},{3,2},{4,7},{5,4},{6,5},{7,6},{8,11},{9,8},{10,9... | collective-permute-start | bytes 1572872 | tf_op jit(solution)/shard_map/ppermute | solution.py:478
  45.2 8.4 %all-to-all-done.1 = bf16[16,16,1024]{2,1,0:T(8,128)(2,1)S(1)} async-done(((bf16[16,16,1024]{2,1,0:T(8,128)(2,1)}), bf16[16,16,1024]{2,1,0:T(8,128)(2,1)S(1)}, u32[]{:S(2)}, u32[]{:S(2)}) %all-to-all-start.1) | async-done | bytes 524320 | tf_op jit(solution)/shard_map/all_to_all | solution.py:712
  53.6 0.4 unpack.1
  54.0 0.1 collective-permute-start.5
  54.1 1.5 %collective-permute-done.5.got_ref = bf16[128,1024]{1,0:T(8,128)(2,1)S(1)} collective-permute-done((bf16[128,1024]{1,0:T(8,128)(2,1)S(1)}, bf16[128,1024]{1,0:T(8,128)(2,1)S(1)}, u32[]{:S(2)}, u32[]{:S(2)}) %collective-permute-start.5) | collective-permute-done | bytes 262176 | tf_op jit(solution)/shard_map/ppermute | solution.py:714
  55.6 0.1 join.1
  55.7 0.6 collective-permute-start.11
  56.2 1.5 %collective-permute-start.10 = (bf16[128,2048]{1,0:T(8,128)(2,1)S(1)}, bf16[128,2048]{1,0:T(8,128)(2,1)S(1)}, u32[]{:S(2)}, u32[]{:S(2)}) collective-permute-start(bf16[128,2048]{1,0:T(8,128)(2,1)S(1)} %get-tuple-element.61.rows_ref.refs_4_), channel_id=1, source_target_pairs={{0,4},{4,8},{8,12},{12,0},{16,20},{20,24},{24,28},{28,16},{32,36},... | collective-permute-start | bytes 1572872 | tf_op jit(solution)/shard_map/ppermute | solution.py:497
  57.8 1.8 %collective-permute-done.7.refs_1_ = bf16[2,4,32,1024]{3,2,1,0:T(8,128)(2,1)} collective-permute-done((bf16[2,4,32,1024]{3,2,1,0:T(8,128)(2,1)S(1)}, bf16[2,4,32,1024]{3,2,1,0:T(8,128)(2,1)}, u32[]{:S(2)}, u32[]{:S(2)}) %collective-permute-start.7) | collective-permute-done | bytes 524320 | tf_op jit(solution)/shard_map/ppermute | solution.py:478
  59.6 0.6 collective-permute-start.9
  60.2 2.5 %collective-permute-start.12 = (bf16[128,2048]{1,0:T(8,128)(2,1)S(1)}, bf16[128,2048]{1,0:T(8,128)(2,1)S(1)}, u32[]{:S(2)}, u32[]{:S(2)}) collective-permute-start(bf16[128,2048]{1,0:T(8,128)(2,1)S(1)} %get-tuple-element.61.rows_ref.refs_4_), channel_id=1, source_target_pairs={{0,8},{4,12},{8,0},{12,4},{16,24},{20,28},{24,16},{28,20},{32,40},... | collective-permute-start | bytes 1572872 | tf_op jit(solution)/shard_map/ppermute | solution.py:497
  62.7 9.1 %dnorm.1 = bf16[128,4096]{1,0:T(8,128)(2,1)} custom-call(bf16[128,2048]{1,0:T(8,128)(2,1)S(1)} %get-tuple-element.61.rows_ref.refs_4_, bf16[128,1024]{1,0:T(8,128)(2,1)S(1)} %collective-permute-done.6.got_ref, bf16[4096,1024]{1,0:T(8,128)(2,1)} %bitcast.14, bf16[4096,1024]{1,0:T(8,128)(2,1)} %bitcast.16), custom_call_target="tpu_custom_call" | custom-call | flops 134217728 | bytes 1048576 | tf_op jit(solution)/shard_map/dnorm/pallas_call | solution.py:427
  71.7 0.0 copy-start.3
  71.8 0.5 collective-permute-done.10.refs_5_
  72.2 4.5 %all-to-all-start.2 = ((bf16[4,32,4096]{2,1,0:T(8,128)(2,1)}), bf16[4,32,4096]{2,1,0:T(8,128)(2,1)S(1)}, u32[]{:S(2)}, u32[]{:S(2)}) async-start(bf16[4,32,4096]{2,1,0:T(8,128)(2,1)} %bitcast.17), calls=%async_computation.2 | async-start | bytes 2097152 | tf_op jit(solution)/shard_map/all_to_all | solution.py:722
  76.8 2.5 %far.1 = (bf16[128,2048]{1,0:T(8,128)(2,1)S(1)}, bf16[128,2048]{1,0:T(8,128)(2,1)S(1)}, bf16[512,2048]{1,0:T(8,128)(2,1)S(1)}, bf16[256,1024]{1,0:T(8,128)(2,1)S(1)}) custom-call(bf16[2,4,32,1024]{3,2,1,0:T(8,128)(2,1)} %copy-done, bf16[2,4,32,1024]{3,2,1,0:T(8,128)(2,1)} %collective-permute-done.7.refs_1_, bf16[2,4,32,1024]{3,2,1,0:T(8,128)(2,1)} %copy-done.5, ...), custom_call_target="tpu_custom_call" | custom-call | flops 50331648 | bytes 524288 | tf_op jit(solution)/shard_map/far/pallas_call | solution.py:559
  79.3 0.1 collective-permute-start.13
  79.4 1.1 collective-permute-start.14
  80.4 2.2 %collective-permute-start.15 = (bf16[128,2048]{1,0:T(8,128)(2,1)S(1)}, bf16[128,2048]{1,0:T(8,128)(2,1)S(1)}, u32[]{:S(2)}, u32[]{:S(2)}) collective-permute-start(bf16[128,2048]{1,0:T(8,128)(2,1)S(1)} %get-tuple-element.69), channel_id=1, source_target_pairs={{0,48},{4,52},{8,56},{12,60},{16,0},{20,4},{24,8},{28,12},{32,16},... | collective-permute-start | bytes 1572872 | tf_op jit(solution)/shard_map/ppermute | solution.py:497
  82.7 2.4 %middle.1.own_hbm = bf16[256,1024]{1,0:T(8,128)(2,1)} custom-call(bf16[2,4,32,1024]{3,2,1,0:T(8,128)(2,1)} %copy-done, bf16[2,4,32,1024]{3,2,1,0:T(8,128)(2,1)} %collective-permute-done.7.refs_1_, bf16[2,4,32,1024]{3,2,1,0:T(8,128)(2,1)} %copy-done.5, bf16[2,4,32,1024]{3,2,1,0:T(8,128)(2,1)} %collective-permute-done.9.refs_3_, ...), custom_call_target="tpu_custom_call" | custom-call | flops 16777216 | bytes 262144 | tf_op jit(solution)/shard_map/middle/pallas_call | solution.py:626
  85.1 4.7 %collective-permute-done.14.refs_5_ = bf16[128,2048]{1,0:T(8,128)(2,1)S(1)} collective-permute-done((bf16[128,2048]{1,0:T(8,128)(2,1)S(1)}, bf16[128,2048]{1,0:T(8,128)(2,1)S(1)}, u32[]{:S(2)}, u32[]{:S(2)}) %collective-permute-start.14) | collective-permute-done | bytes 524320 | tf_op jit(solution)/shard_map/ppermute | solution.py:497
  89.8 2.9 %side.1 = (bf16[256,1024]{1,0:T(8,128)(2,1)S(1)}, bf16[256,1024]{1,0:T(8,128)(2,1)S(1)}, bf16[256,1024]{1,0:T(8,128)(2,1)S(1)}, bf16[256,1024]{1,0:T(8,128)(2,1)S(1)}) custom-call(bf16[2,4,32,1024]{3,2,1,0:T(8,128)(2,1)} %copy-done, bf16[2,4,32,1024]{3,2,1,0:T(8,128)(2,1)} %collective-permute-done.7.refs_1_, bf16[2,4,32,1024]{3,2,1,0:T(8,128)(2,1)} %copy-done.5, ...), custom_call_target="tpu_custom_call" | custom-call | flops 67108864 | bytes 262144 | tf_op jit(solution)/shard_map/side/pallas_call | solution.py:600
  92.8 2.2 %rms_back.1 = bf16[4,32,4096]{2,1,0:T(8,128)(2,1)} custom-call(bf16[128,4096]{1,0:T(8,128)(2,1)} %bitcast.20, f32[1,4096]{1,0:T(1,128)S(1)} %copy-done.3, bf16[4,32,4096]{2,1,0:T(8,128)(2,1)S(1)} %all-to-all-done.2.parts_ref), custom_call_target="tpu_custom_call" | custom-call | flops 81920 | bytes 98304 | tf_op jit(solution)/shard_map/rms_back/pallas_call | solution.py:464
  95.0 4.8 %all-to-all-start.3 = ((bf16[4,32,4096]{2,1,0:T(8,128)(2,1)}), bf16[4,32,4096]{2,1,0:T(8,128)(2,1)S(1)}, u32[]{:S(2)}, u32[]{:S(2)}) async-start(bf16[4,32,4096]{2,1,0:T(8,128)(2,1)} %rms_back.1), calls=%async_computation.3 | async-start | bytes 2097152 | tf_op jit(solution)/shard_map/all_to_all | solution.py:739
  99.8 1.3 %collective-permute-start.16 = (bf16[256,1024]{1,0:T(8,128)(2,1)S(1)}, bf16[256,1024]{1,0:T(8,128)(2,1)S(1)}, u32[]{:S(2)}, u32[]{:S(2)}) collective-permute-start(bf16[256,1024]{1,0:T(8,128)(2,1)S(1)} %get-tuple-element.75), channel_id=1, source_target_pairs={{0,16},{4,20},{8,24},{12,28},{16,32},{20,36},{24,40},{28,44},{32,4... | collective-permute-start | bytes 1572872 | tf_op jit(solution)/shard_map/ppermute | solution.py:497
  101.0 2.0 %collective-permute-start.17 = (bf16[256,1024]{1,0:T(8,128)(2,1)S(1)}, bf16[256,1024]{1,0:T(8,128)(2,1)S(1)}, u32[]{:S(2)}, u32[]{:S(2)}) collective-permute-start(bf16[256,1024]{1,0:T(8,128)(2,1)S(1)} %get-tuple-element.76), channel_id=1, source_target_pairs={{0,48},{4,52},{8,56},{12,60},{16,0},{20,4},{24,8},{28,12},{32,16},... | collective-permute-start | bytes 1572872 | tf_op jit(solution)/shard_map/ppermute | solution.py:497
  103.0 1.8 %collective-permute-start.19 = (bf16[256,1024]{1,0:T(8,128)(2,1)S(1)}, bf16[256,1024]{1,0:T(8,128)(2,1)S(1)}, u32[]{:S(2)}, u32[]{:S(2)}) collective-permute-start(bf16[256,1024]{1,0:T(8,128)(2,1)S(1)} %get-tuple-element.78), channel_id=1, source_target_pairs={{0,112},{4,116},{8,120},{12,124},{16,64},{20,68},{24,72},{28,76},{... | collective-permute-start | bytes 1572872 | tf_op jit(solution)/shard_map/ppermute | solution.py:497
  104.9 5.3 %collective-permute-done.16.refs_0_ = bf16[256,1024]{1,0:T(8,128)(2,1)S(1)} collective-permute-done((bf16[256,1024]{1,0:T(8,128)(2,1)S(1)}, bf16[256,1024]{1,0:T(8,128)(2,1)S(1)}, u32[]{:S(2)}, u32[]{:S(2)}) %collective-permute-start.16) | collective-permute-done | bytes 524320 | tf_op jit(solution)/shard_map/ppermute | solution.py:497
  110.2 0.1 collective-permute-done.17.refs_1_
  110.2 3.9 %collective-permute-done.18.refs_2_ = bf16[256,1024]{1,0:T(8,128)(2,1)S(1)} collective-permute-done((bf16[256,1024]{1,0:T(8,128)(2,1)S(1)}, bf16[256,1024]{1,0:T(8,128)(2,1)S(1)}, u32[]{:S(2)}, u32[]{:S(2)}) %collective-permute-start.18) | collective-permute-done | bytes 524320 | tf_op jit(solution)/shard_map/ppermute | solution.py:497
  114.1 1.2 %collective-permute-done.19.refs_3_ = bf16[256,1024]{1,0:T(8,128)(2,1)S(1)} collective-permute-done((bf16[256,1024]{1,0:T(8,128)(2,1)S(1)}, bf16[256,1024]{1,0:T(8,128)(2,1)S(1)}, u32[]{:S(2)}, u32[]{:S(2)}) %collective-permute-start.19) | collective-permute-done | bytes 524320 | tf_op jit(solution)/shard_map/ppermute | solution.py:497
  115.3 2.5 %own.1 = (f32[256,1024]{1,0:T(8,128)}, f32[256,1024]{1,0:T(8,128)}) custom-call(bf16[256,1024]{1,0:T(8,128)(2,1)} %middle.1.own_hbm, bf16[256,1024]{1,0:T(8,128)(2,1)} %copy-done.6, bf16[256,1024]{1,0:T(8,128)(2,1)S(1)} %collective-permute-done.16.refs_0_, bf16[256,1024]{1,0:T(8,128)(2,1)S(1)} %collective-permute-done.17.refs_1_, ...), custom_call_target="tpu_custom_call" | custom-call | flops 65536 | bytes 327680 | tf_op jit(solution)/shard_map/own/pallas_call | solution.py:679
  117.8 1.0 copy.12
  (26 shorter events, 0.1 us)
Async XLA Ops:
  0.6 11.1 %copy-start.1 = (s32[16,16]{1,0:T(8,128)S(1)}, s32[16,16]{1,0:T(8,128)}, u32[]{:S(2)}) copy-start(s32[16,16]{1,0:T(8,128)} %src_ref.5) | copy-start | bytes 3076
  0.6 11.1 %copy-start.2 = (s32[16,16]{1,0:T(8,128)S(1)}, s32[16,16]{1,0:T(8,128)}, u32[]{:S(2)}) copy-start(s32[16,16]{1,0:T(8,128)} %dest_ref.5) | copy-start | bytes 3076
  0.7 33.5 %copy-start.4 = (s32[16,16]{1,0:T(8,128)S(1)}, s32[16,16]{1,0:T(8,128)}, u32[]{:S(2)}) copy-start(s32[16,16]{1,0:T(8,128)} %tgt_ref.1) | copy-start | bytes 3076
  9.8 1.6 %collective-permute-start = (bf16[128,1024]{1,0:T(8,128)(2,1)S(1)}, bf16[128,1024]{1,0:T(8,128)(2,1)S(1)}, u32[]{:S(2)}, u32[]{:S(2)}) collective-permute-start(bf16[128,1024]{1,0:T(8,128)(2,1)S(1)} %get-tuple-element.43), channel_id=1, source_target_pairs={{0,64},{64,0},{1,65},{65,1},{2,66},{66,2},{3,67},{67,3},{4,68},{68... | collective-permute-start | bytes 786440 | tf_op jit(solution)/shard_map/ppermute | solution.py:702
  10.0 1.8 %collective-permute-start.1 = (bf16[4,32,1024]{2,1,0:T(8,128)(2,1)S(1)}, bf16[4,32,1024]{2,1,0:T(8,128)(2,1)S(1)}, u32[]{:S(2)}, u32[]{:S(2)}) collective-permute-start(bf16[4,32,1024]{2,1,0:T(8,128)(2,1)S(1)} %get-tuple-element.45), channel_id=1, source_target_pairs={{0,64},{64,0},{1,65},{65,1},{2,66},{66,2},{3,67},{67,3},{4,68},{68... | collective-permute-start | bytes 786440 | tf_op jit(solution)/shard_map/ppermute | solution.py:703
  13.0 21.2 %all-to-all-start = ((bf16[16,16,1024]{2,1,0:T(8,128)(2,1)}), bf16[16,16,1024]{2,1,0:T(8,128)(2,1)S(1)}, u32[]{:S(2)}, u32[]{:S(2)}) async-start(bf16[16,16,1024]{2,1,0:T(8,128)(2,1)} %bitcast.3), calls=%async_computation | async-start | bytes 1048576 | tf_op jit(solution)/shard_map/all_to_all | solution.py:706
  21.4 11.0 %collective-permute-start.2 = (bf16[2,32,1024]{2,1,0:T(8,128)(2,1)S(1)}, bf16[2,32,1024]{2,1,0:T(8,128)(2,1)S(1)}, u32[]{:S(2)}, u32[]{:S(2)}) collective-permute-start(bf16[2,32,1024]{2,1,0:T(8,128)(2,1)S(1)} %get-tuple-element.48), channel_id=1, source_target_pairs={{0,4},{4,8},{8,12},{12,0},{16,20},{20,24},{24,28},{28,16},{32,36},... | collective-permute-start | bytes 393224 | tf_op jit(solution)/shard_map/ppermute | solution.py:497
  23.3 9.1 %collective-permute-start.3 = (bf16[2,32,1024]{2,1,0:T(8,128)(2,1)S(1)}, bf16[2,32,1024]{2,1,0:T(8,128)(2,1)S(1)}, u32[]{:S(2)}, u32[]{:S(2)}) collective-permute-start(bf16[2,32,1024]{2,1,0:T(8,128)(2,1)S(1)} %get-tuple-element.49), channel_id=1, source_target_pairs={{0,12},{4,0},{8,4},{12,8},{16,28},{20,16},{24,20},{28,24},{32,44},... | collective-permute-start | bytes 393224 | tf_op jit(solution)/shard_map/ppermute | solution.py:497
  24.7 9.4 %collective-permute-start.4 = (bf16[2,32,1024]{2,1,0:T(8,128)(2,1)S(1)}, bf16[2,32,1024]{2,1,0:T(8,128)(2,1)S(1)}, u32[]{:S(2)}, u32[]{:S(2)}) collective-permute-start(bf16[2,32,1024]{2,1,0:T(8,128)(2,1)S(1)} %get-tuple-element.50), channel_id=1, source_target_pairs={{0,8},{4,12},{8,0},{12,4},{16,24},{20,28},{24,16},{28,20},{32,40},... | collective-permute-start | bytes 393224 | tf_op jit(solution)/shard_map/ppermute | solution.py:497
  37.1 34.6 %copy-start = (bf16[2,4,32,1024]{3,2,1,0:T(8,128)(2,1)}, bf16[2,4,32,1024]{3,2,1,0:T(8,128)(2,1)S(1)}, u32[]{:S(2)}) copy-start(bf16[2,4,32,1024]{3,2,1,0:T(8,128)(2,1)S(1)} %get-tuple-element.51.refs_0_) | copy-start | bytes 1572868
  37.1 16.5 %all-to-all-start.1 = ((bf16[16,16,1024]{2,1,0:T(8,128)(2,1)}), bf16[16,16,1024]{2,1,0:T(8,128)(2,1)S(1)}, u32[]{:S(2)}, u32[]{:S(2)}) async-start(bf16[16,16,1024]{2,1,0:T(8,128)(2,1)} %bitcast.5), calls=%async_computation.1 | async-start | bytes 1048576 | tf_op jit(solution)/shard_map/all_to_all | solution.py:712
  42.1 15.7 %collective-permute-start.8 = (bf16[2,4,32,1024]{3,2,1,0:T(8,128)(2,1)S(1)}, bf16[2,4,32,1024]{3,2,1,0:T(8,128)(2,1)S(1)}, u32[]{:S(2)}, u32[]{:S(2)}) collective-permute-start(bf16[2,4,32,1024]{3,2,1,0:T(8,128)(2,1)S(1)} %get-tuple-element.51.refs_0_), channel_id=1, source_target_pairs={{0,3},{1,0},{2,1},{3,2},{4,7},{5,4},{6,5},{7,6},{8,11},{9,8},{10,9... | collective-permute-start | bytes 1572872 | tf_op jit(solution)/shard_map/ppermute | solution.py:478
  45.2 14.4 %collective-permute-start.7 = (bf16[2,4,32,1024]{3,2,1,0:T(8,128)(2,1)S(1)}, bf16[2,4,32,1024]{3,2,1,0:T(8,128)(2,1)}, u32[]{:S(2)}, u32[]{:S(2)}) collective-permute-start(bf16[2,4,32,1024]{3,2,1,0:T(8,128)(2,1)S(1)} %get-tuple-element.51.refs_0_), channel_id=1, source_target_pairs={{0,1},{1,2},{2,3},{3,0},{4,5},{5,6},{6,7},{7,4},{8,9},{9,10},{10,1... | collective-permute-start | bytes 1572872 | tf_op jit(solution)/shard_map/ppermute | solution.py:478
  54.0 1.6 %collective-permute-start.5 = (bf16[128,1024]{1,0:T(8,128)(2,1)S(1)}, bf16[128,1024]{1,0:T(8,128)(2,1)S(1)}, u32[]{:S(2)}, u32[]{:S(2)}) collective-permute-start(bf16[128,1024]{1,0:T(8,128)(2,1)S(1)} %get-tuple-element.55), channel_id=1, source_target_pairs={{0,64},{64,0},{1,65},{65,1},{2,66},{66,2},{3,67},{67,3},{4,68},{68... | collective-permute-start | bytes 786440 | tf_op jit(solution)/shard_map/ppermute | solution.py:714
  55.7 16.1 %collective-permute-start.11 = (bf16[128,2048]{1,0:T(8,128)(2,1)S(1)}, bf16[128,2048]{1,0:T(8,128)(2,1)S(1)}, u32[]{:S(2)}, u32[]{:S(2)}) collective-permute-start(bf16[128,2048]{1,0:T(8,128)(2,1)S(1)} %get-tuple-element.61.rows_ref.refs_4_), channel_id=1, source_target_pairs={{0,12},{4,0},{8,4},{12,8},{16,28},{20,16},{24,20},{28,24},{32,44},... | collective-permute-start | bytes 1572872 | tf_op jit(solution)/shard_map/ppermute | solution.py:497
  56.2 16.0 %collective-permute-start.10 = (bf16[128,2048]{1,0:T(8,128)(2,1)S(1)}, bf16[128,2048]{1,0:T(8,128)(2,1)S(1)}, u32[]{:S(2)}, u32[]{:S(2)}) collective-permute-start(bf16[128,2048]{1,0:T(8,128)(2,1)S(1)} %get-tuple-element.61.rows_ref.refs_4_), channel_id=1, source_target_pairs={{0,4},{4,8},{8,12},{12,0},{16,20},{20,24},{24,28},{28,16},{32,36},... | collective-permute-start | bytes 1572872 | tf_op jit(solution)/shard_map/ppermute | solution.py:497
  57.7 4.9 %collective-permute-start.6 = (bf16[128,1024]{1,0:T(8,128)(2,1)S(1)}, bf16[128,1024]{1,0:T(8,128)(2,1)S(1)}, u32[]{:S(2)}, u32[]{:S(2)}) collective-permute-start(bf16[128,1024]{1,0:T(8,128)(2,1)S(1)} %get-tuple-element.56), channel_id=1, source_target_pairs={{0,64},{64,0},{1,65},{65,1},{2,66},{66,2},{3,67},{67,3},{4,68},{68... | collective-permute-start | bytes 786440 | tf_op jit(solution)/shard_map/ppermute | solution.py:718
  57.8 1.8 %copy-start.5 = (bf16[2,4,32,1024]{3,2,1,0:T(8,128)(2,1)}, bf16[2,4,32,1024]{3,2,1,0:T(8,128)(2,1)S(1)}, u32[]{:S(2)}) copy-start(bf16[2,4,32,1024]{3,2,1,0:T(8,128)(2,1)S(1)} %collective-permute-done.8.refs_2_) | copy-start | bytes 1572868
  59.6 17.2 %collective-permute-start.9 = (bf16[2,4,32,1024]{3,2,1,0:T(8,128)(2,1)}, bf16[2,4,32,1024]{3,2,1,0:T(8,128)(2,1)}, u32[]{:S(2)}, u32[]{:S(2)}) collective-permute-start(bf16[2,4,32,1024]{3,2,1,0:T(8,128)(2,1)} %collective-permute-done.7.refs_1_), channel_id=1, source_target_pairs={{0,1},{1,2},{2,3},{3,0},{4,5},{5,6},{6,7},{7,4},{8,9},{9,10},{10,1... | collective-permute-start | bytes 1572872 | tf_op jit(solution)/shard_map/ppermute | solution.py:478
  60.2 16.6 %collective-permute-start.12 = (bf16[128,2048]{1,0:T(8,128)(2,1)S(1)}, bf16[128,2048]{1,0:T(8,128)(2,1)S(1)}, u32[]{:S(2)}, u32[]{:S(2)}) collective-permute-start(bf16[128,2048]{1,0:T(8,128)(2,1)S(1)} %get-tuple-element.61.rows_ref.refs_4_), channel_id=1, source_target_pairs={{0,8},{4,12},{8,0},{12,4},{16,24},{20,28},{24,16},{28,20},{32,40},... | collective-permute-start | bytes 1572872 | tf_op jit(solution)/shard_map/ppermute | solution.py:497
  71.7 21.0 %copy-start.3 = (f32[1,4096]{1,0:T(1,128)S(1)}, f32[1,4096]{1,0:T(1,128)}, u32[]{:S(2)}) copy-start(f32[1,4096]{1,0:T(1,128)} %gain_ref.1) | copy-start | bytes 49156
  72.2 20.5 %all-to-all-start.2 = ((bf16[4,32,4096]{2,1,0:T(8,128)(2,1)}), bf16[4,32,4096]{2,1,0:T(8,128)(2,1)S(1)}, u32[]{:S(2)}, u32[]{:S(2)}) async-start(bf16[4,32,4096]{2,1,0:T(8,128)(2,1)} %bitcast.17), calls=%async_computation.2 | async-start | bytes 2097152 | tf_op jit(solution)/shard_map/all_to_all | solution.py:722
  79.3 5.8 %collective-permute-start.13 = (bf16[256,1024]{1,0:T(8,128)(2,1)S(1)}, bf16[256,1024]{1,0:T(8,128)(2,1)S(1)}, u32[]{:S(2)}, u32[]{:S(2)}) collective-permute-start(bf16[256,1024]{1,0:T(8,128)(2,1)S(1)} %get-tuple-element.66), channel_id=1, source_target_pairs={{0,64},{64,0},{1,65},{65,1},{2,66},{66,2},{3,67},{67,3},{4,68},{68... | collective-permute-start | bytes 1572872 | tf_op jit(solution)/shard_map/ppermute | solution.py:728
  79.4 10.5 %collective-permute-start.14 = (bf16[128,2048]{1,0:T(8,128)(2,1)S(1)}, bf16[128,2048]{1,0:T(8,128)(2,1)S(1)}, u32[]{:S(2)}, u32[]{:S(2)}) collective-permute-start(bf16[128,2048]{1,0:T(8,128)(2,1)S(1)} %get-tuple-element.68), channel_id=1, source_target_pairs={{0,16},{4,20},{8,24},{12,28},{16,32},{20,36},{24,40},{28,44},{32,4... | collective-permute-start | bytes 1572872 | tf_op jit(solution)/shard_map/ppermute | solution.py:497
  80.4 9.4 %collective-permute-start.15 = (bf16[128,2048]{1,0:T(8,128)(2,1)S(1)}, bf16[128,2048]{1,0:T(8,128)(2,1)S(1)}, u32[]{:S(2)}, u32[]{:S(2)}) collective-permute-start(bf16[128,2048]{1,0:T(8,128)(2,1)S(1)} %get-tuple-element.69), channel_id=1, source_target_pairs={{0,48},{4,52},{8,56},{12,60},{16,0},{20,4},{24,8},{28,12},{32,16},... | collective-permute-start | bytes 1572872 | tf_op jit(solution)/shard_map/ppermute | solution.py:497
  85.1 4.7 %copy-start.6 = (bf16[256,1024]{1,0:T(8,128)(2,1)}, bf16[256,1024]{1,0:T(8,128)(2,1)S(1)}, u32[]{:S(2)}) copy-start(bf16[256,1024]{1,0:T(8,128)(2,1)S(1)} %collective-permute-done.13.other_hbm) | copy-start | bytes 1572868
  95.0 22.8 %all-to-all-start.3 = ((bf16[4,32,4096]{2,1,0:T(8,128)(2,1)}), bf16[4,32,4096]{2,1,0:T(8,128)(2,1)S(1)}, u32[]{:S(2)}, u32[]{:S(2)}) async-start(bf16[4,32,4096]{2,1,0:T(8,128)(2,1)} %rms_back.1), calls=%async_computation.3 | async-start | bytes 2097152 | tf_op jit(solution)/shard_map/all_to_all | solution.py:739
  99.8 10.4 %collective-permute-start.16 = (bf16[256,1024]{1,0:T(8,128)(2,1)S(1)}, bf16[256,1024]{1,0:T(8,128)(2,1)S(1)}, u32[]{:S(2)}, u32[]{:S(2)}) collective-permute-start(bf16[256,1024]{1,0:T(8,128)(2,1)S(1)} %get-tuple-element.75), channel_id=1, source_target_pairs={{0,16},{4,20},{8,24},{12,28},{16,32},{20,36},{24,40},{28,44},{32,4... | collective-permute-start | bytes 1572872 | tf_op jit(solution)/shard_map/ppermute | solution.py:497
  101.0 9.2 %collective-permute-start.17 = (bf16[256,1024]{1,0:T(8,128)(2,1)S(1)}, bf16[256,1024]{1,0:T(8,128)(2,1)S(1)}, u32[]{:S(2)}, u32[]{:S(2)}) collective-permute-start(bf16[256,1024]{1,0:T(8,128)(2,1)S(1)} %get-tuple-element.76), channel_id=1, source_target_pairs={{0,48},{4,52},{8,56},{12,60},{16,0},{20,4},{24,8},{28,12},{32,16},... | collective-permute-start | bytes 1572872 | tf_op jit(solution)/shard_map/ppermute | solution.py:497
  103.0 11.1 %collective-permute-start.18 = (bf16[256,1024]{1,0:T(8,128)(2,1)S(1)}, bf16[256,1024]{1,0:T(8,128)(2,1)S(1)}, u32[]{:S(2)}, u32[]{:S(2)}) collective-permute-start(bf16[256,1024]{1,0:T(8,128)(2,1)S(1)} %get-tuple-element.77), channel_id=1, source_target_pairs={{0,80},{4,84},{8,88},{12,92},{16,96},{20,100},{24,104},{28,108},{3... | collective-permute-start | bytes 1572872 | tf_op jit(solution)/shard_map/ppermute | solution.py:497
  103.0 12.3 %collective-permute-start.19 = (bf16[256,1024]{1,0:T(8,128)(2,1)S(1)}, bf16[256,1024]{1,0:T(8,128)(2,1)S(1)}, u32[]{:S(2)}, u32[]{:S(2)}) collective-permute-start(bf16[256,1024]{1,0:T(8,128)(2,1)S(1)} %get-tuple-element.78), channel_id=1, source_target_pairs={{0,112},{4,116},{8,120},{12,124},{16,64},{20,68},{24,72},{28,76},{... | collective-permute-start | bytes 1572872 | tf_op jit(solution)/shard_map/ppermute | solution.py:497

commit v11 on v9

--- a/solution.py
+++ b/solution.py
@@ -101,10 +101,6 @@
     get_x.start()
     get_gain.start()
 
-    @pl.when(core != 0)
-    def _():
-        get_left.start()
-
     def fetch(k):
         rows = pl.ds(k * step, step)
         return (
@@ -113,14 +109,27 @@
         )
 
     for k in range(count):
-        for copy in fetch(k):
-            copy.start()
+        copy_a, copy_b = fetch(k)
+        copy_a.start()
+        if k == 0:
+
+            @pl.when(core != 0)
+            def _():
+                get_left.start()
+
+        copy_b.start()
     get_x.wait()
     get_gain.wait()
     xf = x_ref[...].astype(F32)
     scale = lax.rsqrt(jnp.mean(xf * xf, axis=-1, keepdims=True) + EPS)
     normed_ref[...] = (xf * scale * gain_ref[...]).astype(BF16)
 
+    def product(ref, k, buf):
+        return jnp.dot(ref[:, k * step : (k + 1) * step], buf[k], preferred_element_type=F32)
+
+    fetch(0)[0].wait()
+    acc_a = product(normed_ref, 0, a_buf)
+
     @pl.when(core == 0)
     def _():
         left_ref[...] = normed_ref[...]
@@ -129,6 +138,8 @@
     def _():
         get_left.wait()
 
+    fetch(0)[1].wait()
+    acc_b = product(left_ref, 0, b_buf)
     z, x = lax.axis_index("z"), lax.axis_index("x")
     quarter = pl.ds(pl.multiple_of(lax.axis_index("mp") * QUARTER, QUARTER), QUARTER)
     block = cols // RING
@@ -150,15 +161,11 @@
                 )
                 copies[-1].start()
 
-    acc_a = acc_b = None
-    for k in range(count):
+    for k in range(1, count):
         for copy in fetch(k):
             copy.wait()
-        at = slice(k * step, (k + 1) * step)
-        part_a = jnp.dot(normed_ref[:, at], a_buf[k], preferred_element_type=F32)
-        part_b = jnp.dot(left_ref[:, at], b_buf[k], preferred_element_type=F32)
-        acc_a = part_a if acc_a is None else acc_a + part_a
-        acc_b = part_b if acc_b is None else acc_b + part_b
+        acc_a += product(normed_ref, k, a_buf)
+        acc_b += product(left_ref, k, b_buf)
     half = cols // 2
     parts = [[acc[:, i * half : (i + 1) * half].astype(BF16) for acc in (acc_a, acc_b)] for i in range(2)]
 
@@ -240,12 +247,8 @@
 
 
 def attend_kernel(
-    keep_ref, got_ref, slots_ref, src_ref, tgt_ref, dest_ref, *rest
+    keep_ref, got_ref, slots_ref, src_ref, tgt_ref, dest_ref, front_ref, back_ref, own_ref
 ):
-    front_ref, back_ref, stack_ref, own_ref = rest[RING:]
-    for p in range(RING):
-        for m in range(2):
-            stack_ref[m, p] = rest[p][m]
     mask = pair_mask(member_index(), src_ref, tgt_ref, dest_ref)
 
     @pl.when(lax.axis_index("section") == 0)
@@ -294,23 +297,40 @@
         back_ref[:, second] = fold(tn(weight, dout))
 
 
-def attend(keep, got, slots, src_len, tgt_len, dest, pieces):
+def attend(keep, got, slots, src_len, tgt_len, dest):
     rows, width = keep.shape
-    _, quarter, cols = pieces[0].shape
     return pl.pallas_call(
         attend_kernel,
-        in_specs=[VMEM] * (6 + RING),
-        out_specs=[VMEM] * 3,
+        in_specs=[VMEM] * 6,
+        out_specs=[VMEM] * 2,
         out_shape=[
             jax.ShapeDtypeStruct((rows, width), BF16),
             jax.ShapeDtypeStruct((SLOTS, width), BF16),
-            jax.ShapeDtypeStruct((2, RING, quarter, cols), BF16),
         ],
         scratch_shapes=[pltpu.VMEM((rows, width), BF16)],
         compiler_params=params(),
         cost_estimate=cost(24 * rows * SLOTS * width, 8 * SLOTS * width),
         name="attend",
-    )(keep, got, slots, src_len, tgt_len, dest, *pieces)
+    )(keep, got, slots, src_len, tgt_len, dest)
+
+
+def stack_kernel(*refs):
+    for p in range(RING):
+        for m in range(2):
+            refs[RING][m, p] = refs[p][m]
+
+
+def stacked(pieces):
+    _, quarter, cols = pieces[0].shape
+    return pl.pallas_call(
+        stack_kernel,
+        in_specs=[VMEM] * RING,
+        out_specs=VMEM,
+        out_shape=jax.ShapeDtypeStruct((2, RING, quarter, cols), BF16),
+        compiler_params=params(),
+        cost_estimate=cost(0, 4 * RING * pieces[0].size),
+        name="stack",
+    )(*pieces)
 
 
 def unpack_kernel(back_ref, front_ref, src_ref, dest_ref, keep_ref, send_ref):
@@ -726,8 +746,9 @@
     slots = lax.all_to_all(slots, ("z", "x"), split_axis=0, concat_axis=0, tiled=True)
     slots = slots.reshape(SLOTS, width)
     pieces = fetched(slices[0], {1: slices[1], 3: slices[2], 2: slices[3]})
-    front, back, own = attend(keep, got, slots, src_len, tgt_len, dest, pieces)
-    lefts = gathered(own, "mp")
+    front, back = attend(keep, got, slots, src_len, tgt_len, dest)
+    back, pieces = lax.optimization_barrier((back, pieces))
+    lefts = gathered(stacked(pieces), "mp")
     back = back.reshape(SEQ_DEV, MAXLEN, width)
     back = lax.all_to_all(back, ("z", "x"), split_axis=0, concat_axis=0, tiled=True)
     keep, send = unpack(back.reshape(SLOTS, width), front, src_len, dest)
@@ -756,8 +777,10 @@
         moved(left_other, 3, REDUCE, True),
     ]
     quarter = rms_back(rows, gains, parts)
-    grad_states = place(gathered(quarter, "mp"))
+    quarters = gathered(quarter, "mp")
     grad_a, grad_b = own_blocks(own, crossed, sums)
+    quarters[3], grad_a = lax.optimization_barrier((quarters[3], grad_a))
+    grad_states = place(quarters)
     return (grad_states[None], grad_a[None], grad_b[None])
 
 

time: 120 us -> 119 us (level)
  starting transfers between devices: 42.2 us -> 40.7 us
    all_to_all x1, waiting for transfers between devices: 0.01 us -> 6.99 us  [per_device(): lax.all_to_all(slots, ('z', 'x'), split_axis=0, concat_axis=0, tiled=True)]
    ppermute x12, waiting for transfers between devices: 12.5 us -> 7.5 us  [moved(): return lax.ppermute(value, ('section', 'z', 'x'), pairs)]
    all_to_all x1, starting transfers between devices: 4.96 us -> 3.59 us  [per_device(): lax.all_to_all(back, ('z', 'x'), split_axis=0, concat_axis=0, tiled=True)]
    pallas_call x1 -> x2, Pallas kernels: 2.95 us -> 2.98 us  [the longest x1 2.94 us: attend(): pl.pallas_call(attend_kernel, in_specs=[VMEM] * 6, out_specs=[VMEM] * 2,...]
  transfers between devices with their start and end apart: 26 -> 26, of which waited for: 12 -> 13; matrix products, arithmetic and copies ran while one was open for 0% -> 0% of each run, Pallas kernels for 15% -> 19%
where the time goes in v11:
time: 119 us; the launch traced here: 118 us
  waiting for transfers between devices  41.1 us (35%)
  starting transfers between devices  40.7 us (34%)
  Pallas kernels  35.3 us (30%)
    ppermute x12, starting transfers between devices, moved(): return lax.ppermute(value, ('section', 'z', 'x'), pairs)  16.6 us
    ppermute x6, waiting for transfers between devices, shift(): return lax.ppermute(value, axis, [(i, (i + k) % RING) for i in range(RING)])  16.2 us
    pallas_call x1, Pallas kernels, forward(): pl.pallas_call(forward_kernel, in_specs=[HBM] * 5, out_specs=[VMEM] * 4,...  9.1 us
    pallas_call x1, Pallas kernels, dnorm_partial(): pl.pallas_call(dnorm_kernel, in_specs=[VMEM] * 2 + [HBM] * 2, out_specs=H...  9.07 us
    all_to_all x1, starting transfers between devices, per_device(): lax.all_to_all(slots, ('z', 'x'), split_axis=0, concat_axis=0, tiled=True)  8.37 us
    ppermute x12, waiting for transfers between devices, moved(): return lax.ppermute(value, ('section', 'z', 'x'), pairs)  7.5 us
    all_to_all x1, waiting for transfers between devices, per_device(): lax.all_to_all(back, ('z', 'x'), split_axis=0, concat_axis=0, tiled=True)  7.49 us
    all_to_all x1, waiting for transfers between devices, per_device(): lax.all_to_all(slots, ('z', 'x'), split_axis=0, concat_axis=0, tiled=True)  6.99 us
  transfers between devices with their start and end apart: 26, of which 13 were waited for; matrix products, arithmetic and copies ran while one was open for 0% of the time, Pallas kernels for 19%

profile of v11, /device:TPU:0, one launch (start us, length us, event | category | flops | bytes accessed | tf_op | source)
XLA Modules:
  0.0 118.2 jit_solution(6771276749462589208)
XLA Ops:
  0.7 9.1 %forward.1 = (bf16[128,1024]{1,0:T(8,128)(2,1)S(1)}, bf16[128,1024]{1,0:T(8,128)(2,1)S(1)}, bf16[4,32,1024]{2,1,0:T(8,128)(2,1)S(1)}, bf16[4,32,1024]{2,1,0:T(8,128)(2,1)S(1)}) custom-call(bf16[128,4096]{1,0:T(8,128)(2,1)} %bitcast.18, f32[1,4096]{1,0:T(1,128)} %gain_ref.1, bf16[128,4096]{1,0:T(8,128)(2,1)} %cot_hbm.1, bf16[4096,1024]{1,0:T(8,128)(2,1)} %bitcast.13, ...), custom_call_target="tpu_custom_call" | custom-call | flops 134217728 | bytes 1048576 | tf_op jit(solution)/shard_map/forward/pallas_call | solution.py:196
  9.8 0.1 collective-permute-start
  9.9 0.5 collective-permute-start.1
  10.4 1.0 collective-permute-done.got_ref
  11.4 0.4 collective-permute-done.1.other_ref
  11.8 1.2 pack.1
  12.9 8.4 %all-to-all-start = ((bf16[16,16,1024]{2,1,0:T(8,128)(2,1)}), bf16[16,16,1024]{2,1,0:T(8,128)(2,1)S(1)}, u32[]{:S(2)}, u32[]{:S(2)}) async-start(bf16[16,16,1024]{2,1,0:T(8,128)(2,1)} %bitcast.3), calls=%async_computation | async-start | bytes 1048576 | tf_op jit(solution)/shard_map/all_to_all | solution.py:746
  21.3 1.9 %collective-permute-start.2 = (bf16[2,32,1024]{2,1,0:T(8,128)(2,1)S(1)}, bf16[2,32,1024]{2,1,0:T(8,128)(2,1)S(1)}, u32[]{:S(2)}, u32[]{:S(2)}) collective-permute-start(bf16[2,32,1024]{2,1,0:T(8,128)(2,1)S(1)} %get-tuple-element.57), channel_id=1, source_target_pairs={{0,4},{4,8},{8,12},{12,0},{16,20},{20,24},{24,28},{28,16},{32,36},... | collective-permute-start | bytes 393224 | tf_op jit(solution)/shard_map/ppermute | solution.py:537
  23.2 1.4 %collective-permute-start.3 = (bf16[2,32,1024]{2,1,0:T(8,128)(2,1)S(1)}, bf16[2,32,1024]{2,1,0:T(8,128)(2,1)S(1)}, u32[]{:S(2)}, u32[]{:S(2)}) collective-permute-start(bf16[2,32,1024]{2,1,0:T(8,128)(2,1)S(1)} %get-tuple-element.58), channel_id=1, source_target_pairs={{0,12},{4,0},{8,4},{12,8},{16,28},{20,16},{24,20},{28,24},{32,44},... | collective-permute-start | bytes 393224 | tf_op jit(solution)/shard_map/ppermute | solution.py:537
  24.6 2.2 %collective-permute-start.4 = (bf16[2,32,1024]{2,1,0:T(8,128)(2,1)S(1)}, bf16[2,32,1024]{2,1,0:T(8,128)(2,1)S(1)}, u32[]{:S(2)}, u32[]{:S(2)}) collective-permute-start(bf16[2,32,1024]{2,1,0:T(8,128)(2,1)S(1)} %get-tuple-element.59), channel_id=1, source_target_pairs={{0,8},{4,12},{8,0},{12,4},{16,24},{20,28},{24,16},{28,20},{32,40},... | collective-permute-start | bytes 393224 | tf_op jit(solution)/shard_map/ppermute | solution.py:537
  26.8 7.0 %all-to-all-done = bf16[16,16,1024]{2,1,0:T(8,128)(2,1)S(1)} async-done(((bf16[16,16,1024]{2,1,0:T(8,128)(2,1)}), bf16[16,16,1024]{2,1,0:T(8,128)(2,1)S(1)}, u32[]{:S(2)}, u32[]{:S(2)}) %all-to-all-start) | async-done | bytes 524320 | tf_op jit(solution)/shard_map/all_to_all | solution.py:746
  33.8 2.9 %attend.1 = (bf16[128,1024]{1,0:T(8,128)(2,1)S(1)}, bf16[256,1024]{1,0:T(8,128)(2,1)}) custom-call(bf16[128,1024]{1,0:T(8,128)(2,1)S(1)} %get-tuple-element.50.keep_ref, bf16[128,1024]{1,0:T(8,128)(2,1)S(1)} %collective-permute-done.got_ref, bf16[256,1024]{1,0:T(8,128)(2,1)S(1)} %bitcast.12, s32[16,16]{1,0:T(8,128)S(1)} %copy-done.1, ...), custom_call_target="tpu_custom_call" | custom-call | flops 50331648 | bytes 131072 | tf_op jit(solution)/shard_map/attend/pallas_call | solution.py:302
  36.7 0.0 collective-permute-done.2.refs_1_
  36.7 3.6 %all-to-all-start.1 = ((bf16[16,16,1024]{2,1,0:T(8,128)(2,1)}), bf16[16,16,1024]{2,1,0:T(8,128)(2,1)S(1)}, u32[]{:S(2)}, u32[]{:S(2)}) async-start(bf16[16,16,1024]{2,1,0:T(8,128)(2,1)} %bitcast.5), calls=%async_computation.1 | async-start | bytes 1048576 | tf_op jit(solution)/shard_map/all_to_all | solution.py:753
  40.4 0.0 copy-start
  40.4 3.1 %collective-permute-start.8 = (bf16[2,4,32,1024]{3,2,1,0:T(8,128)(2,1)S(1)}, bf16[2,4,32,1024]{3,2,1,0:T(8,128)(2,1)S(1)}, u32[]{:S(2)}, u32[]{:S(2)}) collective-permute-start(bf16[2,4,32,1024]{3,2,1,0:T(8,128)(2,1)S(1)} %stack.1.refs_0_), channel_id=1, source_target_pairs={{0,3},{1,0},{2,1},{3,2},{4,7},{5,4},{6,5},{7,6},{8,11},{9,8},{10,9... | collective-permute-start | bytes 1572872 | tf_op jit(solution)/shard_map/ppermute | solution.py:518
  43.5 7.5 %all-to-all-done.1 = bf16[16,16,1024]{2,1,0:T(8,128)(2,1)S(1)} async-done(((bf16[16,16,1024]{2,1,0:T(8,128)(2,1)}), bf16[16,16,1024]{2,1,0:T(8,128)(2,1)S(1)}, u32[]{:S(2)}, u32[]{:S(2)}) %all-to-all-start.1) | async-done | bytes 524320 | tf_op jit(solution)/shard_map/all_to_all | solution.py:753
  51.0 0.4 unpack.1
  51.4 0.1 collective-permute-start.5
  51.5 1.5 %collective-permute-done.5.got_ref = bf16[128,1024]{1,0:T(8,128)(2,1)S(1)} collective-permute-done((bf16[128,1024]{1,0:T(8,128)(2,1)S(1)}, bf16[128,1024]{1,0:T(8,128)(2,1)S(1)}, u32[]{:S(2)}, u32[]{:S(2)}) %collective-permute-start.5) | collective-permute-done | bytes 262176 | tf_op jit(solution)/shard_map/ppermute | solution.py:755
  53.0 0.1 join.1
  53.1 0.5 collective-permute-start.11
  53.6 1.6 %collective-permute-start.10 = (bf16[128,2048]{1,0:T(8,128)(2,1)S(1)}, bf16[128,2048]{1,0:T(8,128)(2,1)S(1)}, u32[]{:S(2)}, u32[]{:S(2)}) collective-permute-start(bf16[128,2048]{1,0:T(8,128)(2,1)S(1)} %get-tuple-element.73.rows_ref.refs_4_), channel_id=1, source_target_pairs={{0,4},{4,8},{8,12},{12,0},{16,20},{20,24},{24,28},{28,16},{32,36},... | collective-permute-start | bytes 1572872 | tf_op jit(solution)/shard_map/ppermute | solution.py:537
  55.2 1.8 %collective-permute-done.7.refs_1_ = bf16[2,4,32,1024]{3,2,1,0:T(8,128)(2,1)} collective-permute-done((bf16[2,4,32,1024]{3,2,1,0:T(8,128)(2,1)S(1)}, bf16[2,4,32,1024]{3,2,1,0:T(8,128)(2,1)}, u32[]{:S(2)}, u32[]{:S(2)}) %collective-permute-start.7) | collective-permute-done | bytes 524320 | tf_op jit(solution)/shard_map/ppermute | solution.py:518
  57.0 0.6 collective-permute-start.9
  57.6 2.5 %collective-permute-start.12 = (bf16[128,2048]{1,0:T(8,128)(2,1)S(1)}, bf16[128,2048]{1,0:T(8,128)(2,1)S(1)}, u32[]{:S(2)}, u32[]{:S(2)}) collective-permute-start(bf16[128,2048]{1,0:T(8,128)(2,1)S(1)} %get-tuple-element.73.rows_ref.refs_4_), channel_id=1, source_target_pairs={{0,8},{4,12},{8,0},{12,4},{16,24},{20,28},{24,16},{28,20},{32,40},... | collective-permute-start | bytes 1572872 | tf_op jit(solution)/shard_map/ppermute | solution.py:537
  60.0 9.1 %dnorm.1 = bf16[128,4096]{1,0:T(8,128)(2,1)} custom-call(bf16[128,2048]{1,0:T(8,128)(2,1)S(1)} %get-tuple-element.73.rows_ref.refs_4_, bf16[128,1024]{1,0:T(8,128)(2,1)S(1)} %collective-permute-done.6.got_ref, bf16[4096,1024]{1,0:T(8,128)(2,1)} %bitcast.14, bf16[4096,1024]{1,0:T(8,128)(2,1)} %bitcast.16), custom_call_target="tpu_custom_call" | custom-call | flops 134217728 | bytes 1048576 | tf_op jit(solution)/shard_map/dnorm/pallas_call | solution.py:447
  69.1 0.0 copy-start.3
  69.2 0.4 collective-permute-done.10.refs_5_
  69.6 4.5 %all-to-all-start.2 = ((bf16[4,32,4096]{2,1,0:T(8,128)(2,1)}), bf16[4,32,4096]{2,1,0:T(8,128)(2,1)S(1)}, u32[]{:S(2)}, u32[]{:S(2)}) async-start(bf16[4,32,4096]{2,1,0:T(8,128)(2,1)} %bitcast.17), calls=%async_computation.2 | async-start | bytes 2097152 | tf_op jit(solution)/shard_map/all_to_all | solution.py:763
  74.1 2.5 %far.1 = (bf16[128,2048]{1,0:T(8,128)(2,1)S(1)}, bf16[128,2048]{1,0:T(8,128)(2,1)S(1)}, bf16[512,2048]{1,0:T(8,128)(2,1)S(1)}, bf16[256,1024]{1,0:T(8,128)(2,1)S(1)}) custom-call(bf16[2,4,32,1024]{3,2,1,0:T(8,128)(2,1)} %copy-done, bf16[2,4,32,1024]{3,2,1,0:T(8,128)(2,1)} %collective-permute-done.7.refs_1_, bf16[2,4,32,1024]{3,2,1,0:T(8,128)(2,1)} %copy-done.5, ...), custom_call_target="tpu_custom_call" | custom-call | flops 50331648 | bytes 524288 | tf_op jit(solution)/shard_map/far/pallas_call | solution.py:599
  76.6 0.1 collective-permute-start.13
  76.7 1.2 collective-permute-start.14
  77.8 2.1 %collective-permute-start.15 = (bf16[128,2048]{1,0:T(8,128)(2,1)S(1)}, bf16[128,2048]{1,0:T(8,128)(2,1)S(1)}, u32[]{:S(2)}, u32[]{:S(2)}) collective-permute-start(bf16[128,2048]{1,0:T(8,128)(2,1)S(1)} %get-tuple-element.81), channel_id=1, source_target_pairs={{0,48},{4,52},{8,56},{12,60},{16,0},{20,4},{24,8},{28,12},{32,16},... | collective-permute-start | bytes 1572872 | tf_op jit(solution)/shard_map/ppermute | solution.py:537
  80.0 2.4 %middle.1.own_hbm = bf16[256,1024]{1,0:T(8,128)(2,1)} custom-call(bf16[2,4,32,1024]{3,2,1,0:T(8,128)(2,1)} %copy-done, bf16[2,4,32,1024]{3,2,1,0:T(8,128)(2,1)} %collective-permute-done.7.refs_1_, bf16[2,4,32,1024]{3,2,1,0:T(8,128)(2,1)} %copy-done.5, bf16[2,4,32,1024]{3,2,1,0:T(8,128)(2,1)} %collective-permute-done.9.refs_3_, ...), custom_call_target="tpu_custom_call" | custom-call | flops 16777216 | bytes 262144 | tf_op jit(solution)/shard_map/middle/pallas_call | solution.py:666
  82.4 4.7 %collective-permute-done.14.refs_5_ = bf16[128,2048]{1,0:T(8,128)(2,1)S(1)} collective-permute-done((bf16[128,2048]{1,0:T(8,128)(2,1)S(1)}, bf16[128,2048]{1,0:T(8,128)(2,1)S(1)}, u32[]{:S(2)}, u32[]{:S(2)}) %collective-permute-start.14) | collective-permute-done | bytes 524320 | tf_op jit(solution)/shard_map/ppermute | solution.py:537
  87.1 2.9 %side.1 = (bf16[256,1024]{1,0:T(8,128)(2,1)S(1)}, bf16[256,1024]{1,0:T(8,128)(2,1)S(1)}, bf16[256,1024]{1,0:T(8,128)(2,1)S(1)}, bf16[256,1024]{1,0:T(8,128)(2,1)S(1)}) custom-call(bf16[2,4,32,1024]{3,2,1,0:T(8,128)(2,1)} %copy-done, bf16[2,4,32,1024]{3,2,1,0:T(8,128)(2,1)} %collective-permute-done.7.refs_1_, bf16[2,4,32,1024]{3,2,1,0:T(8,128)(2,1)} %copy-done.5, ...), custom_call_target="tpu_custom_call" | custom-call | flops 67108864 | bytes 262144 | tf_op jit(solution)/shard_map/side/pallas_call | solution.py:640
  90.1 1.2 %rms_back.1.refs_0_ = bf16[32,4096]{1,0:T(8,128)(2,1)S(1)} custom-call(bf16[128,4096]{1,0:T(8,128)(2,1)} %bitcast.19, f32[1,4096]{1,0:T(1,128)S(1)} %copy-done.3, bf16[4,32,4096]{2,1,0:T(8,128)(2,1)S(1)} %all-to-all-done.2.parts_ref), custom_call_target="tpu_custom_call" | custom-call | flops 81920 | bytes 98304 | tf_op jit(solution)/shard_map/rms_back/pallas_call | solution.py:479
  91.3 3.3 %collective-permute-start.17 = (bf16[32,4096]{1,0:T(8,128)(2,1)S(1)}, bf16[32,4096]{1,0:T(8,128)(2,1)S(1)}, u32[]{:S(2)}, u32[]{:S(2)}) collective-permute-start(bf16[32,4096]{1,0:T(8,128)(2,1)S(1)} %rms_back.1.refs_0_), channel_id=1, source_target_pairs={{0,3},{1,0},{2,1},{3,2},{4,7},{5,4},{6,5},{7,6},{8,11},{9,8},{10,9... | collective-permute-start | bytes 786440 | tf_op jit(solution)/shard_map/ppermute | solution.py:518
  94.6 1.4 %collective-permute-start.19 = (bf16[256,1024]{1,0:T(8,128)(2,1)S(1)}, bf16[256,1024]{1,0:T(8,128)(2,1)S(1)}, u32[]{:S(2)}, u32[]{:S(2)}) collective-permute-start(bf16[256,1024]{1,0:T(8,128)(2,1)S(1)} %get-tuple-element.89), channel_id=1, source_target_pairs={{0,16},{4,20},{8,24},{12,28},{16,32},{20,36},{24,40},{28,44},{32,4... | collective-permute-start | bytes 1572872 | tf_op jit(solution)/shard_map/ppermute | solution.py:537
  96.0 1.9 %collective-permute-start.20 = (bf16[256,1024]{1,0:T(8,128)(2,1)S(1)}, bf16[256,1024]{1,0:T(8,128)(2,1)S(1)}, u32[]{:S(2)}, u32[]{:S(2)}) collective-permute-start(bf16[256,1024]{1,0:T(8,128)(2,1)S(1)} %get-tuple-element.90), channel_id=1, source_target_pairs={{0,48},{4,52},{8,56},{12,60},{16,0},{20,4},{24,8},{28,12},{32,16},... | collective-permute-start | bytes 1572872 | tf_op jit(solution)/shard_map/ppermute | solution.py:537
  97.8 2.1 %collective-permute-done.17.refs_2_ = bf16[32,4096]{1,0:T(8,128)(2,1)S(1)} collective-permute-done((bf16[32,4096]{1,0:T(8,128)(2,1)S(1)}, bf16[32,4096]{1,0:T(8,128)(2,1)S(1)}, u32[]{:S(2)}, u32[]{:S(2)}) %collective-permute-start.17) | collective-permute-done | bytes 262176 | tf_op jit(solution)/shard_map/ppermute | solution.py:518
  99.9 7.9 %collective-permute-done.16.refs_1_ = bf16[32,4096]{1,0:T(8,128)(2,1)S(1)} collective-permute-done((bf16[32,4096]{1,0:T(8,128)(2,1)S(1)}, bf16[32,4096]{1,0:T(8,128)(2,1)S(1)}, u32[]{:S(2)}, u32[]{:S(2)}) %collective-permute-start.16) | collective-permute-done | bytes 262176 | tf_op jit(solution)/shard_map/ppermute | solution.py:518
  107.8 1.1 collective-permute-done.21.refs_2_
  108.9 1.2 %collective-permute-done.22.refs_3_ = bf16[256,1024]{1,0:T(8,128)(2,1)S(1)} collective-permute-done((bf16[256,1024]{1,0:T(8,128)(2,1)S(1)}, bf16[256,1024]{1,0:T(8,128)(2,1)S(1)}, u32[]{:S(2)}, u32[]{:S(2)}) %collective-permute-start.22) | collective-permute-done | bytes 524320 | tf_op jit(solution)/shard_map/ppermute | solution.py:537
  110.1 2.5 %own.1 = (f32[256,1024]{1,0:T(8,128)}, f32[256,1024]{1,0:T(8,128)}) custom-call(bf16[256,1024]{1,0:T(8,128)(2,1)} %middle.1.own_hbm, bf16[256,1024]{1,0:T(8,128)(2,1)} %copy-done.6, bf16[256,1024]{1,0:T(8,128)(2,1)S(1)} %collective-permute-done.19.refs_0_, bf16[256,1024]{1,0:T(8,128)(2,1)S(1)} %collective-permute-done.20.refs_1_, ...), custom_call_target="tpu_custom_call" | custom-call | flops 65536 | bytes 327680 | tf_op jit(solution)/shard_map/own/pallas_call | solution.py:719
  112.6 4.4 %collective-permute-done.18.refs_3_ = bf16[32,4096]{1,0:T(8,128)(2,1)S(1)} collective-permute-done((bf16[32,4096]{1,0:T(8,128)(2,1)S(1)}, bf16[32,4096]{1,0:T(8,128)(2,1)S(1)}, u32[]{:S(2)}, u32[]{:S(2)}) %collective-permute-start.18) | collective-permute-done | bytes 262176 | tf_op jit(solution)/shard_map/ppermute | solution.py:518
  117.0 1.0 place.1
  (31 shorter events, 0.1 us)
Async XLA Ops:
  0.6 11.1 %copy-start.1 = (s32[16,16]{1,0:T(8,128)S(1)}, s32[16,16]{1,0:T(8,128)}, u32[]{:S(2)}) copy-start(s32[16,16]{1,0:T(8,128)} %src_ref.5) | copy-start | bytes 3076
  0.6 11.1 %copy-start.2 = (s32[16,16]{1,0:T(8,128)S(1)}, s32[16,16]{1,0:T(8,128)}, u32[]{:S(2)}) copy-start(s32[16,16]{1,0:T(8,128)} %dest_ref.5) | copy-start | bytes 3076
  0.7 33.1 %copy-start.4 = (s32[16,16]{1,0:T(8,128)S(1)}, s32[16,16]{1,0:T(8,128)}, u32[]{:S(2)}) copy-start(s32[16,16]{1,0:T(8,128)} %tgt_ref.1) | copy-start | bytes 3076
  9.8 1.6 %collective-permute-start = (bf16[128,1024]{1,0:T(8,128)(2,1)S(1)}, bf16[128,1024]{1,0:T(8,128)(2,1)S(1)}, u32[]{:S(2)}, u32[]{:S(2)}) collective-permute-start(bf16[128,1024]{1,0:T(8,128)(2,1)S(1)} %get-tuple-element.51), channel_id=1, source_target_pairs={{0,64},{64,0},{1,65},{65,1},{2,66},{66,2},{3,67},{67,3},{4,68},{68... | collective-permute-start | bytes 786440 | tf_op jit(solution)/shard_map/ppermute | solution.py:742
  9.9 1.9 %collective-permute-start.1 = (bf16[4,32,1024]{2,1,0:T(8,128)(2,1)S(1)}, bf16[4,32,1024]{2,1,0:T(8,128)(2,1)S(1)}, u32[]{:S(2)}, u32[]{:S(2)}) collective-permute-start(bf16[4,32,1024]{2,1,0:T(8,128)(2,1)S(1)} %get-tuple-element.53), channel_id=1, source_target_pairs={{0,64},{64,0},{1,65},{65,1},{2,66},{66,2},{3,67},{67,3},{4,68},{68... | collective-permute-start | bytes 786440 | tf_op jit(solution)/shard_map/ppermute | solution.py:743
  12.9 20.8 %all-to-all-start = ((bf16[16,16,1024]{2,1,0:T(8,128)(2,1)}), bf16[16,16,1024]{2,1,0:T(8,128)(2,1)S(1)}, u32[]{:S(2)}, u32[]{:S(2)}) async-start(bf16[16,16,1024]{2,1,0:T(8,128)(2,1)} %bitcast.3), calls=%async_computation | async-start | bytes 1048576 | tf_op jit(solution)/shard_map/all_to_all | solution.py:746
  21.3 15.4 %collective-permute-start.2 = (bf16[2,32,1024]{2,1,0:T(8,128)(2,1)S(1)}, bf16[2,32,1024]{2,1,0:T(8,128)(2,1)S(1)}, u32[]{:S(2)}, u32[]{:S(2)}) collective-permute-start(bf16[2,32,1024]{2,1,0:T(8,128)(2,1)S(1)} %get-tuple-element.57), channel_id=1, source_target_pairs={{0,4},{4,8},{8,12},{12,0},{16,20},{20,24},{24,28},{28,16},{32,36},... | collective-permute-start | bytes 393224 | tf_op jit(solution)/shard_map/ppermute | solution.py:537
  23.2 13.5 %collective-permute-start.3 = (bf16[2,32,1024]{2,1,0:T(8,128)(2,1)S(1)}, bf16[2,32,1024]{2,1,0:T(8,128)(2,1)S(1)}, u32[]{:S(2)}, u32[]{:S(2)}) collective-permute-start(bf16[2,32,1024]{2,1,0:T(8,128)(2,1)S(1)} %get-tuple-element.58), channel_id=1, source_target_pairs={{0,12},{4,0},{8,4},{12,8},{16,28},{20,16},{24,20},{28,24},{32,44},... | collective-permute-start | bytes 393224 | tf_op jit(solution)/shard_map/ppermute | solution.py:537
  24.6 12.1 %collective-permute-start.4 = (bf16[2,32,1024]{2,1,0:T(8,128)(2,1)S(1)}, bf16[2,32,1024]{2,1,0:T(8,128)(2,1)S(1)}, u32[]{:S(2)}, u32[]{:S(2)}) collective-permute-start(bf16[2,32,1024]{2,1,0:T(8,128)(2,1)S(1)} %get-tuple-element.59), channel_id=1, source_target_pairs={{0,8},{4,12},{8,0},{12,4},{16,24},{20,28},{24,16},{28,20},{32,40},... | collective-permute-start | bytes 393224 | tf_op jit(solution)/shard_map/ppermute | solution.py:537
  36.7 14.2 %all-to-all-start.1 = ((bf16[16,16,1024]{2,1,0:T(8,128)(2,1)}), bf16[16,16,1024]{2,1,0:T(8,128)(2,1)S(1)}, u32[]{:S(2)}, u32[]{:S(2)}) async-start(bf16[16,16,1024]{2,1,0:T(8,128)(2,1)} %bitcast.5), calls=%async_computation.1 | async-start | bytes 1048576 | tf_op jit(solution)/shard_map/all_to_all | solution.py:753
  40.4 28.8 %copy-start = (bf16[2,4,32,1024]{3,2,1,0:T(8,128)(2,1)}, bf16[2,4,32,1024]{3,2,1,0:T(8,128)(2,1)S(1)}, u32[]{:S(2)}) copy-start(bf16[2,4,32,1024]{3,2,1,0:T(8,128)(2,1)S(1)} %stack.1.refs_0_) | copy-start | bytes 1572868
  40.4 14.8 %collective-permute-start.8 = (bf16[2,4,32,1024]{3,2,1,0:T(8,128)(2,1)S(1)}, bf16[2,4,32,1024]{3,2,1,0:T(8,128)(2,1)S(1)}, u32[]{:S(2)}, u32[]{:S(2)}) collective-permute-start(bf16[2,4,32,1024]{3,2,1,0:T(8,128)(2,1)S(1)} %stack.1.refs_0_), channel_id=1, source_target_pairs={{0,3},{1,0},{2,1},{3,2},{4,7},{5,4},{6,5},{7,6},{8,11},{9,8},{10,9... | collective-permute-start | bytes 1572872 | tf_op jit(solution)/shard_map/ppermute | solution.py:518
  43.5 13.5 %collective-permute-start.7 = (bf16[2,4,32,1024]{3,2,1,0:T(8,128)(2,1)S(1)}, bf16[2,4,32,1024]{3,2,1,0:T(8,128)(2,1)}, u32[]{:S(2)}, u32[]{:S(2)}) collective-permute-start(bf16[2,4,32,1024]{3,2,1,0:T(8,128)(2,1)S(1)} %stack.1.refs_0_), channel_id=1, source_target_pairs={{0,1},{1,2},{2,3},{3,0},{4,5},{5,6},{6,7},{7,4},{8,9},{9,10},{10,1... | collective-permute-start | bytes 1572872 | tf_op jit(solution)/shard_map/ppermute | solution.py:518
  51.4 1.6 %collective-permute-start.5 = (bf16[128,1024]{1,0:T(8,128)(2,1)S(1)}, bf16[128,1024]{1,0:T(8,128)(2,1)S(1)}, u32[]{:S(2)}, u32[]{:S(2)}) collective-permute-start(bf16[128,1024]{1,0:T(8,128)(2,1)S(1)} %get-tuple-element.67), channel_id=1, source_target_pairs={{0,64},{64,0},{1,65},{65,1},{2,66},{66,2},{3,67},{67,3},{4,68},{68... | collective-permute-start | bytes 786440 | tf_op jit(solution)/shard_map/ppermute | solution.py:755
  53.1 16.1 %collective-permute-start.11 = (bf16[128,2048]{1,0:T(8,128)(2,1)S(1)}, bf16[128,2048]{1,0:T(8,128)(2,1)S(1)}, u32[]{:S(2)}, u32[]{:S(2)}) collective-permute-start(bf16[128,2048]{1,0:T(8,128)(2,1)S(1)} %get-tuple-element.73.rows_ref.refs_4_), channel_id=1, source_target_pairs={{0,12},{4,0},{8,4},{12,8},{16,28},{20,16},{24,20},{28,24},{32,44},... | collective-permute-start | bytes 1572872 | tf_op jit(solution)/shard_map/ppermute | solution.py:537
  53.6 16.0 %collective-permute-start.10 = (bf16[128,2048]{1,0:T(8,128)(2,1)S(1)}, bf16[128,2048]{1,0:T(8,128)(2,1)S(1)}, u32[]{:S(2)}, u32[]{:S(2)}) collective-permute-start(bf16[128,2048]{1,0:T(8,128)(2,1)S(1)} %get-tuple-element.73.rows_ref.refs_4_), channel_id=1, source_target_pairs={{0,4},{4,8},{8,12},{12,0},{16,20},{20,24},{24,28},{28,16},{32,36},... | collective-permute-start | bytes 1572872 | tf_op jit(solution)/shard_map/ppermute | solution.py:537
  55.2 4.9 %collective-permute-start.6 = (bf16[128,1024]{1,0:T(8,128)(2,1)S(1)}, bf16[128,1024]{1,0:T(8,128)(2,1)S(1)}, u32[]{:S(2)}, u32[]{:S(2)}) collective-permute-start(bf16[128,1024]{1,0:T(8,128)(2,1)S(1)} %get-tuple-element.68), channel_id=1, source_target_pairs={{0,64},{64,0},{1,65},{65,1},{2,66},{66,2},{3,67},{67,3},{4,68},{68... | collective-permute-start | bytes 786440 | tf_op jit(solution)/shard_map/ppermute | solution.py:759
  55.2 1.8 %copy-start.5 = (bf16[2,4,32,1024]{3,2,1,0:T(8,128)(2,1)}, bf16[2,4,32,1024]{3,2,1,0:T(8,128)(2,1)S(1)}, u32[]{:S(2)}) copy-start(bf16[2,4,32,1024]{3,2,1,0:T(8,128)(2,1)S(1)} %collective-permute-done.8.refs_2_) | copy-start | bytes 1572868
  57.0 17.1 %collective-permute-start.9 = (bf16[2,4,32,1024]{3,2,1,0:T(8,128)(2,1)}, bf16[2,4,32,1024]{3,2,1,0:T(8,128)(2,1)}, u32[]{:S(2)}, u32[]{:S(2)}) collective-permute-start(bf16[2,4,32,1024]{3,2,1,0:T(8,128)(2,1)} %collective-permute-done.7.refs_1_), channel_id=1, source_target_pairs={{0,1},{1,2},{2,3},{3,0},{4,5},{5,6},{6,7},{7,4},{8,9},{9,10},{10,1... | collective-permute-start | bytes 1572872 | tf_op jit(solution)/shard_map/ppermute | solution.py:518
  57.6 16.5 %collective-permute-start.12 = (bf16[128,2048]{1,0:T(8,128)(2,1)S(1)}, bf16[128,2048]{1,0:T(8,128)(2,1)S(1)}, u32[]{:S(2)}, u32[]{:S(2)}) collective-permute-start(bf16[128,2048]{1,0:T(8,128)(2,1)S(1)} %get-tuple-element.73.rows_ref.refs_4_), channel_id=1, source_target_pairs={{0,8},{4,12},{8,0},{12,4},{16,24},{20,28},{24,16},{28,20},{32,40},... | collective-permute-start | bytes 1572872 | tf_op jit(solution)/shard_map/ppermute | solution.py:537
  69.1 21.0 %copy-start.3 = (f32[1,4096]{1,0:T(1,128)S(1)}, f32[1,4096]{1,0:T(1,128)}, u32[]{:S(2)}) copy-start(f32[1,4096]{1,0:T(1,128)} %gain_ref.1) | copy-start | bytes 49156
  69.6 20.5 %all-to-all-start.2 = ((bf16[4,32,4096]{2,1,0:T(8,128)(2,1)}), bf16[4,32,4096]{2,1,0:T(8,128)(2,1)S(1)}, u32[]{:S(2)}, u32[]{:S(2)}) async-start(bf16[4,32,4096]{2,1,0:T(8,128)(2,1)} %bitcast.17), calls=%async_computation.2 | async-start | bytes 2097152 | tf_op jit(solution)/shard_map/all_to_all | solution.py:763
  76.6 5.8 %collective-permute-start.13 = (bf16[256,1024]{1,0:T(8,128)(2,1)S(1)}, bf16[256,1024]{1,0:T(8,128)(2,1)S(1)}, u32[]{:S(2)}, u32[]{:S(2)}) collective-permute-start(bf16[256,1024]{1,0:T(8,128)(2,1)S(1)} %get-tuple-element.78), channel_id=1, source_target_pairs={{0,64},{64,0},{1,65},{65,1},{2,66},{66,2},{3,67},{67,3},{4,68},{68... | collective-permute-start | bytes 1572872 | tf_op jit(solution)/shard_map/ppermute | solution.py:769
  76.7 10.5 %collective-permute-start.14 = (bf16[128,2048]{1,0:T(8,128)(2,1)S(1)}, bf16[128,2048]{1,0:T(8,128)(2,1)S(1)}, u32[]{:S(2)}, u32[]{:S(2)}) collective-permute-start(bf16[128,2048]{1,0:T(8,128)(2,1)S(1)} %get-tuple-element.80), channel_id=1, source_target_pairs={{0,16},{4,20},{8,24},{12,28},{16,32},{20,36},{24,40},{28,44},{32,4... | collective-permute-start | bytes 1572872 | tf_op jit(solution)/shard_map/ppermute | solution.py:537
  77.8 9.3 %collective-permute-start.15 = (bf16[128,2048]{1,0:T(8,128)(2,1)S(1)}, bf16[128,2048]{1,0:T(8,128)(2,1)S(1)}, u32[]{:S(2)}, u32[]{:S(2)}) collective-permute-start(bf16[128,2048]{1,0:T(8,128)(2,1)S(1)} %get-tuple-element.81), channel_id=1, source_target_pairs={{0,48},{4,52},{8,56},{12,60},{16,0},{20,4},{24,8},{28,12},{32,16},... | collective-permute-start | bytes 1572872 | tf_op jit(solution)/shard_map/ppermute | solution.py:537
  82.4 4.7 %copy-start.6 = (bf16[256,1024]{1,0:T(8,128)(2,1)}, bf16[256,1024]{1,0:T(8,128)(2,1)S(1)}, u32[]{:S(2)}) copy-start(bf16[256,1024]{1,0:T(8,128)(2,1)S(1)} %collective-permute-done.13.other_hbm) | copy-start | bytes 1572868
  91.3 8.6 %collective-permute-start.17 = (bf16[32,4096]{1,0:T(8,128)(2,1)S(1)}, bf16[32,4096]{1,0:T(8,128)(2,1)S(1)}, u32[]{:S(2)}, u32[]{:S(2)}) collective-permute-start(bf16[32,4096]{1,0:T(8,128)(2,1)S(1)} %rms_back.1.refs_0_), channel_id=1, source_target_pairs={{0,3},{1,0},{2,1},{3,2},{4,7},{5,4},{6,5},{7,6},{8,11},{9,8},{10,9... | collective-permute-start | bytes 786440 | tf_op jit(solution)/shard_map/ppermute | solution.py:518
  94.6 13.2 %collective-permute-start.19 = (bf16[256,1024]{1,0:T(8,128)(2,1)S(1)}, bf16[256,1024]{1,0:T(8,128)(2,1)S(1)}, u32[]{:S(2)}, u32[]{:S(2)}) collective-permute-start(bf16[256,1024]{1,0:T(8,128)(2,1)S(1)} %get-tuple-element.89), channel_id=1, source_target_pairs={{0,16},{4,20},{8,24},{12,28},{16,32},{20,36},{24,40},{28,44},{32,4... | collective-permute-start | bytes 1572872 | tf_op jit(solution)/shard_map/ppermute | solution.py:537
  96.0 11.9 %collective-permute-start.20 = (bf16[256,1024]{1,0:T(8,128)(2,1)S(1)}, bf16[256,1024]{1,0:T(8,128)(2,1)S(1)}, u32[]{:S(2)}, u32[]{:S(2)}) collective-permute-start(bf16[256,1024]{1,0:T(8,128)(2,1)S(1)} %get-tuple-element.90), channel_id=1, source_target_pairs={{0,48},{4,52},{8,56},{12,60},{16,0},{20,4},{24,8},{28,12},{32,16},... | collective-permute-start | bytes 1572872 | tf_op jit(solution)/shard_map/ppermute | solution.py:537
  97.8 11.1 %collective-permute-start.21 = (bf16[256,1024]{1,0:T(8,128)(2,1)S(1)}, bf16[256,1024]{1,0:T(8,128)(2,1)S(1)}, u32[]{:S(2)}, u32[]{:S(2)}) collective-permute-start(bf16[256,1024]{1,0:T(8,128)(2,1)S(1)} %get-tuple-element.91), channel_id=1, source_target_pairs={{0,80},{4,84},{8,88},{12,92},{16,96},{20,100},{24,104},{28,108},{3... | collective-permute-start | bytes 1572872 | tf_op jit(solution)/shard_map/ppermute | solution.py:537
  97.8 10.0 %collective-permute-start.16 = (bf16[32,4096]{1,0:T(8,128)(2,1)S(1)}, bf16[32,4096]{1,0:T(8,128)(2,1)S(1)}, u32[]{:S(2)}, u32[]{:S(2)}) collective-permute-start(bf16[32,4096]{1,0:T(8,128)(2,1)S(1)} %rms_back.1.refs_0_), channel_id=1, source_target_pairs={{0,1},{1,2},{2,3},{3,0},{4,5},{5,6},{6,7},{7,4},{8,9},{9,10},{10,1... | collective-permute-start | bytes 786440 | tf_op jit(solution)/shard_map/ppermute | solution.py:518
  99.9 10.3 %collective-permute-start.22 = (bf16[256,1024]{1,0:T(8,128)(2,1)S(1)}, bf16[256,1024]{1,0:T(8,128)(2,1)S(1)}, u32[]{:S(2)}, u32[]{:S(2)}) collective-permute-start(bf16[256,1024]{1,0:T(8,128)(2,1)S(1)} %get-tuple-element.92), channel_id=1, source_target_pairs={{0,112},{4,116},{8,120},{12,124},{16,64},{20,68},{24,72},{28,76},{... | collective-permute-start | bytes 1572872 | tf_op jit(solution)/shard_map/ppermute | solution.py:537
  107.8 9.2 %collective-permute-start.18 = (bf16[32,4096]{1,0:T(8,128)(2,1)S(1)}, bf16[32,4096]{1,0:T(8,128)(2,1)S(1)}, u32[]{:S(2)}, u32[]{:S(2)}) collective-permute-start(bf16[32,4096]{1,0:T(8,128)(2,1)S(1)} %collective-permute-done.16.refs_1_), channel_id=1, source_target_pairs={{0,1},{1,2},{2,3},{3,0},{4,5},{5,6},{6,7},{7,4},{8,9},{9,10},{10,1... | collective-permute-start | bytes 786440 | tf_op jit(solution)/shard_map/ppermute | solution.py:518

commit v12 on v11

--- a/solution.py
+++ b/solution.py
@@ -488,32 +488,6 @@
     )(in_hbm(x), gain, parts)
 
 
-def place_kernel(*refs):
-    pieces, (out_hbm, sems) = refs[:RING], refs[RING:]
-    rows = pieces[0].shape[0]
-    copies = []
-    for i, k in enumerate(ORDER):
-        at = pl.multiple_of((lax.axis_index("mp") + k) % RING * rows, rows)
-        copies.append(pltpu.make_async_copy(pieces[i], out_hbm.at[pl.ds(at, rows), :], sems.at[i]))
-        copies[-1].start()
-    for copy in copies:
-        copy.wait()
-
-
-def place(pieces):
-    rows, width = pieces[0].shape
-    return pl.pallas_call(
-        place_kernel,
-        in_specs=[ANY] * RING,
-        out_specs=HBM,
-        out_shape=pltpu.HBM((RING * rows, width), BF16),
-        scratch_shapes=[pltpu.SemaphoreType.DMA((RING,))],
-        compiler_params=params(),
-        cost_estimate=cost(0, 4 * RING * rows * width),
-        name="place",
-    )(*pieces)
-
-
 def shift(value, axis, k):
     return lax.ppermute(value, axis, [(i, (i + k) % RING) for i in range(RING)])
 
@@ -678,13 +652,22 @@
 
 
 def own_kernel(own_hbm, other_hbm, *refs):
-    parts, outs, (base_ref, out_buf, base_sems, out_sems) = refs[:4], refs[4:6], refs[6:]
+    parts, quarters, outs, states_hbm = refs[:4], refs[4 : 4 + RING], refs[4 + RING : 6 + RING], refs[6 + RING]
+    base_ref, out_buf, base_sems, out_sems, quarter_sems = refs[7 + RING :]
     gets = [
         pltpu.make_async_copy(base, base_ref.at[m], base_sems.at[m])
         for m, base in enumerate((own_hbm, other_hbm))
     ]
     for get in gets:
         get.start()
+    rows = quarters[0].shape[0]
+    places = []
+    for i, k in enumerate(ORDER):
+        at = pl.multiple_of((lax.axis_index("mp") + k) % RING * rows, rows)
+        places.append(
+            pltpu.make_async_copy(quarters[i], states_hbm.at[pl.ds(at, rows), :], quarter_sems.at[i])
+        )
+        places[-1].start()
     core = lax.axis_index("section")
     chunks = out_sems.shape[1]
     size = out_buf.shape[1] // chunks
@@ -709,28 +692,31 @@
             total_of = base_ref[m, at].astype(F32) + parts[2 * m][at].astype(F32)
             out_buf[m, at] = total_of + parts[2 * m + 1][at].astype(F32)
             write(m, c)
+    wait_all(places)
     for m in range(2):
         for c in range(chunks):
             put(m, c, outs[0]).wait()
 
 
-def own_blocks(own, other, parts):
+def own_blocks(own, other, parts, quarters):
     block, cols = own.shape
+    rows, width = quarters[0].shape
     return pl.pallas_call(
         own_kernel,
-        in_specs=[HBM] * 2 + [VMEM] * 4,
-        out_specs=[HBM] * 2,
-        out_shape=[pltpu.HBM((block, cols), F32)] * 2,
+        in_specs=[HBM] * 2 + [VMEM] * 4 + [ANY] * RING,
+        out_specs=[HBM] * 3,
+        out_shape=[pltpu.HBM((block, cols), F32)] * 2 + [pltpu.HBM((RING * rows, width), BF16)],
         scratch_shapes=[
             pltpu.VMEM((2, block, cols), BF16),
             pltpu.VMEM((2, block, cols), F32),
             pltpu.SemaphoreType.DMA((2,)),
             pltpu.SemaphoreType.DMA((2, 4)),
+            pltpu.SemaphoreType.DMA((RING,)),
         ],
         compiler_params=params(),
-        cost_estimate=cost(4 * block * cols, 20 * block * cols),
+        cost_estimate=cost(4 * block * cols, 28 * block * cols),
         name="own",
-    )(in_hbm(own), in_hbm(other), *parts)
+    )(in_hbm(own), in_hbm(other), *parts, *quarters)
 
 
 def per_device(states, gains, proj_a, proj_b, cotangent, src_len, tgt_len, dest):
@@ -777,10 +763,9 @@
         moved(left_other, 3, REDUCE, True),
     ]
     quarter = rms_back(rows, gains, parts)
-    quarters = gathered(quarter, "mp")
-    grad_a, grad_b = own_blocks(own, crossed, sums)
-    quarters[3], grad_a = lax.optimization_barrier((quarters[3], grad_a))
-    grad_states = place(quarters)
+    before, after = shift(quarter, "mp", 1), shift(quarter, "mp", 3)
+    quarters = [quarter, before, after, shift(after, "mp", 3)]
+    grad_a, grad_b, grad_states = own_blocks(own, crossed, sums, quarters)
     return (grad_states[None], grad_a[None], grad_b[None])
 
 

time: 119 us -> 119 us (level)
  waiting for transfers between devices: 41.1 us -> 42.4 us
    ppermute x6, waiting for transfers between devices: 16.2 us -> 18.7 us  [shift(): return lax.ppermute(value, axis, [(i, (i + k) % RING) for i in range(RING)])]
    ppermute x12, waiting for transfers between devices: 7.5 us -> 6.29 us  [moved(): return lax.ppermute(value, ('section', 'z', 'x'), pairs)]
    pallas_call x2 -> x1, Pallas kernels: 3.47 us -> 2.87 us  [own_blocks(): pl.pallas_call(own_kernel, in_specs=[HBM] * 2 + [VMEM] * 4 + [ANY] * RING...]
  transfers between devices with their start and end apart: 26 -> 26, of which waited for: 13 -> 12; matrix products, arithmetic and copies ran while one was open for 0% -> 0% of each run, Pallas kernels for 19% -> 17%
where the time goes in v12:
time: 119 us
  waiting for transfers between devices  42.4 us (36%)
  starting transfers between devices  40.7 us (34%)
  Pallas kernels  34.7 us (29%)
    ppermute x6, waiting for transfers between devices, shift(): return lax.ppermute(value, axis, [(i, (i + k) % RING) for i in range(RING)])  18.7 us
    ppermute x12, starting transfers between devices, moved(): return lax.ppermute(value, ('section', 'z', 'x'), pairs)  16.6 us
    pallas_call x1, Pallas kernels, forward(): pl.pallas_call(forward_kernel, in_specs=[HBM] * 5, out_specs=[VMEM] * 4,...  9.1 us
    pallas_call x1, Pallas kernels, dnorm_partial(): pl.pallas_call(dnorm_kernel, in_specs=[VMEM] * 2 + [HBM] * 2, out_specs=H...  9.07 us
    all_to_all x1, starting transfers between devices, per_device(): lax.all_to_all(slots, ('z', 'x'), split_axis=0, concat_axis=0, tiled=True)  8.37 us
    all_to_all x1, waiting for transfers between devices, per_device(): lax.all_to_all(back, ('z', 'x'), split_axis=0, concat_axis=0, tiled=True)  7.49 us
    all_to_all x1, waiting for transfers between devices, per_device(): lax.all_to_all(slots, ('z', 'x'), split_axis=0, concat_axis=0, tiled=True)  6.99 us
    ppermute x6, starting transfers between devices, shift(): return lax.ppermute(value, axis, [(i, (i + k) % RING) for i in range(RING)])  6.94 us
  transfers between devices with their start and end apart: 26, of which 12 were waited for; matrix products, arithmetic and copies ran while one was open for 0% of the time, Pallas kernels for 17%

profile of v12, /device:TPU:0, one launch (start us, length us, event | category | flops | bytes accessed | tf_op | source)
XLA Modules:
  0.0 118.9 jit_solution(13586101308648477661)
XLA Ops:
  0.7 9.1 %forward.1 = (bf16[128,1024]{1,0:T(8,128)(2,1)S(1)}, bf16[128,1024]{1,0:T(8,128)(2,1)S(1)}, bf16[4,32,1024]{2,1,0:T(8,128)(2,1)S(1)}, bf16[4,32,1024]{2,1,0:T(8,128)(2,1)S(1)}) custom-call(bf16[128,4096]{1,0:T(8,128)(2,1)} %bitcast.18, f32[1,4096]{1,0:T(1,128)} %gain_ref.1, bf16[128,4096]{1,0:T(8,128)(2,1)} %cot_hbm.1, bf16[4096,1024]{1,0:T(8,128)(2,1)} %bitcast.13, ...), custom_call_target="tpu_custom_call" | custom-call | flops 134217728 | bytes 1048576 | tf_op jit(solution)/shard_map/forward/pallas_call | solution.py:196
  9.8 0.1 collective-permute-start
  9.9 0.5 collective-permute-start.1
  10.4 1.0 collective-permute-done.got_ref
  11.4 0.4 collective-permute-done.1.other_ref
  11.8 1.2 pack.1
  12.9 8.4 %all-to-all-start = ((bf16[16,16,1024]{2,1,0:T(8,128)(2,1)}), bf16[16,16,1024]{2,1,0:T(8,128)(2,1)S(1)}, u32[]{:S(2)}, u32[]{:S(2)}) async-start(bf16[16,16,1024]{2,1,0:T(8,128)(2,1)} %bitcast.3), calls=%async_computation | async-start | bytes 1048576 | tf_op jit(solution)/shard_map/all_to_all | solution.py:732
  21.3 1.9 %collective-permute-start.2 = (bf16[2,32,1024]{2,1,0:T(8,128)(2,1)S(1)}, bf16[2,32,1024]{2,1,0:T(8,128)(2,1)S(1)}, u32[]{:S(2)}, u32[]{:S(2)}) collective-permute-start(bf16[2,32,1024]{2,1,0:T(8,128)(2,1)S(1)} %get-tuple-element.54), channel_id=1, source_target_pairs={{0,4},{4,8},{8,12},{12,0},{16,20},{20,24},{24,28},{28,16},{32,36},... | collective-permute-start | bytes 393224 | tf_op jit(solution)/shard_map/ppermute | solution.py:511
  23.2 1.4 %collective-permute-start.3 = (bf16[2,32,1024]{2,1,0:T(8,128)(2,1)S(1)}, bf16[2,32,1024]{2,1,0:T(8,128)(2,1)S(1)}, u32[]{:S(2)}, u32[]{:S(2)}) collective-permute-start(bf16[2,32,1024]{2,1,0:T(8,128)(2,1)S(1)} %get-tuple-element.55), channel_id=1, source_target_pairs={{0,12},{4,0},{8,4},{12,8},{16,28},{20,16},{24,20},{28,24},{32,44},... | collective-permute-start | bytes 393224 | tf_op jit(solution)/shard_map/ppermute | solution.py:511
  24.6 2.2 %collective-permute-start.4 = (bf16[2,32,1024]{2,1,0:T(8,128)(2,1)S(1)}, bf16[2,32,1024]{2,1,0:T(8,128)(2,1)S(1)}, u32[]{:S(2)}, u32[]{:S(2)}) collective-permute-start(bf16[2,32,1024]{2,1,0:T(8,128)(2,1)S(1)} %get-tuple-element.56), channel_id=1, source_target_pairs={{0,8},{4,12},{8,0},{12,4},{16,24},{20,28},{24,16},{28,20},{32,40},... | collective-permute-start | bytes 393224 | tf_op jit(solution)/shard_map/ppermute | solution.py:511
  26.8 7.0 %all-to-all-done = bf16[16,16,1024]{2,1,0:T(8,128)(2,1)S(1)} async-done(((bf16[16,16,1024]{2,1,0:T(8,128)(2,1)}), bf16[16,16,1024]{2,1,0:T(8,128)(2,1)S(1)}, u32[]{:S(2)}, u32[]{:S(2)}) %all-to-all-start) | async-done | bytes 524320 | tf_op jit(solution)/shard_map/all_to_all | solution.py:732
  33.8 2.9 %attend.1 = (bf16[128,1024]{1,0:T(8,128)(2,1)S(1)}, bf16[256,1024]{1,0:T(8,128)(2,1)}) custom-call(bf16[128,1024]{1,0:T(8,128)(2,1)S(1)} %get-tuple-element.47.keep_ref, bf16[128,1024]{1,0:T(8,128)(2,1)S(1)} %collective-permute-done.got_ref, bf16[256,1024]{1,0:T(8,128)(2,1)S(1)} %bitcast.12, s32[16,16]{1,0:T(8,128)S(1)} %copy-done.1, ...), custom_call_target="tpu_custom_call" | custom-call | flops 50331648 | bytes 131072 | tf_op jit(solution)/shard_map/attend/pallas_call | solution.py:302
  36.7 0.0 collective-permute-done.2.refs_1_
  36.7 0.0 collective-permute-done.3.refs_2_
  36.7 0.0 collective-permute-done.4.refs_3_
  36.7 3.6 %all-to-all-start.1 = ((bf16[16,16,1024]{2,1,0:T(8,128)(2,1)}), bf16[16,16,1024]{2,1,0:T(8,128)(2,1)S(1)}, u32[]{:S(2)}, u32[]{:S(2)}) async-start(bf16[16,16,1024]{2,1,0:T(8,128)(2,1)} %bitcast.5), calls=%async_computation.1 | async-start | bytes 1048576 | tf_op jit(solution)/shard_map/all_to_all | solution.py:739
  40.4 0.0 copy-start
  40.4 3.1 %collective-permute-start.8 = (bf16[2,4,32,1024]{3,2,1,0:T(8,128)(2,1)S(1)}, bf16[2,4,32,1024]{3,2,1,0:T(8,128)(2,1)S(1)}, u32[]{:S(2)}, u32[]{:S(2)}) collective-permute-start(bf16[2,4,32,1024]{3,2,1,0:T(8,128)(2,1)S(1)} %stack.1.refs_0_), channel_id=1, source_target_pairs={{0,3},{1,0},{2,1},{3,2},{4,7},{5,4},{6,5},{7,6},{8,11},{9,8},{10,9... | collective-permute-start | bytes 1572872 | tf_op jit(solution)/shard_map/ppermute | solution.py:492
  43.5 7.5 %all-to-all-done.1 = bf16[16,16,1024]{2,1,0:T(8,128)(2,1)S(1)} async-done(((bf16[16,16,1024]{2,1,0:T(8,128)(2,1)}), bf16[16,16,1024]{2,1,0:T(8,128)(2,1)S(1)}, u32[]{:S(2)}, u32[]{:S(2)}) %all-to-all-start.1) | async-done | bytes 524320 | tf_op jit(solution)/shard_map/all_to_all | solution.py:739
  51.0 0.4 unpack.1
  51.4 0.1 collective-permute-start.5
  51.5 1.5 %collective-permute-done.5.got_ref = bf16[128,1024]{1,0:T(8,128)(2,1)S(1)} collective-permute-done((bf16[128,1024]{1,0:T(8,128)(2,1)S(1)}, bf16[128,1024]{1,0:T(8,128)(2,1)S(1)}, u32[]{:S(2)}, u32[]{:S(2)}) %collective-permute-start.5) | collective-permute-done | bytes 262176 | tf_op jit(solution)/shard_map/ppermute | solution.py:741
  53.0 0.1 join.1
  53.1 0.5 collective-permute-start.11
  53.6 1.6 %collective-permute-start.10 = (bf16[128,2048]{1,0:T(8,128)(2,1)S(1)}, bf16[128,2048]{1,0:T(8,128)(2,1)S(1)}, u32[]{:S(2)}, u32[]{:S(2)}) collective-permute-start(bf16[128,2048]{1,0:T(8,128)(2,1)S(1)} %get-tuple-element.70.rows_ref.refs_4_), channel_id=1, source_target_pairs={{0,4},{4,8},{8,12},{12,0},{16,20},{20,24},{24,28},{28,16},{32,36},... | collective-permute-start | bytes 1572872 | tf_op jit(solution)/shard_map/ppermute | solution.py:511
  55.2 1.8 %collective-permute-done.7.refs_1_ = bf16[2,4,32,1024]{3,2,1,0:T(8,128)(2,1)} collective-permute-done((bf16[2,4,32,1024]{3,2,1,0:T(8,128)(2,1)S(1)}, bf16[2,4,32,1024]{3,2,1,0:T(8,128)(2,1)}, u32[]{:S(2)}, u32[]{:S(2)}) %collective-permute-start.7) | collective-permute-done | bytes 524320 | tf_op jit(solution)/shard_map/ppermute | solution.py:492
  57.0 0.6 collective-permute-start.9
  57.6 2.5 %collective-permute-start.12 = (bf16[128,2048]{1,0:T(8,128)(2,1)S(1)}, bf16[128,2048]{1,0:T(8,128)(2,1)S(1)}, u32[]{:S(2)}, u32[]{:S(2)}) collective-permute-start(bf16[128,2048]{1,0:T(8,128)(2,1)S(1)} %get-tuple-element.70.rows_ref.refs_4_), channel_id=1, source_target_pairs={{0,8},{4,12},{8,0},{12,4},{16,24},{20,28},{24,16},{28,20},{32,40},... | collective-permute-start | bytes 1572872 | tf_op jit(solution)/shard_map/ppermute | solution.py:511
  60.0 9.1 %dnorm.1 = bf16[128,4096]{1,0:T(8,128)(2,1)} custom-call(bf16[128,2048]{1,0:T(8,128)(2,1)S(1)} %get-tuple-element.70.rows_ref.refs_4_, bf16[128,1024]{1,0:T(8,128)(2,1)S(1)} %collective-permute-done.6.got_ref, bf16[4096,1024]{1,0:T(8,128)(2,1)} %bitcast.14, bf16[4096,1024]{1,0:T(8,128)(2,1)} %bitcast.16), custom_call_target="tpu_custom_call" | custom-call | flops 134217728 | bytes 1048576 | tf_op jit(solution)/shard_map/dnorm/pallas_call | solution.py:447
  69.1 0.0 copy-start.3
  69.2 0.4 collective-permute-done.10.refs_5_
  69.6 4.5 %all-to-all-start.2 = ((bf16[4,32,4096]{2,1,0:T(8,128)(2,1)}), bf16[4,32,4096]{2,1,0:T(8,128)(2,1)S(1)}, u32[]{:S(2)}, u32[]{:S(2)}) async-start(bf16[4,32,4096]{2,1,0:T(8,128)(2,1)} %bitcast.17), calls=%async_computation.2 | async-start | bytes 2097152 | tf_op jit(solution)/shard_map/all_to_all | solution.py:749
  74.1 2.5 %far.1 = (bf16[128,2048]{1,0:T(8,128)(2,1)S(1)}, bf16[128,2048]{1,0:T(8,128)(2,1)S(1)}, bf16[512,2048]{1,0:T(8,128)(2,1)S(1)}, bf16[256,1024]{1,0:T(8,128)(2,1)S(1)}) custom-call(bf16[2,4,32,1024]{3,2,1,0:T(8,128)(2,1)} %copy-done, bf16[2,4,32,1024]{3,2,1,0:T(8,128)(2,1)} %collective-permute-done.7.refs_1_, bf16[2,4,32,1024]{3,2,1,0:T(8,128)(2,1)} %copy-done.5, ...), custom_call_target="tpu_custom_call" | custom-call | flops 50331648 | bytes 524288 | tf_op jit(solution)/shard_map/far/pallas_call | solution.py:573
  76.6 0.1 collective-permute-start.13
  76.7 1.2 collective-permute-start.14
  77.8 2.1 %collective-permute-start.15 = (bf16[128,2048]{1,0:T(8,128)(2,1)S(1)}, bf16[128,2048]{1,0:T(8,128)(2,1)S(1)}, u32[]{:S(2)}, u32[]{:S(2)}) collective-permute-start(bf16[128,2048]{1,0:T(8,128)(2,1)S(1)} %get-tuple-element.80), channel_id=1, source_target_pairs={{0,48},{4,52},{8,56},{12,60},{16,0},{20,4},{24,8},{28,12},{32,16},... | collective-permute-start | bytes 1572872 | tf_op jit(solution)/shard_map/ppermute | solution.py:511
  80.0 2.4 %middle.1.own_hbm = bf16[256,1024]{1,0:T(8,128)(2,1)} custom-call(bf16[2,4,32,1024]{3,2,1,0:T(8,128)(2,1)} %copy-done, bf16[2,4,32,1024]{3,2,1,0:T(8,128)(2,1)} %collective-permute-done.7.refs_1_, bf16[2,4,32,1024]{3,2,1,0:T(8,128)(2,1)} %copy-done.5, bf16[2,4,32,1024]{3,2,1,0:T(8,128)(2,1)} %collective-permute-done.9.refs_3_, ...), custom_call_target="tpu_custom_call" | custom-call | flops 16777216 | bytes 262144 | tf_op jit(solution)/shard_map/middle/pallas_call | solution.py:640
  82.4 4.7 %collective-permute-done.14.refs_5_ = bf16[128,2048]{1,0:T(8,128)(2,1)S(1)} collective-permute-done((bf16[128,2048]{1,0:T(8,128)(2,1)S(1)}, bf16[128,2048]{1,0:T(8,128)(2,1)S(1)}, u32[]{:S(2)}, u32[]{:S(2)}) %collective-permute-start.14) | collective-permute-done | bytes 524320 | tf_op jit(solution)/shard_map/ppermute | solution.py:511
  87.1 2.9 %side.1 = (bf16[256,1024]{1,0:T(8,128)(2,1)S(1)}, bf16[256,1024]{1,0:T(8,128)(2,1)S(1)}, bf16[256,1024]{1,0:T(8,128)(2,1)S(1)}, bf16[256,1024]{1,0:T(8,128)(2,1)S(1)}) custom-call(bf16[2,4,32,1024]{3,2,1,0:T(8,128)(2,1)} %copy-done, bf16[2,4,32,1024]{3,2,1,0:T(8,128)(2,1)} %collective-permute-done.7.refs_1_, bf16[2,4,32,1024]{3,2,1,0:T(8,128)(2,1)} %copy-done.5, ...), custom_call_target="tpu_custom_call" | custom-call | flops 67108864 | bytes 262144 | tf_op jit(solution)/shard_map/side/pallas_call | solution.py:614
  90.1 1.2 rms_back.1.refs_4_
  91.3 3.3 %collective-permute-start.21 = (bf16[32,4096]{1,0:T(8,128)(2,1)S(1)}, bf16[32,4096]{1,0:T(8,128)(2,1)S(1)}, u32[]{:S(2)}, u32[]{:S(2)}) collective-permute-start(bf16[32,4096]{1,0:T(8,128)(2,1)S(1)} %rms_back.1.refs_4_), channel_id=1, source_target_pairs={{0,3},{1,0},{2,1},{3,2},{4,7},{5,4},{6,5},{7,6},{8,11},{9,8},{10,9... | collective-permute-start | bytes 786440 | tf_op jit(solution)/shard_map/ppermute | solution.py:492
  94.6 1.4 %collective-permute-start.16 = (bf16[256,1024]{1,0:T(8,128)(2,1)S(1)}, bf16[256,1024]{1,0:T(8,128)(2,1)S(1)}, u32[]{:S(2)}, u32[]{:S(2)}) collective-permute-start(bf16[256,1024]{1,0:T(8,128)(2,1)S(1)} %get-tuple-element.81), channel_id=1, source_target_pairs={{0,16},{4,20},{8,24},{12,28},{16,32},{20,36},{24,40},{28,44},{32,4... | collective-permute-start | bytes 1572872 | tf_op jit(solution)/shard_map/ppermute | solution.py:511
  96.0 1.9 %collective-permute-start.17 = (bf16[256,1024]{1,0:T(8,128)(2,1)S(1)}, bf16[256,1024]{1,0:T(8,128)(2,1)S(1)}, u32[]{:S(2)}, u32[]{:S(2)}) collective-permute-start(bf16[256,1024]{1,0:T(8,128)(2,1)S(1)} %get-tuple-element.82), channel_id=1, source_target_pairs={{0,48},{4,52},{8,56},{12,60},{16,0},{20,4},{24,8},{28,12},{32,16},... | collective-permute-start | bytes 1572872 | tf_op jit(solution)/shard_map/ppermute | solution.py:511
  97.8 2.1 %collective-permute-done.21.refs_6_ = bf16[32,4096]{1,0:T(8,128)(2,1)S(1)} collective-permute-done((bf16[32,4096]{1,0:T(8,128)(2,1)S(1)}, bf16[32,4096]{1,0:T(8,128)(2,1)S(1)}, u32[]{:S(2)}, u32[]{:S(2)}) %collective-permute-start.21) | collective-permute-done | bytes 262176 | tf_op jit(solution)/shard_map/ppermute | solution.py:492
  99.9 7.9 %collective-permute-done.20.refs_5_ = bf16[32,4096]{1,0:T(8,128)(2,1)S(1)} collective-permute-done((bf16[32,4096]{1,0:T(8,128)(2,1)S(1)}, bf16[32,4096]{1,0:T(8,128)(2,1)S(1)}, u32[]{:S(2)}, u32[]{:S(2)}) %collective-permute-start.20) | collective-permute-done | bytes 262176 | tf_op jit(solution)/shard_map/ppermute | solution.py:492
  107.8 1.1 collective-permute-done.18.refs_2_
  108.9 6.9 %collective-permute-done.22.refs_7_ = bf16[32,4096]{1,0:T(8,128)(2,1)S(1)} collective-permute-done((bf16[32,4096]{1,0:T(8,128)(2,1)S(1)}, bf16[32,4096]{1,0:T(8,128)(2,1)S(1)}, u32[]{:S(2)}, u32[]{:S(2)}) %collective-permute-start.22) | collective-permute-done | bytes 262176 | tf_op jit(solution)/shard_map/ppermute | solution.py:492
  115.8 2.9 %own.1 = (f32[256,1024]{1,0:T(8,128)}, f32[256,1024]{1,0:T(8,128)}, bf16[128,4096]{1,0:T(8,128)(2,1)}) custom-call(bf16[256,1024]{1,0:T(8,128)(2,1)} %middle.1.own_hbm, bf16[256,1024]{1,0:T(8,128)(2,1)} %copy-done.6, bf16[256,1024]{1,0:T(8,128)(2,1)S(1)} %collective-permute-done.16.refs_0_, bf16[256,1024]{1,0:T(8,128)(2,1)S(1)} %collective-permute-done.17.refs_1_, ...), custom_call_target="tpu_custom_call" | custom-call | flops 65536 | bytes 458752 | tf_op jit(solution)/shard_map/own/pallas_call | solution.py:704
  (30 shorter events, 0.1 us)
Async XLA Ops:
  0.6 11.1 %copy-start.1 = (s32[16,16]{1,0:T(8,128)S(1)}, s32[16,16]{1,0:T(8,128)}, u32[]{:S(2)}) copy-start(s32[16,16]{1,0:T(8,128)} %src_ref.5) | copy-start | bytes 3076
  0.6 11.1 %copy-start.2 = (s32[16,16]{1,0:T(8,128)S(1)}, s32[16,16]{1,0:T(8,128)}, u32[]{:S(2)}) copy-start(s32[16,16]{1,0:T(8,128)} %dest_ref.5) | copy-start | bytes 3076
  0.7 33.1 %copy-start.4 = (s32[16,16]{1,0:T(8,128)S(1)}, s32[16,16]{1,0:T(8,128)}, u32[]{:S(2)}) copy-start(s32[16,16]{1,0:T(8,128)} %tgt_ref.1) | copy-start | bytes 3076
  9.8 1.6 %collective-permute-start = (bf16[128,1024]{1,0:T(8,128)(2,1)S(1)}, bf16[128,1024]{1,0:T(8,128)(2,1)S(1)}, u32[]{:S(2)}, u32[]{:S(2)}) collective-permute-start(bf16[128,1024]{1,0:T(8,128)(2,1)S(1)} %get-tuple-element.48), channel_id=1, source_target_pairs={{0,64},{64,0},{1,65},{65,1},{2,66},{66,2},{3,67},{67,3},{4,68},{68... | collective-permute-start | bytes 786440 | tf_op jit(solution)/shard_map/ppermute | solution.py:728
  9.9 1.9 %collective-permute-start.1 = (bf16[4,32,1024]{2,1,0:T(8,128)(2,1)S(1)}, bf16[4,32,1024]{2,1,0:T(8,128)(2,1)S(1)}, u32[]{:S(2)}, u32[]{:S(2)}) collective-permute-start(bf16[4,32,1024]{2,1,0:T(8,128)(2,1)S(1)} %get-tuple-element.50), channel_id=1, source_target_pairs={{0,64},{64,0},{1,65},{65,1},{2,66},{66,2},{3,67},{67,3},{4,68},{68... | collective-permute-start | bytes 786440 | tf_op jit(solution)/shard_map/ppermute | solution.py:729
  12.9 20.8 %all-to-all-start = ((bf16[16,16,1024]{2,1,0:T(8,128)(2,1)}), bf16[16,16,1024]{2,1,0:T(8,128)(2,1)S(1)}, u32[]{:S(2)}, u32[]{:S(2)}) async-start(bf16[16,16,1024]{2,1,0:T(8,128)(2,1)} %bitcast.3), calls=%async_computation | async-start | bytes 1048576 | tf_op jit(solution)/shard_map/all_to_all | solution.py:732
  21.3 15.4 %collective-permute-start.2 = (bf16[2,32,1024]{2,1,0:T(8,128)(2,1)S(1)}, bf16[2,32,1024]{2,1,0:T(8,128)(2,1)S(1)}, u32[]{:S(2)}, u32[]{:S(2)}) collective-permute-start(bf16[2,32,1024]{2,1,0:T(8,128)(2,1)S(1)} %get-tuple-element.54), channel_id=1, source_target_pairs={{0,4},{4,8},{8,12},{12,0},{16,20},{20,24},{24,28},{28,16},{32,36},... | collective-permute-start | bytes 393224 | tf_op jit(solution)/shard_map/ppermute | solution.py:511
  23.2 13.5 %collective-permute-start.3 = (bf16[2,32,1024]{2,1,0:T(8,128)(2,1)S(1)}, bf16[2,32,1024]{2,1,0:T(8,128)(2,1)S(1)}, u32[]{:S(2)}, u32[]{:S(2)}) collective-permute-start(bf16[2,32,1024]{2,1,0:T(8,128)(2,1)S(1)} %get-tuple-element.55), channel_id=1, source_target_pairs={{0,12},{4,0},{8,4},{12,8},{16,28},{20,16},{24,20},{28,24},{32,44},... | collective-permute-start | bytes 393224 | tf_op jit(solution)/shard_map/ppermute | solution.py:511
  24.6 12.1 %collective-permute-start.4 = (bf16[2,32,1024]{2,1,0:T(8,128)(2,1)S(1)}, bf16[2,32,1024]{2,1,0:T(8,128)(2,1)S(1)}, u32[]{:S(2)}, u32[]{:S(2)}) collective-permute-start(bf16[2,32,1024]{2,1,0:T(8,128)(2,1)S(1)} %get-tuple-element.56), channel_id=1, source_target_pairs={{0,8},{4,12},{8,0},{12,4},{16,24},{20,28},{24,16},{28,20},{32,40},... | collective-permute-start | bytes 393224 | tf_op jit(solution)/shard_map/ppermute | solution.py:511
  36.7 14.2 %all-to-all-start.1 = ((bf16[16,16,1024]{2,1,0:T(8,128)(2,1)}), bf16[16,16,1024]{2,1,0:T(8,128)(2,1)S(1)}, u32[]{:S(2)}, u32[]{:S(2)}) async-start(bf16[16,16,1024]{2,1,0:T(8,128)(2,1)} %bitcast.5), calls=%async_computation.1 | async-start | bytes 1048576 | tf_op jit(solution)/shard_map/all_to_all | solution.py:739
  40.4 28.8 %copy-start = (bf16[2,4,32,1024]{3,2,1,0:T(8,128)(2,1)}, bf16[2,4,32,1024]{3,2,1,0:T(8,128)(2,1)S(1)}, u32[]{:S(2)}) copy-start(bf16[2,4,32,1024]{3,2,1,0:T(8,128)(2,1)S(1)} %stack.1.refs_0_) | copy-start | bytes 1572868
  40.4 14.8 %collective-permute-start.8 = (bf16[2,4,32,1024]{3,2,1,0:T(8,128)(2,1)S(1)}, bf16[2,4,32,1024]{3,2,1,0:T(8,128)(2,1)S(1)}, u32[]{:S(2)}, u32[]{:S(2)}) collective-permute-start(bf16[2,4,32,1024]{3,2,1,0:T(8,128)(2,1)S(1)} %stack.1.refs_0_), channel_id=1, source_target_pairs={{0,3},{1,0},{2,1},{3,2},{4,7},{5,4},{6,5},{7,6},{8,11},{9,8},{10,9... | collective-permute-start | bytes 1572872 | tf_op jit(solution)/shard_map/ppermute | solution.py:492
  43.5 13.5 %collective-permute-start.7 = (bf16[2,4,32,1024]{3,2,1,0:T(8,128)(2,1)S(1)}, bf16[2,4,32,1024]{3,2,1,0:T(8,128)(2,1)}, u32[]{:S(2)}, u32[]{:S(2)}) collective-permute-start(bf16[2,4,32,1024]{3,2,1,0:T(8,128)(2,1)S(1)} %stack.1.refs_0_), channel_id=1, source_target_pairs={{0,1},{1,2},{2,3},{3,0},{4,5},{5,6},{6,7},{7,4},{8,9},{9,10},{10,1... | collective-permute-start | bytes 1572872 | tf_op jit(solution)/shard_map/ppermute | solution.py:492
  51.4 1.6 %collective-permute-start.5 = (bf16[128,1024]{1,0:T(8,128)(2,1)S(1)}, bf16[128,1024]{1,0:T(8,128)(2,1)S(1)}, u32[]{:S(2)}, u32[]{:S(2)}) collective-permute-start(bf16[128,1024]{1,0:T(8,128)(2,1)S(1)} %get-tuple-element.64), channel_id=1, source_target_pairs={{0,64},{64,0},{1,65},{65,1},{2,66},{66,2},{3,67},{67,3},{4,68},{68... | collective-permute-start | bytes 786440 | tf_op jit(solution)/shard_map/ppermute | solution.py:741
  53.1 16.1 %collective-permute-start.11 = (bf16[128,2048]{1,0:T(8,128)(2,1)S(1)}, bf16[128,2048]{1,0:T(8,128)(2,1)S(1)}, u32[]{:S(2)}, u32[]{:S(2)}) collective-permute-start(bf16[128,2048]{1,0:T(8,128)(2,1)S(1)} %get-tuple-element.70.rows_ref.refs_4_), channel_id=1, source_target_pairs={{0,12},{4,0},{8,4},{12,8},{16,28},{20,16},{24,20},{28,24},{32,44},... | collective-permute-start | bytes 1572872 | tf_op jit(solution)/shard_map/ppermute | solution.py:511
  53.6 16.0 %collective-permute-start.10 = (bf16[128,2048]{1,0:T(8,128)(2,1)S(1)}, bf16[128,2048]{1,0:T(8,128)(2,1)S(1)}, u32[]{:S(2)}, u32[]{:S(2)}) collective-permute-start(bf16[128,2048]{1,0:T(8,128)(2,1)S(1)} %get-tuple-element.70.rows_ref.refs_4_), channel_id=1, source_target_pairs={{0,4},{4,8},{8,12},{12,0},{16,20},{20,24},{24,28},{28,16},{32,36},... | collective-permute-start | bytes 1572872 | tf_op jit(solution)/shard_map/ppermute | solution.py:511
  55.2 4.9 %collective-permute-start.6 = (bf16[128,1024]{1,0:T(8,128)(2,1)S(1)}, bf16[128,1024]{1,0:T(8,128)(2,1)S(1)}, u32[]{:S(2)}, u32[]{:S(2)}) collective-permute-start(bf16[128,1024]{1,0:T(8,128)(2,1)S(1)} %get-tuple-element.65), channel_id=1, source_target_pairs={{0,64},{64,0},{1,65},{65,1},{2,66},{66,2},{3,67},{67,3},{4,68},{68... | collective-permute-start | bytes 786440 | tf_op jit(solution)/shard_map/ppermute | solution.py:745
  55.2 1.8 %copy-start.5 = (bf16[2,4,32,1024]{3,2,1,0:T(8,128)(2,1)}, bf16[2,4,32,1024]{3,2,1,0:T(8,128)(2,1)S(1)}, u32[]{:S(2)}) copy-start(bf16[2,4,32,1024]{3,2,1,0:T(8,128)(2,1)S(1)} %collective-permute-done.8.refs_2_) | copy-start | bytes 1572868
  57.0 17.1 %collective-permute-start.9 = (bf16[2,4,32,1024]{3,2,1,0:T(8,128)(2,1)}, bf16[2,4,32,1024]{3,2,1,0:T(8,128)(2,1)}, u32[]{:S(2)}, u32[]{:S(2)}) collective-permute-start(bf16[2,4,32,1024]{3,2,1,0:T(8,128)(2,1)} %collective-permute-done.7.refs_1_), channel_id=1, source_target_pairs={{0,1},{1,2},{2,3},{3,0},{4,5},{5,6},{6,7},{7,4},{8,9},{9,10},{10,1... | collective-permute-start | bytes 1572872 | tf_op jit(solution)/shard_map/ppermute | solution.py:492
  57.6 16.5 %collective-permute-start.12 = (bf16[128,2048]{1,0:T(8,128)(2,1)S(1)}, bf16[128,2048]{1,0:T(8,128)(2,1)S(1)}, u32[]{:S(2)}, u32[]{:S(2)}) collective-permute-start(bf16[128,2048]{1,0:T(8,128)(2,1)S(1)} %get-tuple-element.70.rows_ref.refs_4_), channel_id=1, source_target_pairs={{0,8},{4,12},{8,0},{12,4},{16,24},{20,28},{24,16},{28,20},{32,40},... | collective-permute-start | bytes 1572872 | tf_op jit(solution)/shard_map/ppermute | solution.py:511
  69.1 21.0 %copy-start.3 = (f32[1,4096]{1,0:T(1,128)S(1)}, f32[1,4096]{1,0:T(1,128)}, u32[]{:S(2)}) copy-start(f32[1,4096]{1,0:T(1,128)} %gain_ref.1) | copy-start | bytes 49156
  69.6 20.5 %all-to-all-start.2 = ((bf16[4,32,4096]{2,1,0:T(8,128)(2,1)}), bf16[4,32,4096]{2,1,0:T(8,128)(2,1)S(1)}, u32[]{:S(2)}, u32[]{:S(2)}) async-start(bf16[4,32,4096]{2,1,0:T(8,128)(2,1)} %bitcast.17), calls=%async_computation.2 | async-start | bytes 2097152 | tf_op jit(solution)/shard_map/all_to_all | solution.py:749
  76.6 5.8 %collective-permute-start.13 = (bf16[256,1024]{1,0:T(8,128)(2,1)S(1)}, bf16[256,1024]{1,0:T(8,128)(2,1)S(1)}, u32[]{:S(2)}, u32[]{:S(2)}) collective-permute-start(bf16[256,1024]{1,0:T(8,128)(2,1)S(1)} %get-tuple-element.75), channel_id=1, source_target_pairs={{0,64},{64,0},{1,65},{65,1},{2,66},{66,2},{3,67},{67,3},{4,68},{68... | collective-permute-start | bytes 1572872 | tf_op jit(solution)/shard_map/ppermute | solution.py:755
  76.7 10.5 %collective-permute-start.14 = (bf16[128,2048]{1,0:T(8,128)(2,1)S(1)}, bf16[128,2048]{1,0:T(8,128)(2,1)S(1)}, u32[]{:S(2)}, u32[]{:S(2)}) collective-permute-start(bf16[128,2048]{1,0:T(8,128)(2,1)S(1)} %get-tuple-element.79), channel_id=1, source_target_pairs={{0,16},{4,20},{8,24},{12,28},{16,32},{20,36},{24,40},{28,44},{32,4... | collective-permute-start | bytes 1572872 | tf_op jit(solution)/shard_map/ppermute | solution.py:511
  77.8 9.3 %collective-permute-start.15 = (bf16[128,2048]{1,0:T(8,128)(2,1)S(1)}, bf16[128,2048]{1,0:T(8,128)(2,1)S(1)}, u32[]{:S(2)}, u32[]{:S(2)}) collective-permute-start(bf16[128,2048]{1,0:T(8,128)(2,1)S(1)} %get-tuple-element.80), channel_id=1, source_target_pairs={{0,48},{4,52},{8,56},{12,60},{16,0},{20,4},{24,8},{28,12},{32,16},... | collective-permute-start | bytes 1572872 | tf_op jit(solution)/shard_map/ppermute | solution.py:511
  82.4 4.7 %copy-start.6 = (bf16[256,1024]{1,0:T(8,128)(2,1)}, bf16[256,1024]{1,0:T(8,128)(2,1)S(1)}, u32[]{:S(2)}) copy-start(bf16[256,1024]{1,0:T(8,128)(2,1)S(1)} %collective-permute-done.13.other_hbm) | copy-start | bytes 1572868
  91.3 8.6 %collective-permute-start.21 = (bf16[32,4096]{1,0:T(8,128)(2,1)S(1)}, bf16[32,4096]{1,0:T(8,128)(2,1)S(1)}, u32[]{:S(2)}, u32[]{:S(2)}) collective-permute-start(bf16[32,4096]{1,0:T(8,128)(2,1)S(1)} %rms_back.1.refs_4_), channel_id=1, source_target_pairs={{0,3},{1,0},{2,1},{3,2},{4,7},{5,4},{6,5},{7,6},{8,11},{9,8},{10,9... | collective-permute-start | bytes 786440 | tf_op jit(solution)/shard_map/ppermute | solution.py:492
  94.6 13.2 %collective-permute-start.16 = (bf16[256,1024]{1,0:T(8,128)(2,1)S(1)}, bf16[256,1024]{1,0:T(8,128)(2,1)S(1)}, u32[]{:S(2)}, u32[]{:S(2)}) collective-permute-start(bf16[256,1024]{1,0:T(8,128)(2,1)S(1)} %get-tuple-element.81), channel_id=1, source_target_pairs={{0,16},{4,20},{8,24},{12,28},{16,32},{20,36},{24,40},{28,44},{32,4... | collective-permute-start | bytes 1572872 | tf_op jit(solution)/shard_map/ppermute | solution.py:511
  96.0 11.9 %collective-permute-start.17 = (bf16[256,1024]{1,0:T(8,128)(2,1)S(1)}, bf16[256,1024]{1,0:T(8,128)(2,1)S(1)}, u32[]{:S(2)}, u32[]{:S(2)}) collective-permute-start(bf16[256,1024]{1,0:T(8,128)(2,1)S(1)} %get-tuple-element.82), channel_id=1, source_target_pairs={{0,48},{4,52},{8,56},{12,60},{16,0},{20,4},{24,8},{28,12},{32,16},... | collective-permute-start | bytes 1572872 | tf_op jit(solution)/shard_map/ppermute | solution.py:511
  97.8 11.1 %collective-permute-start.18 = (bf16[256,1024]{1,0:T(8,128)(2,1)S(1)}, bf16[256,1024]{1,0:T(8,128)(2,1)S(1)}, u32[]{:S(2)}, u32[]{:S(2)}) collective-permute-start(bf16[256,1024]{1,0:T(8,128)(2,1)S(1)} %get-tuple-element.83), channel_id=1, source_target_pairs={{0,80},{4,84},{8,88},{12,92},{16,96},{20,100},{24,104},{28,108},{3... | collective-permute-start | bytes 1572872 | tf_op jit(solution)/shard_map/ppermute | solution.py:511
  97.8 10.0 %collective-permute-start.20 = (bf16[32,4096]{1,0:T(8,128)(2,1)S(1)}, bf16[32,4096]{1,0:T(8,128)(2,1)S(1)}, u32[]{:S(2)}, u32[]{:S(2)}) collective-permute-start(bf16[32,4096]{1,0:T(8,128)(2,1)S(1)} %rms_back.1.refs_4_), channel_id=1, source_target_pairs={{0,1},{1,2},{2,3},{3,0},{4,5},{5,6},{6,7},{7,4},{8,9},{9,10},{10,1... | collective-permute-start | bytes 786440 | tf_op jit(solution)/shard_map/ppermute | solution.py:492
  99.9 15.9 %collective-permute-start.19 = (bf16[256,1024]{1,0:T(8,128)(2,1)S(1)}, bf16[256,1024]{1,0:T(8,128)(2,1)S(1)}, u32[]{:S(2)}, u32[]{:S(2)}) collective-permute-start(bf16[256,1024]{1,0:T(8,128)(2,1)S(1)} %get-tuple-element.86), channel_id=1, source_target_pairs={{0,112},{4,116},{8,120},{12,124},{16,64},{20,68},{24,72},{28,76},{... | collective-permute-start | bytes 1572872 | tf_op jit(solution)/shard_map/ppermute | solution.py:511
  107.8 8.0 %collective-permute-start.22 = (bf16[32,4096]{1,0:T(8,128)(2,1)S(1)}, bf16[32,4096]{1,0:T(8,128)(2,1)S(1)}, u32[]{:S(2)}, u32[]{:S(2)}) collective-permute-start(bf16[32,4096]{1,0:T(8,128)(2,1)S(1)} %collective-permute-done.21.refs_6_), channel_id=1, source_target_pairs={{0,3},{1,0},{2,1},{3,2},{4,7},{5,4},{6,5},{7,6},{8,11},{9,8},{10,9... | collective-permute-start | bytes 786440 | tf_op jit(solution)/shard_map/ppermute | solution.py:492

commit v13 on v7

--- a/solution.py
+++ b/solution.py
@@ -101,10 +101,6 @@
     get_x.start()
     get_gain.start()
 
-    @pl.when(core != 0)
-    def _():
-        get_left.start()
-
     def fetch(k):
         rows = pl.ds(k * step, step)
         return (
@@ -113,14 +109,27 @@
         )
 
     for k in range(count):
-        for copy in fetch(k):
-            copy.start()
+        copy_a, copy_b = fetch(k)
+        copy_a.start()
+        if k == 0:
+
+            @pl.when(core != 0)
+            def _():
+                get_left.start()
+
+        copy_b.start()
     get_x.wait()
     get_gain.wait()
     xf = x_ref[...].astype(F32)
     scale = lax.rsqrt(jnp.mean(xf * xf, axis=-1, keepdims=True) + EPS)
     normed_ref[...] = (xf * scale * gain_ref[...]).astype(BF16)
 
+    def product(ref, k, buf):
+        return jnp.dot(ref[:, k * step : (k + 1) * step], buf[k], preferred_element_type=F32)
+
+    fetch(0)[0].wait()
+    acc_a = product(normed_ref, 0, a_buf)
+
     @pl.when(core == 0)
     def _():
         left_ref[...] = normed_ref[...]
@@ -129,6 +138,8 @@
     def _():
         get_left.wait()
 
+    fetch(0)[1].wait()
+    acc_b = product(left_ref, 0, b_buf)
     z, x = lax.axis_index("z"), lax.axis_index("x")
     quarter = pl.ds(pl.multiple_of(lax.axis_index("mp") * QUARTER, QUARTER), QUARTER)
     block = cols // RING
@@ -150,15 +161,11 @@
                 )
                 copies[-1].start()
 
-    acc_a = acc_b = None
-    for k in range(count):
+    for k in range(1, count):
         for copy in fetch(k):
             copy.wait()
-        at = slice(k * step, (k + 1) * step)
-        part_a = jnp.dot(normed_ref[:, at], a_buf[k], preferred_element_type=F32)
-        part_b = jnp.dot(left_ref[:, at], b_buf[k], preferred_element_type=F32)
-        acc_a = part_a if acc_a is None else acc_a + part_a
-        acc_b = part_b if acc_b is None else acc_b + part_b
+        acc_a += product(normed_ref, k, a_buf)
+        acc_b += product(left_ref, k, b_buf)
     half = cols // 2
     parts = [[acc[:, i * half : (i + 1) * half].astype(BF16) for acc in (acc_a, acc_b)] for i in range(2)]
 
@@ -240,12 +247,8 @@
 
 
 def attend_kernel(
-    keep_ref, got_ref, slots_ref, src_ref, tgt_ref, dest_ref, *rest
+    keep_ref, got_ref, slots_ref, src_ref, tgt_ref, dest_ref, front_ref, back_ref, own_ref
 ):
-    front_ref, back_ref, stack_ref, own_ref = rest[RING:]
-    for p in range(RING):
-        for m in range(2):
-            stack_ref[m, p] = rest[p][m]
     mask = pair_mask(member_index(), src_ref, tgt_ref, dest_ref)
 
     @pl.when(lax.axis_index("section") == 0)
@@ -294,23 +297,40 @@
         back_ref[:, second] = fold(tn(weight, dout))
 
 
-def attend(keep, got, slots, src_len, tgt_len, dest, pieces):
+def attend(keep, got, slots, src_len, tgt_len, dest):
     rows, width = keep.shape
-    _, quarter, cols = pieces[0].shape
     return pl.pallas_call(
         attend_kernel,
-        in_specs=[VMEM] * (6 + RING),
-        out_specs=[VMEM] * 3,
+        in_specs=[VMEM] * 6,
+        out_specs=[VMEM] * 2,
         out_shape=[
             jax.ShapeDtypeStruct((rows, width), BF16),
             jax.ShapeDtypeStruct((SLOTS, width), BF16),
-            jax.ShapeDtypeStruct((2, RING, quarter, cols), BF16),
         ],
         scratch_shapes=[pltpu.VMEM((rows, width), BF16)],
         compiler_params=params(),
         cost_estimate=cost(24 * rows * SLOTS * width, 8 * SLOTS * width),
         name="attend",
-    )(keep, got, slots, src_len, tgt_len, dest, *pieces)
+    )(keep, got, slots, src_len, tgt_len, dest)
+
+
+def stack_kernel(*refs):
+    for p in range(RING):
+        for m in range(2):
+            refs[RING][m, p] = refs[p][m]
+
+
+def stacked(pieces):
+    _, quarter, cols = pieces[0].shape
+    return pl.pallas_call(
+        stack_kernel,
+        in_specs=[VMEM] * RING,
+        out_specs=VMEM,
+        out_shape=jax.ShapeDtypeStruct((2, RING, quarter, cols), BF16),
+        compiler_params=params(),
+        cost_estimate=cost(0, 4 * RING * pieces[0].size),
+        name="stack",
+    )(*pieces)
 
 
 def unpack_kernel(back_ref, front_ref, src_ref, dest_ref, keep_ref, send_ref):
@@ -718,8 +738,9 @@
     slots = lax.all_to_all(slots, ("z", "x"), split_axis=0, concat_axis=0, tiled=True)
     slots = slots.reshape(SLOTS, width)
     pieces = fetched(slices[0], {1: slices[1], 3: slices[2], 2: slices[3]})
-    front, back, own = attend(keep, got, slots, src_len, tgt_len, dest, pieces)
-    lefts = gathered(own, "mp")
+    front, back = attend(keep, got, slots, src_len, tgt_len, dest)
+    back, pieces = lax.optimization_barrier((back, pieces))
+    lefts = gathered(stacked(pieces), "mp")
     back = back.reshape(SEQ_DEV, MAXLEN, width)
     back = lax.all_to_all(back, ("z", "x"), split_axis=0, concat_axis=0, tiled=True)
     keep, send = unpack(back.reshape(SLOTS, width), front, src_len, dest)

time: 117 us -> 115 us (0.983)
  starting transfers between devices: 46.2 us -> 44.8 us
  waiting for transfers between devices: 32.6 us -> 31.3 us
    ppermute x12, waiting for transfers between devices: 19.6 us -> 12.3 us  [moved(): return lax.ppermute(value, ('section', 'z', 'x'), pairs)]
    all_to_all x1, waiting for transfers between devices: 0.01 us -> 6.99 us  [per_device(): lax.all_to_all(slots, ('z', 'x'), split_axis=0, concat_axis=0, tiled=True)]
    all_to_all x1, starting transfers between devices: 4.96 us -> 3.59 us  [per_device(): lax.all_to_all(back, ('z', 'x'), split_axis=0, concat_axis=0, tiled=True)]
    pallas_call x1 -> x2, Pallas kernels: 2.95 us -> 2.98 us  [the longest x1 2.94 us: attend(): pl.pallas_call(attend_kernel, in_specs=[VMEM] * 6, out_specs=[VMEM] * 2,...]
  transfers between devices with their start and end apart: 26 -> 26, of which waited for: 11 -> 11; matrix products, arithmetic and copies ran while one was open for 0% -> 0% of each run, Pallas kernels for 17% -> 20%
where the time goes in v13:
time: 115 us; the launch traced here: 113 us
  starting transfers between devices  44.8 us (39%)
  Pallas kernels  35.2 us (31%)
  waiting for transfers between devices  31.3 us (27%)
    ppermute x12, starting transfers between devices, moved(): return lax.ppermute(value, ('section', 'z', 'x'), pairs)  18.4 us
    ppermute x12, waiting for transfers between devices, moved(): return lax.ppermute(value, ('section', 'z', 'x'), pairs)  12.3 us
    pallas_call x1, Pallas kernels, forward(): pl.pallas_call(forward_kernel, in_specs=[HBM] * 5, out_specs=[VMEM] * 4,...  9.1 us
    pallas_call x1, Pallas kernels, dnorm_partial(): pl.pallas_call(dnorm_kernel, in_specs=[VMEM] * 2 + [HBM] * 2, out_specs=H...  9.08 us
    ppermute x6, starting transfers between devices, shift(): return lax.ppermute(value, axis, [(i, (i + k) % RING) for i in range(RING)])  9.06 us
    all_to_all x1, starting transfers between devices, per_device(): lax.all_to_all(slots, ('z', 'x'), split_axis=0, concat_axis=0, tiled=True)  8.37 us
    all_to_all x1, waiting for transfers between devices, per_device(): lax.all_to_all(back, ('z', 'x'), split_axis=0, concat_axis=0, tiled=True)  7.28 us
    all_to_all x1, waiting for transfers between devices, per_device(): lax.all_to_all(slots, ('z', 'x'), split_axis=0, concat_axis=0, tiled=True)  6.99 us
  transfers between devices with their start and end apart: 26, of which 11 were waited for; matrix products, arithmetic and copies ran while one was open for 0% of the time, Pallas kernels for 20%

profile of v13, /device:TPU:0, one launch (start us, length us, event | category | flops | bytes accessed | tf_op | source)
XLA Modules:
  0.0 113.1 jit_solution(17750600693149166958)
XLA Ops:
  0.7 9.1 %forward.1 = (bf16[128,1024]{1,0:T(8,128)(2,1)S(1)}, bf16[128,1024]{1,0:T(8,128)(2,1)S(1)}, bf16[4,32,1024]{2,1,0:T(8,128)(2,1)S(1)}, bf16[4,32,1024]{2,1,0:T(8,128)(2,1)S(1)}) custom-call(bf16[128,4096]{1,0:T(8,128)(2,1)} %bitcast.18, f32[1,4096]{1,0:T(1,128)} %gain_ref.1, bf16[128,4096]{1,0:T(8,128)(2,1)} %cot_hbm.1, bf16[4096,1024]{1,0:T(8,128)(2,1)} %bitcast.13, ...), custom_call_target="tpu_custom_call" | custom-call | flops 134217728 | bytes 1048576 | tf_op jit(solution)/shard_map/forward/pallas_call | solution.py:196
  9.8 0.1 collective-permute-start
  9.9 0.5 collective-permute-start.1
  10.4 1.0 collective-permute-done.got_ref
  11.4 0.4 collective-permute-done.1.other_ref
  11.8 1.2 %pack.1 = (bf16[256,1024]{1,0:T(8,128)(2,1)}, bf16[2,32,1024]{2,1,0:T(8,128)(2,1)S(1)}, bf16[2,32,1024]{2,1,0:T(8,128)(2,1)S(1)}, bf16[2,32,1024]{2,1,0:T(8,128)(2,1)S(1)}, bf16[2,32,1024]{2,1,0:T(8,128)(2,1)S(1)}) custom-call(bf16[128,1024]{1,0:T(8,128)(2,1)S(1)} %get-tuple-element.46.keep_ref, bf16[128,1024]{1,0:T(8,128)(2,1)S(1)} %collective-permute-done.got_ref, ...), custom_call_target="tpu_custom_call" | custom-call | flops 4194304 | bytes 32768 | tf_op jit(solution)/shard_map/pack/pallas_call | solution.py:236
  12.9 8.4 %all-to-all-start = ((bf16[16,16,1024]{2,1,0:T(8,128)(2,1)}), bf16[16,16,1024]{2,1,0:T(8,128)(2,1)S(1)}, u32[]{:S(2)}, u32[]{:S(2)}) async-start(bf16[16,16,1024]{2,1,0:T(8,128)(2,1)} %bitcast.3), calls=%async_computation | async-start | bytes 1048576 | tf_op jit(solution)/shard_map/all_to_all | solution.py:738
  21.3 1.9 %collective-permute-start.2 = (bf16[2,32,1024]{2,1,0:T(8,128)(2,1)S(1)}, bf16[2,32,1024]{2,1,0:T(8,128)(2,1)S(1)}, u32[]{:S(2)}, u32[]{:S(2)}) collective-permute-start(bf16[2,32,1024]{2,1,0:T(8,128)(2,1)S(1)} %get-tuple-element.53), channel_id=1, source_target_pairs={{0,4},{4,8},{8,12},{12,0},{16,20},{20,24},{24,28},{28,16},{32,36},... | collective-permute-start | bytes 393224 | tf_op jit(solution)/shard_map/ppermute | solution.py:537
  23.2 1.4 %collective-permute-start.3 = (bf16[2,32,1024]{2,1,0:T(8,128)(2,1)S(1)}, bf16[2,32,1024]{2,1,0:T(8,128)(2,1)S(1)}, u32[]{:S(2)}, u32[]{:S(2)}) collective-permute-start(bf16[2,32,1024]{2,1,0:T(8,128)(2,1)S(1)} %get-tuple-element.54), channel_id=1, source_target_pairs={{0,12},{4,0},{8,4},{12,8},{16,28},{20,16},{24,20},{28,24},{32,44},... | collective-permute-start | bytes 393224 | tf_op jit(solution)/shard_map/ppermute | solution.py:537
  24.6 2.2 %collective-permute-start.4 = (bf16[2,32,1024]{2,1,0:T(8,128)(2,1)S(1)}, bf16[2,32,1024]{2,1,0:T(8,128)(2,1)S(1)}, u32[]{:S(2)}, u32[]{:S(2)}) collective-permute-start(bf16[2,32,1024]{2,1,0:T(8,128)(2,1)S(1)} %get-tuple-element.55), channel_id=1, source_target_pairs={{0,8},{4,12},{8,0},{12,4},{16,24},{20,28},{24,16},{28,20},{32,40},... | collective-permute-start | bytes 393224 | tf_op jit(solution)/shard_map/ppermute | solution.py:537
  26.8 7.0 %all-to-all-done = bf16[16,16,1024]{2,1,0:T(8,128)(2,1)S(1)} async-done(((bf16[16,16,1024]{2,1,0:T(8,128)(2,1)}), bf16[16,16,1024]{2,1,0:T(8,128)(2,1)S(1)}, u32[]{:S(2)}, u32[]{:S(2)}) %all-to-all-start) | async-done | bytes 524320 | tf_op jit(solution)/shard_map/all_to_all | solution.py:738
  33.8 2.9 %attend.1 = (bf16[128,1024]{1,0:T(8,128)(2,1)S(1)}, bf16[256,1024]{1,0:T(8,128)(2,1)}) custom-call(bf16[128,1024]{1,0:T(8,128)(2,1)S(1)} %get-tuple-element.46.keep_ref, bf16[128,1024]{1,0:T(8,128)(2,1)S(1)} %collective-permute-done.got_ref, bf16[256,1024]{1,0:T(8,128)(2,1)S(1)} %bitcast.12, s32[16,16]{1,0:T(8,128)S(1)} %copy-done.1, ...), custom_call_target="tpu_custom_call" | custom-call | flops 50331648 | bytes 131072 | tf_op jit(solution)/shard_map/attend/pallas_call | solution.py:302
  36.7 3.6 %all-to-all-start.1 = ((bf16[16,16,1024]{2,1,0:T(8,128)(2,1)}), bf16[16,16,1024]{2,1,0:T(8,128)(2,1)S(1)}, u32[]{:S(2)}, u32[]{:S(2)}) async-start(bf16[16,16,1024]{2,1,0:T(8,128)(2,1)} %bitcast.5), calls=%async_computation.1 | async-start | bytes 1048576 | tf_op jit(solution)/shard_map/all_to_all | solution.py:745
  40.4 0.0 copy-start
  40.4 1.7 %collective-permute-start.7 = (bf16[2,4,32,1024]{3,2,1,0:T(8,128)(2,1)S(1)}, bf16[2,4,32,1024]{3,2,1,0:T(8,128)(2,1)}, u32[]{:S(2)}, u32[]{:S(2)}) collective-permute-start(bf16[2,4,32,1024]{3,2,1,0:T(8,128)(2,1)S(1)} %stack.1.refs_0_), channel_id=1, source_target_pairs={{0,1},{1,2},{2,3},{3,0},{4,5},{5,6},{6,7},{7,4},{8,9},{9,10},{10,1... | collective-permute-start | bytes 1572872 | tf_op jit(solution)/shard_map/ppermute | solution.py:518
  42.0 1.6 %collective-permute-start.8 = (bf16[2,4,32,1024]{3,2,1,0:T(8,128)(2,1)S(1)}, bf16[2,4,32,1024]{3,2,1,0:T(8,128)(2,1)S(1)}, u32[]{:S(2)}, u32[]{:S(2)}) collective-permute-start(bf16[2,4,32,1024]{3,2,1,0:T(8,128)(2,1)S(1)} %stack.1.refs_0_), channel_id=1, source_target_pairs={{0,3},{1,0},{2,1},{3,2},{4,7},{5,4},{6,5},{7,6},{8,11},{9,8},{10,9... | collective-permute-start | bytes 1572872 | tf_op jit(solution)/shard_map/ppermute | solution.py:518
  43.7 7.3 %all-to-all-done.1 = bf16[16,16,1024]{2,1,0:T(8,128)(2,1)S(1)} async-done(((bf16[16,16,1024]{2,1,0:T(8,128)(2,1)}), bf16[16,16,1024]{2,1,0:T(8,128)(2,1)S(1)}, u32[]{:S(2)}, u32[]{:S(2)}) %all-to-all-start.1) | async-done | bytes 524320 | tf_op jit(solution)/shard_map/all_to_all | solution.py:745
  51.0 0.4 unpack.1
  51.4 0.1 collective-permute-start.5
  51.5 1.5 %collective-permute-done.5.got_ref = bf16[128,1024]{1,0:T(8,128)(2,1)S(1)} collective-permute-done((bf16[128,1024]{1,0:T(8,128)(2,1)S(1)}, bf16[128,1024]{1,0:T(8,128)(2,1)S(1)}, u32[]{:S(2)}, u32[]{:S(2)}) %collective-permute-start.5) | collective-permute-done | bytes 262176 | tf_op jit(solution)/shard_map/ppermute | solution.py:747
  53.0 0.1 join.1
  53.1 0.6 collective-permute-start.9
  53.7 2.7 %collective-permute-start.10 = (bf16[128,2048]{1,0:T(8,128)(2,1)S(1)}, bf16[128,2048]{1,0:T(8,128)(2,1)S(1)}, u32[]{:S(2)}, u32[]{:S(2)}) collective-permute-start(bf16[128,2048]{1,0:T(8,128)(2,1)S(1)} %get-tuple-element.60.rows_ref.refs_4_), channel_id=1, source_target_pairs={{0,12},{4,0},{8,4},{12,8},{16,28},{20,16},{24,20},{28,24},{32,44},... | collective-permute-start | bytes 1572872 | tf_op jit(solution)/shard_map/ppermute | solution.py:537
  56.4 0.8 copy-done.5
  57.2 1.6 %collective-permute-start.11 = (bf16[2,4,32,1024]{3,2,1,0:T(8,128)(2,1)}, bf16[2,4,32,1024]{3,2,1,0:T(8,128)(2,1)}, u32[]{:S(2)}, u32[]{:S(2)}) collective-permute-start(bf16[2,4,32,1024]{3,2,1,0:T(8,128)(2,1)} %collective-permute-done.7.refs_1_), channel_id=1, source_target_pairs={{0,1},{1,2},{2,3},{3,0},{4,5},{5,6},{6,7},{7,4},{8,9},{9,10},{10,1... | collective-permute-start | bytes 1572872 | tf_op jit(solution)/shard_map/ppermute | solution.py:518
  58.8 0.9 collective-permute-start.12
  59.6 9.1 %dnorm.1 = bf16[128,4096]{1,0:T(8,128)(2,1)} custom-call(bf16[128,2048]{1,0:T(8,128)(2,1)S(1)} %get-tuple-element.60.rows_ref.refs_4_, bf16[128,1024]{1,0:T(8,128)(2,1)S(1)} %collective-permute-done.6.got_ref, bf16[4096,1024]{1,0:T(8,128)(2,1)} %bitcast.14, bf16[4096,1024]{1,0:T(8,128)(2,1)} %bitcast.16), custom_call_target="tpu_custom_call" | custom-call | flops 134217728 | bytes 1048576 | tf_op jit(solution)/shard_map/dnorm/pallas_call | solution.py:447
  68.8 4.7 %all-to-all-start.2 = ((bf16[4,32,4096]{2,1,0:T(8,128)(2,1)}), bf16[4,32,4096]{2,1,0:T(8,128)(2,1)S(1)}, u32[]{:S(2)}, u32[]{:S(2)}) async-start(bf16[4,32,4096]{2,1,0:T(8,128)(2,1)} %bitcast.17), calls=%async_computation.2 | async-start | bytes 2097152 | tf_op jit(solution)/shard_map/all_to_all | solution.py:755
  73.4 2.0 %far.1 = (bf16[128,2048]{1,0:T(8,128)(2,1)S(1)}, bf16[128,2048]{1,0:T(8,128)(2,1)S(1)}, bf16[512,2048]{1,0:T(8,128)(2,1)S(1)}) custom-call(bf16[2,4,32,1024]{3,2,1,0:T(8,128)(2,1)} %copy-done, bf16[2,4,32,1024]{3,2,1,0:T(8,128)(2,1)} %collective-permute-done.7.refs_1_, bf16[2,4,32,1024]{3,2,1,0:T(8,128)(2,1)} %copy-done.5, ...), custom_call_target="tpu_custom_call" | custom-call | flops 33554432 | bytes 524288 | tf_op jit(solution)/shard_map/far/pallas_call | solution.py:596
  75.4 1.1 collective-permute-start.13
  76.5 2.2 %collective-permute-start.14 = (bf16[128,2048]{1,0:T(8,128)(2,1)S(1)}, bf16[128,2048]{1,0:T(8,128)(2,1)S(1)}, u32[]{:S(2)}, u32[]{:S(2)}) collective-permute-start(bf16[128,2048]{1,0:T(8,128)(2,1)S(1)} %get-tuple-element.75), channel_id=1, source_target_pairs={{0,48},{4,52},{8,56},{12,60},{16,0},{20,4},{24,8},{28,12},{32,16},... | collective-permute-start | bytes 1572872 | tf_op jit(solution)/shard_map/ppermute | solution.py:537
  78.7 2.7 %middle.1 = (bf16[256,1024]{1,0:T(8,128)(2,1)}, bf16[256,1024]{1,0:T(8,128)(2,1)}) custom-call(bf16[2,4,32,1024]{3,2,1,0:T(8,128)(2,1)} %copy-done, bf16[2,4,32,1024]{3,2,1,0:T(8,128)(2,1)} %collective-permute-done.7.refs_1_, bf16[2,4,32,1024]{3,2,1,0:T(8,128)(2,1)} %copy-done.5, bf16[2,4,32,1024]{3,2,1,0:T(8,128)(2,1)} %collective-permute-done.11.refs_3_, ...), custom_call_target="tpu_custom_call" | custom-call | flops 33554432 | bytes 262144 | tf_op jit(solution)/shard_map/middle/pallas_call | solution.py:661
  81.5 4.4 %collective-permute-done.13.refs_5_ = bf16[128,2048]{1,0:T(8,128)(2,1)S(1)} collective-permute-done((bf16[128,2048]{1,0:T(8,128)(2,1)S(1)}, bf16[128,2048]{1,0:T(8,128)(2,1)S(1)}, u32[]{:S(2)}, u32[]{:S(2)}) %collective-permute-start.13) | collective-permute-done | bytes 524320 | tf_op jit(solution)/shard_map/ppermute | solution.py:537
  85.9 2.9 %side.1 = (bf16[256,1024]{1,0:T(8,128)(2,1)S(1)}, bf16[256,1024]{1,0:T(8,128)(2,1)S(1)}, bf16[256,1024]{1,0:T(8,128)(2,1)S(1)}, bf16[256,1024]{1,0:T(8,128)(2,1)S(1)}) custom-call(bf16[2,4,32,1024]{3,2,1,0:T(8,128)(2,1)} %copy-done, bf16[2,4,32,1024]{3,2,1,0:T(8,128)(2,1)} %collective-permute-done.7.refs_1_, bf16[2,4,32,1024]{3,2,1,0:T(8,128)(2,1)} %copy-done.5, ...), custom_call_target="tpu_custom_call" | custom-call | flops 67108864 | bytes 262144 | tf_op jit(solution)/shard_map/side/pallas_call | solution.py:632
  88.8 1.2 %rms_back.1.refs_0_ = bf16[32,4096]{1,0:T(8,128)(2,1)S(1)} custom-call(bf16[128,4096]{1,0:T(8,128)(2,1)} %bitcast.19, f32[1,4096]{1,0:T(1,128)S(1)} %copy-done.3, bf16[4,32,4096]{2,1,0:T(8,128)(2,1)S(1)} %all-to-all-done.2.parts_ref), custom_call_target="tpu_custom_call" | custom-call | flops 81920 | bytes 98304 | tf_op jit(solution)/shard_map/rms_back/pallas_call | solution.py:479
  90.0 2.1 %collective-permute-start.15 = (bf16[32,4096]{1,0:T(8,128)(2,1)S(1)}, bf16[32,4096]{1,0:T(8,128)(2,1)S(1)}, u32[]{:S(2)}, u32[]{:S(2)}) collective-permute-start(bf16[32,4096]{1,0:T(8,128)(2,1)S(1)} %rms_back.1.refs_0_), channel_id=1, source_target_pairs={{0,1},{1,2},{2,3},{3,0},{4,5},{5,6},{6,7},{7,4},{8,9},{9,10},{10,1... | collective-permute-start | bytes 786440 | tf_op jit(solution)/shard_map/ppermute | solution.py:518
  92.1 1.3 %collective-permute-start.16 = (bf16[32,4096]{1,0:T(8,128)(2,1)S(1)}, bf16[32,4096]{1,0:T(8,128)(2,1)S(1)}, u32[]{:S(2)}, u32[]{:S(2)}) collective-permute-start(bf16[32,4096]{1,0:T(8,128)(2,1)S(1)} %rms_back.1.refs_0_), channel_id=1, source_target_pairs={{0,3},{1,0},{2,1},{3,2},{4,7},{5,4},{6,5},{7,6},{8,11},{9,8},{10,9... | collective-permute-start | bytes 786440 | tf_op jit(solution)/shard_map/ppermute | solution.py:518
  93.4 1.3 %collective-permute-start.19 = (bf16[256,1024]{1,0:T(8,128)(2,1)S(1)}, bf16[256,1024]{1,0:T(8,128)(2,1)S(1)}, u32[]{:S(2)}, u32[]{:S(2)}) collective-permute-start(bf16[256,1024]{1,0:T(8,128)(2,1)S(1)} %get-tuple-element.82), channel_id=1, source_target_pairs={{0,16},{4,20},{8,24},{12,28},{16,32},{20,36},{24,40},{28,44},{32,4... | collective-permute-start | bytes 1572872 | tf_op jit(solution)/shard_map/ppermute | solution.py:537
  94.7 2.0 %collective-permute-start.20 = (bf16[256,1024]{1,0:T(8,128)(2,1)S(1)}, bf16[256,1024]{1,0:T(8,128)(2,1)S(1)}, u32[]{:S(2)}, u32[]{:S(2)}) collective-permute-start(bf16[256,1024]{1,0:T(8,128)(2,1)S(1)} %get-tuple-element.84), channel_id=1, source_target_pairs={{0,48},{4,52},{8,56},{12,60},{16,0},{20,4},{24,8},{28,12},{32,16},... | collective-permute-start | bytes 1572872 | tf_op jit(solution)/shard_map/ppermute | solution.py:537
  96.6 1.5 %collective-permute-done.15.refs_1_ = bf16[32,4096]{1,0:T(8,128)(2,1)S(1)} collective-permute-done((bf16[32,4096]{1,0:T(8,128)(2,1)S(1)}, bf16[32,4096]{1,0:T(8,128)(2,1)S(1)}, u32[]{:S(2)}, u32[]{:S(2)}) %collective-permute-start.15) | collective-permute-done | bytes 262176 | tf_op jit(solution)/shard_map/ppermute | solution.py:518
  98.1 0.4 collective-permute-done.16.refs_2_
  98.5 2.3 %collective-permute-start.22 = (bf16[256,1024]{1,0:T(8,128)(2,1)S(1)}, bf16[256,1024]{1,0:T(8,128)(2,1)S(1)}, u32[]{:S(2)}, u32[]{:S(2)}) collective-permute-start(bf16[256,1024]{1,0:T(8,128)(2,1)S(1)} %get-tuple-element.86), channel_id=1, source_target_pairs={{0,112},{4,116},{8,120},{12,124},{16,64},{20,68},{24,72},{28,76},{... | collective-permute-start | bytes 1572872 | tf_op jit(solution)/shard_map/ppermute | solution.py:537
  100.7 0.8 collective-permute-start.17
  101.5 2.3 %collective-permute-done.19.refs_0_ = bf16[256,1024]{1,0:T(8,128)(2,1)S(1)} collective-permute-done((bf16[256,1024]{1,0:T(8,128)(2,1)S(1)}, bf16[256,1024]{1,0:T(8,128)(2,1)S(1)}, u32[]{:S(2)}, u32[]{:S(2)}) %collective-permute-start.19) | collective-permute-done | bytes 524320 | tf_op jit(solution)/shard_map/ppermute | solution.py:537
  103.8 0.1 collective-permute-done.20.refs_1_
  103.9 5.5 %collective-permute-done.21.refs_2_ = bf16[256,1024]{1,0:T(8,128)(2,1)S(1)} collective-permute-done((bf16[256,1024]{1,0:T(8,128)(2,1)S(1)}, bf16[256,1024]{1,0:T(8,128)(2,1)S(1)}, u32[]{:S(2)}, u32[]{:S(2)}) %collective-permute-start.21) | collective-permute-done | bytes 524320 | tf_op jit(solution)/shard_map/ppermute | solution.py:537
  109.4 2.5 %own.1 = (f32[256,1024]{1,0:T(8,128)}, f32[256,1024]{1,0:T(8,128)}) custom-call(bf16[256,1024]{1,0:T(8,128)(2,1)} %get-tuple-element.80.own_hbm, bf16[256,1024]{1,0:T(8,128)(2,1)S(1)} %collective-permute-done.18.other_ref, bf16[256,1024]{1,0:T(8,128)(2,1)S(1)} %collective-permute-done.19.refs_0_, bf16[256,1024]{1,0:T(8,128)(2,1)S(1)} %collective-permute-done.20.refs_1_, ...), custom_call_target="tpu_custom_call" | custom-call | flops 65536 | bytes 327680 | tf_op jit(solution)/shard_map/own/pallas_call | solution.py:711
  112.0 1.0 place.1
  (29 shorter events, 0.1 us)
Async XLA Ops:
  0.6 11.1 %copy-start.1 = (s32[16,16]{1,0:T(8,128)S(1)}, s32[16,16]{1,0:T(8,128)}, u32[]{:S(2)}) copy-start(s32[16,16]{1,0:T(8,128)} %src_ref.5) | copy-start | bytes 3076
  0.6 11.1 %copy-start.2 = (s32[16,16]{1,0:T(8,128)S(1)}, s32[16,16]{1,0:T(8,128)}, u32[]{:S(2)}) copy-start(s32[16,16]{1,0:T(8,128)} %dest_ref.5) | copy-start | bytes 3076
  0.7 33.1 %copy-start.4 = (s32[16,16]{1,0:T(8,128)S(1)}, s32[16,16]{1,0:T(8,128)}, u32[]{:S(2)}) copy-start(s32[16,16]{1,0:T(8,128)} %tgt_ref.1) | copy-start | bytes 3076
  9.8 1.6 %collective-permute-start = (bf16[128,1024]{1,0:T(8,128)(2,1)S(1)}, bf16[128,1024]{1,0:T(8,128)(2,1)S(1)}, u32[]{:S(2)}, u32[]{:S(2)}) collective-permute-start(bf16[128,1024]{1,0:T(8,128)(2,1)S(1)} %get-tuple-element.47), channel_id=1, source_target_pairs={{0,64},{64,0},{1,65},{65,1},{2,66},{66,2},{3,67},{67,3},{4,68},{68... | collective-permute-start | bytes 786440 | tf_op jit(solution)/shard_map/ppermute | solution.py:734
  9.9 1.9 %collective-permute-start.1 = (bf16[4,32,1024]{2,1,0:T(8,128)(2,1)S(1)}, bf16[4,32,1024]{2,1,0:T(8,128)(2,1)S(1)}, u32[]{:S(2)}, u32[]{:S(2)}) collective-permute-start(bf16[4,32,1024]{2,1,0:T(8,128)(2,1)S(1)} %get-tuple-element.49), channel_id=1, source_target_pairs={{0,64},{64,0},{1,65},{65,1},{2,66},{66,2},{3,67},{67,3},{4,68},{68... | collective-permute-start | bytes 786440 | tf_op jit(solution)/shard_map/ppermute | solution.py:735
  12.9 20.8 %all-to-all-start = ((bf16[16,16,1024]{2,1,0:T(8,128)(2,1)}), bf16[16,16,1024]{2,1,0:T(8,128)(2,1)S(1)}, u32[]{:S(2)}, u32[]{:S(2)}) async-start(bf16[16,16,1024]{2,1,0:T(8,128)(2,1)} %bitcast.3), calls=%async_computation | async-start | bytes 1048576 | tf_op jit(solution)/shard_map/all_to_all | solution.py:738
  21.3 15.4 %collective-permute-start.2 = (bf16[2,32,1024]{2,1,0:T(8,128)(2,1)S(1)}, bf16[2,32,1024]{2,1,0:T(8,128)(2,1)S(1)}, u32[]{:S(2)}, u32[]{:S(2)}) collective-permute-start(bf16[2,32,1024]{2,1,0:T(8,128)(2,1)S(1)} %get-tuple-element.53), channel_id=1, source_target_pairs={{0,4},{4,8},{8,12},{12,0},{16,20},{20,24},{24,28},{28,16},{32,36},... | collective-permute-start | bytes 393224 | tf_op jit(solution)/shard_map/ppermute | solution.py:537
  23.2 13.5 %collective-permute-start.3 = (bf16[2,32,1024]{2,1,0:T(8,128)(2,1)S(1)}, bf16[2,32,1024]{2,1,0:T(8,128)(2,1)S(1)}, u32[]{:S(2)}, u32[]{:S(2)}) collective-permute-start(bf16[2,32,1024]{2,1,0:T(8,128)(2,1)S(1)} %get-tuple-element.54), channel_id=1, source_target_pairs={{0,12},{4,0},{8,4},{12,8},{16,28},{20,16},{24,20},{28,24},{32,44},... | collective-permute-start | bytes 393224 | tf_op jit(solution)/shard_map/ppermute | solution.py:537
  24.6 12.1 %collective-permute-start.4 = (bf16[2,32,1024]{2,1,0:T(8,128)(2,1)S(1)}, bf16[2,32,1024]{2,1,0:T(8,128)(2,1)S(1)}, u32[]{:S(2)}, u32[]{:S(2)}) collective-permute-start(bf16[2,32,1024]{2,1,0:T(8,128)(2,1)S(1)} %get-tuple-element.55), channel_id=1, source_target_pairs={{0,8},{4,12},{8,0},{12,4},{16,24},{20,28},{24,16},{28,20},{32,40},... | collective-permute-start | bytes 393224 | tf_op jit(solution)/shard_map/ppermute | solution.py:537
  36.7 14.2 %all-to-all-start.1 = ((bf16[16,16,1024]{2,1,0:T(8,128)(2,1)}), bf16[16,16,1024]{2,1,0:T(8,128)(2,1)S(1)}, u32[]{:S(2)}, u32[]{:S(2)}) async-start(bf16[16,16,1024]{2,1,0:T(8,128)(2,1)} %bitcast.5), calls=%async_computation.1 | async-start | bytes 1048576 | tf_op jit(solution)/shard_map/all_to_all | solution.py:745
  40.4 28.4 %copy-start = (bf16[2,4,32,1024]{3,2,1,0:T(8,128)(2,1)}, bf16[2,4,32,1024]{3,2,1,0:T(8,128)(2,1)S(1)}, u32[]{:S(2)}) copy-start(bf16[2,4,32,1024]{3,2,1,0:T(8,128)(2,1)S(1)} %stack.1.refs_0_) | copy-start | bytes 1572868
  40.4 16.0 %collective-permute-start.7 = (bf16[2,4,32,1024]{3,2,1,0:T(8,128)(2,1)S(1)}, bf16[2,4,32,1024]{3,2,1,0:T(8,128)(2,1)}, u32[]{:S(2)}, u32[]{:S(2)}) collective-permute-start(bf16[2,4,32,1024]{3,2,1,0:T(8,128)(2,1)S(1)} %stack.1.refs_0_), channel_id=1, source_target_pairs={{0,1},{1,2},{2,3},{3,0},{4,5},{5,6},{6,7},{7,4},{8,9},{9,10},{10,1... | collective-permute-start | bytes 1572872 | tf_op jit(solution)/shard_map/ppermute | solution.py:518
  42.0 14.3 %collective-permute-start.8 = (bf16[2,4,32,1024]{3,2,1,0:T(8,128)(2,1)S(1)}, bf16[2,4,32,1024]{3,2,1,0:T(8,128)(2,1)S(1)}, u32[]{:S(2)}, u32[]{:S(2)}) collective-permute-start(bf16[2,4,32,1024]{3,2,1,0:T(8,128)(2,1)S(1)} %stack.1.refs_0_), channel_id=1, source_target_pairs={{0,3},{1,0},{2,1},{3,2},{4,7},{5,4},{6,5},{7,6},{8,11},{9,8},{10,9... | collective-permute-start | bytes 1572872 | tf_op jit(solution)/shard_map/ppermute | solution.py:518
  51.4 1.6 %collective-permute-start.5 = (bf16[128,1024]{1,0:T(8,128)(2,1)S(1)}, bf16[128,1024]{1,0:T(8,128)(2,1)S(1)}, u32[]{:S(2)}, u32[]{:S(2)}) collective-permute-start(bf16[128,1024]{1,0:T(8,128)(2,1)S(1)} %get-tuple-element.59), channel_id=1, source_target_pairs={{0,64},{64,0},{1,65},{65,1},{2,66},{66,2},{3,67},{67,3},{4,68},{68... | collective-permute-start | bytes 786440 | tf_op jit(solution)/shard_map/ppermute | solution.py:747
  53.1 15.7 %collective-permute-start.9 = (bf16[128,2048]{1,0:T(8,128)(2,1)S(1)}, bf16[128,2048]{1,0:T(8,128)(2,1)S(1)}, u32[]{:S(2)}, u32[]{:S(2)}) collective-permute-start(bf16[128,2048]{1,0:T(8,128)(2,1)S(1)} %get-tuple-element.60.rows_ref.refs_4_), channel_id=1, source_target_pairs={{0,4},{4,8},{8,12},{12,0},{16,20},{20,24},{24,28},{28,16},{32,36},... | collective-permute-start | bytes 1572872 | tf_op jit(solution)/shard_map/ppermute | solution.py:537
  53.7 15.1 %collective-permute-start.10 = (bf16[128,2048]{1,0:T(8,128)(2,1)S(1)}, bf16[128,2048]{1,0:T(8,128)(2,1)S(1)}, u32[]{:S(2)}, u32[]{:S(2)}) collective-permute-start(bf16[128,2048]{1,0:T(8,128)(2,1)S(1)} %get-tuple-element.60.rows_ref.refs_4_), channel_id=1, source_target_pairs={{0,12},{4,0},{8,4},{12,8},{16,28},{20,16},{24,20},{28,24},{32,44},... | collective-permute-start | bytes 1572872 | tf_op jit(solution)/shard_map/ppermute | solution.py:537
  56.4 3.3 %collective-permute-start.6 = (bf16[128,1024]{1,0:T(8,128)(2,1)S(1)}, bf16[128,1024]{1,0:T(8,128)(2,1)S(1)}, u32[]{:S(2)}, u32[]{:S(2)}) collective-permute-start(bf16[128,1024]{1,0:T(8,128)(2,1)S(1)} %get-tuple-element.61), channel_id=1, source_target_pairs={{0,64},{64,0},{1,65},{65,1},{2,66},{66,2},{3,67},{67,3},{4,68},{68... | collective-permute-start | bytes 786440 | tf_op jit(solution)/shard_map/ppermute | solution.py:751
  56.4 0.8 copy-start.5
  57.2 16.3 %collective-permute-start.11 = (bf16[2,4,32,1024]{3,2,1,0:T(8,128)(2,1)}, bf16[2,4,32,1024]{3,2,1,0:T(8,128)(2,1)}, u32[]{:S(2)}, u32[]{:S(2)}) collective-permute-start(bf16[2,4,32,1024]{3,2,1,0:T(8,128)(2,1)} %collective-permute-done.7.refs_1_), channel_id=1, source_target_pairs={{0,1},{1,2},{2,3},{3,0},{4,5},{5,6},{6,7},{7,4},{8,9},{9,10},{10,1... | collective-permute-start | bytes 1572872 | tf_op jit(solution)/shard_map/ppermute | solution.py:518
  58.8 14.7 %collective-permute-start.12 = (bf16[128,2048]{1,0:T(8,128)(2,1)S(1)}, bf16[128,2048]{1,0:T(8,128)(2,1)S(1)}, u32[]{:S(2)}, u32[]{:S(2)}) collective-permute-start(bf16[128,2048]{1,0:T(8,128)(2,1)S(1)} %get-tuple-element.60.rows_ref.refs_4_), channel_id=1, source_target_pairs={{0,8},{4,12},{8,0},{12,4},{16,24},{20,28},{24,16},{28,20},{32,40},... | collective-permute-start | bytes 1572872 | tf_op jit(solution)/shard_map/ppermute | solution.py:537
  68.7 20.1 %copy-start.3 = (f32[1,4096]{1,0:T(1,128)S(1)}, f32[1,4096]{1,0:T(1,128)}, u32[]{:S(2)}) copy-start(f32[1,4096]{1,0:T(1,128)} %gain_ref.1) | copy-start | bytes 49156
  68.8 20.0 %all-to-all-start.2 = ((bf16[4,32,4096]{2,1,0:T(8,128)(2,1)}), bf16[4,32,4096]{2,1,0:T(8,128)(2,1)S(1)}, u32[]{:S(2)}, u32[]{:S(2)}) async-start(bf16[4,32,4096]{2,1,0:T(8,128)(2,1)} %bitcast.17), calls=%async_computation.2 | async-start | bytes 2097152 | tf_op jit(solution)/shard_map/all_to_all | solution.py:755
  75.4 10.5 %collective-permute-start.13 = (bf16[128,2048]{1,0:T(8,128)(2,1)S(1)}, bf16[128,2048]{1,0:T(8,128)(2,1)S(1)}, u32[]{:S(2)}, u32[]{:S(2)}) collective-permute-start(bf16[128,2048]{1,0:T(8,128)(2,1)S(1)} %get-tuple-element.74), channel_id=1, source_target_pairs={{0,16},{4,20},{8,24},{12,28},{16,32},{20,36},{24,40},{28,44},{32,4... | collective-permute-start | bytes 1572872 | tf_op jit(solution)/shard_map/ppermute | solution.py:537
  76.5 9.4 %collective-permute-start.14 = (bf16[128,2048]{1,0:T(8,128)(2,1)S(1)}, bf16[128,2048]{1,0:T(8,128)(2,1)S(1)}, u32[]{:S(2)}, u32[]{:S(2)}) collective-permute-start(bf16[128,2048]{1,0:T(8,128)(2,1)S(1)} %get-tuple-element.75), channel_id=1, source_target_pairs={{0,48},{4,52},{8,56},{12,60},{16,0},{20,4},{24,8},{28,12},{32,16},... | collective-permute-start | bytes 1572872 | tf_op jit(solution)/shard_map/ppermute | solution.py:537
  90.0 8.1 %collective-permute-start.15 = (bf16[32,4096]{1,0:T(8,128)(2,1)S(1)}, bf16[32,4096]{1,0:T(8,128)(2,1)S(1)}, u32[]{:S(2)}, u32[]{:S(2)}) collective-permute-start(bf16[32,4096]{1,0:T(8,128)(2,1)S(1)} %rms_back.1.refs_0_), channel_id=1, source_target_pairs={{0,1},{1,2},{2,3},{3,0},{4,5},{5,6},{6,7},{7,4},{8,9},{9,10},{10,1... | collective-permute-start | bytes 786440 | tf_op jit(solution)/shard_map/ppermute | solution.py:518
  92.1 6.4 %collective-permute-start.16 = (bf16[32,4096]{1,0:T(8,128)(2,1)S(1)}, bf16[32,4096]{1,0:T(8,128)(2,1)S(1)}, u32[]{:S(2)}, u32[]{:S(2)}) collective-permute-start(bf16[32,4096]{1,0:T(8,128)(2,1)S(1)} %rms_back.1.refs_0_), channel_id=1, source_target_pairs={{0,3},{1,0},{2,1},{3,2},{4,7},{5,4},{6,5},{7,6},{8,11},{9,8},{10,9... | collective-permute-start | bytes 786440 | tf_op jit(solution)/shard_map/ppermute | solution.py:518
  93.4 7.3 %collective-permute-start.18 = (bf16[256,1024]{1,0:T(8,128)(2,1)}, bf16[256,1024]{1,0:T(8,128)(2,1)S(1)}, u32[]{:S(2)}, u32[]{:S(2)}) collective-permute-start(bf16[256,1024]{1,0:T(8,128)(2,1)} %get-tuple-element.83), channel_id=1, source_target_pairs={{0,64},{64,0},{1,65},{65,1},{2,66},{66,2},{3,67},{67,3},{4,68},{68... | collective-permute-start | bytes 1572872 | tf_op jit(solution)/shard_map/ppermute | solution.py:772
  93.4 10.4 %collective-permute-start.19 = (bf16[256,1024]{1,0:T(8,128)(2,1)S(1)}, bf16[256,1024]{1,0:T(8,128)(2,1)S(1)}, u32[]{:S(2)}, u32[]{:S(2)}) collective-permute-start(bf16[256,1024]{1,0:T(8,128)(2,1)S(1)} %get-tuple-element.82), channel_id=1, source_target_pairs={{0,16},{4,20},{8,24},{12,28},{16,32},{20,36},{24,40},{28,44},{32,4... | collective-permute-start | bytes 1572872 | tf_op jit(solution)/shard_map/ppermute | solution.py:537
  94.7 9.2 %collective-permute-start.20 = (bf16[256,1024]{1,0:T(8,128)(2,1)S(1)}, bf16[256,1024]{1,0:T(8,128)(2,1)S(1)}, u32[]{:S(2)}, u32[]{:S(2)}) collective-permute-start(bf16[256,1024]{1,0:T(8,128)(2,1)S(1)} %get-tuple-element.84), channel_id=1, source_target_pairs={{0,48},{4,52},{8,56},{12,60},{16,0},{20,4},{24,8},{28,12},{32,16},... | collective-permute-start | bytes 1572872 | tf_op jit(solution)/shard_map/ppermute | solution.py:537
  98.1 11.3 %collective-permute-start.21 = (bf16[256,1024]{1,0:T(8,128)(2,1)S(1)}, bf16[256,1024]{1,0:T(8,128)(2,1)S(1)}, u32[]{:S(2)}, u32[]{:S(2)}) collective-permute-start(bf16[256,1024]{1,0:T(8,128)(2,1)S(1)} %get-tuple-element.85), channel_id=1, source_target_pairs={{0,80},{4,84},{8,88},{12,92},{16,96},{20,100},{24,104},{28,108},{3... | collective-permute-start | bytes 1572872 | tf_op jit(solution)/shard_map/ppermute | solution.py:537
  98.5 10.9 %collective-permute-start.22 = (bf16[256,1024]{1,0:T(8,128)(2,1)S(1)}, bf16[256,1024]{1,0:T(8,128)(2,1)S(1)}, u32[]{:S(2)}, u32[]{:S(2)}) collective-permute-start(bf16[256,1024]{1,0:T(8,128)(2,1)S(1)} %get-tuple-element.86), channel_id=1, source_target_pairs={{0,112},{4,116},{8,120},{12,124},{16,64},{20,68},{24,72},{28,76},{... | collective-permute-start | bytes 1572872 | tf_op jit(solution)/shard_map/ppermute | solution.py:537
  100.7 11.2 %collective-permute-start.17 = (bf16[32,4096]{1,0:T(8,128)(2,1)S(1)}, bf16[32,4096]{1,0:T(8,128)(2,1)S(1)}, u32[]{:S(2)}, u32[]{:S(2)}) collective-permute-start(bf16[32,4096]{1,0:T(8,128)(2,1)S(1)} %collective-permute-done.15.refs_1_), channel_id=1, source_target_pairs={{0,1},{1,2},{2,3},{3,0},{4,5},{5,6},{6,7},{7,4},{8,9},{9,10},{10,1... | collective-permute-start | bytes 786440 | tf_op jit(solution)/shard_map/ppermute | solution.py:518
